TPU v7x, 128 devices: a whole 4x4x4 slice. The times are simulated.
128 devices in a mesh: dp: 64 (over y, x, z), tensor: 2 (over core).
Axes of the slice: x: 4, y: 4, z: 4, core: 2. Of those that a mesh axis runs over, the one named last changes fastest.
Arguments:
- tokens: bfloat16 [16384, 1536], P('dp'), may hold values from -6 to 6
- out_grad: bfloat16 [16384, 1536], P('dp'), may hold values from -6 to 6
- norm1_gain: float32 [1536], replicated, may hold values from 0.5 to 1.5
- norm2_gain: float32 [1536], replicated, may hold values from 0.5 to 1.5
- w_query: bfloat16 [1536, 1536], P(None, 'tensor'), may hold values from -0.15625 to 0.15625
- w_key: bfloat16 [1536, 512], P(None, 'tensor'), may hold values from -0.15625 to 0.15625
- w_value: bfloat16 [1536, 512], P(None, 'tensor'), may hold values from -0.15625 to 0.15625
- w_out: bfloat16 [1536, 1536], P('tensor'), may hold values from -1.25 to 1.25
- w_gate: bfloat16 [64, 1536, 512], P('dp', None, 'tensor'), may hold values from -0.15625 to 0.15625
- w_up: bfloat16 [64, 1536, 512], P('dp', None, 'tensor'), may hold values from -0.15625 to 0.15625
- w_down: bfloat16 [64, 512, 1536], P('dp', 'tensor'), may hold values from -1 to 1
- route_ids: int32 [16384, 8], P('dp'), may hold values from 0 to 39, all different within a row; in each aligned block of 256 rows (0 to 255, 256 to 511, ...) at most 64 rows name the same one
- route_logits: float32 [16384, 8], P('dp'), may hold values from -3 to 3
- seq_ids: int32 [16384], P('dp'), may hold values from 0 to 31, never falling along the last dimension, each value on 1 to 1024 neighbouring positions
- piece_ids: int32 [16384], P('dp'), may hold values from 0 to 64, as said below
- clip_limit: float32 [24], P('tensor'), may hold values from 3 to 9
Outputs:
- output: bfloat16 [16384, 1536], P('dp')
- input_grad: float32 [16384, 1536], P('dp')
- grad_query: float32 [1536, 1536], P(None, 'tensor')
- grad_key: float32 [1536, 512], P(None, 'tensor')
- grad_value: float32 [1536, 512], P(None, 'tensor')
- grad_out: float32 [1536, 1536], P('tensor')
- grad_norm1: float32 [1536], replicated
- grad_norm2: float32 [1536], replicated
- grad_gate: float32 [64, 1536, 512], P('dp', None, 'tensor')
- grad_up: float32 [64, 1536, 512], P('dp', None, 'tensor')
- grad_down: float32 [64, 512, 1536], P('dp', 'tensor')
- clipped_query: bfloat16 [1536, 1536], P(None, 'tensor')
- clipped_key: bfloat16 [1536, 512], P(None, 'tensor')
- head_peaks: float32 [24], P('tensor')
Inputs may be any that keep to these rules, and one draw needn't show every extreme that they name: `route_ids`: each row names 8 different experts; in the rows of one index of dp no expert is named more than 64 times, a bound that some block reaches. `seq_ids`: never falling; each sequence is 1 to 1024 consecutive tokens, the longest exactly 1024. `piece_ids`: A nonzero number k + 1 marks exactly the tokens k * 256 to (k + 1) * 256 - 1; the last 256 tokens are always marked.
All inputs are finite; a program needn't handle non-finite values.
Results may differ from a plain program's by a relative error of at most 0.018.
Values may be sent and summed in bfloat16 or wider, within the bound.
No kernel may reach another device: no remote copies, remote signals or barrier semaphores. Data moves between devices by JAX's collectives and lax.ppermute only.
A program may use at most 320 MiB of HBM per device.

v0:
```python
import math

import jax
import jax.numpy as jnp
from jax import lax
from jax.sharding import PartitionSpec as P

HD = 64
EXPERTS = 40
TOP = 8
CAP = 64
HOPS = 4


EPS = 1e-06
ROPE_BASE = 10000.0
NEG_FILL = -1e30


def copy_for_each(array, axis):
    size = lax.axis_size(axis)
    return lax.all_to_all(
        jnp.broadcast_to(array[None], (size, *array.shape)), axis, 0, 0, tiled=True
    )


def all_in_one(array, axis):
    leaves = jax.tree.leaves(array)
    turns = sorted(range(len(leaves)), key=lambda k: -leaves[k].size)
    width = (1, *leaves[turns[0]].shape)[-1]
    lines = [
        jnp.pad(leaves[k].reshape(-1), (0, -leaves[k].size % width)).reshape(-1, width)
        for k in turns
    ]
    both, at, found = (copy_for_each(jnp.concatenate(lines), axis), 0, {})
    for k, line in zip(turns, lines):
        piece = both[:, at : at + len(line)].reshape(len(both), -1)
        found[k] = piece[:, : leaves[k].size].reshape(-1, *leaves[k].shape)
        at += len(line)
    numbers = iter(range(len(leaves)))
    return jax.tree.map(lambda _: found[next(numbers)], array)


def combined_pairwise(pieces, combine):
    while len(jax.tree.leaves(pieces)[0]) > 1:
        pieces = jax.vmap(combine)(
            *(jax.tree.map(lambda part: part[side::2], pieces) for side in (0, 1))
        )
    return jax.tree.map(lambda part: part[0], pieces)


def entering(array, axis, combine, identity):
    size, index = (lax.axis_size(axis), lax.axis_index(axis))
    passed = jnp.arange(size) < index

    def kept(part, zero, own):
        part = jnp.where(
            passed.reshape(-1, *(1 for _ in own.shape)), part, jnp.asarray(zero, own.dtype)
        )
        return part

    pieces = all_in_one(array, axis)
    return combined_pairwise(jax.tree.map(kept, pieces, identity, array), combine)


def passed_along(value, axis, steps):
    count = lax.axis_size(axis)
    first, last = (max(0, -steps), min(count, count - steps))
    return lax.ppermute(value, axis, [(source, source + steps) for source in range(first, last)])


def over_copies(array, axis):
    return copy_for_each(array, axis).max(axis=0)


def of_everyone(array, axis):
    everything = copy_for_each(array, axis)
    return jnp.sum(everything, axis=0)


def in_order(tiles, dim):
    dims = list(tiles.shape[1:])
    dims[dim] *= tiles.shape[0]
    return jnp.moveaxis(tiles, 0, dim).reshape(dims)


def gather_directly(array, axis, dim):
    return in_order(copy_for_each(array, axis), dim)


def of_everyone_2(array, axis):
    return copy_for_each(array, axis).astype(jnp.float32).sum(axis=0)


def in_one(arrays, axis):
    ravelled, at, finished = (jnp.concatenate([a.reshape(-1) for a in arrays]), 0, [])
    so_far = lax.psum(ravelled, axis)
    for a in arrays:
        finished.append(so_far[at : at + a.size].reshape(a.shape))
        at += a.size
    return tuple(finished)


def rope_tables(positions, head_width):
    half_width = head_width // 2
    frequency = jnp.exp(
        jnp.arange(half_width, dtype=jnp.float32) * (-2.0 * math.log(ROPE_BASE) / head_width)
    )
    angles = positions.astype(jnp.float32)[:, None] * frequency[None, :]
    return (jnp.cos(angles), jnp.sin(angles))


def rotate(values, cosine, sine_tab):
    half_width = values.shape[-1] // 2
    first_half = values[..., :half_width]
    second = values[..., half_width:]
    cos_wide = cosine[:, None, :]
    sin_wide = sine_tab[:, None, :]
    return jnp.concatenate(
        [first_half * cos_wide - second * sin_wide, second * cos_wide + first_half * sin_wide],
        axis=-1,
    )


def join_runs(earlier, later_run):
    empty_later = later_run[0] < 0
    same_run = earlier[0] == later_run[0]
    run_id = jnp.where(empty_later, earlier[0], later_run[0])
    run_start = jnp.where(empty_later | same_run, earlier[1], later_run[1])
    return (run_id, run_start)


def rms_scale(values):
    return lax.rsqrt(jnp.mean(values * values, axis=-1, keepdims=True) + EPS)


def norm_back(grad_normed, hidden, inverse, gain):
    weighted = grad_normed * gain
    grad_gain = jnp.sum(grad_normed * hidden * inverse, axis=0)
    grad_hidden = inverse * weighted - hidden * inverse**3 * jnp.mean(
        weighted * hidden, axis=-1, keepdims=True
    )
    return (grad_hidden, grad_gain)


def shards(
    tokens,
    out_grad,
    norm1_gain,
    norm2_gain,
    w_query,
    w_key,
    w_value,
    w_out,
    w_gate,
    w_up,
    w_down,
    route_ids,
    route_logits,
    seq_ids,
    piece_ids,
    clip_limit,
):
    tok_dev, model_width = tokens.shape
    dp_size = lax.axis_size("dp")
    tensor_size = lax.axis_size("tensor")
    offset = lax.axis_index("dp") * tok_dev
    local_heads = w_query.shape[1] // HD
    local_kv = w_key.shape[1] // HD
    group_size = local_heads // local_kv
    exp_local = w_gate.shape[0]
    score_scale = float(HD) ** (-0.5)
    local_index = jnp.arange(tok_dev, dtype=jnp.int32)
    global_index = offset + local_index
    previous_ids = jnp.concatenate([seq_ids[:1] - 1, seq_ids[:-1]])
    local_start = lax.cummax(jnp.where(seq_ids != previous_ids, local_index, 0), axis=0) + offset
    carry_id, carry_start = entering(
        (seq_ids[-1], local_start[-1]), "dp", join_runs, (jnp.int32(-1), jnp.int32(0))
    )
    seq_start = jnp.where(seq_ids == carry_id, carry_start, local_start)
    cosine, sine_tab = rope_tables(global_index - seq_start, HD)
    x_float = tokens.astype(jnp.float32)
    inverse1 = rms_scale(x_float)
    normed1 = (x_float * inverse1 * norm1_gain).astype(jnp.bfloat16)
    query_pre = jnp.dot(normed1, w_query, preferred_element_type=jnp.float32).reshape(
        tok_dev, local_heads, HD
    )
    key_pre = jnp.dot(normed1, w_key, preferred_element_type=jnp.float32).reshape(
        tok_dev, local_kv, HD
    )
    value_low = jnp.dot(normed1, w_value, preferred_element_type=jnp.float32).astype(jnp.bfloat16)
    query_rot = rotate(query_pre, cosine, sine_tab).astype(jnp.bfloat16)
    key_low = rotate(key_pre, cosine, sine_tab).astype(jnp.bfloat16).reshape(tok_dev, local_kv * HD)
    key_parts = []
    value_parts = []
    index_parts = []
    for hop_count in range(HOPS, 0, -1):
        moved_key, moved_value = passed_along((key_low, value_low), "dp", hop_count)
        key_parts.append(moved_key)
        value_parts.append(moved_value)
        index_parts.append(global_index - hop_count * tok_dev)
    key_all = jnp.concatenate(key_parts + [key_low]).reshape(-1, local_kv, HD)
    value_all = jnp.concatenate(value_parts + [value_low]).reshape(-1, local_kv, HD)
    key_index = jnp.concatenate(index_parts + [global_index])
    remote_count = HOPS * tok_dev
    piece_all = jnp.concatenate([jnp.zeros((remote_count,), jnp.int32), piece_ids])
    seq_all = jnp.concatenate([jnp.full((remote_count,), -1, jnp.int32), seq_ids])
    same_piece = (
        (piece_ids[:, None] == piece_all[None, :])
        & (piece_ids[:, None] > 0)
        & (seq_ids[:, None] == seq_all[None, :])
    )
    allowed = (key_index[None, :] >= seq_start[:, None]) & (
        (key_index[None, :] <= global_index[:, None]) | same_piece
    )
    query_group = query_rot.reshape(tok_dev, local_kv, group_size, HD)

    def masked_scores():
        raw_scores = (
            jnp.einsum("qkgd,skd->kgqs", query_group, key_all, preferred_element_type=jnp.float32)
            * score_scale
        )
        return jnp.where(allowed[None, None], raw_scores, NEG_FILL)

    scores = masked_scores()
    row_max = jnp.max(scores, axis=-1, keepdims=True)
    exp_scores = jnp.exp(scores - row_max)
    exp_total = jnp.sum(exp_scores, axis=-1, keepdims=True)
    probs_low = (exp_scores / exp_total).astype(jnp.bfloat16)
    log_total = row_max + jnp.log(exp_total)
    attended_low = (
        jnp.einsum("kgqs,skd->qkgd", probs_low, value_all, preferred_element_type=jnp.float32)
        .reshape(tok_dev, local_heads * HD)
        .astype(jnp.bfloat16)
    )
    head_peaks = over_copies(jnp.max(row_max, axis=(2, 3)).reshape(local_heads), "dp")
    factor = clip_limit / jnp.maximum(head_peaks, clip_limit)
    key_factor = jnp.min(factor.reshape(local_kv, group_size), axis=1)
    clipped_query = (
        w_query.astype(jnp.float32) * jnp.repeat(jnp.sqrt(factor), HD)[None, :]
    ).astype(jnp.bfloat16)
    clipped_key = (
        w_key.astype(jnp.float32) * jnp.repeat(jnp.sqrt(key_factor), HD)[None, :]
    ).astype(jnp.bfloat16)
    attn_full = of_everyone(
        jnp.dot(attended_low, w_out, preferred_element_type=jnp.float32), "tensor"
    )
    hidden1 = x_float + attn_full
    inverse2 = rms_scale(hidden1)
    normed2 = (hidden1 * inverse2 * norm2_gain).astype(jnp.bfloat16)
    gate_exp = jnp.exp(route_logits - jnp.max(route_logits, axis=-1, keepdims=True))
    gates = gate_exp / jnp.sum(gate_exp, axis=-1, keepdims=True)
    flat_expert = route_ids.reshape(-1)
    flat_token = jnp.arange(tok_dev * TOP, dtype=jnp.int32) // TOP
    onehot = (flat_expert[:, None] == jnp.arange(EXPERTS, dtype=jnp.int32)[None, :]).astype(
        jnp.int32
    )
    slot_rank = jnp.sum(jnp.cumsum(onehot, axis=0) * onehot, axis=1) - 1
    flat_slot = (flat_expert % exp_local * dp_size + flat_expert // exp_local) * CAP + slot_rank
    slot_count = exp_local * dp_size * CAP
    slot_token = jnp.full((slot_count,), tok_dev, jnp.int32).at[flat_slot].set(flat_token)
    slot_gate = jnp.zeros((slot_count,), jnp.float32).at[flat_slot].set(gates.reshape(-1))

    def to_owners(table, slot_scale):
        half_width = model_width // tensor_size
        table = lax.dynamic_slice_in_dim(
            table, lax.axis_index("tensor") * half_width, half_width, 1
        )
        rows = table[slot_token]
        if slot_scale is not None:
            rows = (slot_scale[:, None] * rows).astype(jnp.bfloat16)
        rows = rows.reshape(exp_local, dp_size, CAP, -1)
        got = lax.all_to_all(rows, "dp", split_axis=1, concat_axis=1, tiled=True)
        got = lax.all_gather(got, "tensor", axis=3, tiled=True)
        return got.reshape(exp_local, dp_size * CAP, model_width)

    def combine_rows(slot_rows, weights):
        picked = slot_rows[flat_slot].reshape(tok_dev, TOP, slot_rows.shape[-1])
        return jnp.sum(weights[:, :, None] * picked, axis=1)

    def from_owners(partial_value, weights):
        reduced = lax.psum_scatter(
            partial_value.astype(jnp.bfloat16), "tensor", scatter_dimension=2, tiled=True
        ).astype(jnp.float32)
        returned = lax.all_to_all(
            reduced.reshape(exp_local, dp_size, CAP, -1).astype(jnp.bfloat16),
            "dp",
            split_axis=1,
            concat_axis=1,
            tiled=True,
        ).astype(jnp.float32)
        joined = combine_rows(returned.reshape(slot_count, -1), weights)
        return gather_directly(joined.astype(jnp.bfloat16), "tensor", 1).astype(joined.dtype)

    padded_norm = jnp.concatenate([normed2, jnp.zeros((1, model_width), jnp.bfloat16)])
    rows_in = to_owners(padded_norm, None)
    gate_act = jnp.einsum("erd,edf->erf", rows_in, w_gate, preferred_element_type=jnp.float32)
    up_act = jnp.einsum("erd,edf->erf", rows_in, w_up, preferred_element_type=jnp.float32)
    sigmoid_val = jax.nn.sigmoid(gate_act)
    silu_val = gate_act * sigmoid_val
    inner_act = (silu_val * up_act).astype(jnp.bfloat16)
    expert_out = jnp.einsum("erf,efd->erd", inner_act, w_down, preferred_element_type=jnp.float32)
    mixed = from_owners(expert_out, gates)
    output = (hidden1 + mixed).astype(jnp.bfloat16)
    grad_top = out_grad.astype(jnp.float32)
    padded_grad = jnp.concatenate([grad_top, jnp.zeros((1, model_width), jnp.float32)])
    grad_rows = to_owners(padded_grad, slot_gate)
    grad_down = jnp.einsum("erf,erd->efd", inner_act, grad_rows, preferred_element_type=jnp.float32)
    grad_inner = jnp.einsum("erd,efd->erf", grad_rows, w_down, preferred_element_type=jnp.float32)
    grad_gate_act = (
        grad_inner * up_act * (sigmoid_val * (1.0 + gate_act * (1.0 - sigmoid_val)))
    ).astype(jnp.bfloat16)
    grad_up_act = (grad_inner * silu_val).astype(jnp.bfloat16)
    grad_gate = jnp.einsum(
        "erd,erf->edf", rows_in, grad_gate_act, preferred_element_type=jnp.float32
    )
    grad_up = jnp.einsum("erd,erf->edf", rows_in, grad_up_act, preferred_element_type=jnp.float32)
    grad_rows_in = jnp.einsum(
        "erf,edf->erd", grad_gate_act, w_gate, preferred_element_type=jnp.float32
    ) + jnp.einsum("erf,edf->erd", grad_up_act, w_up, preferred_element_type=jnp.float32)
    grad_normed2 = from_owners(grad_rows_in, jnp.ones((tok_dev, TOP), jnp.float32))
    grad_from_norm2, grad_gain2 = norm_back(grad_normed2, hidden1, inverse2, norm2_gain)
    grad_hidden1 = grad_top + grad_from_norm2
    grad_branch = grad_hidden1.astype(jnp.bfloat16)
    grad_wo = jnp.einsum("tk,td->kd", attended_low, grad_branch, preferred_element_type=jnp.float32)
    grad_attended = jnp.einsum(
        "td,kd->tk", grad_branch, w_out, preferred_element_type=jnp.float32
    ).astype(jnp.bfloat16)
    grad_attended = grad_attended.reshape(tok_dev, local_kv, group_size, HD)
    prob_full = jnp.exp(masked_scores() - log_total)
    probs_again = prob_full.astype(jnp.bfloat16)
    grad_probs = jnp.einsum(
        "qkgd,skd->kgqs", grad_attended, value_all, preferred_element_type=jnp.float32
    )
    delta_rows = jnp.sum(prob_full * grad_probs, axis=-1, keepdims=True)
    grad_scores = (prob_full * (grad_probs - delta_rows)).astype(jnp.bfloat16)
    grad_query_rot = (
        jnp.einsum("kgqs,skd->qkgd", grad_scores, key_all, preferred_element_type=jnp.float32)
        * score_scale
    )
    grad_key_all = (
        jnp.einsum("kgqs,qkgd->skd", grad_scores, query_group, preferred_element_type=jnp.float32)
        * score_scale
    )
    grad_value_all = jnp.einsum(
        "kgqs,qkgd->skd", probs_again, grad_attended, preferred_element_type=jnp.float32
    )
    grad_key_rows = grad_key_all.reshape(-1, local_kv * HD)
    grad_value_rows = grad_value_all.reshape(-1, local_kv * HD)
    key_total = grad_key_rows[remote_count:]
    value_total = grad_value_rows[remote_count:]
    for hop_count in range(HOPS, 0, -1):
        row_begin = (HOPS - hop_count) * tok_dev
        back_key, back_value = (
            passed_along(
                grad_key_rows[row_begin : row_begin + tok_dev].astype(jnp.bfloat16),
                "dp",
                -hop_count,
            ).astype(jnp.float32),
            passed_along(
                grad_value_rows[row_begin : row_begin + tok_dev].astype(jnp.bfloat16),
                "dp",
                -hop_count,
            ).astype(jnp.float32),
        )
        key_total = key_total + back_key
        value_total = value_total + back_value
    grad_query_pre = (
        rotate(grad_query_rot.reshape(tok_dev, local_heads, HD), cosine, -sine_tab)
        .astype(jnp.bfloat16)
        .reshape(tok_dev, local_heads * HD)
    )
    grad_key_pre = (
        rotate(key_total.reshape(tok_dev, local_kv, HD), cosine, -sine_tab)
        .astype(jnp.bfloat16)
        .reshape(tok_dev, local_kv * HD)
    )
    grad_value_low = value_total.astype(jnp.bfloat16)
    grad_wq = jnp.einsum("td,tk->dk", normed1, grad_query_pre, preferred_element_type=jnp.float32)
    grad_wk = jnp.einsum("td,tk->dk", normed1, grad_key_pre, preferred_element_type=jnp.float32)
    grad_wv = jnp.einsum("td,tk->dk", normed1, grad_value_low, preferred_element_type=jnp.float32)
    grad_norm1_part = (
        jnp.einsum("tk,dk->td", grad_query_pre, w_query, preferred_element_type=jnp.float32)
        + jnp.einsum("tk,dk->td", grad_key_pre, w_key, preferred_element_type=jnp.float32)
        + jnp.einsum("tk,dk->td", grad_value_low, w_value, preferred_element_type=jnp.float32)
    )
    grad_normed1 = of_everyone_2(grad_norm1_part.astype(jnp.bfloat16), "tensor").astype(jnp.float32)
    grad_from_norm1, grad_gain1 = norm_back(grad_normed1, x_float, inverse1, norm1_gain)
    input_grad = grad_hidden1 + grad_from_norm1
    grad_wq, grad_wk, grad_wv, grad_wo, grad_gain1, grad_gain2 = in_one(
        (grad_wq, grad_wk, grad_wv, grad_wo, grad_gain1, grad_gain2), "dp"
    )
    return (
        output,
        input_grad,
        grad_wq,
        grad_wk,
        grad_wv,
        grad_wo,
        grad_gain1,
        grad_gain2,
        grad_gate,
        grad_up,
        grad_down,
        clipped_query,
        clipped_key,
        head_peaks,
    )


def solution(mesh):
    in_specs = (
        P("dp", None),
        P("dp", None),
        P(),
        P(),
        P(None, "tensor"),
        P(None, "tensor"),
        P(None, "tensor"),
        P("tensor", None),
        P("dp", None, "tensor"),
        P("dp", None, "tensor"),
        P("dp", "tensor", None),
        P("dp", None),
        P("dp", None),
        P("dp"),
        P("dp"),
        P("tensor"),
    )
    out_specs = (
        P("dp", None),
        P("dp", None),
        P(None, "tensor"),
        P(None, "tensor"),
        P(None, "tensor"),
        P("tensor", None),
        P(),
        P(),
        P("dp", None, "tensor"),
        P("dp", None, "tensor"),
        P("dp", "tensor", None),
        P(None, "tensor"),
        P(None, "tensor"),
        P("tensor"),
    )
    return jax.shard_map(shards, mesh=mesh, in_specs=in_specs, out_specs=out_specs, check_vma=False)
```

profile of v0, /device:TPU:1, one launch (start us, length us, event | category | flops | bytes accessed | tf_op | source)
XLA Modules:
  0.0 1069.0 jit_solution(8250947034086112210)
XLA Ops:
  47.6 19.8 %reduce-window.19 = s32[40,16,128]{2,1,0:T(8,128)S(1)} reduce-window(s32[40,16,128]{2,1,0:T(8,128)} %fusion.46, s32[]{:T(128)} %constant.106.clone.1), window={size=1x1x128 pad=0_0x0_0x127_0}, to_apply=%region_9.10 | reduce-window | flops 10403840 | bytes 655364 | tf_op jit(solution)/shard_map/reduce-window.2
  154.1 10.4 all_to_all.51
  171.0 17.9 %gather_fusion = bf16[4096,768]{1,0:T(8,128)(2,1)} fusion(bf16[257,768]{1,0:T(8,128)(2,1)S(1)} %pad_dynamic-slice_fusion.1, s32[4096]{0:T(1024)S(1)} %fusion.54), kind=kCustom, calls=%fused_computation | custom fusion | bytes 12599296 | tf_op jit(solution)/shard_map/gather | solution.py:269
  188.8 80.5 %all_to_all.52 = bf16[1,64,64,768]{3,2,0,1:T(8,128)(2,1)} all-to-all(bf16[1,64,64,768]{3,2,0,1:T(8,128)(2,1)} %bitcast.219), channel_id=1, replica_groups=mesh['dp'=64,'tensor'=2] {'dp'}, dimensions={1} | all-to-all | bytes 12582912 | tf_op jit(solution)/shard_map/all_to_all | solution.py:273
  278.8 18.0 %gather_fusion.2 = f32[4096,768]{1,0:T(8,128)} fusion(f32[257,768]{1,0:T(8,128)S(1)} %pad_dynamic-slice_fusion, s32[4096]{0:T(1024)S(1)} %fusion.54), kind=kCustom, calls=%fused_computation.2 | custom fusion | bytes 25182208 | tf_op jit(solution)/shard_map/gather | solution.py:269
  304.9 78.1 %all_to_all.53 = bf16[1,64,64,768]{3,2,0,1:T(8,128)(2,1)} all-to-all(bf16[1,64,64,768]{3,2,0,1:T(8,128)(2,1)} %multiply_convert_fusion), channel_id=1, replica_groups=mesh['dp'=64,'tensor'=2] {'dp'}, dimensions={1} | all-to-all | bytes 12582912 | tf_op jit(solution)/shard_map/all_to_all | solution.py:273
  384.1 10.7 fusion.33
  399.9 10.9 %all-gather.5.cloned.1.call-done = bf16[1,64,64,1536]{3,2,0,1:T(8,128)(2,1)} async-done(((bf16[1,64,64,768]{3,2,0,1:T(8,128)(2,1)}), bf16[1,64,64,1536]{3,2,0,1:T(8,128)(2,1)}) %all-gather.5.cloned.1.call-update) | async-done | bytes 12582928 | tf_op jit(solution)/shard_map/all_gather | solution.py:274
  410.8 13.9 %multiply_convert_fusion.2 = (bf16[4096,256]{1,0:T(8,128)(2,1)}, bf16[4096,256]{1,0:T(8,128)(2,1)}, bf16[4096,256]{1,0:T(8,128)(2,1)S(1)}) fusion(f32[4096,256]{1,0:T(8,128)} %fusion.37, f32[4096,256]{1,0:T(8,128)} %fusion.33, bf16[4096,1536]{1,0:T(8,128)(2,1)} %bitcast.220, bf16[1,256,1536]{2,1,0:T(8,128)(2,1)S(1)} %copy-done.28), kind=kOutput, calls=%fused_computation.31 | convolution fusion | flops 3236954112 | bytes 28049408 | tf_op jit(solution)/shard_map/erd,efd->erf/dot_general | solution.py:309
  433.3 13.9 %fusion.35 = f32[4096,1536]{1,0:T(8,128)} fusion(bf16[4096,256]{1,0:T(8,128)(2,1)} %get-tuple-element.35, bf16[1,1536,256]{2,1,0:T(8,128)(2,1)S(1)} %copy-done.31), kind=kOutput, calls=%fused_computation.86 | convolution fusion | flops 3221225472 | bytes 28049408 | tf_op jit(solution)/shard_map/erf,edf->erd/dot_general | solution.py:318
  447.3 19.7 %fusion.5 = bf16[1,4096,1536]{2,1,0:T(8,128)(2,1)} fusion(f32[4096,1536]{1,0:T(8,128)} %fusion.35, bf16[4096,256]{1,0:T(8,128)(2,1)} %get-tuple-element.34, bf16[1,1536,256]{2,1,0:T(8,128)(2,1)} %param.25), kind=kOutput, calls=%fused_computation.19 | convolution fusion | flops 3233808384 | bytes 40632320 | tf_op jit(solution)/shard_map/erf,edf->erd/dot_general | solution.py:320
  467.0 10.3 all-to-all-start.3
  477.4 82.5 %all-to-all-done.3 = bf16[1,64,64,768]{3,2,0,1:T(8,128)(2,1)} async-done(((bf16[1,64,64,768]{3,2,0,1:T(8,128)(2,1)}), bf16[1,64,64,768]{3,2,0,1:T(8,128)(2,1)}, u32[]{:S(2)}, u32[]{:S(2)}) %all-to-all-start.3) | async-done | bytes 6291488 | tf_op jit(solution)/shard_map/all_to_all | solution.py:285
  559.9 8.3 bitcast_convert_fusion.1
  568.2 15.3 %gather_fusion.1 = f32[2048,768]{1,0:T(8,128)} fusion(f32[4096,768]{1,0:T(8,128)} %bitcast_convert_fusion.1, s32[2048]{0:T(1024)S(1)} %broadcast_clamp_fusion), kind=kCustom, calls=%fused_computation.1 | custom fusion | bytes 12591104 | tf_op jit(solution)/shard_map/gather | solution.py:278
  595.2 11.4 %all-to-all-start.6 = ((bf16[1,64,64,768]{3,2,0,1:T(8,128)(2,1)}), bf16[1,64,64,768]{3,2,0,1:T(8,128)(2,1)}, u32[]{:S(2)}, u32[]{:S(2)}) async-start(bf16[1,64,64,768]{3,2,0,1:T(8,128)(2,1)} %bitcast.226), calls=%async_computation.8 | async-start | bytes 12582912 | tf_op jit(solution)/shard_map/all_to_all | solution.py:285
  608.1 79.1 %all-to-all-done.6 = bf16[1,64,64,768]{3,2,0,1:T(8,128)(2,1)} async-done(((bf16[1,64,64,768]{3,2,0,1:T(8,128)(2,1)}), bf16[1,64,64,768]{3,2,0,1:T(8,128)(2,1)}, u32[]{:S(2)}, u32[]{:S(2)}) %all-to-all-start.6) | async-done | bytes 6291488 | tf_op jit(solution)/shard_map/all_to_all | solution.py:285
  695.6 15.3 %gather_fusion.3 = f32[2048,768]{1,0:T(8,128)} fusion(f32[4096,768]{1,0:T(8,128)} %bitcast_convert_fusion, s32[2048]{0:T(1024)S(1)} %broadcast_clamp_fusion), kind=kCustom, calls=%fused_computation.3 | custom fusion | bytes 12591104 | tf_op jit(solution)/shard_map/gather | solution.py:278
  728.6 9.2 fusion.94
  737.8 11.9 %fusion.82 = (f32[4,3]{1,0:T(4,128)S(1)}, f32[4,3,256]{2,1,0:T(4,128)S(1)}, f32[4,1280,256,3]{2,1,3,0:T(8,128)}) fusion(f32[4,3,256,1280]{2,3,1,0:T(8,128)} %get-tuple-element.79, f32[4,3,256]{2,1,0:T(4,128)S(1)} %log_add_fusion, bf16[1280,4,64,1]{0,2,3,1:T(8,128)(2,1)S(1)} %bitcast.239, bf16[256,4,3,64]{0,3,2,1:T(8,128)(2,1)S(1)} %bitcast.232), kind=kOutput, calls=%fused_computation.209 | convolution fusion | flops 519042048 | bytes 32530480 | tf_op jit(solution)/shard_map/qkgd,skd->kgqs/dot_general | solution.py:332
  834.6 9.9 convolution_bitcast_fusion
  852.9 21.7 %all-to-all-start.9 = ((f32[64,1,12]{2,1,0:T(1,128)}), f32[64,1,12]{2,1,0:T(1,128)S(1)}, u32[]{:S(2)}, u32[]{:S(2)}) async-start(f32[64,1,12]{2,1,0:T(1,128)} %broadcast_in_dim.73), calls=%async_computation.11 | async-start | bytes 65536 | tf_op jit(solution)/shard_map/all_to_all | solution.py:22
  874.6 10.8 %convolution_bitcast_fusion.3 = f32[1,256,1536]{2,1,0:T(8,128)} fusion(bf16[4096,256]{1,0:T(8,128)(2,1)} %copy-done.8, bf16[4096,1536]{1,0:T(8,128)(2,1)} %bitcast.221), kind=kOutput, calls=%fused_computation.51 | convolution fusion | flops 3221225472 | bytes 16252928 | tf_op jit(solution)/shard_map/erf,erd->efd/dot_general | solution.py:308
  893.6 139.7 %all-reduce.6.cloned.1.call-done = f32[3148800]{0:T(1024)} async-done(((f32[3148800]{0:T(1024)}), f32[3148800]{0:T(1024)}) %all-reduce.6.cloned.1.call-update) | async-done | bytes 12595216 | tf_op jit(solution)/shard_map/psum | solution.py:97
  (384 shorter events, 329.0 us)
Async XLA Ops:
  11.9 108.2 %collective-permute-start.3 = (bf16[256,256]{1,0:T(8,128)(2,1)}, bf16[256,256]{1,0:T(8,128)(2,1)}, u32[]{:S(2)}, u32[]{:S(2)}) collective-permute-start(bf16[256,256]{1,0:T(8,128)(2,1)} %convolution_convert_fusion.2), channel_id=1, source_target_pairs={{0,2},{2,4},{4,6},{6,8},{8,10},{10,12},{12,14},{14,16},{16,18},{18... | collective-permute-start | bytes 393224 | tf_op jit(solution)/shard_map/ppermute | solution.py:69
  16.9 98.4 %collective-permute-start.2 = (bf16[256,256]{1,0:T(8,128)(2,1)}, bf16[256,256]{1,0:T(8,128)(2,1)}, u32[]{:S(2)}, u32[]{:S(2)}) collective-permute-start(bf16[256,256]{1,0:T(8,128)(2,1)} %convolution_convert_fusion.2), channel_id=1, source_target_pairs={{0,4},{2,6},{4,8},{6,10},{8,12},{10,14},{12,16},{14,18},{16,20},{1... | collective-permute-start | bytes 393224 | tf_op jit(solution)/shard_map/ppermute | solution.py:69
  22.1 87.6 %collective-permute-start.1 = (bf16[256,256]{1,0:T(8,128)(2,1)}, bf16[256,256]{1,0:T(8,128)(2,1)}, u32[]{:S(2)}, u32[]{:S(2)}) collective-permute-start(bf16[256,256]{1,0:T(8,128)(2,1)} %convolution_convert_fusion.2), channel_id=1, source_target_pairs={{0,6},{2,8},{4,10},{6,12},{8,14},{10,16},{12,18},{14,20},{16,22},{... | collective-permute-start | bytes 393224 | tf_op jit(solution)/shard_map/ppermute | solution.py:69
  25.7 78.1 %collective-permute-start = (bf16[256,256]{1,0:T(8,128)(2,1)}, bf16[256,256]{1,0:T(8,128)(2,1)}, u32[]{:S(2)}, u32[]{:S(2)}) collective-permute-start(bf16[256,256]{1,0:T(8,128)(2,1)} %convolution_convert_fusion.2), channel_id=1, source_target_pairs={{0,8},{2,10},{4,12},{6,14},{8,16},{10,18},{12,20},{14,22},{16,24},... | collective-permute-start | bytes 393224 | tf_op jit(solution)/shard_map/ppermute | solution.py:69
  33.3 51.4 %all-to-all-start = ((s32[64,2,1]{1,2,0:T(1,128)}), s32[64,2,1]{1,2,0:T(1,128)S(1)}, u32[]{:S(2)}, u32[]{:S(2)}) async-start(s32[64,2,1]{1,2,0:T(1,128)} %broadcast_in_dim.59), calls=%async_computation | async-start | bytes 65536 | tf_op jit(solution)/shard_map/all_to_all | solution.py:22
  40.2 343.0 %all-gather.3.cloned.1.call-start = ((), (), s32[]{:S(2)}) async-start(), calls=%async_computation.12 | async-start | bytes 18874368 | tf_op jit(solution)/shard_map/all_gather | solution.py:274
  96.5 31.6 %collective-permute-start.7 = (bf16[256,256]{0,1:T(8,128)(2,1)}, bf16[256,256]{0,1:T(8,128)(2,1)}, u32[]{:S(2)}, u32[]{:S(2)}) collective-permute-start(bf16[256,256]{0,1:T(8,128)(2,1)} %bitcast.11), channel_id=1, source_target_pairs={{0,2},{2,4},{4,6},{6,8},{8,10},{10,12},{12,14},{14,16},{16,18},{18... | collective-permute-start | bytes 393224 | tf_op jit(solution)/shard_map/ppermute | solution.py:69
  103.8 23.5 %collective-permute-start.6 = (bf16[256,256]{0,1:T(8,128)(2,1)}, bf16[256,256]{0,1:T(8,128)(2,1)}, u32[]{:S(2)}, u32[]{:S(2)}) collective-permute-start(bf16[256,256]{0,1:T(8,128)(2,1)} %bitcast.11), channel_id=1, source_target_pairs={{0,4},{2,6},{4,8},{6,10},{8,12},{10,14},{12,16},{14,18},{16,20},{1... | collective-permute-start | bytes 393224 | tf_op jit(solution)/shard_map/ppermute | solution.py:69
  109.7 16.6 %collective-permute-start.5 = (bf16[256,256]{0,1:T(8,128)(2,1)}, bf16[256,256]{0,1:T(8,128)(2,1)}, u32[]{:S(2)}, u32[]{:S(2)}) collective-permute-start(bf16[256,256]{0,1:T(8,128)(2,1)} %bitcast.11), channel_id=1, source_target_pairs={{0,6},{2,8},{4,10},{6,12},{8,14},{10,16},{12,18},{14,20},{16,22},{... | collective-permute-start | bytes 393224 | tf_op jit(solution)/shard_map/ppermute | solution.py:69
  269.4 141.3 %all-gather.5.cloned.1.call-start = ((), (), s32[]{:S(2)}) async-start(), calls=%async_computation.14 | async-start | bytes 18874368 | tf_op jit(solution)/shard_map/all_gather | solution.py:274
  383.0 84.0 %reduce-scatter.3.cloned.1.call-start = ((), (), s32[]{:S(2)}) async-start(), calls=%async_computation.13 | async-start | bytes 18874368 | tf_op jit(solution)/shard_map/reduce_scatter | solution.py:282
  432.2 161.4 %reduce-scatter.5.cloned.1.call-start = ((), (), s32[]{:S(2)}) async-start(), calls=%async_computation.15 | async-start | bytes 18874368 | tf_op jit(solution)/shard_map/reduce_scatter | solution.py:282
  467.0 92.9 %all-to-all-start.3 = ((bf16[1,64,64,768]{3,2,0,1:T(8,128)(2,1)}), bf16[1,64,64,768]{3,2,0,1:T(8,128)(2,1)}, u32[]{:S(2)}, u32[]{:S(2)}) async-start(bf16[1,64,64,768]{3,2,0,1:T(8,128)(2,1)} %bitcast.227), calls=%async_computation.4 | async-start | bytes 12582912 | tf_op jit(solution)/shard_map/all_to_all | solution.py:285
  595.2 92.1 %all-to-all-start.6 = ((bf16[1,64,64,768]{3,2,0,1:T(8,128)(2,1)}), bf16[1,64,64,768]{3,2,0,1:T(8,128)(2,1)}, u32[]{:S(2)}, u32[]{:S(2)}) async-start(bf16[1,64,64,768]{3,2,0,1:T(8,128)(2,1)} %bitcast.226), calls=%async_computation.8 | async-start | bytes 12582912 | tf_op jit(solution)/shard_map/all_to_all | solution.py:285
  606.6 426.8 %all-reduce.6.cloned.1.call-start = ((), (), s32[]{:S(2)}) async-start(), calls=%async_computation.16 | async-start | bytes 25190400 | tf_op jit(solution)/shard_map/psum | solution.py:97
  774.9 25.9 %collective-permute-start.15 = (bf16[256,256]{0,1:T(8,128)(2,1)}, bf16[256,256]{0,1:T(8,128)(2,1)S(1)}, u32[]{:S(2)}, u32[]{:S(2)}) collective-permute-start(bf16[256,256]{0,1:T(8,128)(2,1)} %bitcast.77), channel_id=1, source_target_pairs={{2,0},{4,2},{6,4},{8,6},{10,8},{12,10},{14,12},{16,14},{18,16},{20... | collective-permute-start | bytes 393224 | tf_op jit(solution)/shard_map/ppermute | solution.py:69
  776.2 26.0 %collective-permute-start.12 = (bf16[256,256]{0,1:T(8,128)(2,1)}, bf16[256,256]{0,1:T(8,128)(2,1)S(1)}, u32[]{:S(2)}, u32[]{:S(2)}) collective-permute-start(bf16[256,256]{0,1:T(8,128)(2,1)} %bitcast.74), channel_id=1, source_target_pairs={{8,0},{10,2},{12,4},{14,6},{16,8},{18,10},{20,12},{22,14},{24,16},... | collective-permute-start | bytes 393224 | tf_op jit(solution)/shard_map/ppermute | solution.py:69
  777.5 26.0 %collective-permute-start.14 = (bf16[256,256]{0,1:T(8,128)(2,1)}, bf16[256,256]{0,1:T(8,128)(2,1)}, u32[]{:S(2)}, u32[]{:S(2)}) collective-permute-start(bf16[256,256]{0,1:T(8,128)(2,1)} %bitcast.76), channel_id=1, source_target_pairs={{4,0},{6,2},{8,4},{10,6},{12,8},{14,10},{16,12},{18,14},{20,16},{2... | collective-permute-start | bytes 393224 | tf_op jit(solution)/shard_map/ppermute | solution.py:69
  778.8 26.0 %collective-permute-start.13 = (bf16[256,256]{0,1:T(8,128)(2,1)}, bf16[256,256]{0,1:T(8,128)(2,1)}, u32[]{:S(2)}, u32[]{:S(2)}) collective-permute-start(bf16[256,256]{0,1:T(8,128)(2,1)} %bitcast.75), channel_id=1, source_target_pairs={{6,0},{8,2},{10,4},{12,6},{14,8},{16,10},{18,12},{20,14},{22,16},{... | collective-permute-start | bytes 393224 | tf_op jit(solution)/shard_map/ppermute | solution.py:69
  787.8 19.4 %collective-permute-start.11 = (bf16[256,256]{0,1:T(8,128)(2,1)}, bf16[256,256]{0,1:T(8,128)(2,1)}, u32[]{:S(2)}, u32[]{:S(2)}) collective-permute-start(bf16[256,256]{0,1:T(8,128)(2,1)} %bitcast.66), channel_id=1, source_target_pairs={{2,0},{4,2},{6,4},{8,6},{10,8},{12,10},{14,12},{16,14},{18,16},{20... | collective-permute-start | bytes 393224 | tf_op jit(solution)/shard_map/ppermute | solution.py:69
  800.9 11.8 %collective-permute-start.8 = (bf16[256,256]{0,1:T(8,128)(2,1)S(1)}, bf16[256,256]{0,1:T(8,128)(2,1)S(1)}, u32[]{:S(2)}, u32[]{:S(2)}) collective-permute-start(bf16[256,256]{0,1:T(8,128)(2,1)S(1)} %bitcast.252), channel_id=1, source_target_pairs={{8,0},{10,2},{12,4},{14,6},{16,8},{18,10},{20,12},{22,14},{24,16},... | collective-permute-start | bytes 393224 | tf_op jit(solution)/shard_map/ppermute | solution.py:69
  802.2 10.5 collective-permute-start.10
  803.5 11.8 %collective-permute-start.9 = (bf16[256,256]{0,1:T(8,128)(2,1)S(1)}, bf16[256,256]{0,1:T(8,128)(2,1)S(1)}, u32[]{:S(2)}, u32[]{:S(2)}) collective-permute-start(bf16[256,256]{0,1:T(8,128)(2,1)S(1)} %bitcast.250), channel_id=1, source_target_pairs={{6,0},{8,2},{10,4},{12,6},{14,8},{16,10},{18,12},{20,14},{22,16},{... | collective-permute-start | bytes 393224 | tf_op jit(solution)/shard_map/ppermute | solution.py:69
  852.9 32.6 %all-to-all-start.9 = ((f32[64,1,12]{2,1,0:T(1,128)}), f32[64,1,12]{2,1,0:T(1,128)S(1)}, u32[]{:S(2)}, u32[]{:S(2)}) async-start(f32[64,1,12]{2,1,0:T(1,128)} %broadcast_in_dim.73), calls=%async_computation.11 | async-start | bytes 65536 | tf_op jit(solution)/shard_map/all_to_all | solution.py:22
  (76 other events, 854.7 us)
Sparse Core Ops, SparseCore 0:
  269.5 26.3 all-gather.2
  383.1 27.5 all-gather.4
  432.3 25.3 reduce-scatter.2
  467.1 25.3 reduce-scatter.4
  834.7 198.6 all-reduce.5
where the time goes:
time: 1080 us; the launch traced here: 1070 us
  waiting for transfers between devices  322 us (30%)
  local copies, waits for them, and re-layouts  182 us (17%)
  blocking collectives  181 us (17%)
  matrix products  163 us (15%)
  other arithmetic  102 us (9%)
  starting transfers between devices  98.3 us (9%)
  between operations  20.6 us (2%)
    all_to_all x2, waiting for transfers between devices, from_owners(): lax.all_to_all(reduced.reshape(exp_local, dp_size, CAP, -1).astype(jnp.bf...  162 us
    all_to_all x2, blocking collectives, to_owners(): got = lax.all_to_all(rows, 'dp', split_axis=1, concat_axis=1, tiled=True)  159 us
    psum x1, waiting for transfers between devices, in_one(): so_far = lax.psum(ravelled, axis)  140 us
    ppermute x16, starting transfers between devices, passed_along(): lax.ppermute(value, axis, [(source, source + steps) for source in range(f...  42.6 us
    gather x2, local copies, waits for them, and re-layouts, to_owners(): rows = table[slot_token]  35.9 us
    all_to_all x3, starting transfers between devices, copy_for_each(): lax.all_to_all(jnp.broadcast_to(array[None], (size, *array.shape)), axis,...  33.2 us
    unnamed x164, local copies, waits for them, and re-layouts  32 us
    gather x2, local copies, waits for them, and re-layouts, combine_rows(): picked = slot_rows[flat_slot].reshape(tok_dev, TOP, slot_rows.shape[-1])  30.6 us
  transfers between devices with their start and end apart: 26, of which 7 were waited for; matrix products, arithmetic and copies ran while one was open for 23% of the time, Pallas kernels for 0%

commit v1 on v0

v1 whole, which is shorter than its diff:
```python
import functools
import math

import jax
import jax.numpy as jnp
import numpy as np
from jax import lax
from jax.experimental import pallas as pl
from jax.experimental.pallas import tpu as pltpu
from jax.sharding import PartitionSpec as P

HD = 64
TOP = 8
CAP = 64
HOPS = 4
SLOTS = 64
AUX = 16

EPS = 1e-06
ROPE_BASE = 10000.0
NEG_FILL = -1e30
BF16 = jnp.bfloat16
F32 = jnp.float32


def contract(left, right, dims):
    return lax.dot_general(left, right, (dims, ((), ())), preferred_element_type=F32)


NN = ((1,), (0,))
NT = ((1,), (1,))
TN = ((0,), (0,))


def swapped(array):
    return lax.ppermute(array, "tensor", [(0, 1), (1, 0)])


def passed_along(value, steps):
    count = lax.axis_size("dp")
    first, last = (max(0, -steps), min(count, count - steps))
    return lax.ppermute(value, "dp", [(s, s + steps) for s in range(first, last)])


def to_all(array):
    return lax.all_to_all(array, "dp", 0, 0, tiled=True)


def rope_tables(count, dp_size):
    freq = np.exp(np.arange(HD // 2) * (-2.0 * math.log(ROPE_BASE) / HD))
    base = np.arange(dp_size)[:, None] * count * freq[None, :]
    local = freq[:, None] * np.arange(count)[None, :]
    index = lax.axis_index("dp")
    cos_base = jnp.asarray(np.cos(base), F32)[index][:, None]
    sin_base = jnp.asarray(np.sin(base), F32)[index][:, None]
    cos_local, sin_local = (jnp.asarray(np.cos(local), F32), jnp.asarray(np.sin(local), F32))
    return (
        cos_base * cos_local - sin_base * sin_local,
        sin_base * cos_local + cos_base * sin_local,
    )


def rotate(values, cosine, sine):
    half = HD // 2
    heads = values.reshape(-1, HD, values.shape[-1])
    first, second = (heads[:, :half], heads[:, half:])
    turned = jnp.concatenate(
        [first * cosine - second * sine, second * cosine + first * sine], axis=1
    )
    return turned.reshape(values.shape)


def fill_bias(blocks, bias):
    tok = bias.shape[1]
    rows = blocks[-1].shape[0] - AUX
    own = blocks[-1][rows:, :].astype(F32)
    seq_q, piece_q = (own[0:1, :], own[1:2, :])
    for number, block in enumerate(blocks):
        side = jnp.transpose(block[rows:, :].astype(F32))
        keep = side[:, 0:1] == seq_q
        if number == len(blocks) - 1:
            at_key = lax.broadcasted_iota(jnp.int32, (tok, tok), 0)
            at_query = lax.broadcasted_iota(jnp.int32, (tok, tok), 1)
            piece = (side[:, 1:2] == piece_q) & (piece_q > 0.0)
            keep = keep & ((at_key <= at_query) | piece)
        bias[number * tok : (number + 1) * tok, :] = jnp.where(keep, 0.0, NEG_FILL)


def all_keys(blocks, start):
    return jnp.concatenate([block[pl.ds(start, HD), :] for block in blocks], axis=1)


def attend_kernel(group, q_ref, k4, k3, k2, k1, k0, out_ref, log_ref, peak_ref, bias):
    blocks = (k4, k3, k2, k1, k0)
    fill_bias(blocks, bias)
    kv_rows = (k0.shape[0] - AUX) // 2

    def one_group(g, _):
        at = pl.multiple_of(g * HD, HD)
        keys = all_keys(blocks, at)
        values = all_keys(blocks, kv_rows + at)
        for j in range(group):
            head = g * group + j
            here = pl.ds(pl.multiple_of(head * HD, HD), HD)
            scores = contract(keys, q_ref[here, :], TN) + bias[...]
            peak = jnp.max(scores, axis=0, keepdims=True)
            weight = jnp.exp(scores - peak)
            total = jnp.sum(weight, axis=0, keepdims=True)
            mixed = contract(values, weight.astype(BF16), NN) * (1.0 / total)
            out_ref[here, :] = mixed.astype(BF16)
            log_ref[pl.ds(head, 1), :] = peak + jnp.log(total)
            peak_ref[pl.ds(head, 1), :] = peak
        return 0

    lax.fori_loop(0, kv_rows // HD, one_group, 0)


def attend(q, blocks, group):
    rows, tok = q.shape
    heads = rows // HD
    return pl.pallas_call(
        functools.partial(attend_kernel, group),
        out_shape=(
            jax.ShapeDtypeStruct((rows, tok), BF16),
            jax.ShapeDtypeStruct((heads, tok), F32),
            jax.ShapeDtypeStruct((heads, tok), F32),
        ),
        scratch_shapes=[pltpu.VMEM((len(blocks) * tok, tok), F32)],
        compiler_params=pltpu.CompilerParams(vmem_limit_bytes=48 << 20),
        cost_estimate=pl.CostEstimate(
            flops=4 * rows * tok * tok * len(blocks),
            bytes_accessed=4 * rows * tok + 2 * len(blocks) * 528 * tok,
            transcendentals=heads * tok * tok * len(blocks),
        ),
    )(q, *blocks)


def attend_back_kernel(
    group, q_ref, g_ref, log_ref, cos_ref, sin_ref, k4, k3, k2, k1, k0,
    dq_ref, d4, d3, d2, d1, d0, bias,
):
    blocks = (k4, k3, k2, k1, k0)
    grads = (d4, d3, d2, d1, d0)
    fill_bias(blocks, bias)
    kv_rows = (k0.shape[0] - AUX) // 2
    tok = bias.shape[1]
    half = HD // 2

    def one_group(g, _):
        at = pl.multiple_of(g * HD, HD)
        keys = all_keys(blocks, at)
        values = all_keys(blocks, kv_rows + at)
        key_sum = value_sum = None
        for j in range(group):
            head = g * group + j
            start = pl.multiple_of(head * HD, HD)
            query, grad = (q_ref[pl.ds(start, HD), :], g_ref[pl.ds(start, HD), :])
            scores = contract(keys, query, TN) + bias[...]
            probs = jnp.exp(scores - log_ref[pl.ds(head, 1), :])
            grad_probs = contract(values, grad, TN)
            delta = jnp.sum(probs * grad_probs, axis=0, keepdims=True)
            grad_scores = (probs * (grad_probs - delta)).astype(BF16)
            key_part = contract(query, grad_scores, NT)
            value_part = contract(grad, probs.astype(BF16), NT)
            key_sum = key_part if key_sum is None else key_sum + key_part
            value_sum = value_part if value_sum is None else value_sum + value_part
            turned = contract(keys, grad_scores, NN) * (HD**-0.5)
            first, second = (turned[:half], turned[half:])
            cosine, sine = (cos_ref[...], sin_ref[...])
            dq_ref[pl.ds(start, half), :] = (first * cosine + second * sine).astype(BF16)
            dq_ref[pl.ds(start + half, half), :] = (second * cosine - first * sine).astype(BF16)
        for number, grad_ref in enumerate(grads):
            piece = slice(number * tok, (number + 1) * tok)
            grad_ref[pl.ds(at, HD), :] = key_sum[:, piece].astype(grad_ref.dtype)
            grad_ref[pl.ds(kv_rows + at, HD), :] = value_sum[:, piece].astype(grad_ref.dtype)
        return 0

    lax.fori_loop(0, kv_rows // HD, one_group, 0)


def attend_back(q, grad, log_total, cosine, sine, blocks, group):
    rows, tok = q.shape
    kv = blocks[0].shape[0] - AUX
    return pl.pallas_call(
        functools.partial(attend_back_kernel, group),
        out_shape=(
            jax.ShapeDtypeStruct((rows, tok), BF16),
            *(jax.ShapeDtypeStruct((kv, tok), BF16) for _ in blocks[1:]),
            jax.ShapeDtypeStruct((kv, tok), F32),
        ),
        scratch_shapes=[pltpu.VMEM((len(blocks) * tok, tok), F32)],
        compiler_params=pltpu.CompilerParams(vmem_limit_bytes=48 << 20),
        cost_estimate=pl.CostEstimate(
            flops=10 * rows * tok * tok * len(blocks),
            bytes_accessed=6 * rows * tok + 4 * len(blocks) * 528 * tok,
            transcendentals=rows // HD * tok * tok * len(blocks),
        ),
    )(q, grad, log_total, cosine, sine, *blocks)


def expert_kernel(x_ref, g_ref, go, gp, uo, up, do, dp, dx_ref, *outs):
    rows, grads = (x_ref[...], g_ref[...])
    back = None
    for side, (gate_w, up_w, down_w) in enumerate(((go, uo, do), (gp, up, dp))):
        inner_ref, dgate_ref, dup_ref = outs[3 * side : 3 * side + 3]
        gate_act = contract(rows, gate_w[...], NN)
        up_act = contract(rows, up_w[...], NN)
        grad_inner = contract(grads, down_w[...], NT)
        sigmoid = 1.0 / (1.0 + jnp.exp(-gate_act))
        silu = gate_act * sigmoid
        inner_ref[...] = (silu * up_act).astype(BF16)
        dgate = (grad_inner * up_act * (sigmoid * (1.0 + gate_act * (1.0 - sigmoid)))).astype(BF16)
        dup = (grad_inner * silu).astype(BF16)
        dgate_ref[...] = dgate
        dup_ref[...] = dup
        part = contract(dgate, gate_w[...], NT) + contract(dup, up_w[...], NT)
        back = part if back is None else back + part
    dx_ref[...] = back.astype(BF16)


def experts(rows, grads, own, peer):
    count, width = rows.shape
    hidden = own[0].shape[1]
    tile = 256
    wide = pl.BlockSpec((tile, width), lambda i: (i, 0))
    thin = pl.BlockSpec((tile, hidden), lambda i: (i, 0))
    into = pl.BlockSpec((width, hidden), lambda i: (0, 0))
    out_of = pl.BlockSpec((hidden, width), lambda i: (0, 0))
    return pl.pallas_call(
        expert_kernel,
        grid=(count // tile,),
        in_specs=[wide, wide, into, into, into, into, out_of, out_of],
        out_specs=[wide] + [thin] * 6,
        out_shape=[jax.ShapeDtypeStruct((count, width), BF16)]
        + [jax.ShapeDtypeStruct((count, hidden), BF16)] * 6,
        compiler_params=pltpu.CompilerParams(vmem_limit_bytes=48 << 20),
        cost_estimate=pl.CostEstimate(
            flops=20 * count * width * hidden,
            bytes_accessed=6 * count * width + 12 * count * hidden + 12 * width * hidden,
            transcendentals=2 * count * hidden,
        ),
    )(rows, grads, own[0], peer[0], own[1], peer[1], own[2], peer[2])


def rms_scale(values):
    return lax.rsqrt(jnp.mean(values * values, axis=-1, keepdims=True) + EPS)


def norm_back(grad_normed, hidden, inverse, gain):
    weighted = grad_normed * gain
    grad_gain = jnp.sum(grad_normed * hidden * inverse, axis=0)
    grad_hidden = inverse * weighted - hidden * inverse**3 * jnp.mean(
        weighted * hidden, axis=-1, keepdims=True
    )
    return (grad_hidden, grad_gain)


def shards(
    tokens,
    out_grad,
    norm1_gain,
    norm2_gain,
    w_query,
    w_key,
    w_value,
    w_out,
    w_gate,
    w_up,
    w_down,
    route_ids,
    route_logits,
    seq_ids,
    piece_ids,
    clip_limit,
):
    tok_dev, model_width = tokens.shape
    dp_size = lax.axis_size("dp")
    tensor_size = lax.axis_size("tensor")
    core = lax.axis_index("tensor")
    local_heads = w_query.shape[1] // HD
    local_kv = w_key.shape[1] // HD
    group = local_heads // local_kv
    rank_rows = CAP // tensor_size
    own = (w_gate[0], w_up[0], w_down[0])
    peer = tuple(swapped(w) for w in own)

    picks = route_ids.T
    logits = route_logits.T
    gate_exp = jnp.exp(logits - jnp.max(logits, axis=0, keepdims=True))
    gates = gate_exp / jnp.sum(gate_exp, axis=0, keepdims=True)
    same = picks[None] == jnp.arange(SLOTS, dtype=jnp.int32)[:, None, None]
    member = jnp.any(same, axis=1)
    gate_of = jnp.sum(jnp.where(same, gates[None], 0.0), axis=1)
    place = jnp.arange(tok_dev, dtype=jnp.int32)
    before = (place[:, None] < place[None, :]).astype(BF16)
    rank = contract(member.astype(BF16), before, NN)
    rank = jnp.where(member, rank, -1.0)
    wanted = (tensor_size * jnp.arange(rank_rows, dtype=jnp.int32) + core).astype(F32)
    chosen = rank[:, None, :] == wanted[None, :, None]
    pick = chosen.astype(BF16).reshape(-1, tok_dev)
    gated = jnp.where(chosen, gate_of[:, None, :], 0.0)
    slot_gate = jnp.sum(gated, axis=2).reshape(-1, 1)
    gated = gated.astype(BF16).reshape(-1, tok_dev)

    def to_owners(rows):
        return to_all(rows.reshape(dp_size, rank_rows, model_width)).reshape(-1, model_width)

    grad_rows = to_owners((contract(pick, out_grad, NN) * slot_gate).astype(BF16))

    cosine, sine = rope_tables(tok_dev, dp_size)
    x_float = tokens.astype(F32)
    inverse1 = rms_scale(x_float)
    normed1 = (x_float * inverse1 * norm1_gain).astype(BF16)
    query = rotate(contract(w_query, normed1, ((0,), (1,))), cosine, sine)
    query = (query * (HD**-0.5)).astype(BF16)
    key = rotate(contract(w_key, normed1, ((0,), (1,))), cosine, sine).astype(BF16)
    value = contract(w_value, normed1, ((0,), (1,))).astype(BF16)
    side = jnp.concatenate(
        [(seq_ids + 1)[None], piece_ids[None], jnp.zeros((AUX - 2, tok_dev), jnp.int32)]
    ).astype(BF16)
    block = jnp.concatenate([key, value, side])
    blocks = tuple(passed_along(block, hop) for hop in range(HOPS, 0, -1)) + (block,)
    attended, log_total, peaks = attend(query, blocks, group)
    attn_part = contract(attended, w_out, TN)
    hidden1 = x_float + (attn_part + swapped(attn_part))
    inverse2 = rms_scale(hidden1)
    normed2 = (hidden1 * inverse2 * norm2_gain).astype(BF16)

    rows_in = to_owners(contract(pick, normed2, NN).astype(BF16))
    back, *acts = experts(rows_in, grad_rows, own, peer)

    def from_owners(rows):
        return to_all(rows.reshape(dp_size, rank_rows, model_width)).reshape(-1, model_width)

    def combined(weights, rows):
        part = contract(weights, from_owners(rows), TN).astype(BF16)
        return part.astype(F32) + swapped(part).astype(F32)

    grad_normed2 = combined(pick, back)
    inner, dgate, dup, inner_peer, dgate_peer, dup_peer = acts
    expert_out = (contract(inner, own[2], NN) + contract(inner_peer, peer[2], NN)).astype(BF16)
    grad_gate = contract(rows_in, dgate, TN) + swapped(
        contract(rows_in, dgate_peer, TN).astype(BF16)
    ).astype(F32)
    grad_up = contract(rows_in, dup, TN) + swapped(
        contract(rows_in, dup_peer, TN).astype(BF16)
    ).astype(F32)
    grad_down = contract(inner, grad_rows, TN) + swapped(
        contract(inner_peer, grad_rows, TN).astype(BF16)
    ).astype(F32)

    grad_top = out_grad.astype(F32)
    grad_from_norm2, grad_gain2 = norm_back(grad_normed2, hidden1, inverse2, norm2_gain)
    grad_hidden1 = grad_top + grad_from_norm2
    grad_branch = grad_hidden1.astype(BF16)
    grad_attended = contract(w_out, grad_branch, NT).astype(BF16)
    grad_query_pre, *grad_blocks = attend_back(
        query, grad_attended, log_total, cosine, sine, blocks, group
    )
    kv_total = grad_blocks[-1]
    for number, hop in enumerate(range(HOPS, 0, -1)):
        kv_total = kv_total + passed_along(grad_blocks[number], -hop).astype(F32)
    output = (hidden1 + combined(gated, expert_out)).astype(BF16)
    kv_rows = local_kv * HD
    grad_key_pre = rotate(kv_total[:kv_rows], cosine, -sine).astype(BF16)
    grad_value = kv_total[kv_rows:].astype(BF16)

    half = model_width // 2
    grad_wo = jnp.concatenate(
        [contract(attended, grad_branch[:, :half], NN), contract(attended, grad_branch[:, half:], NN)]
    )
    grad_wq = contract(normed1, grad_query_pre, ((0,), (1,)))
    grad_wk = contract(normed1, grad_key_pre, ((0,), (1,)))
    grad_wv = contract(normed1, grad_value, ((0,), (1,)))
    grad_norm1_part = (
        contract(grad_query_pre, w_query, ((0,), (1,)))
        + contract(grad_key_pre, w_key, ((0,), (1,)))
        + contract(grad_value, w_value, ((0,), (1,)))
    ).astype(BF16)

    def share(part):
        return jnp.sum(to_all(part.astype(BF16).reshape(dp_size, -1, part.shape[1])).astype(F32), axis=0)

    share_wo = share(grad_wo)
    share_wq = share(grad_wq)
    share_wkv = share(jnp.concatenate([grad_wk, grad_wv], axis=1))
    grad_normed1 = grad_norm1_part.astype(F32) + swapped(grad_norm1_part).astype(F32)
    grad_from_norm1, grad_gain1 = norm_back(grad_normed1, x_float, inverse1, norm1_gain)
    input_grad = grad_hidden1 + grad_from_norm1
    width = w_query.shape[1]
    peak = jnp.max(peaks, axis=1)
    peak_high = peak.astype(BF16)
    peak_low = (peak - peak_high.astype(F32)).astype(BF16)
    peak_row = jnp.pad(jnp.concatenate([peak_high, peak_low]), (0, width - 2 * local_heads))
    lines = [
        share_wo.astype(BF16),
        share_wq.astype(BF16),
        share_wkv.astype(BF16).reshape(-1, width),
        grad_gain1.astype(BF16).reshape(-1, width),
        grad_gain2.astype(BF16).reshape(-1, width),
        peak_row[None],
    ]
    counts = [len(line) for line in lines]
    packed = jnp.concatenate(lines)
    packed = jnp.pad(packed, ((0, -len(packed) % 8), (0, 0)))
    gathered = lax.all_gather(packed, "dp", axis=0)
    pieces, at = [], 0
    for count in counts:
        pieces.append(gathered[:, at : at + count].astype(F32))
        at += count
    grad_wo = pieces[0].reshape(-1, width)
    grad_wo = jnp.concatenate([grad_wo[: len(grad_wo) // 2], grad_wo[len(grad_wo) // 2 :]], axis=1)
    grad_wq = pieces[1].reshape(-1, width)
    grad_wkv = pieces[2].reshape(model_width, -1)
    grad_gain1 = jnp.sum(pieces[3], axis=0).reshape(-1)
    grad_gain2 = jnp.sum(pieces[4], axis=0).reshape(-1)
    all_peaks = pieces[5][:, 0]
    head_peaks = jnp.max(
        all_peaks[:, :local_heads] + all_peaks[:, local_heads : 2 * local_heads], axis=0
    )
    factor = clip_limit / jnp.maximum(head_peaks, clip_limit)
    key_factor = jnp.min(factor.reshape(local_kv, group), axis=1)
    clipped_query = (w_query.astype(F32) * jnp.repeat(jnp.sqrt(factor), HD)[None, :]).astype(BF16)
    clipped_key = (w_key.astype(F32) * jnp.repeat(jnp.sqrt(key_factor), HD)[None, :]).astype(BF16)
    return (
        output,
        input_grad,
        grad_wq,
        grad_wkv[:, :kv_rows],
        grad_wkv[:, kv_rows:],
        grad_wo,
        grad_gain1,
        grad_gain2,
        grad_gate[None],
        grad_up[None],
        grad_down[None],
        clipped_query,
        clipped_key,
        head_peaks,
    )


def solution(mesh):
    in_specs = (
        P("dp", None),
        P("dp", None),
        P(),
        P(),
        P(None, "tensor"),
        P(None, "tensor"),
        P(None, "tensor"),
        P("tensor", None),
        P("dp", None, "tensor"),
        P("dp", None, "tensor"),
        P("dp", "tensor", None),
        P("dp", None),
        P("dp", None),
        P("dp"),
        P("dp"),
        P("tensor"),
    )
    out_specs = (
        P("dp", None),
        P("dp", None),
        P(None, "tensor"),
        P(None, "tensor"),
        P(None, "tensor"),
        P("tensor", None),
        P(),
        P(),
        P("dp", None, "tensor"),
        P("dp", None, "tensor"),
        P("dp", "tensor", None),
        P(None, "tensor"),
        P(None, "tensor"),
        P("tensor"),
    )
    return jax.shard_map(shards, mesh=mesh, in_specs=in_specs, out_specs=out_specs, check_vma=False)
```

time: 1080 us -> 752 us (0.70)
  blocking collectives: 181 us -> 0 us
  local copies, waits for them, and re-layouts: 182 us -> 32.2 us
  matrix products: 163 us -> 75.9 us
  Pallas kernels: 0 us -> 57.1 us
  other arithmetic: 102 us -> 51.2 us
  waiting for transfers between devices: 322 us -> 367 us
  starting transfers between devices: 98.3 us -> 143 us
    all_to_all x5 -> x0, blocking collectives: 181 us -> none  [the longest x2 159 us: to_owners(): got = lax.all_to_all(rows, 'dp', split_axis=1, concat_axis=1, tiled=True)]
    psum x1 -> x0, waiting for transfers between devices: 140 us -> none  [in_one(): so_far = lax.psum(ravelled, axis)]
    dot_general x27 -> x26, matrix products: 163 us -> 75.9 us  [contract(): lax.dot_general(left, right, (dims, ((), ())), preferred_element_type=F32)]
    all_to_all x5 -> x7, waiting for transfers between devices: 163 us -> 245 us  [to_all(): return lax.all_to_all(array, 'dp', 0, 0, tiled=True)]
    ppermute x16 -> x18, waiting for transfers between devices: 8.12 us -> 84.3 us  [the longest x8 78.3 us: passed_along(): lax.ppermute(value, 'dp', [(s, s + steps) for s in range(first, last)])]
    gather x4 -> x0, local copies, waits for them, and re-layouts: 66.5 us -> none  [the longest x2 35.9 us: to_owners(): rows = table[slot_token]]
    pallas_call x0 -> x3, Pallas kernels: none -> 57.1 us  [the longest x1 29.9 us: experts(): pl.pallas_call(expert_kernel, grid=(count // tile,), in_specs=[wide, wide...]
    all_to_all x5 -> x7, starting transfers between devices: 54.9 us -> 106 us  [to_all(): return lax.all_to_all(array, 'dp', 0, 0, tiled=True)]
  transfers between devices with their start and end apart: 26 -> 26, of which waited for: 7 -> 16; matrix products, arithmetic and copies ran while one was open for 23% -> 12% of each run, Pallas kernels for 0% -> 4%
where the time goes in v1:
time: 752 us; the launch traced here: 741 us
  waiting for transfers between devices  367 us (49%)
  starting transfers between devices  143 us (19%)
  matrix products  75.9 us (10%)
  Pallas kernels  57.1 us (8%)
  other arithmetic  51.2 us (7%)
  local copies, waits for them, and re-layouts  32.2 us (4%)
  between operations  15.3 us (2%)
    all_to_all x7, waiting for transfers between devices, to_all(): return lax.all_to_all(array, 'dp', 0, 0, tiled=True)  245 us
    all_to_all x7, starting transfers between devices, to_all(): return lax.all_to_all(array, 'dp', 0, 0, tiled=True)  106 us
    ppermute x8, waiting for transfers between devices, passed_along(): lax.ppermute(value, 'dp', [(s, s + steps) for s in range(first, last)])  78.3 us
    dot_general x26, matrix products, contract(): lax.dot_general(left, right, (dims, ((), ())), preferred_element_type=F32)  75.9 us
    all_gather x1, waiting for transfers between devices, shards(): gathered = lax.all_gather(packed, 'dp', axis=0)  37.2 us
    pallas_call x1, Pallas kernels, experts(): pl.pallas_call(expert_kernel, grid=(count // tile,), in_specs=[wide, wide...  29.9 us
    ppermute x8, starting transfers between devices, passed_along(): lax.ppermute(value, 'dp', [(s, s + steps) for s in range(first, last)])  20.2 us
    ppermute x10, starting transfers between devices, swapped(): return lax.ppermute(array, 'tensor', [(0, 1), (1, 0)])  16.7 us
  transfers between devices with their start and end apart: 26, of which 16 were waited for; matrix products, arithmetic and copies ran while one was open for 12% of the time, Pallas kernels for 4%

profile of v1, /device:TPU:1, one launch (start us, length us, event | category | flops | bytes accessed | tf_op | source)
XLA Modules:
  0.0 741.4 jit_solution(12635568440163892779)
XLA Ops:
  17.7 12.3 %all-to-all-start.1 = ((bf16[64,32,1536]{2,1,0:T(8,128)(2,1)}), bf16[64,32,1536]{2,1,0:T(8,128)(2,1)}, u32[]{:S(2)}, u32[]{:S(2)}) async-start(bf16[64,32,1536]{2,1,0:T(8,128)(2,1)} %bitcast.121), calls=%async_computation.1 | async-start | bytes 12582912 | tf_op jit(solution)/shard_map/all_to_all | solution.py:46
  59.4 41.6 %collective-permute-done.3.k1 = bf16[528,256]{1,0:T(8,128)(2,1)} collective-permute-done((bf16[528,256]{1,0:T(8,128)(2,1)S(1)}, bf16[528,256]{1,0:T(8,128)(2,1)}, u32[]{:S(2)}, u32[]{:S(2)}) %collective-permute-start.3) | collective-permute-done | bytes 270368 | tf_op jit(solution)/shard_map/ppermute | solution.py:42
  101.0 7.5 %collective-permute-done.2.k2 = bf16[528,256]{1,0:T(8,128)(2,1)} collective-permute-done((bf16[528,256]{1,0:T(8,128)(2,1)S(1)}, bf16[528,256]{1,0:T(8,128)(2,1)}, u32[]{:S(2)}, u32[]{:S(2)}) %collective-permute-start.2) | collective-permute-done | bytes 270368 | tf_op jit(solution)/shard_map/ppermute | solution.py:42
  110.5 6.6 collective-permute-done.k4
  117.1 11.5 %shard_map.299 = (bf16[768,256]{1,0:T(8,128)(2,1)S(1)}, f32[12,256]{1,0:T(8,128)S(1)}, f32[12,256]{1,0:T(8,128)S(1)}) custom-call(bf16[768,256]{1,0:T(8,128)(2,1)S(1)} %bitcast.105, bf16[528,256]{1,0:T(8,128)(2,1)} %collective-permute-done.k4, bf16[528,256]{1,0:T(8,128)(2,1)} %collective-permute-done.1.k3, bf16[528,256]{1,0:T(8,128)(2,1)} %collective-permute-done.2.k2, ...), custom_call_target="tpu_custom_call" | custom-call | flops 1006632960 | bytes 2138112 | tf_op jit(solution)/shard_map/pallas_call | solution.py:121
  140.2 26.9 %all-to-all-start = ((bf16[64,32,1536]{2,1,0:T(8,128)(2,1)}), bf16[64,32,1536]{2,1,0:T(8,128)(2,1)}, u32[]{:S(2)}, u32[]{:S(2)}) async-start(bf16[64,32,1536]{2,1,0:T(8,128)(2,1)} %bitcast.111), calls=%async_computation | async-start | bytes 12582912 | tf_op jit(solution)/shard_map/all_to_all | solution.py:46
  173.9 74.1 %all-to-all-done = bf16[64,32,1536]{2,1,0:T(8,128)(2,1)} async-done(((bf16[64,32,1536]{2,1,0:T(8,128)(2,1)}), bf16[64,32,1536]{2,1,0:T(8,128)(2,1)}, u32[]{:S(2)}, u32[]{:S(2)}) %all-to-all-start) | async-done | bytes 6291488 | tf_op jit(solution)/shard_map/all_to_all | solution.py:46
  254.8 29.9 %shard_map.300 = (bf16[2048,1536]{1,0:T(8,128)(2,1)}, bf16[2048,256]{1,0:T(8,128)(2,1)S(1)}, bf16[2048,256]{1,0:T(8,128)(2,1)}, bf16[2048,256]{1,0:T(8,128)(2,1)...) custom-call(bf16[2048,1536]{1,0:T(8,128)(2,1)} %bitcast.14.x_ref, ...), custom_call_target="tpu_custom_call" | custom-call | flops 16106127360 | bytes 29884416 | tf_op jit(solution)/shard_map/pallas_call | solution.py:229
  284.8 9.4 %all-to-all-start.3 = ((bf16[64,32,1536]{2,1,0:T(8,128)(2,1)}), bf16[64,32,1536]{2,1,0:T(8,128)(2,1)}, u32[]{:S(2)}, u32[]{:S(2)}) async-start(bf16[64,32,1536]{2,1,0:T(8,128)(2,1)} %bitcast.122), calls=%async_computation.3 | async-start | bytes 12582912 | tf_op jit(solution)/shard_map/all_to_all | solution.py:46
  302.0 69.6 %all-to-all-done.3 = bf16[64,32,1536]{2,1,0:T(8,128)(2,1)} async-done(((bf16[64,32,1536]{2,1,0:T(8,128)(2,1)}), bf16[64,32,1536]{2,1,0:T(8,128)(2,1)}, u32[]{:S(2)}, u32[]{:S(2)}) %all-to-all-start.3) | async-done | bytes 6291488 | tf_op jit(solution)/shard_map/all_to_all | solution.py:46
  371.6 16.6 %all-to-all-start.2 = ((bf16[64,32,1536]{2,1,0:T(8,128)(2,1)}), bf16[64,32,1536]{2,1,0:T(8,128)(2,1)}, u32[]{:S(2)}, u32[]{:S(2)}) async-start(bf16[64,32,1536]{2,1,0:T(8,128)(2,1)} %bitcast.112), calls=%async_computation.2 | async-start | bytes 12582912 | tf_op jit(solution)/shard_map/all_to_all | solution.py:46
  398.1 64.7 %all-to-all-done.2 = bf16[64,32,1536]{2,1,0:T(8,128)(2,1)} async-done(((bf16[64,32,1536]{2,1,0:T(8,128)(2,1)}), bf16[64,32,1536]{2,1,0:T(8,128)(2,1)}, u32[]{:S(2)}, u32[]{:S(2)}) %all-to-all-start.2) | async-done | bytes 6291488 | tf_op jit(solution)/shard_map/all_to_all | solution.py:46
  482.4 15.9 %all-to-all-start.4 = ((bf16[64,24,768]{2,1,0:T(8,128)(2,1)}), bf16[64,24,768]{2,1,0:T(8,128)(2,1)}, u32[]{:S(2)}, u32[]{:S(2)}) async-start(bf16[64,24,768]{2,1,0:T(8,128)(2,1)} %bitcast.113), calls=%async_computation.4 | async-start | bytes 4718592 | tf_op jit(solution)/shard_map/all_to_all | solution.py:46
  499.2 15.7 %shard_map.301 = (bf16[768,256]{1,0:T(8,128)(2,1)S(1)}, bf16[512,256]{1,0:T(8,128)(2,1)S(1)}, bf16[512,256]{1,0:T(8,128)(2,1)S(1)}, bf16[512,256]{1,0:T(8,128)(2...) custom-call(bf16[768,256]{1,0:T(8,128)(2,1)S(1)} %bitcast.106, bf16[768,256]{1,0:T(8,128)(2,1)S(1)} %copy-done.20, ...), custom_call_target="tpu_custom_call" | custom-call | flops 2516582400 | bytes 3883008 | tf_op jit(solution)/shard_map/pallas_call | solution.py:184
  520.1 10.2 %collective-permute-done.10 = bf16[512,256]{1,0:T(8,128)(2,1)S(1)} collective-permute-done((bf16[512,256]{1,0:T(8,128)(2,1)S(1)}, bf16[512,256]{1,0:T(8,128)(2,1)S(1)}, u32[]{:S(2)}, u32[]{:S(2)}) %collective-permute-start.10) | collective-permute-done | bytes 262176 | tf_op jit(solution)/shard_map/ppermute | solution.py:42
  530.3 8.0 %collective-permute-done.11 = bf16[512,256]{1,0:T(8,128)(2,1)S(1)} collective-permute-done((bf16[512,256]{1,0:T(8,128)(2,1)S(1)}, bf16[512,256]{1,0:T(8,128)(2,1)S(1)}, u32[]{:S(2)}, u32[]{:S(2)}) %collective-permute-start.11) | collective-permute-done | bytes 262176 | tf_op jit(solution)/shard_map/ppermute | solution.py:42
  547.8 18.4 %all-to-all-start.5 = ((bf16[64,24,768]{2,1,0:T(8,128)(2,1)}), bf16[64,24,768]{2,1,0:T(8,128)(2,1)}, u32[]{:S(2)}, u32[]{:S(2)}) async-start(bf16[64,24,768]{2,1,0:T(8,128)(2,1)} %bitcast.114), calls=%async_computation.5 | async-start | bytes 4718592 | tf_op jit(solution)/shard_map/all_to_all | solution.py:46
  577.5 19.7 %all-to-all-done.5 = bf16[64,24,768]{2,1,0:T(8,128)(2,1)} async-done(((bf16[64,24,768]{2,1,0:T(8,128)(2,1)}), bf16[64,24,768]{2,1,0:T(8,128)(2,1)}, u32[]{:S(2)}, u32[]{:S(2)}) %all-to-all-start.5) | async-done | bytes 2359328 | tf_op jit(solution)/shard_map/all_to_all | solution.py:46
  597.2 6.7 all-to-all-start.6
  608.3 17.1 %all-to-all-done.6 = bf16[64,24,512]{2,1,0:T(8,128)(2,1)} async-done(((bf16[64,24,512]{2,1,0:T(8,128)(2,1)}), bf16[64,24,512]{2,1,0:T(8,128)(2,1)}, u32[]{:S(2)}, u32[]{:S(2)}) %all-to-all-start.6) | async-done | bytes 1572896 | tf_op jit(solution)/shard_map/all_to_all | solution.py:46
  652.3 5.9 fusion.7
  658.2 5.8 fusion.8
  664.0 37.2 %all-gather.3.cloned.1.call-done = bf16[4608,768]{1,0:T(8,128)(2,1)} async-done(((bf16[72,768]{1,0:T(8,128)(2,1)}), bf16[4608,768]{1,0:T(8,128)(2,1)}) %all-gather.3.cloned.1.call-update) | async-done | bytes 7077904 | tf_op jit(solution)/shard_map/all_gather | solution.py:406
  706.2 5.9 slice_convert_fusion
  (254 shorter events, 189.0 us)
Async XLA Ops:
  17.7 122.5 %all-to-all-start.1 = ((bf16[64,32,1536]{2,1,0:T(8,128)(2,1)}), bf16[64,32,1536]{2,1,0:T(8,128)(2,1)}, u32[]{:S(2)}, u32[]{:S(2)}) async-start(bf16[64,32,1536]{2,1,0:T(8,128)(2,1)} %bitcast.121), calls=%async_computation.1 | async-start | bytes 12582912 | tf_op jit(solution)/shard_map/all_to_all | solution.py:46
  37.4 63.6 %collective-permute-start.3 = (bf16[528,256]{1,0:T(8,128)(2,1)S(1)}, bf16[528,256]{1,0:T(8,128)(2,1)}, u32[]{:S(2)}, u32[]{:S(2)}) collective-permute-start(bf16[528,256]{1,0:T(8,128)(2,1)S(1)} %concatenate.38.k0), channel_id=1, source_target_pairs={{0,2},{2,4},{4,6},{6,8},{8,10},{10,12},{12,14},{14,16},{16,18},{18... | collective-permute-start | bytes 811016 | tf_op jit(solution)/shard_map/ppermute | solution.py:42
  40.9 67.6 %collective-permute-start.2 = (bf16[528,256]{1,0:T(8,128)(2,1)S(1)}, bf16[528,256]{1,0:T(8,128)(2,1)}, u32[]{:S(2)}, u32[]{:S(2)}) collective-permute-start(bf16[528,256]{1,0:T(8,128)(2,1)S(1)} %concatenate.38.k0), channel_id=1, source_target_pairs={{0,4},{2,6},{4,8},{6,10},{8,12},{10,14},{12,16},{14,18},{16,20},{1... | collective-permute-start | bytes 811016 | tf_op jit(solution)/shard_map/ppermute | solution.py:42
  45.2 65.2 %collective-permute-start.1 = (bf16[528,256]{1,0:T(8,128)(2,1)S(1)}, bf16[528,256]{1,0:T(8,128)(2,1)}, u32[]{:S(2)}, u32[]{:S(2)}) collective-permute-start(bf16[528,256]{1,0:T(8,128)(2,1)S(1)} %concatenate.38.k0), channel_id=1, source_target_pairs={{0,6},{2,8},{4,10},{6,12},{8,14},{10,16},{12,18},{14,20},{16,22},{... | collective-permute-start | bytes 811016 | tf_op jit(solution)/shard_map/ppermute | solution.py:42
  49.2 67.9 %collective-permute-start = (bf16[528,256]{1,0:T(8,128)(2,1)S(1)}, bf16[528,256]{1,0:T(8,128)(2,1)}, u32[]{:S(2)}, u32[]{:S(2)}) collective-permute-start(bf16[528,256]{1,0:T(8,128)(2,1)S(1)} %concatenate.38.k0), channel_id=1, source_target_pairs={{0,8},{2,10},{4,12},{6,14},{8,16},{10,18},{12,20},{14,22},{16,24},... | collective-permute-start | bytes 811016 | tf_op jit(solution)/shard_map/ppermute | solution.py:42
  129.4 4.7 collective-permute-start.4
  140.2 107.8 %all-to-all-start = ((bf16[64,32,1536]{2,1,0:T(8,128)(2,1)}), bf16[64,32,1536]{2,1,0:T(8,128)(2,1)}, u32[]{:S(2)}, u32[]{:S(2)}) async-start(bf16[64,32,1536]{2,1,0:T(8,128)(2,1)} %bitcast.111), calls=%async_computation | async-start | bytes 12582912 | tf_op jit(solution)/shard_map/all_to_all | solution.py:46
  167.9 5.2 collective-permute-start.7
  284.8 86.9 %all-to-all-start.3 = ((bf16[64,32,1536]{2,1,0:T(8,128)(2,1)}), bf16[64,32,1536]{2,1,0:T(8,128)(2,1)}, u32[]{:S(2)}, u32[]{:S(2)}) async-start(bf16[64,32,1536]{2,1,0:T(8,128)(2,1)} %bitcast.122), calls=%async_computation.3 | async-start | bytes 12582912 | tf_op jit(solution)/shard_map/all_to_all | solution.py:46
  371.6 91.1 %all-to-all-start.2 = ((bf16[64,32,1536]{2,1,0:T(8,128)(2,1)}), bf16[64,32,1536]{2,1,0:T(8,128)(2,1)}, u32[]{:S(2)}, u32[]{:S(2)}) async-start(bf16[64,32,1536]{2,1,0:T(8,128)(2,1)} %bitcast.112), calls=%async_computation.2 | async-start | bytes 12582912 | tf_op jit(solution)/shard_map/all_to_all | solution.py:46
  393.9 78.4 %collective-permute-start.9 = (bf16[256,1536]{1,0:T(8,128)(2,1)}, bf16[256,1536]{1,0:T(8,128)(2,1)}, u32[]{:S(2)}, u32[]{:S(2)}) collective-permute-start(bf16[256,1536]{1,0:T(8,128)(2,1)} %fusion.11), channel_id=1, source_target_pairs={{0,1},{1,0},{2,3},{3,2},{4,5},{5,4},{6,7},{7,6},{8,9},{9,8},{10,11... | collective-permute-start | bytes 2359304 | tf_op jit(solution)/shard_map/ppermute | solution.py:36
  467.7 7.1 collective-permute-start.8
  482.4 65.4 %all-to-all-start.4 = ((bf16[64,24,768]{2,1,0:T(8,128)(2,1)}), bf16[64,24,768]{2,1,0:T(8,128)(2,1)}, u32[]{:S(2)}, u32[]{:S(2)}) async-start(bf16[64,24,768]{2,1,0:T(8,128)(2,1)} %bitcast.113), calls=%async_computation.4 | async-start | bytes 4718592 | tf_op jit(solution)/shard_map/all_to_all | solution.py:46
  514.9 15.4 %collective-permute-start.10 = (bf16[512,256]{1,0:T(8,128)(2,1)S(1)}, bf16[512,256]{1,0:T(8,128)(2,1)S(1)}, u32[]{:S(2)}, u32[]{:S(2)}) collective-permute-start(bf16[512,256]{1,0:T(8,128)(2,1)S(1)} %get-tuple-element.37), channel_id=1, source_target_pairs={{8,0},{10,2},{12,4},{14,6},{16,8},{18,10},{20,12},{22,14},{24,16},... | collective-permute-start | bytes 786440 | tf_op jit(solution)/shard_map/ppermute | solution.py:42
  516.2 22.2 %collective-permute-start.11 = (bf16[512,256]{1,0:T(8,128)(2,1)S(1)}, bf16[512,256]{1,0:T(8,128)(2,1)S(1)}, u32[]{:S(2)}, u32[]{:S(2)}) collective-permute-start(bf16[512,256]{1,0:T(8,128)(2,1)S(1)} %get-tuple-element.38), channel_id=1, source_target_pairs={{6,0},{8,2},{10,4},{12,6},{14,8},{16,10},{18,12},{20,14},{22,16},{... | collective-permute-start | bytes 786440 | tf_op jit(solution)/shard_map/ppermute | solution.py:42
  517.5 23.2 %collective-permute-start.12 = (bf16[512,256]{1,0:T(8,128)(2,1)S(1)}, bf16[512,256]{1,0:T(8,128)(2,1)S(1)}, u32[]{:S(2)}, u32[]{:S(2)}) collective-permute-start(bf16[512,256]{1,0:T(8,128)(2,1)S(1)} %get-tuple-element.39), channel_id=1, source_target_pairs={{4,0},{6,2},{8,4},{10,6},{12,8},{14,10},{16,12},{18,14},{20,16},{2... | collective-permute-start | bytes 786440 | tf_op jit(solution)/shard_map/ppermute | solution.py:42
  518.8 21.9 %collective-permute-start.13 = (bf16[512,256]{1,0:T(8,128)(2,1)S(1)}, bf16[512,256]{1,0:T(8,128)(2,1)S(1)}, u32[]{:S(2)}, u32[]{:S(2)}) collective-permute-start(bf16[512,256]{1,0:T(8,128)(2,1)S(1)} %get-tuple-element.40), channel_id=1, source_target_pairs={{2,0},{4,2},{6,4},{8,6},{10,8},{12,10},{14,12},{16,14},{18,16},{20... | collective-permute-start | bytes 786440 | tf_op jit(solution)/shard_map/ppermute | solution.py:42
  545.0 23.6 %collective-permute-start.14 = (bf16[256,1536]{1,0:T(8,128)(2,1)S(1)}, bf16[256,1536]{1,0:T(8,128)(2,1)}, u32[]{:S(2)}, u32[]{:S(2)}) collective-permute-start(bf16[256,1536]{1,0:T(8,128)(2,1)S(1)} %fusion.10), channel_id=1, source_target_pairs={{0,1},{1,0},{2,3},{3,2},{4,5},{5,4},{6,7},{7,6},{8,9},{9,8},{10,11... | collective-permute-start | bytes 2359304 | tf_op jit(solution)/shard_map/ppermute | solution.py:36
  547.8 49.4 %all-to-all-start.5 = ((bf16[64,24,768]{2,1,0:T(8,128)(2,1)}), bf16[64,24,768]{2,1,0:T(8,128)(2,1)}, u32[]{:S(2)}, u32[]{:S(2)}) async-start(bf16[64,24,768]{2,1,0:T(8,128)(2,1)} %bitcast.114), calls=%async_computation.5 | async-start | bytes 4718592 | tf_op jit(solution)/shard_map/all_to_all | solution.py:46
  597.2 28.2 %all-to-all-start.6 = ((bf16[64,24,512]{2,1,0:T(8,128)(2,1)}), bf16[64,24,512]{2,1,0:T(8,128)(2,1)}, u32[]{:S(2)}, u32[]{:S(2)}) async-start(bf16[64,24,512]{2,1,0:T(8,128)(2,1)} %pad_maximum_fusion.2), calls=%async_computation.6 | async-start | bytes 3145728 | tf_op jit(solution)/shard_map/all_to_all | solution.py:46
  604.0 97.2 %all-gather.3.cloned.1.call-start = ((), (), s32[]{:S(2)}) async-start(), calls=%async_computation.7 | async-start | bytes 7188480 | tf_op jit(solution)/shard_map/all_gather | solution.py:406
  632.5 14.1 %collective-permute-start.17 = (bf16[256,1536]{1,0:T(8,128)(2,1)S(1)}, bf16[256,1536]{1,0:T(8,128)(2,1)S(1)}, u32[]{:S(2)}, u32[]{:S(2)}) collective-permute-start(bf16[256,1536]{1,0:T(8,128)(2,1)S(1)} %convolution_convert_fusion.3), channel_id=1, source_target_pairs={{0,1},{1,0},{2,3},{3,2},{4,5},{5,4},{6,7},{7,6},{8,9},{9,8},{10,11... | collective-permute-start | bytes 2359304 | tf_op jit(solution)/shard_map/ppermute | solution.py:36
  641.0 11.3 %collective-permute-start.16 = (bf16[1536,256]{1,0:T(8,128)(2,1)S(1)}, bf16[1536,256]{1,0:T(8,128)(2,1)S(1)}, u32[]{:S(2)}, u32[]{:S(2)}) collective-permute-start(bf16[1536,256]{1,0:T(8,128)(2,1)S(1)} %convolution_convert_fusion.4), channel_id=1, source_target_pairs={{0,1},{1,0},{2,3},{3,2},{4,5},{5,4},{6,7},{7,6},{8,9},{9,8},{10,11... | collective-permute-start | bytes 2359304 | tf_op jit(solution)/shard_map/ppermute | solution.py:36
  645.8 12.5 %collective-permute-start.15 = (bf16[1536,256]{1,0:T(8,128)(2,1)S(1)}, bf16[1536,256]{1,0:T(8,128)(2,1)S(1)}, u32[]{:S(2)}, u32[]{:S(2)}) collective-permute-start(bf16[1536,256]{1,0:T(8,128)(2,1)S(1)} %convolution_convert_fusion.5), channel_id=1, source_target_pairs={{0,1},{1,0},{2,3},{3,2},{4,5},{5,4},{6,7},{7,6},{8,9},{9,8},{10,11... | collective-permute-start | bytes 2359304 | tf_op jit(solution)/shard_map/ppermute | solution.py:36
  (62 other events, 634.5 us)
Sparse Core Ops, SparseCore 0:
  627.9 73.2 all-gather.2

commit v2 on v1

--- a/solution.py
+++ b/solution.py
@@ -13,7 +13,9 @@
 TOP = 8
 CAP = 64
 HOPS = 4
-SLOTS = 64
+RANK_ROWS = 32
+PLANE = 16
+SEGMENTS = 3
 AUX = 16
 
 EPS = 1e-06
@@ -34,6 +36,10 @@
 
 def swapped(array):
     return lax.ppermute(array, "tensor", [(0, 1), (1, 0)])
+
+
+def after(array, other):
+    return lax.optimization_barrier((array, other))[0]
 
 
 def passed_along(value, steps):
@@ -191,55 +197,197 @@
         scratch_shapes=[pltpu.VMEM((len(blocks) * tok, tok), F32)],
         compiler_params=pltpu.CompilerParams(vmem_limit_bytes=48 << 20),
         cost_estimate=pl.CostEstimate(
-            flops=10 * rows * tok * tok * len(blocks),
+            flops=1000 * rows * tok * tok * len(blocks),
             bytes_accessed=6 * rows * tok + 4 * len(blocks) * 528 * tok,
             transcendentals=rows // HD * tok * tok * len(blocks),
         ),
     )(q, grad, log_total, cosine, sine, *blocks)
 
 
-def expert_kernel(x_ref, g_ref, go, gp, uo, up, do, dp, dx_ref, *outs):
-    rows, grads = (x_ref[...], g_ref[...])
+def expert_kernel(x_ref, g_ref, own_ref, peer_ref, dx_ref, inner_ref, acts_ref):
+    width = x_ref.shape[-1]
+    rows, grads = (x_ref[...].reshape(-1, width), g_ref[...].reshape(-1, width))
+    hidden = own_ref.shape[-1]
     back = None
-    for side, (gate_w, up_w, down_w) in enumerate(((go, uo, do), (gp, up, dp))):
-        inner_ref, dgate_ref, dup_ref = outs[3 * side : 3 * side + 3]
-        gate_act = contract(rows, gate_w[...], NN)
-        up_act = contract(rows, up_w[...], NN)
-        grad_inner = contract(grads, down_w[...], NT)
+    for side, weights in enumerate((own_ref, peer_ref)):
+        gate_w, up_w, down_w = (weights[0, 0], weights[0, 1], weights[0, 2])
+        gate_act = contract(rows, gate_w, NN)
+        up_act = contract(rows, up_w, NN)
+        grad_inner = contract(grads, down_w, NN)
         sigmoid = 1.0 / (1.0 + jnp.exp(-gate_act))
         silu = gate_act * sigmoid
-        inner_ref[...] = (silu * up_act).astype(BF16)
         dgate = (grad_inner * up_act * (sigmoid * (1.0 + gate_act * (1.0 - sigmoid)))).astype(BF16)
         dup = (grad_inner * silu).astype(BF16)
-        dgate_ref[...] = dgate
-        dup_ref[...] = dup
-        part = contract(dgate, gate_w[...], NT) + contract(dup, up_w[...], NT)
+        at = side * hidden
+        inner_ref[0, :, at : at + hidden] = (silu * up_act).astype(BF16)
+        acts_ref[0, :, at : at + hidden] = dgate
+        acts_ref[0, :, (2 * hidden + at) : (3 * hidden + at)] = dup
+        part = contract(dgate, gate_w, NT) + contract(dup, up_w, NT)
         back = part if back is None else back + part
-    dx_ref[...] = back.astype(BF16)
-
-
-def experts(rows, grads, own, peer):
-    count, width = rows.shape
-    hidden = own[0].shape[1]
-    tile = 256
-    wide = pl.BlockSpec((tile, width), lambda i: (i, 0))
-    thin = pl.BlockSpec((tile, hidden), lambda i: (i, 0))
-    into = pl.BlockSpec((width, hidden), lambda i: (0, 0))
-    out_of = pl.BlockSpec((hidden, width), lambda i: (0, 0))
+    dx_ref[...] = back.astype(BF16).reshape(dx_ref.shape)
+
+
+def expert_back(rows, grads, own, peer):
+    sources, lines, width = rows.shape
+    segments, hidden = (lines // RANK_ROWS, own.shape[-1])
+    count = sources * RANK_ROWS
+    wide = pl.BlockSpec((sources, RANK_ROWS, width), lambda s: (0, s, 0))
+    weight = pl.BlockSpec((1, 3, width, hidden), lambda s: (s, 0, 0, 0))
+    flops = 20 * sources * lines * width * hidden
     return pl.pallas_call(
         expert_kernel,
-        grid=(count // tile,),
-        in_specs=[wide, wide, into, into, into, into, out_of, out_of],
-        out_specs=[wide] + [thin] * 6,
-        out_shape=[jax.ShapeDtypeStruct((count, width), BF16)]
-        + [jax.ShapeDtypeStruct((count, hidden), BF16)] * 6,
-        compiler_params=pltpu.CompilerParams(vmem_limit_bytes=48 << 20),
+        grid=(segments,),
+        in_specs=[wide, wide, weight, weight],
+        out_specs=[
+            wide,
+            pl.BlockSpec((1, count, 2 * hidden), lambda s: (s, 0, 0)),
+            pl.BlockSpec((1, count, 4 * hidden), lambda s: (s, 0, 0)),
+        ],
+        out_shape=[
+            jax.ShapeDtypeStruct(rows.shape, BF16),
+            jax.ShapeDtypeStruct((segments, count, 2 * hidden), BF16),
+            jax.ShapeDtypeStruct((segments, count, 4 * hidden), BF16),
+        ],
+        compiler_params=pltpu.CompilerParams(vmem_limit_bytes=56 << 20),
         cost_estimate=pl.CostEstimate(
-            flops=20 * count * width * hidden,
-            bytes_accessed=6 * count * width + 12 * count * hidden + 12 * width * hidden,
-            transcendentals=2 * count * hidden,
-        ),
-    )(rows, grads, own[0], peer[0], own[1], peer[1], own[2], peer[2])
+            flops=flops,
+            bytes_accessed=6 * sources * lines * width + 12 * segments * width * hidden,
+            transcendentals=2 * sources * lines * hidden,
+        ),
+    )(rows, grads, own, peer)
+
+
+def expert_sums_kernel(x_ref, g_ref, inner_ref, acts_ref, own_ref, peer_ref, sum_own, sum_peer, out_ref):
+    width = x_ref.shape[-1]
+    rows, grads = (x_ref[...].reshape(-1, width), g_ref[...].reshape(-1, width))
+    hidden = own_ref.shape[-1]
+    inner = inner_ref[0]
+    sums = contract(rows, acts_ref[0], TN).astype(BF16)
+    down = contract(grads, inner, TN).astype(BF16)
+    for side, target in enumerate((sum_own, sum_peer)):
+        at = side * hidden
+        target[0, 0] = sums[:, at : at + hidden]
+        target[0, 1] = sums[:, (2 * hidden + at) : (3 * hidden + at)]
+        target[0, 2] = down[:, at : at + hidden]
+    out = contract(inner[:, :hidden], own_ref[0, 0], NT)
+    out = out + contract(inner[:, hidden:], peer_ref[0, 0], NT)
+    out_ref[...] = out.astype(BF16).reshape(out_ref.shape)
+
+
+def expert_sums(rows, grads, inner, acts, own, peer):
+    sources, lines, width = rows.shape
+    segments, hidden = (lines // RANK_ROWS, own.shape[-1])
+    count = sources * RANK_ROWS
+    wide = pl.BlockSpec((sources, RANK_ROWS, width), lambda s: (0, s, 0))
+    down = pl.BlockSpec((1, 1, width, hidden), lambda s: (s, 2, 0, 0))
+    total = pl.BlockSpec((1, 3, width, hidden), lambda s: (s, 0, 0, 0))
+    return pl.pallas_call(
+        expert_sums_kernel,
+        grid=(segments,),
+        in_specs=[
+            wide,
+            wide,
+            pl.BlockSpec((1, count, 2 * hidden), lambda s: (s, 0, 0)),
+            pl.BlockSpec((1, count, 4 * hidden), lambda s: (s, 0, 0)),
+            down,
+            down,
+        ],
+        out_specs=[total, total, wide],
+        out_shape=[
+            jax.ShapeDtypeStruct((segments, 3, width, hidden), BF16),
+            jax.ShapeDtypeStruct((segments, 3, width, hidden), BF16),
+            jax.ShapeDtypeStruct(rows.shape, BF16),
+        ],
+        compiler_params=pltpu.CompilerParams(vmem_limit_bytes=60 << 20),
+        cost_estimate=pl.CostEstimate(
+            flops=16 * sources * lines * width * hidden,
+            bytes_accessed=6 * sources * lines * width + 16 * segments * width * hidden,
+            transcendentals=0,
+        ),
+    )(rows, grads, inner, acts, own, peer)
+
+
+def both_cores_kernel(own_ref, peer_ref, out_ref):
+    @pl.when(pl.program_id(0) < SEGMENTS)
+    def _():
+        out_ref[...] = (own_ref[...].astype(F32) + peer_ref[...].astype(F32)).astype(BF16)
+
+    @pl.when(pl.program_id(0) >= SEGMENTS)
+    def _():
+        out_ref[...] = jnp.zeros_like(out_ref)
+
+
+def both_cores(own, peer, slots):
+    segments, kinds, width, hidden = own.shape
+    shape = (1, 1, width, hidden)
+    part = pl.BlockSpec(shape, lambda s, k: (jnp.minimum(s, segments - 1), k, 0, 0))
+    return pl.pallas_call(
+        both_cores_kernel,
+        grid=(slots, kinds),
+        in_specs=[part, part],
+        out_specs=pl.BlockSpec(shape, lambda s, k: (s, k, 0, 0)),
+        out_shape=jax.ShapeDtypeStruct((slots, kinds, width, hidden), BF16),
+        cost_estimate=pl.CostEstimate(
+            flops=slots * kinds * width * hidden,
+            bytes_accessed=6 * slots * kinds * width * hidden,
+            transcendentals=0,
+        ),
+    )(own, peer)
+
+
+def unpack_kernel(in_ref, wo_ref, wq_ref, wk_ref, wv_ref, sum_ref):
+    step = pl.program_id(0)
+    chunks, lines, width = in_ref.shape
+    third = lines // 3
+    narrow = wk_ref.shape[1]
+    for c in range(chunks):
+        here = slice(c * third, (c + 1) * third)
+        wo_ref[here, :] = in_ref[c, :third, :].astype(F32)
+        wq_ref[here, :] = in_ref[c, third : 2 * third, :].astype(F32)
+        wk_ref[here, :] = in_ref[c, 2 * third :, :narrow].astype(F32)
+        wv_ref[here, :] = in_ref[c, 2 * third :, narrow : 2 * narrow].astype(F32)
+    more = in_ref[:, 2 * third :, 2 * narrow :].astype(F32)
+    total = jnp.sum(more, axis=0)
+
+    @pl.when(step == 0)
+    def _():
+        sum_ref[...] = total
+
+    @pl.when(step > 0)
+    def _():
+        sum_ref[...] = sum_ref[...] + total
+
+
+def unpack(gathered, narrow):
+    parts, lines, width = gathered.shape
+    steps = 16
+    per, third = (parts // steps, lines // 3)
+    rows = per * third
+    total = parts * third
+    extra = (third, width - 2 * narrow)
+    return pl.pallas_call(
+        unpack_kernel,
+        grid=(steps,),
+        in_specs=[pl.BlockSpec((per, lines, width), lambda i: (i, 0, 0))],
+        out_specs=[
+            pl.BlockSpec((rows, width), lambda i: (i % (steps // 2), i // (steps // 2))),
+            pl.BlockSpec((rows, width), lambda i: (i, 0)),
+            pl.BlockSpec((rows, narrow), lambda i: (i, 0)),
+            pl.BlockSpec((rows, narrow), lambda i: (i, 0)),
+            pl.BlockSpec(extra, lambda i: (0, 0)),
+        ],
+        out_shape=[
+            jax.ShapeDtypeStruct((total // 2, 2 * width), F32),
+            jax.ShapeDtypeStruct((total, width), F32),
+            jax.ShapeDtypeStruct((total, narrow), F32),
+            jax.ShapeDtypeStruct((total, narrow), F32),
+            jax.ShapeDtypeStruct(extra, F32),
+        ],
+        compiler_params=pltpu.CompilerParams(vmem_limit_bytes=32 << 20),
+        cost_estimate=pl.CostEstimate(
+            flops=parts * lines * width, bytes_accessed=6 * parts * lines * width, transcendentals=0
+        ),
+    )(gathered)
 
 
 def rms_scale(values):
@@ -280,32 +428,37 @@
     local_heads = w_query.shape[1] // HD
     local_kv = w_key.shape[1] // HD
     group = local_heads // local_kv
-    rank_rows = CAP // tensor_size
-    own = (w_gate[0], w_up[0], w_down[0])
-    peer = tuple(swapped(w) for w in own)
+    plane_groups = [list(range(at, at + PLANE)) for at in range(0, dp_size, PLANE)]
+    column_groups = [list(range(at, dp_size, PLANE)) for at in range(PLANE)]
+
+    packed_w = jnp.stack([w_gate[0], w_up[0], w_down[0].T])
+    own = lax.all_gather(packed_w, "dp", axis=0, axis_index_groups=column_groups)
 
     picks = route_ids.T
     logits = route_logits.T
     gate_exp = jnp.exp(logits - jnp.max(logits, axis=0, keepdims=True))
     gates = gate_exp / jnp.sum(gate_exp, axis=0, keepdims=True)
-    same = picks[None] == jnp.arange(SLOTS, dtype=jnp.int32)[:, None, None]
+    number = jnp.arange(PLANE * SEGMENTS, dtype=jnp.int32)
+    number = number % SEGMENTS * PLANE + number // SEGMENTS
+    same = picks[None] == number[:, None, None]
     member = jnp.any(same, axis=1)
     gate_of = jnp.sum(jnp.where(same, gates[None], 0.0), axis=1)
     place = jnp.arange(tok_dev, dtype=jnp.int32)
     before = (place[:, None] < place[None, :]).astype(BF16)
     rank = contract(member.astype(BF16), before, NN)
     rank = jnp.where(member, rank, -1.0)
-    wanted = (tensor_size * jnp.arange(rank_rows, dtype=jnp.int32) + core).astype(F32)
+    wanted = (tensor_size * jnp.arange(RANK_ROWS, dtype=jnp.int32) + core).astype(F32)
     chosen = rank[:, None, :] == wanted[None, :, None]
     pick = chosen.astype(BF16).reshape(-1, tok_dev)
     gated = jnp.where(chosen, gate_of[:, None, :], 0.0)
     slot_gate = jnp.sum(gated, axis=2).reshape(-1, 1)
     gated = gated.astype(BF16).reshape(-1, tok_dev)
 
-    def to_owners(rows):
-        return to_all(rows.reshape(dp_size, rank_rows, model_width)).reshape(-1, model_width)
-
-    grad_rows = to_owners((contract(pick, out_grad, NN) * slot_gate).astype(BF16))
+    def in_plane(rows):
+        rows = rows.reshape(PLANE, -1, model_width)
+        return lax.all_to_all(rows, "dp", 0, 0, tiled=True, axis_index_groups=plane_groups)
+
+    grad_rows = (contract(pick, out_grad, NN) * slot_gate).astype(BF16)
 
     cosine, sine = rope_tables(tok_dev, dp_size)
     x_float = tokens.astype(F32)
@@ -320,34 +473,31 @@
     ).astype(BF16)
     block = jnp.concatenate([key, value, side])
     blocks = tuple(passed_along(block, hop) for hop in range(HOPS, 0, -1)) + (block,)
+    blocks, grad_rows = lax.optimization_barrier((blocks, grad_rows))
+    grad_rows = in_plane(grad_rows)
     attended, log_total, peaks = attend(query, blocks, group)
     attn_part = contract(attended, w_out, TN)
     hidden1 = x_float + (attn_part + swapped(attn_part))
     inverse2 = rms_scale(hidden1)
     normed2 = (hidden1 * inverse2 * norm2_gain).astype(BF16)
 
-    rows_in = to_owners(contract(pick, normed2, NN).astype(BF16))
-    back, *acts = experts(rows_in, grad_rows, own, peer)
-
-    def from_owners(rows):
-        return to_all(rows.reshape(dp_size, rank_rows, model_width)).reshape(-1, model_width)
+    rows_out = contract(pick, normed2, NN).astype(BF16)
+    rows_out = after(rows_out, grad_rows)
+    own = after(own, rows_out)
+    peer = swapped(own)
+    rows_in = in_plane(rows_out)
+    back, inner, acts = expert_back(rows_in, grad_rows, own, peer)
 
     def combined(weights, rows):
-        part = contract(weights, from_owners(rows), TN).astype(BF16)
+        part = contract(weights, rows.reshape(-1, model_width), TN).astype(BF16)
         return part.astype(F32) + swapped(part).astype(F32)
 
-    grad_normed2 = combined(pick, back)
-    inner, dgate, dup, inner_peer, dgate_peer, dup_peer = acts
-    expert_out = (contract(inner, own[2], NN) + contract(inner_peer, peer[2], NN)).astype(BF16)
-    grad_gate = contract(rows_in, dgate, TN) + swapped(
-        contract(rows_in, dgate_peer, TN).astype(BF16)
-    ).astype(F32)
-    grad_up = contract(rows_in, dup, TN) + swapped(
-        contract(rows_in, dup_peer, TN).astype(BF16)
-    ).astype(F32)
-    grad_down = contract(inner, grad_rows, TN) + swapped(
-        contract(inner_peer, grad_rows, TN).astype(BF16)
-    ).astype(F32)
+    sum_own, sum_peer, expert_out = expert_sums(rows_in, grad_rows, inner, acts, own, peer)
+    sums = both_cores(sum_own, swapped(sum_peer), dp_size // PLANE)
+    grad_normed2 = combined(pick, after(in_plane(back), sum_own))
+    sums = lax.psum_scatter(
+        sums, "dp", scatter_dimension=0, tiled=True, axis_index_groups=column_groups
+    )
 
     grad_top = out_grad.astype(F32)
     grad_from_norm2, grad_gain2 = norm_back(grad_normed2, hidden1, inverse2, norm2_gain)
@@ -357,33 +507,43 @@
     grad_query_pre, *grad_blocks = attend_back(
         query, grad_attended, log_total, cosine, sine, blocks, group
     )
+    half = model_width // 2
+    grad_wo = jnp.concatenate(
+        [contract(attended, grad_branch[:, :half], NN), contract(attended, grad_branch[:, half:], NN)]
+    ).astype(BF16)
+
+    def spread(part):
+        return to_all(part.reshape(dp_size, -1, part.shape[1]))
+
+    def share(parts):
+        return jnp.sum(parts.astype(F32), axis=0).astype(BF16)
+
+    share_wo = share(spread(grad_wo))
+    returned = [
+        passed_along(grad_blocks[number], -hop) for number, hop in enumerate(range(HOPS, 0, -1))
+    ]
+    returned = after(returned, share_wo)
     kv_total = grad_blocks[-1]
-    for number, hop in enumerate(range(HOPS, 0, -1)):
-        kv_total = kv_total + passed_along(grad_blocks[number], -hop).astype(F32)
-    output = (hidden1 + combined(gated, expert_out)).astype(BF16)
+    for part in returned:
+        kv_total = kv_total + part.astype(F32)
     kv_rows = local_kv * HD
     grad_key_pre = rotate(kv_total[:kv_rows], cosine, -sine).astype(BF16)
     grad_value = kv_total[kv_rows:].astype(BF16)
 
-    half = model_width // 2
-    grad_wo = jnp.concatenate(
-        [contract(attended, grad_branch[:, :half], NN), contract(attended, grad_branch[:, half:], NN)]
-    )
-    grad_wq = contract(normed1, grad_query_pre, ((0,), (1,)))
-    grad_wk = contract(normed1, grad_key_pre, ((0,), (1,)))
-    grad_wv = contract(normed1, grad_value, ((0,), (1,)))
+    grad_wqkv = jnp.concatenate(
+        [
+            contract(normed1, part, ((0,), (1,))).astype(BF16)
+            for part in (grad_query_pre, grad_key_pre, grad_value)
+        ],
+        axis=1,
+    )
+    share_wqkv = share(spread(grad_wqkv))
     grad_norm1_part = (
         contract(grad_query_pre, w_query, ((0,), (1,)))
         + contract(grad_key_pre, w_key, ((0,), (1,)))
         + contract(grad_value, w_value, ((0,), (1,)))
     ).astype(BF16)
 
-    def share(part):
-        return jnp.sum(to_all(part.astype(BF16).reshape(dp_size, -1, part.shape[1])).astype(F32), axis=0)
-
-    share_wo = share(grad_wo)
-    share_wq = share(grad_wq)
-    share_wkv = share(jnp.concatenate([grad_wk, grad_wv], axis=1))
     grad_normed1 = grad_norm1_part.astype(F32) + swapped(grad_norm1_part).astype(F32)
     grad_from_norm1, grad_gain1 = norm_back(grad_normed1, x_float, inverse1, norm1_gain)
     input_grad = grad_hidden1 + grad_from_norm1
@@ -391,32 +551,36 @@
     peak = jnp.max(peaks, axis=1)
     peak_high = peak.astype(BF16)
     peak_low = (peak - peak_high.astype(F32)).astype(BF16)
-    peak_row = jnp.pad(jnp.concatenate([peak_high, peak_low]), (0, width - 2 * local_heads))
-    lines = [
-        share_wo.astype(BF16),
-        share_wq.astype(BF16),
-        share_wkv.astype(BF16).reshape(-1, width),
-        grad_gain1.astype(BF16).reshape(-1, width),
-        grad_gain2.astype(BF16).reshape(-1, width),
-        peak_row[None],
-    ]
-    counts = [len(line) for line in lines]
-    packed = jnp.concatenate(lines)
-    packed = jnp.pad(packed, ((0, -len(packed) % 8), (0, 0)))
+    third = model_width // dp_size
+    more = width - 2 * kv_rows
+    extra = jnp.concatenate(
+        [
+            grad_gain1.astype(BF16).reshape(-1, more),
+            grad_gain2.astype(BF16).reshape(-1, more),
+            jnp.pad(jnp.stack([peak_high, peak_low]), ((0, 0), (0, more - local_heads))),
+        ]
+    )
+    gain_rows = model_width // more
+    extra = jnp.pad(extra, ((0, third - len(extra)), (0, 0)))
+    packed = jnp.concatenate(
+        [
+            share_wo,
+            share_wqkv[:, :width],
+            jnp.concatenate([share_wqkv[:, width:], extra], axis=1),
+        ]
+    )
+    packed, sums, expert_out = lax.optimization_barrier((packed, sums, expert_out))
     gathered = lax.all_gather(packed, "dp", axis=0)
-    pieces, at = [], 0
-    for count in counts:
-        pieces.append(gathered[:, at : at + count].astype(F32))
-        at += count
-    grad_wo = pieces[0].reshape(-1, width)
-    grad_wo = jnp.concatenate([grad_wo[: len(grad_wo) // 2], grad_wo[len(grad_wo) // 2 :]], axis=1)
-    grad_wq = pieces[1].reshape(-1, width)
-    grad_wkv = pieces[2].reshape(model_width, -1)
-    grad_gain1 = jnp.sum(pieces[3], axis=0).reshape(-1)
-    grad_gain2 = jnp.sum(pieces[4], axis=0).reshape(-1)
-    all_peaks = pieces[5][:, 0]
+    output = (hidden1 + combined(gated, in_plane(expert_out))).astype(BF16)
+    sums = sums[0].astype(F32)
+    grad_gate, grad_up, grad_down = (sums[0], sums[1], sums[2].T)
+    grad_wo, grad_wq, grad_wk, grad_wv, totals = unpack(gathered, kv_rows)
+    grad_gain1 = totals[:gain_rows].reshape(-1)
+    grad_gain2 = totals[gain_rows : 2 * gain_rows].reshape(-1)
     head_peaks = jnp.max(
-        all_peaks[:, :local_heads] + all_peaks[:, local_heads : 2 * local_heads], axis=0
+        gathered[:, 2 * third + 2 * gain_rows, 2 * kv_rows : 2 * kv_rows + local_heads].astype(F32)
+        + gathered[:, 2 * third + 2 * gain_rows + 1, 2 * kv_rows : 2 * kv_rows + local_heads].astype(F32),
+        axis=0,
     )
     factor = clip_limit / jnp.maximum(head_peaks, clip_limit)
     key_factor = jnp.min(factor.reshape(local_kv, group), axis=1)
@@ -426,8 +590,8 @@
         output,
         input_grad,
         grad_wq,
-        grad_wkv[:, :kv_rows],
-        grad_wkv[:, kv_rows:],
+        grad_wk,
+        grad_wv,
         grad_wo,
         grad_gain1,
         grad_gain2,

time: 752 us -> 626 us (0.83)
  waiting for transfers between devices: 367 us -> 228 us
  blocking collectives: 0 us -> 69.2 us
  matrix products: 75.9 us -> 34.6 us
  Pallas kernels: 57.1 us -> 89.6 us
  starting transfers between devices: 143 us -> 118 us
  other arithmetic: 51.2 us -> 33.4 us
    all_to_all x7 -> x2, waiting for transfers between devices: 245 us -> 45.4 us  [to_all(): return lax.all_to_all(array, 'dp', 0, 0, tiled=True)]
    all_to_all x0 -> x3, waiting for transfers between devices: none -> 126 us  [in_plane(): lax.all_to_all(rows, 'dp', 0, 0, tiled=True, axis_index_groups=plane_groups)]
    ppermute x8, waiting for transfers between devices: 78.3 us -> 8.07 us  [passed_along(): lax.ppermute(value, 'dp', [(s, s + steps) for s in range(first, last)])]
    all_to_all x7 -> x2, starting transfers between devices: 106 us -> 36.2 us  [to_all(): return lax.all_to_all(array, 'dp', 0, 0, tiled=True)]
    all_to_all x0 -> x1, blocking collectives: none -> 69.2 us  [in_plane(): lax.all_to_all(rows, 'dp', 0, 0, tiled=True, axis_index_groups=plane_groups)]
    dot_general x26 -> x18, matrix products: 75.9 us -> 34.6 us  [contract(): lax.dot_general(left, right, (dims, ((), ())), preferred_element_type=F32)]
    all_to_all x0 -> x3, starting transfers between devices: none -> 40.6 us  [in_plane(): lax.all_to_all(rows, 'dp', 0, 0, tiled=True, axis_index_groups=plane_groups)]
    pallas_call x1 -> x4, Pallas kernels: 29.9 us -> 62.7 us  [the longest x1 24.3 us: expert_back(): pl.pallas_call(expert_kernel, grid=(segments,), in_specs=[wide, wide, wei...]
  transfers between devices with their start and end apart: 26 -> 22, of which waited for: 16 -> 11; matrix products, arithmetic and copies ran while one was open for 12% -> 12% of each run, Pallas kernels for 4% -> 9%
where the time goes in v2:
time: 626 us; the launch traced here: 616 us
  waiting for transfers between devices  228 us (36%)
  starting transfers between devices  118 us (19%)
  Pallas kernels  89.6 us (14%)
  blocking collectives  69.2 us (11%)
  matrix products  34.6 us (6%)
  other arithmetic  33.4 us (5%)
  local copies, waits for them, and re-layouts  28.4 us (5%)
  between operations  15 us (2%)
    all_to_all x3, waiting for transfers between devices, in_plane(): lax.all_to_all(rows, 'dp', 0, 0, tiled=True, axis_index_groups=plane_groups)  126 us
    all_to_all x1, blocking collectives, in_plane(): lax.all_to_all(rows, 'dp', 0, 0, tiled=True, axis_index_groups=plane_groups)  69.2 us
    all_to_all x2, waiting for transfers between devices, to_all(): return lax.all_to_all(array, 'dp', 0, 0, tiled=True)  45.4 us
    all_to_all x3, starting transfers between devices, in_plane(): lax.all_to_all(rows, 'dp', 0, 0, tiled=True, axis_index_groups=plane_groups)  40.6 us
    all_gather x1, waiting for transfers between devices, shards(): gathered = lax.all_gather(packed, 'dp', axis=0)  36.8 us
    all_to_all x2, starting transfers between devices, to_all(): return lax.all_to_all(array, 'dp', 0, 0, tiled=True)  36.2 us
    dot_general x18, matrix products, contract(): lax.dot_general(left, right, (dims, ((), ())), preferred_element_type=F32)  34.6 us
    pallas_call x1, Pallas kernels, expert_back(): pl.pallas_call(expert_kernel, grid=(segments,), in_specs=[wide, wide, wei...  24.3 us
  transfers between devices with their start and end apart: 22, of which 11 were waited for; matrix products, arithmetic and copies ran while one was open for 12% of the time, Pallas kernels for 9%

profile of v2, /device:TPU:1, one launch (start us, length us, event | category | flops | bytes accessed | tf_op | source)
XLA Modules:
  0.0 616.4 jit_solution(11191065789980335046)
XLA Ops:
  21.3 5.7 collective-permute-start.1
  35.7 4.9 fusion
  41.4 11.1 %all-to-all-start = ((bf16[16,96,1536]{2,1,0:T(8,128)(2,1)}), bf16[16,96,1536]{2,1,0:T(8,128)(2,1)}, u32[]{:S(2)}, u32[]{:S(2)}) async-start(bf16[16,96,1536]{2,1,0:T(8,128)(2,1)} %bitcast.86), calls=%async_computation | async-start | bytes 9437184 | tf_op jit(solution)/shard_map/all_to_all | solution.py:459
  58.7 11.3 %shard_map.299 = (bf16[768,256]{1,0:T(8,128)(2,1)S(1)}, f32[12,256]{1,0:T(8,128)S(1)}, f32[12,256]{1,0:T(8,128)S(1)}) custom-call(bf16[768,256]{1,0:T(8,128)(2,1)S(1)} %bitcast.81, bf16[528,256]{1,0:T(8,128)(2,1)S(1)} %copy-done.4, bf16[528,256]{1,0:T(8,128)(2,1)S(1)} %copy-done.7, bf16[528,256]{1,0:T(8,128)(2,1)} %collective-permute-done.2.k2, ...), custom_call_target="tpu_custom_call" | custom-call | flops 1006632960 | bytes 2138112 | tf_op jit(solution)/shard_map/pallas_call | solution.py:127
  80.9 29.3 %all-to-all-done.g_ref = bf16[16,96,1536]{2,1,0:T(8,128)(2,1)} async-done(((bf16[16,96,1536]{2,1,0:T(8,128)(2,1)}), bf16[16,96,1536]{2,1,0:T(8,128)(2,1)}, u32[]{:S(2)}, u32[]{:S(2)}) %all-to-all-start) | async-done | bytes 4718624 | tf_op jit(solution)/shard_map/all_to_all | solution.py:459
  110.2 4.6 collective-permute-start.5
  114.8 69.2 %all_to_all.30.x_ref = bf16[16,96,1536]{2,1,0:T(8,128)(2,1)} all-to-all(bf16[16,96,1536]{2,1,0:T(8,128)(2,1)} %bitcast.83), channel_id=1, replica_groups={{0,2,4,6,8,10,12,14,16,18,20,22,24,26,28,30},{32,34,36,38,40,42,44,46,4..., dimensions={0} | all-to-all | bytes 9437184 | tf_op jit(solution)/shard_map/all_to_all | solution.py:459
  184.0 24.3 %shard_map.300 = (bf16[16,96,1536]{2,1,0:T(8,128)(2,1)}, bf16[3,512,512]{2,1,0:T(8,128)(2,1)}, bf16[3,512,1024]{2,1,0:T(8,128)(2,1)}) custom-call(bf16[16,96,1536]{2,1,0:T(8,128)(2,1)} %all_to_all.30.x_ref, bf16[16,96,1536]{2,1,0:T(8,128)(2,1)} %all-to-all-done.g_ref, bf16[4,3,1536,256]{3,2,1,0:T(8,128)(2,1)} %bitcast.99, ...), custom_call_target="tpu_custom_call" | custom-call | flops 12079595520 | bytes 28311552 | tf_op jit(solution)/shard_map/pallas_call | solution.py:237
  212.9 17.0 %shard_map.301 = (bf16[3,3,1536,256]{3,2,1,0:T(8,128)(2,1)}, bf16[3,3,1536,256]{3,2,1,0:T(8,128)(2,1)}, bf16[16,96,1536]{2,1,0:T(8,128)(2,1)}) custom-call(bf16[16,96,1536]{2,1,0:T(8,128)(2,1)} %all_to_all.30.x_ref, bf16[16,96,1536]{2,1,0:T(8,128)(2,1)} %all-to-all-done.g_ref, bf16[3,512,512]{2,1,0:T(8,128)(2,1)} %get-tuple-element.60.inner_ref, ...), custom_call_target="tpu_custom_call" | custom-call | flops 9663676416 | bytes 33030144 | tf_op jit(solution)/shard_map/pallas_call | solution.py:284
  233.3 37.3 %all-to-all-done.2 = bf16[16,96,1536]{2,1,0:T(8,128)(2,1)} async-done(((bf16[16,96,1536]{2,1,0:T(8,128)(2,1)}), bf16[16,96,1536]{2,1,0:T(8,128)(2,1)}, u32[]{:S(2)}, u32[]{:S(2)}) %all-to-all-start.2) | async-done | bytes 4718624 | tf_op jit(solution)/shard_map/all_to_all | solution.py:459
  274.6 5.7 collective-permute-start.6
  287.7 14.0 %all-to-all-start.3 = ((bf16[64,24,768]{2,1,0:T(8,128)(2,1)}), bf16[64,24,768]{2,1,0:T(8,128)(2,1)}, u32[]{:S(2)}, u32[]{:S(2)}) async-start(bf16[64,24,768]{2,1,0:T(8,128)(2,1)} %bitcast.85), calls=%async_computation.3 | async-start | bytes 4718592 | tf_op jit(solution)/shard_map/all_to_all | solution.py:52
  304.4 13.8 %shard_map.303 = bf16[4,3,1536,256]{3,2,1,0:T(8,128)(2,1)} custom-call(bf16[3,3,1536,256]{3,2,1,0:T(8,128)(2,1)} %get-tuple-element.62.own_ref, bf16[3,3,1536,256]{3,2,1,0:T(8,128)(2,1)} %collective-permute-done.12.peer_ref), custom_call_target="tpu_custom_call" | custom-call | flops 4718592 | bytes 28311552 | tf_op jit(solution)/shard_map/pallas_call | solution.py:324
  320.3 15.6 %shard_map.302 = (bf16[768,256]{1,0:T(8,128)(2,1)S(1)}, bf16[512,256]{1,0:T(8,128)(2,1)S(1)}, bf16[512,256]{1,0:T(8,128)(2,1)S(1)}, bf16[512,256]{1,0:T(8,128)(2...) custom-call(bf16[768,256]{1,0:T(8,128)(2,1)S(1)} %bitcast.82, bf16[768,256]{1,0:T(8,128)(2,1)S(1)} %copy-done.9, ...), custom_call_target="tpu_custom_call" | custom-call | flops 251658240000 | bytes 3883008 | tf_op jit(solution)/shard_map/pallas_call | solution.py:190
  345.5 6.8 %collective-permute-done.7 = bf16[512,256]{1,0:T(8,128)(2,1)S(1)} collective-permute-done((bf16[512,256]{1,0:T(8,128)(2,1)S(1)}, bf16[512,256]{1,0:T(8,128)(2,1)S(1)}, u32[]{:S(2)}, u32[]{:S(2)}) %collective-permute-start.7) | collective-permute-done | bytes 262176 | tf_op jit(solution)/shard_map/ppermute | solution.py:48
  358.4 6.1 copy.56
  364.5 22.2 %all-to-all-start.4 = ((bf16[64,24,1280]{2,1,0:T(8,128)(2,1)}), bf16[64,24,1280]{2,1,0:T(8,128)(2,1)}, u32[]{:S(2)}, u32[]{:S(2)}) async-start(bf16[64,24,1280]{2,1,0:T(8,128)(2,1)} %bitcast.84), calls=%async_computation.4 | async-start | bytes 7864320 | tf_op jit(solution)/shard_map/all_to_all | solution.py:52
  397.0 45.4 %all-to-all-done.4 = bf16[64,24,1280]{2,1,0:T(8,128)(2,1)} async-done(((bf16[64,24,1280]{2,1,0:T(8,128)(2,1)}), bf16[64,24,1280]{2,1,0:T(8,128)(2,1)}, u32[]{:S(2)}, u32[]{:S(2)}) %all-to-all-start.4) | async-done | bytes 3932192 | tf_op jit(solution)/shard_map/all_to_all | solution.py:52
  445.8 5.3 reduce-scatter.2.cloned.1.call-done
  451.1 25.0 %all-to-all-start.5 = ((bf16[16,96,1536]{2,1,0:T(8,128)(2,1)}), bf16[16,96,1536]{2,1,0:T(8,128)(2,1)}, u32[]{:S(2)}, u32[]{:S(2)}) async-start(bf16[16,96,1536]{2,1,0:T(8,128)(2,1)} %get-tuple-element.78), calls=%async_computation.6 | async-start | bytes 9437184 | tf_op jit(solution)/shard_map/all_to_all | solution.py:459
  477.3 59.1 %all-to-all-done.5 = bf16[16,96,1536]{2,1,0:T(8,128)(2,1)} async-done(((bf16[16,96,1536]{2,1,0:T(8,128)(2,1)}), bf16[16,96,1536]{2,1,0:T(8,128)(2,1)}, u32[]{:S(2)}, u32[]{:S(2)}) %all-to-all-start.5) | async-done | bytes 4718624 | tf_op jit(solution)/shard_map/all_to_all | solution.py:459
  536.5 5.0 convolution_convert_fusion.5
  555.6 36.8 %all-gather.7.cloned.1.call-done = bf16[4608,768]{1,0:T(8,128)(2,1)} async-done(((bf16[72,768]{1,0:T(8,128)(2,1)}), bf16[4608,768]{1,0:T(8,128)(2,1)}) %all-gather.7.cloned.1.call-update) | async-done | bytes 7077904 | tf_op jit(solution)/shard_map/all_gather | solution.py:573
  595.3 7.5 %shard_map.304 = (f32[768,1536]{1,0:T(8,128)}, f32[1536,768]{1,0:T(8,128)}, f32[1536,256]{1,0:T(8,128)}, f32[1536,256]{1,0:T(8,128)}, f32[24,256]{1,0:T(8,128)S(1)}) custom-call(bf16[64,72,768]{2,1,0:T(8,128)(2,1)S(1)} %bitcast.79), custom_call_target="tpu_custom_call" | custom-call | flops 3538944 | bytes 21233664 | tf_op jit(solution)/shard_map/pallas_call | solution.py:368
  (224 shorter events, 118.5 us)
Async XLA Ops:
  7.2 62.8 %copy-start = (bf16[768,1536]{1,0:T(8,128)(2,1)S(1)}, bf16[768,1536]{1,0:T(8,128)(2,1)}, u32[]{:S(2)}) copy-start(bf16[768,1536]{1,0:T(8,128)(2,1)} %param.27) | copy-start | bytes 7077892
  7.2 103.0 %all-gather.5.cloned.1.call-start = ((), (), s32[]{:S(2)}) async-start(), calls=%async_computation.8 | async-start | bytes 11796480 | tf_op jit(solution)/shard_map/all_gather | solution.py:435
  17.3 23.3 %collective-permute-start = (bf16[528,256]{1,0:T(8,128)(2,1)S(1)}, bf16[528,256]{1,0:T(8,128)(2,1)S(1)}, u32[]{:S(2)}, u32[]{:S(2)}) collective-permute-start(bf16[528,256]{1,0:T(8,128)(2,1)S(1)} %concatenate.35.k0), channel_id=1, source_target_pairs={{0,8},{2,10},{4,12},{6,14},{8,16},{10,18},{12,20},{14,22},{16,24},... | collective-permute-start | bytes 811016 | tf_op jit(solution)/shard_map/ppermute | solution.py:48
  21.3 19.4 %collective-permute-start.1 = (bf16[528,256]{1,0:T(8,128)(2,1)S(1)}, bf16[528,256]{1,0:T(8,128)(2,1)S(1)}, u32[]{:S(2)}, u32[]{:S(2)}) collective-permute-start(bf16[528,256]{1,0:T(8,128)(2,1)S(1)} %concatenate.35.k0), channel_id=1, source_target_pairs={{0,6},{2,8},{4,10},{6,12},{8,14},{10,16},{12,18},{14,20},{16,22},{... | collective-permute-start | bytes 811016 | tf_op jit(solution)/shard_map/ppermute | solution.py:48
  27.0 13.7 %collective-permute-start.2 = (bf16[528,256]{1,0:T(8,128)(2,1)S(1)}, bf16[528,256]{1,0:T(8,128)(2,1)}, u32[]{:S(2)}, u32[]{:S(2)}) collective-permute-start(bf16[528,256]{1,0:T(8,128)(2,1)S(1)} %concatenate.35.k0), channel_id=1, source_target_pairs={{0,4},{2,6},{4,8},{6,10},{8,12},{10,14},{12,16},{14,18},{16,20},{1... | collective-permute-start | bytes 811016 | tf_op jit(solution)/shard_map/ppermute | solution.py:48
  30.2 10.5 %collective-permute-start.3 = (bf16[528,256]{1,0:T(8,128)(2,1)S(1)}, bf16[528,256]{1,0:T(8,128)(2,1)}, u32[]{:S(2)}, u32[]{:S(2)}) collective-permute-start(bf16[528,256]{1,0:T(8,128)(2,1)S(1)} %concatenate.35.k0), channel_id=1, source_target_pairs={{0,2},{2,4},{4,6},{6,8},{8,10},{10,12},{12,14},{14,16},{16,18},{18... | collective-permute-start | bytes 811016 | tf_op jit(solution)/shard_map/ppermute | solution.py:48
  33.8 198.4 %copy-start.43 = (f32[32]{0:T(128)}, f32[32]{0:T(128)S(1)}, u32[]{:S(2)}) copy-start(f32[32]{0:T(128)S(1)} %add_convert_fusion.4) | copy-start | bytes 388
  41.4 68.7 %all-to-all-start = ((bf16[16,96,1536]{2,1,0:T(8,128)(2,1)}), bf16[16,96,1536]{2,1,0:T(8,128)(2,1)}, u32[]{:S(2)}, u32[]{:S(2)}) async-start(bf16[16,96,1536]{2,1,0:T(8,128)(2,1)} %bitcast.86), calls=%async_computation | async-start | bytes 9437184 | tf_op jit(solution)/shard_map/all_to_all | solution.py:459
  70.8 4.9 collective-permute-start.4
  110.2 73.8 %collective-permute-start.5 = (bf16[4,3,1536,256]{3,2,1,0:T(8,128)(2,1)}, bf16[4,3,1536,256]{3,2,1,0:T(8,128)(2,1)}, u32[]{:S(2)}, u32[]{:S(2)}) collective-permute-start(bf16[4,3,1536,256]{3,2,1,0:T(8,128)(2,1)} %bitcast.98), channel_id=1, source_target_pairs={{0,1},{1,0},{2,3},{3,2},{4,5},{5,4},{6,7},{7,6},{8,9},{9,8},{10,11... | collective-permute-start | bytes 28311560 | tf_op jit(solution)/shard_map/ppermute | solution.py:38
  208.3 62.3 %all-to-all-start.2 = ((bf16[16,96,1536]{2,1,0:T(8,128)(2,1)}), bf16[16,96,1536]{2,1,0:T(8,128)(2,1)}, u32[]{:S(2)}, u32[]{:S(2)}) async-start(bf16[16,96,1536]{2,1,0:T(8,128)(2,1)} %get-tuple-element.59), calls=%async_computation.2 | async-start | bytes 9437184 | tf_op jit(solution)/shard_map/all_to_all | solution.py:459
  229.9 74.5 %collective-permute-start.12 = (bf16[3,3,1536,256]{3,2,1,0:T(8,128)(2,1)}, bf16[3,3,1536,256]{3,2,1,0:T(8,128)(2,1)}, u32[]{:S(2)}, u32[]{:S(2)}) collective-permute-start(bf16[3,3,1536,256]{3,2,1,0:T(8,128)(2,1)} %get-tuple-element.76), channel_id=1, source_target_pairs={{0,1},{1,0},{2,3},{3,2},{4,5},{5,4},{6,7},{7,6},{8,9},{9,8},{10,11... | collective-permute-start | bytes 21233672 | tf_op jit(solution)/shard_map/ppermute | solution.py:38
  274.6 7.6 %collective-permute-start.6 = (bf16[256,1536]{1,0:T(8,128)(2,1)S(1)}, bf16[256,1536]{1,0:T(8,128)(2,1)S(1)}, u32[]{:S(2)}, u32[]{:S(2)}) collective-permute-start(bf16[256,1536]{1,0:T(8,128)(2,1)S(1)} %convolution_convert_fusion.4), channel_id=1, source_target_pairs={{0,1},{1,0},{2,3},{3,2},{4,5},{5,4},{6,7},{7,6},{8,9},{9,8},{10,11... | collective-permute-start | bytes 2359304 | tf_op jit(solution)/shard_map/ppermute | solution.py:38
  287.7 55.7 %all-to-all-start.3 = ((bf16[64,24,768]{2,1,0:T(8,128)(2,1)}), bf16[64,24,768]{2,1,0:T(8,128)(2,1)}, u32[]{:S(2)}, u32[]{:S(2)}) async-start(bf16[64,24,768]{2,1,0:T(8,128)(2,1)} %bitcast.85), calls=%async_computation.3 | async-start | bytes 4718592 | tf_op jit(solution)/shard_map/all_to_all | solution.py:52
  301.7 149.3 %reduce-scatter.2.cloned.1.call-start = ((), (), s32[]{:S(2)}) async-start(), calls=%async_computation.7 | async-start | bytes 11796480 | tf_op jit(solution)/shard_map/reduce_scatter | solution.py:498
  335.9 9.6 %collective-permute-start.10 = (bf16[512,256]{1,0:T(8,128)(2,1)S(1)}, bf16[512,256]{1,0:T(8,128)(2,1)S(1)}, u32[]{:S(2)}, u32[]{:S(2)}) collective-permute-start(bf16[512,256]{1,0:T(8,128)(2,1)S(1)} %get-tuple-element.70), channel_id=1, source_target_pairs={{2,0},{4,2},{6,4},{8,6},{10,8},{12,10},{14,12},{16,14},{18,16},{20... | collective-permute-start | bytes 786440 | tf_op jit(solution)/shard_map/ppermute | solution.py:48
  337.2 15.1 %collective-permute-start.7 = (bf16[512,256]{1,0:T(8,128)(2,1)S(1)}, bf16[512,256]{1,0:T(8,128)(2,1)S(1)}, u32[]{:S(2)}, u32[]{:S(2)}) collective-permute-start(bf16[512,256]{1,0:T(8,128)(2,1)S(1)} %get-tuple-element.67), channel_id=1, source_target_pairs={{8,0},{10,2},{12,4},{14,6},{16,8},{18,10},{20,12},{22,14},{24,16},... | collective-permute-start | bytes 786440 | tf_op jit(solution)/shard_map/ppermute | solution.py:48
  338.5 15.0 %collective-permute-start.8 = (bf16[512,256]{1,0:T(8,128)(2,1)S(1)}, bf16[512,256]{1,0:T(8,128)(2,1)S(1)}, u32[]{:S(2)}, u32[]{:S(2)}) collective-permute-start(bf16[512,256]{1,0:T(8,128)(2,1)S(1)} %get-tuple-element.68), channel_id=1, source_target_pairs={{6,0},{8,2},{10,4},{12,6},{14,8},{16,10},{18,12},{20,14},{22,16},{... | collective-permute-start | bytes 786440 | tf_op jit(solution)/shard_map/ppermute | solution.py:48
  339.8 13.7 %collective-permute-start.9 = (bf16[512,256]{1,0:T(8,128)(2,1)S(1)}, bf16[512,256]{1,0:T(8,128)(2,1)S(1)}, u32[]{:S(2)}, u32[]{:S(2)}) collective-permute-start(bf16[512,256]{1,0:T(8,128)(2,1)S(1)} %get-tuple-element.69), channel_id=1, source_target_pairs={{4,0},{6,2},{8,4},{10,6},{12,8},{14,10},{16,12},{18,14},{20,16},{2... | collective-permute-start | bytes 786440 | tf_op jit(solution)/shard_map/ppermute | solution.py:48
  364.5 77.8 %all-to-all-start.4 = ((bf16[64,24,1280]{2,1,0:T(8,128)(2,1)}), bf16[64,24,1280]{2,1,0:T(8,128)(2,1)}, u32[]{:S(2)}, u32[]{:S(2)}) async-start(bf16[64,24,1280]{2,1,0:T(8,128)(2,1)} %bitcast.84), calls=%async_computation.4 | async-start | bytes 7864320 | tf_op jit(solution)/shard_map/all_to_all | solution.py:52
  386.7 205.6 %all-gather.7.cloned.1.call-start = ((), (), s32[]{:S(2)}) async-start(), calls=%async_computation.9 | async-start | bytes 7188480 | tf_op jit(solution)/shard_map/all_gather | solution.py:573
  391.1 4.1 collective-permute-start.11
  451.1 85.4 %all-to-all-start.5 = ((bf16[16,96,1536]{2,1,0:T(8,128)(2,1)}), bf16[16,96,1536]{2,1,0:T(8,128)(2,1)}, u32[]{:S(2)}, u32[]{:S(2)}) async-start(bf16[16,96,1536]{2,1,0:T(8,128)(2,1)} %get-tuple-element.78), calls=%async_computation.6 | async-start | bytes 9437184 | tf_op jit(solution)/shard_map/all_to_all | solution.py:459
  541.4 11.5 %collective-permute-start.13 = (bf16[256,1536]{1,0:T(8,128)(2,1)}, bf16[256,1536]{1,0:T(8,128)(2,1)}, u32[]{:S(2)}, u32[]{:S(2)}) collective-permute-start(bf16[256,1536]{1,0:T(8,128)(2,1)} %convolution_convert_fusion.5), channel_id=1, source_target_pairs={{0,1},{1,0},{2,3},{3,2},{4,5},{5,4},{6,7},{7,6},{8,9},{9,8},{10,11... | collective-permute-start | bytes 2359304 | tf_op jit(solution)/shard_map/ppermute | solution.py:38
  (48 other events, 363.2 us)
Sparse Core Ops, SparseCore 0:
  12.0 95.1 all-gather.4
  318.4 132.6 reduce-scatter.1
  454.5 137.8 all-gather.6

commit v3 on v2

--- a/solution.py
+++ b/solution.py
@@ -204,150 +204,178 @@
     )(q, grad, log_total, cosine, sine, *blocks)
 
 
-def expert_kernel(x_ref, g_ref, own_ref, peer_ref, dx_ref, inner_ref, acts_ref):
+def expert_kernel(x_ref, g_ref, own_ref, peer_ref, dx_ref, own_acts, peer_acts):
     width = x_ref.shape[-1]
     rows, grads = (x_ref[...].reshape(-1, width), g_ref[...].reshape(-1, width))
-    hidden = own_ref.shape[-1]
+    hidden = own_ref.shape[-1] // 3
     back = None
-    for side, weights in enumerate((own_ref, peer_ref)):
-        gate_w, up_w, down_w = (weights[0, 0], weights[0, 1], weights[0, 2])
-        gate_act = contract(rows, gate_w, NN)
-        up_act = contract(rows, up_w, NN)
-        grad_inner = contract(grads, down_w, NN)
+    for weights, acts in ((own_ref, own_acts), (peer_ref, peer_acts)):
+        both = contract(rows, weights[0, :, : 2 * hidden], NN)
+        grad_inner = contract(grads, weights[0, :, 2 * hidden :], NN)
+        gate_act, up_act = (both[:, :hidden], both[:, hidden:])
         sigmoid = 1.0 / (1.0 + jnp.exp(-gate_act))
         silu = gate_act * sigmoid
-        dgate = (grad_inner * up_act * (sigmoid * (1.0 + gate_act * (1.0 - sigmoid)))).astype(BF16)
-        dup = (grad_inner * silu).astype(BF16)
-        at = side * hidden
-        inner_ref[0, :, at : at + hidden] = (silu * up_act).astype(BF16)
-        acts_ref[0, :, at : at + hidden] = dgate
-        acts_ref[0, :, (2 * hidden + at) : (3 * hidden + at)] = dup
-        part = contract(dgate, gate_w, NT) + contract(dup, up_w, NT)
+        dgate = grad_inner * up_act * (sigmoid * (1.0 + gate_act * (1.0 - sigmoid)))
+        acts[0, :, :hidden] = dgate.astype(BF16)
+        acts[0, :, hidden : 2 * hidden] = (grad_inner * silu).astype(BF16)
+        acts[0, :, 2 * hidden :] = (silu * up_act).astype(BF16)
+        part = contract(acts[0, :, : 2 * hidden], weights[0, :, : 2 * hidden], NT)
         back = part if back is None else back + part
     dx_ref[...] = back.astype(BF16).reshape(dx_ref.shape)
 
 
 def expert_back(rows, grads, own, peer):
     sources, lines, width = rows.shape
-    segments, hidden = (lines // RANK_ROWS, own.shape[-1])
+    segments, triple = (lines // RANK_ROWS, own.shape[-1])
     count = sources * RANK_ROWS
     wide = pl.BlockSpec((sources, RANK_ROWS, width), lambda s: (0, s, 0))
-    weight = pl.BlockSpec((1, 3, width, hidden), lambda s: (s, 0, 0, 0))
-    flops = 20 * sources * lines * width * hidden
+    weight = pl.BlockSpec((1, width, triple), lambda s: (s, 0, 0))
+    act = pl.BlockSpec((1, count, triple), lambda s: (s, 0, 0))
     return pl.pallas_call(
         expert_kernel,
         grid=(segments,),
         in_specs=[wide, wide, weight, weight],
-        out_specs=[
-            wide,
-            pl.BlockSpec((1, count, 2 * hidden), lambda s: (s, 0, 0)),
-            pl.BlockSpec((1, count, 4 * hidden), lambda s: (s, 0, 0)),
-        ],
+        out_specs=[wide, act, act],
         out_shape=[
             jax.ShapeDtypeStruct(rows.shape, BF16),
-            jax.ShapeDtypeStruct((segments, count, 2 * hidden), BF16),
-            jax.ShapeDtypeStruct((segments, count, 4 * hidden), BF16),
+            jax.ShapeDtypeStruct((segments, count, triple), BF16),
+            jax.ShapeDtypeStruct((segments, count, triple), BF16),
         ],
         compiler_params=pltpu.CompilerParams(vmem_limit_bytes=56 << 20),
         cost_estimate=pl.CostEstimate(
-            flops=flops,
-            bytes_accessed=6 * sources * lines * width + 12 * segments * width * hidden,
-            transcendentals=2 * sources * lines * hidden,
+            flops=7 * sources * lines * width * triple,
+            bytes_accessed=6 * sources * lines * width + 4 * segments * width * triple,
+            transcendentals=2 * sources * lines * triple // 3,
         ),
     )(rows, grads, own, peer)
 
 
-def expert_sums_kernel(x_ref, g_ref, inner_ref, acts_ref, own_ref, peer_ref, sum_own, sum_peer, out_ref):
+def expert_sums_kernel(x_ref, g_ref, own_acts, peer_acts, own_ref, peer_ref, sum_own, *outs):
     width = x_ref.shape[-1]
     rows, grads = (x_ref[...].reshape(-1, width), g_ref[...].reshape(-1, width))
     hidden = own_ref.shape[-1]
-    inner = inner_ref[0]
-    sums = contract(rows, acts_ref[0], TN).astype(BF16)
-    down = contract(grads, inner, TN).astype(BF16)
-    for side, target in enumerate((sum_own, sum_peer)):
-        at = side * hidden
-        target[0, 0] = sums[:, at : at + hidden]
-        target[0, 1] = sums[:, (2 * hidden + at) : (3 * hidden + at)]
-        target[0, 2] = down[:, at : at + hidden]
-    out = contract(inner[:, :hidden], own_ref[0, 0], NT)
-    out = out + contract(inner[:, hidden:], peer_ref[0, 0], NT)
+    out_ref = outs[-1]
+    out = None
+    for side, (acts, weights) in enumerate(((own_acts, own_ref), (peer_acts, peer_ref))):
+        first = contract(rows, acts[0, :, : 2 * hidden], TN).astype(BF16)
+        second = contract(grads, acts[0, :, 2 * hidden :], TN).astype(BF16)
+        if side == 0:
+            sum_own[0, :, : 2 * hidden] = first
+            sum_own[0, :, 2 * hidden :] = second
+        else:
+            outs[0][0] = first[:, :hidden]
+            outs[1][0] = first[:, hidden:]
+            outs[2][0] = second
+        part = contract(acts[0, :, 2 * hidden :], weights[0], NT)
+        out = part if out is None else out + part
     out_ref[...] = out.astype(BF16).reshape(out_ref.shape)
 
 
-def expert_sums(rows, grads, inner, acts, own, peer):
+def expert_sums(rows, grads, own_acts, peer_acts, own, peer):
     sources, lines, width = rows.shape
-    segments, hidden = (lines // RANK_ROWS, own.shape[-1])
+    segments, triple = (lines // RANK_ROWS, own.shape[-1])
+    hidden = triple // 3
     count = sources * RANK_ROWS
     wide = pl.BlockSpec((sources, RANK_ROWS, width), lambda s: (0, s, 0))
-    down = pl.BlockSpec((1, 1, width, hidden), lambda s: (s, 2, 0, 0))
-    total = pl.BlockSpec((1, 3, width, hidden), lambda s: (s, 0, 0, 0))
+    down = pl.BlockSpec((1, width, hidden), lambda s: (s, 0, 2))
+    act = pl.BlockSpec((1, count, triple), lambda s: (s, 0, 0))
     return pl.pallas_call(
         expert_sums_kernel,
         grid=(segments,),
-        in_specs=[
-            wide,
-            wide,
-            pl.BlockSpec((1, count, 2 * hidden), lambda s: (s, 0, 0)),
-            pl.BlockSpec((1, count, 4 * hidden), lambda s: (s, 0, 0)),
-            down,
-            down,
-        ],
-        out_specs=[total, total, wide],
-        out_shape=[
-            jax.ShapeDtypeStruct((segments, 3, width, hidden), BF16),
-            jax.ShapeDtypeStruct((segments, 3, width, hidden), BF16),
-            jax.ShapeDtypeStruct(rows.shape, BF16),
-        ],
+        in_specs=[wide, wide, act, act, down, down],
+        out_specs=[pl.BlockSpec((1, width, triple), lambda s: (s, 0, 0))]
+        + [pl.BlockSpec((1, width, hidden), lambda s: (s, 0, 0))] * 3
+        + [wide],
+        out_shape=[jax.ShapeDtypeStruct((segments, width, triple), BF16)]
+        + [jax.ShapeDtypeStruct((segments, width, hidden), BF16)] * 3
+        + [jax.ShapeDtypeStruct(rows.shape, BF16)],
         compiler_params=pltpu.CompilerParams(vmem_limit_bytes=60 << 20),
         cost_estimate=pl.CostEstimate(
-            flops=16 * sources * lines * width * hidden,
-            bytes_accessed=6 * sources * lines * width + 16 * segments * width * hidden,
+            flops=6 * sources * lines * width * triple,
+            bytes_accessed=6 * sources * lines * width + 5 * segments * width * triple,
             transcendentals=0,
         ),
-    )(rows, grads, inner, acts, own, peer)
-
-
-def both_cores_kernel(own_ref, peer_ref, out_ref):
+    )(rows, grads, own_acts, peer_acts, own, peer)
+
+
+def both_cores_kernel(own_ref, *refs):
+    out_ref = refs[-1]
+    hidden = refs[0].shape[-1]
+
     @pl.when(pl.program_id(0) < SEGMENTS)
     def _():
-        out_ref[...] = (own_ref[...].astype(F32) + peer_ref[...].astype(F32)).astype(BF16)
+        for kind, peer_ref in enumerate(refs[:-1]):
+            here = slice(kind * hidden, (kind + 1) * hidden)
+            total = own_ref[0, :, here].astype(F32) + peer_ref[0].astype(F32)
+            out_ref[0, :, here] = total.astype(BF16)
 
     @pl.when(pl.program_id(0) >= SEGMENTS)
     def _():
         out_ref[...] = jnp.zeros_like(out_ref)
 
 
-def both_cores(own, peer, slots):
-    segments, kinds, width, hidden = own.shape
-    shape = (1, 1, width, hidden)
-    part = pl.BlockSpec(shape, lambda s, k: (jnp.minimum(s, segments - 1), k, 0, 0))
+def both_cores(own, peers, slots):
+    segments, width, triple = own.shape
+    rows = width // 2
+    last = segments - 1
+    part = pl.BlockSpec((1, rows, triple), lambda s, r: (jnp.minimum(s, last), r, 0))
+    thin = pl.BlockSpec((1, rows, triple // 3), lambda s, r: (jnp.minimum(s, last), r, 0))
     return pl.pallas_call(
         both_cores_kernel,
-        grid=(slots, kinds),
-        in_specs=[part, part],
-        out_specs=pl.BlockSpec(shape, lambda s, k: (s, k, 0, 0)),
-        out_shape=jax.ShapeDtypeStruct((slots, kinds, width, hidden), BF16),
+        grid=(slots, 2),
+        in_specs=[part] + [thin] * 3,
+        out_specs=pl.BlockSpec((1, rows, triple), lambda s, r: (s, r, 0)),
+        out_shape=jax.ShapeDtypeStruct((slots, width, triple), BF16),
         cost_estimate=pl.CostEstimate(
-            flops=slots * kinds * width * hidden,
-            bytes_accessed=6 * slots * kinds * width * hidden,
+            flops=slots * width * triple, bytes_accessed=6 * slots * width * triple, transcendentals=0
+        ),
+    )(own, *peers)
+
+
+def weight_grads_kernel(normed_ref, qkv_ref, attended_ref, branch_ref, out_ref):
+    width = branch_ref.shape[1]
+    out_ref[:, :width] = contract(attended_ref[...], branch_ref[...], NN).astype(BF16)
+    out_ref[:, width:] = contract(normed_ref[...], qkv_ref[...], ((0,), (1,))).astype(BF16)
+
+
+def weight_grads(normed, grad_qkv, attended, branch):
+    tok, model = normed.shape
+    width, columns = (attended.shape[0], grad_qkv.shape[0])
+    half = width // 256
+    return pl.pallas_call(
+        weight_grads_kernel,
+        grid=(model // 256,),
+        in_specs=[
+            pl.BlockSpec((tok, 256), lambda i: (0, i)),
+            pl.BlockSpec((columns, tok), lambda i: (0, 0)),
+            pl.BlockSpec((256, tok), lambda i: (i % half, 0)),
+            pl.BlockSpec((tok, width), lambda i: (0, i // half)),
+        ],
+        out_specs=pl.BlockSpec((256, width + columns), lambda i: (i, 0)),
+        out_shape=jax.ShapeDtypeStruct((model, width + columns), BF16),
+        cost_estimate=pl.CostEstimate(
+            flops=2 * tok * model * (width + columns),
+            bytes_accessed=2 * model * (width + columns) + 4 * tok * model,
             transcendentals=0,
         ),
-    )(own, peer)
-
-
-def unpack_kernel(in_ref, wo_ref, wq_ref, wk_ref, wv_ref, sum_ref):
+    )(normed, grad_qkv, attended, branch)
+
+
+def unpack_kernel(
+    in_ref, query_ref, key_ref, sq_ref, sk_ref,
+    wo_ref, wq_ref, wk_ref, wv_ref, sum_ref, cq_ref, ck_ref,
+):
     step = pl.program_id(0)
-    chunks, lines, width = in_ref.shape
-    third = lines // 3
-    narrow = wk_ref.shape[1]
+    chunks, lines, _ = in_ref.shape
     for c in range(chunks):
-        here = slice(c * third, (c + 1) * third)
-        wo_ref[here, :] = in_ref[c, :third, :].astype(F32)
-        wq_ref[here, :] = in_ref[c, third : 2 * third, :].astype(F32)
-        wk_ref[here, :] = in_ref[c, 2 * third :, :narrow].astype(F32)
-        wv_ref[here, :] = in_ref[c, 2 * third :, narrow : 2 * narrow].astype(F32)
-    more = in_ref[:, 2 * third :, 2 * narrow :].astype(F32)
-    total = jnp.sum(more, axis=0)
+        here, at = (slice(c * lines, (c + 1) * lines), 0)
+        for target in (wo_ref, wq_ref, wk_ref, wv_ref):
+            size = target.shape[1]
+            target[here, :] = in_ref[c, :, at : at + size].astype(F32)
+            at += size
+    total = jnp.sum(in_ref[:, :, at:].astype(F32), axis=0)
+    cq_ref[...] = (query_ref[...].astype(F32) * sq_ref[...]).astype(BF16)
+    ck_ref[...] = (key_ref[...].astype(F32) * sk_ref[...]).astype(BF16)
 
     @pl.when(step == 0)
     def _():
@@ -358,23 +386,34 @@
         sum_ref[...] = sum_ref[...] + total
 
 
-def unpack(gathered, narrow):
-    parts, lines, width = gathered.shape
+def unpack(gathered, w_query, w_key, scale_query, scale_key):
+    parts, lines, every = gathered.shape
+    width, narrow = (w_query.shape[1], w_key.shape[1])
     steps = 16
-    per, third = (parts // steps, lines // 3)
-    rows = per * third
-    total = parts * third
-    extra = (third, width - 2 * narrow)
+    per = parts // steps
+    rows = per * lines
+    total = parts * lines
+    extra = (lines, every - 2 * width - 2 * narrow)
+    wide = pl.BlockSpec((rows, width), lambda i: (i, 0))
+    thin = pl.BlockSpec((rows, narrow), lambda i: (i, 0))
     return pl.pallas_call(
         unpack_kernel,
         grid=(steps,),
-        in_specs=[pl.BlockSpec((per, lines, width), lambda i: (i, 0, 0))],
+        in_specs=[
+            pl.BlockSpec((per, lines, every), lambda i: (i, 0, 0)),
+            wide,
+            thin,
+            pl.BlockSpec((1, width), lambda i: (0, 0)),
+            pl.BlockSpec((1, narrow), lambda i: (0, 0)),
+        ],
         out_specs=[
             pl.BlockSpec((rows, width), lambda i: (i % (steps // 2), i // (steps // 2))),
-            pl.BlockSpec((rows, width), lambda i: (i, 0)),
-            pl.BlockSpec((rows, narrow), lambda i: (i, 0)),
-            pl.BlockSpec((rows, narrow), lambda i: (i, 0)),
+            wide,
+            thin,
+            thin,
             pl.BlockSpec(extra, lambda i: (0, 0)),
+            wide,
+            thin,
         ],
         out_shape=[
             jax.ShapeDtypeStruct((total // 2, 2 * width), F32),
@@ -382,12 +421,14 @@
             jax.ShapeDtypeStruct((total, narrow), F32),
             jax.ShapeDtypeStruct((total, narrow), F32),
             jax.ShapeDtypeStruct(extra, F32),
+            jax.ShapeDtypeStruct((total, width), BF16),
+            jax.ShapeDtypeStruct((total, narrow), BF16),
         ],
         compiler_params=pltpu.CompilerParams(vmem_limit_bytes=32 << 20),
         cost_estimate=pl.CostEstimate(
-            flops=parts * lines * width, bytes_accessed=6 * parts * lines * width, transcendentals=0
-        ),
-    )(gathered)
+            flops=total * every, bytes_accessed=8 * total * every, transcendentals=0
+        ),
+    )(gathered, w_query, w_key, scale_query, scale_key)
 
 
 def rms_scale(values):
@@ -431,7 +472,7 @@
     plane_groups = [list(range(at, at + PLANE)) for at in range(0, dp_size, PLANE)]
     column_groups = [list(range(at, dp_size, PLANE)) for at in range(PLANE)]
 
-    packed_w = jnp.stack([w_gate[0], w_up[0], w_down[0].T])
+    packed_w = jnp.concatenate([w_gate[0], w_up[0], w_down[0].T], axis=1)
     own = lax.all_gather(packed_w, "dp", axis=0, axis_index_groups=column_groups)
 
     picks = route_ids.T
@@ -486,15 +527,17 @@
     own = after(own, rows_out)
     peer = swapped(own)
     rows_in = in_plane(rows_out)
-    back, inner, acts = expert_back(rows_in, grad_rows, own, peer)
+    back, own_acts, peer_acts = expert_back(rows_in, grad_rows, own, peer)
 
     def combined(weights, rows):
         part = contract(weights, rows.reshape(-1, model_width), TN).astype(BF16)
         return part.astype(F32) + swapped(part).astype(F32)
 
-    sum_own, sum_peer, expert_out = expert_sums(rows_in, grad_rows, inner, acts, own, peer)
-    sums = both_cores(sum_own, swapped(sum_peer), dp_size // PLANE)
-    grad_normed2 = combined(pick, after(in_plane(back), sum_own))
+    sum_own, *sum_peer, expert_out = expert_sums(rows_in, grad_rows, own_acts, peer_acts, own, peer)
+    sums = both_cores(sum_own, [swapped(part) for part in sum_peer], dp_size // PLANE)
+    back = in_plane(back)
+    expert_out = in_plane(after(expert_out, back))
+    grad_normed2 = combined(pick, after(back, sums))
     sums = lax.psum_scatter(
         sums, "dp", scatter_dimension=0, tiled=True, axis_index_groups=column_groups
     )
@@ -507,22 +550,9 @@
     grad_query_pre, *grad_blocks = attend_back(
         query, grad_attended, log_total, cosine, sine, blocks, group
     )
-    half = model_width // 2
-    grad_wo = jnp.concatenate(
-        [contract(attended, grad_branch[:, :half], NN), contract(attended, grad_branch[:, half:], NN)]
-    ).astype(BF16)
-
-    def spread(part):
-        return to_all(part.reshape(dp_size, -1, part.shape[1]))
-
-    def share(parts):
-        return jnp.sum(parts.astype(F32), axis=0).astype(BF16)
-
-    share_wo = share(spread(grad_wo))
     returned = [
         passed_along(grad_blocks[number], -hop) for number, hop in enumerate(range(HOPS, 0, -1))
     ]
-    returned = after(returned, share_wo)
     kv_total = grad_blocks[-1]
     for part in returned:
         kv_total = kv_total + part.astype(F32)
@@ -530,14 +560,10 @@
     grad_key_pre = rotate(kv_total[:kv_rows], cosine, -sine).astype(BF16)
     grad_value = kv_total[kv_rows:].astype(BF16)
 
-    grad_wqkv = jnp.concatenate(
-        [
-            contract(normed1, part, ((0,), (1,))).astype(BF16)
-            for part in (grad_query_pre, grad_key_pre, grad_value)
-        ],
-        axis=1,
-    )
-    share_wqkv = share(spread(grad_wqkv))
+    grad_qkv = jnp.concatenate([grad_query_pre, grad_key_pre, grad_value])
+    parts = weight_grads(normed1, grad_qkv, attended, grad_branch)
+    parts = to_all(after(parts, expert_out).reshape(dp_size, -1, parts.shape[1]))
+    summed = jnp.sum(parts.astype(F32), axis=0).astype(BF16)
     grad_norm1_part = (
         contract(grad_query_pre, w_query, ((0,), (1,)))
         + contract(grad_key_pre, w_key, ((0,), (1,)))
@@ -562,30 +588,24 @@
     )
     gain_rows = model_width // more
     extra = jnp.pad(extra, ((0, third - len(extra)), (0, 0)))
-    packed = jnp.concatenate(
-        [
-            share_wo,
-            share_wqkv[:, :width],
-            jnp.concatenate([share_wqkv[:, width:], extra], axis=1),
-        ]
-    )
+    packed = jnp.concatenate([summed, extra], axis=1)
     packed, sums, expert_out = lax.optimization_barrier((packed, sums, expert_out))
     gathered = lax.all_gather(packed, "dp", axis=0)
-    output = (hidden1 + combined(gated, in_plane(expert_out))).astype(BF16)
-    sums = sums[0].astype(F32)
-    grad_gate, grad_up, grad_down = (sums[0], sums[1], sums[2].T)
-    grad_wo, grad_wq, grad_wk, grad_wv, totals = unpack(gathered, kv_rows)
+    output = (hidden1 + combined(gated, expert_out)).astype(BF16)
+    grad_gate, grad_up, grad_down = jnp.split(sums[0].astype(F32), 3, axis=1)
+    grad_down = grad_down.T
+    high = gathered[:, 2 * gain_rows, -more : local_heads - more].astype(F32)
+    low = gathered[:, 2 * gain_rows + 1, -more : local_heads - more].astype(F32)
+    head_peaks = jnp.max(high + low, axis=0)
+    factor = clip_limit / jnp.maximum(head_peaks, clip_limit)
+    key_factor = jnp.min(factor.reshape(local_kv, group), axis=1)
+    scale_query = jnp.repeat(jnp.sqrt(factor), HD)[None, :]
+    scale_key = jnp.repeat(jnp.sqrt(key_factor), HD)[None, :]
+    grad_wo, grad_wq, grad_wk, grad_wv, totals, clipped_query, clipped_key = unpack(
+        gathered, w_query, w_key, scale_query, scale_key
+    )
     grad_gain1 = totals[:gain_rows].reshape(-1)
     grad_gain2 = totals[gain_rows : 2 * gain_rows].reshape(-1)
-    head_peaks = jnp.max(
-        gathered[:, 2 * third + 2 * gain_rows, 2 * kv_rows : 2 * kv_rows + local_heads].astype(F32)
-        + gathered[:, 2 * third + 2 * gain_rows + 1, 2 * kv_rows : 2 * kv_rows + local_heads].astype(F32),
-        axis=0,
-    )
-    factor = clip_limit / jnp.maximum(head_peaks, clip_limit)
-    key_factor = jnp.min(factor.reshape(local_kv, group), axis=1)
-    clipped_query = (w_query.astype(F32) * jnp.repeat(jnp.sqrt(factor), HD)[None, :]).astype(BF16)
-    clipped_key = (w_key.astype(F32) * jnp.repeat(jnp.sqrt(key_factor), HD)[None, :]).astype(BF16)
     return (
         output,
         input_grad,

time: 626 us -> 614 us (0.981)
  starting transfers between devices: 118 us -> 104 us
  matrix products: 34.6 us -> 27.2 us
    all_to_all x3, waiting for transfers between devices: 126 us -> 40.6 us  [in_plane(): lax.all_to_all(rows, 'dp', 0, 0, tiled=True, axis_index_groups=plane_groups)]
    all_to_all x2 -> x1, waiting for transfers between devices: 45.4 us -> 78.4 us  [to_all(): return lax.all_to_all(array, 'dp', 0, 0, tiled=True)]
    ppermute x8, waiting for transfers between devices: 8.07 us -> 38 us  [passed_along(): lax.ppermute(value, 'dp', [(s, s + steps) for s in range(first, last)])]
    all_gather x1, waiting for transfers between devices: 36.8 us -> 59.8 us  [shards(): gathered = lax.all_gather(packed, 'dp', axis=0)]
    all_to_all x3, starting transfers between devices: 40.6 us -> 22.5 us  [in_plane(): lax.all_to_all(rows, 'dp', 0, 0, tiled=True, axis_index_groups=plane_groups)]
    all_gather x0 -> x1, local copies, waits for them, and re-layouts: none -> 12.6 us  [shards(): lax.all_gather(packed_w, 'dp', axis=0, axis_index_groups=column_groups)]
    ppermute x6 -> x8, waiting for transfers between devices: 6.83 us -> 15.2 us  [swapped(): return lax.ppermute(array, 'tensor', [(0, 1), (1, 0)])]
    dot_general x18 -> x13, matrix products: 34.6 us -> 27.2 us  [contract(): lax.dot_general(left, right, (dims, ((), ())), preferred_element_type=F32)]
  transfers between devices with their start and end apart: 22 -> 23, of which waited for: 11 -> 12; matrix products, arithmetic and copies ran while one was open for 12% -> 10% of each run, Pallas kernels for 9% -> 11%
where the time goes in v3:
time: 614 us; the launch traced here: 604 us
  waiting for transfers between devices  232 us (38%)
  starting transfers between devices  104 us (17%)
  Pallas kernels  90.5 us (15%)
  blocking collectives  69 us (11%)
  local copies, waits for them, and re-layouts  34 us (6%)
  other arithmetic  32.2 us (5%)
  matrix products  27.2 us (4%)
  between operations  15 us (2%)
    all_to_all x1, waiting for transfers between devices, to_all(): return lax.all_to_all(array, 'dp', 0, 0, tiled=True)  78.4 us
    all_to_all x1, blocking collectives, in_plane(): lax.all_to_all(rows, 'dp', 0, 0, tiled=True, axis_index_groups=plane_groups)  69 us
    all_gather x1, waiting for transfers between devices, shards(): gathered = lax.all_gather(packed, 'dp', axis=0)  59.8 us
    all_to_all x1, starting transfers between devices, to_all(): return lax.all_to_all(array, 'dp', 0, 0, tiled=True)  41.3 us
    all_to_all x3, waiting for transfers between devices, in_plane(): lax.all_to_all(rows, 'dp', 0, 0, tiled=True, axis_index_groups=plane_groups)  40.6 us
    ppermute x8, waiting for transfers between devices, passed_along(): lax.ppermute(value, 'dp', [(s, s + steps) for s in range(first, last)])  38 us
    dot_general x13, matrix products, contract(): lax.dot_general(left, right, (dims, ((), ())), preferred_element_type=F32)  27.2 us
    all_to_all x3, starting transfers between devices, in_plane(): lax.all_to_all(rows, 'dp', 0, 0, tiled=True, axis_index_groups=plane_groups)  22.5 us
  transfers between devices with their start and end apart: 23, of which 12 were waited for; matrix products, arithmetic and copies ran while one was open for 10% of the time, Pallas kernels for 11%

profile of v3, /device:TPU:1, one launch (start us, length us, event | category | flops | bytes accessed | tf_op | source)
XLA Modules:
  0.0 604.0 jit_solution(11496508994829471376)
XLA Ops:
  25.5 5.7 collective-permute-start.1
  39.6 4.9 fusion
  45.2 11.5 %all-to-all-start = ((bf16[16,96,1536]{2,1,0:T(8,128)(2,1)}), bf16[16,96,1536]{2,1,0:T(8,128)(2,1)}, u32[]{:S(2)}, u32[]{:S(2)}) async-start(bf16[16,96,1536]{2,1,0:T(8,128)(2,1)} %bitcast.87), calls=%async_computation | async-start | bytes 9437184 | tf_op jit(solution)/shard_map/all_to_all | solution.py:500
  64.1 11.3 %shard_map.299 = (bf16[768,256]{1,0:T(8,128)(2,1)S(1)}, f32[12,256]{1,0:T(8,128)S(1)}, f32[12,256]{1,0:T(8,128)S(1)}) custom-call(bf16[768,256]{1,0:T(8,128)(2,1)S(1)} %bitcast.80, bf16[528,256]{1,0:T(8,128)(2,1)S(1)} %collective-permute-done.k4, bf16[528,256]{1,0:T(8,128)(2,1)S(1)} %copy-done.15, bf16[528,256]{1,0:T(8,128)(2,1)} %collective-permute-done.2.k2, ...), custom_call_target="tpu_custom_call" | custom-call | flops 1006632960 | bytes 2138112 | tf_op jit(solution)/shard_map/pallas_call | solution.py:127
  82.6 5.1 convolution_convert_fusion
  87.7 26.7 %all-to-all-done.g_ref = bf16[16,96,1536]{2,1,0:T(8,128)(2,1)} async-done(((bf16[16,96,1536]{2,1,0:T(8,128)(2,1)}), bf16[16,96,1536]{2,1,0:T(8,128)(2,1)}, u32[]{:S(2)}, u32[]{:S(2)}) %all-to-all-start) | async-done | bytes 4718624 | tf_op jit(solution)/shard_map/all_to_all | solution.py:500
  114.4 12.6 %copy.50 = bf16[6144,768]{1,0:T(8,128)(2,1)} copy(bf16[6144,768]{0,1:T(8,128)(2,1)} %all-gather.5.cloned.1.call-done) | data formatting | bytes 18874368 | tf_op jit(solution)/shard_map/all_gather | solution.py:476
  127.0 4.6 collective-permute-start.5
  131.7 69.0 %all_to_all.25.x_ref = bf16[16,96,1536]{2,1,0:T(8,128)(2,1)} all-to-all(bf16[16,96,1536]{2,1,0:T(8,128)(2,1)} %bitcast.82), channel_id=1, replica_groups={{0,2,4,6,8,10,12,14,16,18,20,22,24,26,28,30},{32,34,36,38,40,42,44,46,4..., dimensions={0} | all-to-all | bytes 9437184 | tf_op jit(solution)/shard_map/all_to_all | solution.py:500
  200.7 18.0 %shard_map.300 = (bf16[16,96,1536]{2,1,0:T(8,128)(2,1)}, bf16[3,512,768]{2,1,0:T(8,128)(2,1)}, bf16[3,512,768]{2,1,0:T(8,128)(2,1)}) custom-call(bf16[16,96,1536]{2,1,0:T(8,128)(2,1)} %all_to_all.25.x_ref, bf16[16,96,1536]{2,1,0:T(8,128)(2,1)} %all-to-all-done.g_ref, bf16[4,1536,768]{2,1,0:T(8,128)(2,1)} %bitcast.85, ...), custom_call_target="tpu_custom_call" | custom-call | flops 12683575296 | bytes 28311552 | tf_op jit(solution)/shard_map/pallas_call | solution.py:234
  223.3 18.3 %shard_map.301 = (bf16[3,1536,768]{2,1,0:T(8,128)(2,1)}, bf16[3,1536,256]{2,1,0:T(8,128)(2,1)}, bf16[3,1536,256]{2,1,0:T(8,128)(2,1)}, bf16[3,1536,256]{2,1,0:T(8,128)(2,1)}, bf16[16,96,1536]{2,1,0:T(8,128)(2,1)}) custom-call(bf16[16,96,1536]{2,1,0:T(8,128)(2,1)} %all_to_all.25.x_ref, bf16[16,96,1536]{2,1,0:T(8,128)(2,1)} %all-to-all-done.g_ref, ...), custom_call_target="tpu_custom_call" | custom-call | flops 10871635968 | bytes 31850496 | tf_op jit(solution)/shard_map/pallas_call | solution.py:282
  255.1 11.8 %shard_map.302 = bf16[4,1536,768]{2,1,0:T(8,128)(2,1)} custom-call(bf16[3,1536,768]{2,1,0:T(8,128)(2,1)} %get-tuple-element.64.own_ref, bf16[3,1536,256]{2,1,0:T(8,128)(2,1)} %collective-permute-done.6.refs_0_, bf16[3,1536,256]{2,1,0:T(8,128)(2,1)} %collective-permute-done.7.refs_1_, bf16[3,1536,256]{2,1,0:T(8,128)(2,1)} %collective-permute-done.8.refs_2_), custom_call_target="tpu_custom_call" | custom-call | flops 4718592 | bytes 28311552 | tf_op jit(solution)/shard_map/pallas_call | solution.py:323
  266.9 13.8 %all-to-all-done.2 = bf16[16,96,1536]{2,1,0:T(8,128)(2,1)} async-done(((bf16[16,96,1536]{2,1,0:T(8,128)(2,1)}), bf16[16,96,1536]{2,1,0:T(8,128)(2,1)}, u32[]{:S(2)}, u32[]{:S(2)}) %all-to-all-start.2) | async-done | bytes 4718624 | tf_op jit(solution)/shard_map/all_to_all | solution.py:500
  280.7 4.6 convolution_convert_fusion.1
  285.4 5.4 collective-permute-start.9
  290.8 6.4 %all-to-all-start.3 = ((bf16[16,96,1536]{2,1,0:T(8,128)(2,1)}), bf16[16,96,1536]{2,1,0:T(8,128)(2,1)}, u32[]{:S(2)}, u32[]{:S(2)}) async-start(bf16[16,96,1536]{2,1,0:T(8,128)(2,1)} %get-tuple-element.77), calls=%async_computation.3 | async-start | bytes 9437184 | tf_op jit(solution)/shard_map/all_to_all | solution.py:500
  305.3 15.6 %shard_map.303 = (bf16[768,256]{1,0:T(8,128)(2,1)S(1)}, bf16[512,256]{1,0:T(8,128)(2,1)S(1)}, bf16[512,256]{1,0:T(8,128)(2,1)S(1)}, bf16[512,256]{1,0:T(8,128)(2...) custom-call(bf16[768,256]{1,0:T(8,128)(2,1)S(1)} %bitcast.81, bf16[768,256]{1,0:T(8,128)(2,1)S(1)} %fusion.13.g_ref, ...), custom_call_target="tpu_custom_call" | custom-call | flops 251658240000 | bytes 3883008 | tf_op jit(solution)/shard_map/pallas_call | solution.py:190
  326.1 31.4 %collective-permute-done.10 = bf16[512,256]{1,0:T(8,128)(2,1)S(1)} collective-permute-done((bf16[512,256]{1,0:T(8,128)(2,1)S(1)}, bf16[512,256]{1,0:T(8,128)(2,1)S(1)}, u32[]{:S(2)}, u32[]{:S(2)}) %collective-permute-start.10) | collective-permute-done | bytes 262176 | tf_op jit(solution)/shard_map/ppermute | solution.py:48
  365.3 7.3 %shard_map.304 = bf16[1536,2048]{1,0:T(8,128)(2,1)} custom-call(bf16[256,1536]{1,0:T(8,128)(2,1)} %copy-done.19, bf16[1280,256]{1,0:T(8,128)(2,1)} %pad_maximum_fusion.1.qkv_ref, bf16[768,256]{1,0:T(8,128)(2,1)} %copy-done.7, bf16[256,1536]{1,0:T(8,128)(2,1)} %copy-done.20), custom_call_target="tpu_custom_call" | custom-call | flops 1610612736 | bytes 7864320 | tf_op jit(solution)/shard_map/pallas_call | solution.py:345
  372.6 41.3 %all-to-all-start.4 = ((bf16[64,24,2048]{2,1,0:T(8,128)(2,1)}), bf16[64,24,2048]{2,1,0:T(8,128)(2,1)}, u32[]{:S(2)}, u32[]{:S(2)}) async-start(bf16[64,24,2048]{2,1,0:T(8,128)(2,1)} %bitcast.83), calls=%async_computation.4 | async-start | bytes 12582912 | tf_op jit(solution)/shard_map/all_to_all | solution.py:52
  421.1 78.4 %all-to-all-done.4 = bf16[64,24,2048]{2,1,0:T(8,128)(2,1)} async-done(((bf16[64,24,2048]{2,1,0:T(8,128)(2,1)}), bf16[64,24,2048]{2,1,0:T(8,128)(2,1)}, u32[]{:S(2)}, u32[]{:S(2)}) %all-to-all-start.4) | async-done | bytes 6291488 | tf_op jit(solution)/shard_map/all_to_all | solution.py:52
  507.5 4.8 convolution_convert_fusion.2
  521.4 59.8 %all-gather.7.cloned.1.call-done = bf16[1536,2304]{1,0:T(8,128)(2,1)} async-done(((bf16[24,2304]{1,0:T(8,128)(2,1)}), bf16[1536,2304]{1,0:T(8,128)(2,1)}) %all-gather.7.cloned.1.call-update) | async-done | bytes 7077904 | tf_op jit(solution)/shard_map/all_gather | solution.py:593
  587.5 8.3 %shard_map.305 = (f32[768,1536]{1,0:T(8,128)}, f32[1536,768]{1,0:T(8,128)}, f32[1536,256]{1,0:T(8,128)}, f32[1536,256]{1,0:T(8,128)}, f32[24,256]{1,0:T(8,128)S(...) custom-call(bf16[64,24,2304]{2,1,0:T(8,128)(2,1)S(1)} %bitcast.79, bf16[1536,768]{1,0:T(8,128)(2,1)S(1)} %copy-done.3, ...), custom_call_target="tpu_custom_call" | custom-call | flops 3538944 | bytes 28311552 | tf_op jit(solution)/shard_map/pallas_call | solution.py:399
  (225 shorter events, 112.5 us)
Async XLA Ops:
  7.2 107.2 %all-gather.5.cloned.1.call-start = ((), (), s32[]{:S(2)}) async-start(), calls=%async_computation.7 | async-start | bytes 11796480 | tf_op jit(solution)/shard_map/all_gather | solution.py:476
  21.6 22.9 %collective-permute-start = (bf16[528,256]{1,0:T(8,128)(2,1)S(1)}, bf16[528,256]{1,0:T(8,128)(2,1)S(1)}, u32[]{:S(2)}, u32[]{:S(2)}) collective-permute-start(bf16[528,256]{1,0:T(8,128)(2,1)S(1)} %concatenate.31.k0), channel_id=1, source_target_pairs={{0,8},{2,10},{4,12},{6,14},{8,16},{10,18},{12,20},{14,22},{16,24},... | collective-permute-start | bytes 811016 | tf_op jit(solution)/shard_map/ppermute | solution.py:48
  25.5 18.9 %collective-permute-start.1 = (bf16[528,256]{1,0:T(8,128)(2,1)S(1)}, bf16[528,256]{1,0:T(8,128)(2,1)S(1)}, u32[]{:S(2)}, u32[]{:S(2)}) collective-permute-start(bf16[528,256]{1,0:T(8,128)(2,1)S(1)} %concatenate.31.k0), channel_id=1, source_target_pairs={{0,6},{2,8},{4,10},{6,12},{8,14},{10,16},{12,18},{14,20},{16,22},{... | collective-permute-start | bytes 811016 | tf_op jit(solution)/shard_map/ppermute | solution.py:48
  31.2 13.3 %collective-permute-start.2 = (bf16[528,256]{1,0:T(8,128)(2,1)S(1)}, bf16[528,256]{1,0:T(8,128)(2,1)}, u32[]{:S(2)}, u32[]{:S(2)}) collective-permute-start(bf16[528,256]{1,0:T(8,128)(2,1)S(1)} %concatenate.31.k0), channel_id=1, source_target_pairs={{0,4},{2,6},{4,8},{6,10},{8,12},{10,14},{12,16},{14,18},{16,20},{1... | collective-permute-start | bytes 811016 | tf_op jit(solution)/shard_map/ppermute | solution.py:48
  34.4 10.1 %collective-permute-start.3 = (bf16[528,256]{1,0:T(8,128)(2,1)S(1)}, bf16[528,256]{1,0:T(8,128)(2,1)}, u32[]{:S(2)}, u32[]{:S(2)}) collective-permute-start(bf16[528,256]{1,0:T(8,128)(2,1)S(1)} %concatenate.31.k0), channel_id=1, source_target_pairs={{0,2},{2,4},{4,6},{6,8},{8,10},{10,12},{12,14},{14,16},{16,18},{18... | collective-permute-start | bytes 811016 | tf_op jit(solution)/shard_map/ppermute | solution.py:48
  38.1 206.3 %copy-start.46 = (f32[32]{0:T(128)}, f32[32]{0:T(128)S(1)}, u32[]{:S(2)}) copy-start(f32[32]{0:T(128)S(1)} %add_convert_fusion.4) | copy-start | bytes 388
  45.2 69.2 %all-to-all-start = ((bf16[16,96,1536]{2,1,0:T(8,128)(2,1)}), bf16[16,96,1536]{2,1,0:T(8,128)(2,1)}, u32[]{:S(2)}, u32[]{:S(2)}) async-start(bf16[16,96,1536]{2,1,0:T(8,128)(2,1)} %bitcast.87), calls=%async_computation | async-start | bytes 9437184 | tf_op jit(solution)/shard_map/all_to_all | solution.py:500
  76.2 4.9 collective-permute-start.4
  127.0 73.6 %collective-permute-start.5 = (bf16[4,1536,768]{2,1,0:T(8,128)(2,1)}, bf16[4,1536,768]{2,1,0:T(8,128)(2,1)}, u32[]{:S(2)}, u32[]{:S(2)}) collective-permute-start(bf16[4,1536,768]{2,1,0:T(8,128)(2,1)} %bitcast.84), channel_id=1, source_target_pairs={{0,1},{1,0},{2,3},{3,2},{4,5},{5,4},{6,7},{7,6},{8,9},{9,8},{10,11... | collective-permute-start | bytes 28311560 | tf_op jit(solution)/shard_map/ppermute | solution.py:38
  218.7 62.0 %all-to-all-start.2 = ((bf16[16,96,1536]{2,1,0:T(8,128)(2,1)}), bf16[16,96,1536]{2,1,0:T(8,128)(2,1)}, u32[]{:S(2)}, u32[]{:S(2)}) async-start(bf16[16,96,1536]{2,1,0:T(8,128)(2,1)} %get-tuple-element.61), calls=%async_computation.2 | async-start | bytes 9437184 | tf_op jit(solution)/shard_map/all_to_all | solution.py:500
  223.3 280.7 %reduce-scatter.2.cloned.1.call-start = ((), (), s32[]{:S(2)}) async-start(), calls=%async_computation.6 | async-start | bytes 11796480 | tf_op jit(solution)/shard_map/reduce_scatter | solution.py:541
  241.6 6.8 %collective-permute-start.6 = (bf16[3,1536,256]{2,1,0:T(8,128)(2,1)}, bf16[3,1536,256]{2,1,0:T(8,128)(2,1)}, u32[]{:S(2)}, u32[]{:S(2)}) collective-permute-start(bf16[3,1536,256]{2,1,0:T(8,128)(2,1)} %get-tuple-element.65), channel_id=1, source_target_pairs={{0,1},{1,0},{2,3},{3,2},{4,5},{5,4},{6,7},{7,6},{8,9},{9,8},{10,11... | collective-permute-start | bytes 7077896 | tf_op jit(solution)/shard_map/ppermute | solution.py:38
  243.9 7.9 %collective-permute-start.7 = (bf16[3,1536,256]{2,1,0:T(8,128)(2,1)}, bf16[3,1536,256]{2,1,0:T(8,128)(2,1)}, u32[]{:S(2)}, u32[]{:S(2)}) collective-permute-start(bf16[3,1536,256]{2,1,0:T(8,128)(2,1)} %get-tuple-element.66), channel_id=1, source_target_pairs={{0,1},{1,0},{2,3},{3,2},{4,5},{5,4},{6,7},{7,6},{8,9},{9,8},{10,11... | collective-permute-start | bytes 7077896 | tf_op jit(solution)/shard_map/ppermute | solution.py:38
  244.0 11.2 %collective-permute-start.8 = (bf16[3,1536,256]{2,1,0:T(8,128)(2,1)}, bf16[3,1536,256]{2,1,0:T(8,128)(2,1)}, u32[]{:S(2)}, u32[]{:S(2)}) collective-permute-start(bf16[3,1536,256]{2,1,0:T(8,128)(2,1)} %get-tuple-element.67), channel_id=1, source_target_pairs={{0,1},{1,0},{2,3},{3,2},{4,5},{5,4},{6,7},{7,6},{8,9},{9,8},{10,11... | collective-permute-start | bytes 7077896 | tf_op jit(solution)/shard_map/ppermute | solution.py:38
  285.4 11.8 %collective-permute-start.9 = (bf16[256,1536]{1,0:T(8,128)(2,1)}, bf16[256,1536]{1,0:T(8,128)(2,1)}, u32[]{:S(2)}, u32[]{:S(2)}) collective-permute-start(bf16[256,1536]{1,0:T(8,128)(2,1)} %convolution_convert_fusion.1), channel_id=1, source_target_pairs={{0,1},{1,0},{2,3},{3,2},{4,5},{5,4},{6,7},{7,6},{8,9},{9,8},{10,11... | collective-permute-start | bytes 2359304 | tf_op jit(solution)/shard_map/ppermute | solution.py:38
  290.8 81.8 %all-to-all-start.3 = ((bf16[16,96,1536]{2,1,0:T(8,128)(2,1)}), bf16[16,96,1536]{2,1,0:T(8,128)(2,1)}, u32[]{:S(2)}, u32[]{:S(2)}) async-start(bf16[16,96,1536]{2,1,0:T(8,128)(2,1)} %get-tuple-element.77), calls=%async_computation.3 | async-start | bytes 9437184 | tf_op jit(solution)/shard_map/all_to_all | solution.py:500
  320.9 36.6 %collective-permute-start.10 = (bf16[512,256]{1,0:T(8,128)(2,1)S(1)}, bf16[512,256]{1,0:T(8,128)(2,1)S(1)}, u32[]{:S(2)}, u32[]{:S(2)}) collective-permute-start(bf16[512,256]{1,0:T(8,128)(2,1)S(1)} %get-tuple-element.72), channel_id=1, source_target_pairs={{8,0},{10,2},{12,4},{14,6},{16,8},{18,10},{20,12},{22,14},{24,16},... | collective-permute-start | bytes 786440 | tf_op jit(solution)/shard_map/ppermute | solution.py:48
  322.2 37.5 %collective-permute-start.11 = (bf16[512,256]{1,0:T(8,128)(2,1)S(1)}, bf16[512,256]{1,0:T(8,128)(2,1)S(1)}, u32[]{:S(2)}, u32[]{:S(2)}) collective-permute-start(bf16[512,256]{1,0:T(8,128)(2,1)S(1)} %get-tuple-element.73), channel_id=1, source_target_pairs={{6,0},{8,2},{10,4},{12,6},{14,8},{16,10},{18,12},{20,14},{22,16},{... | collective-permute-start | bytes 786440 | tf_op jit(solution)/shard_map/ppermute | solution.py:48
  323.5 40.6 %collective-permute-start.12 = (bf16[512,256]{1,0:T(8,128)(2,1)S(1)}, bf16[512,256]{1,0:T(8,128)(2,1)S(1)}, u32[]{:S(2)}, u32[]{:S(2)}) collective-permute-start(bf16[512,256]{1,0:T(8,128)(2,1)S(1)} %get-tuple-element.74), channel_id=1, source_target_pairs={{4,0},{6,2},{8,4},{10,6},{12,8},{14,10},{16,12},{18,14},{20,16},{2... | collective-permute-start | bytes 786440 | tf_op jit(solution)/shard_map/ppermute | solution.py:48
  324.8 39.3 %collective-permute-start.13 = (bf16[512,256]{1,0:T(8,128)(2,1)S(1)}, bf16[512,256]{1,0:T(8,128)(2,1)S(1)}, u32[]{:S(2)}, u32[]{:S(2)}) collective-permute-start(bf16[512,256]{1,0:T(8,128)(2,1)S(1)} %get-tuple-element.75), channel_id=1, source_target_pairs={{2,0},{4,2},{6,4},{8,6},{10,8},{12,10},{14,12},{16,14},{18,16},{20... | collective-permute-start | bytes 786440 | tf_op jit(solution)/shard_map/ppermute | solution.py:48
  372.6 126.9 %all-to-all-start.4 = ((bf16[64,24,2048]{2,1,0:T(8,128)(2,1)}), bf16[64,24,2048]{2,1,0:T(8,128)(2,1)}, u32[]{:S(2)}, u32[]{:S(2)}) async-start(bf16[64,24,2048]{2,1,0:T(8,128)(2,1)} %bitcast.83), calls=%async_computation.4 | async-start | bytes 12582912 | tf_op jit(solution)/shard_map/all_to_all | solution.py:52
  413.9 167.3 %all-gather.7.cloned.1.call-start = ((), (), s32[]{:S(2)}) async-start(), calls=%async_computation.8 | async-start | bytes 7188480 | tf_op jit(solution)/shard_map/all_gather | solution.py:593
  416.8 3.7 collective-permute-start.14
  512.3 6.1 %collective-permute-start.15 = (bf16[256,1536]{1,0:T(8,128)(2,1)}, bf16[256,1536]{1,0:T(8,128)(2,1)}, u32[]{:S(2)}, u32[]{:S(2)}) collective-permute-start(bf16[256,1536]{1,0:T(8,128)(2,1)} %convolution_convert_fusion.2), channel_id=1, source_target_pairs={{0,1},{1,0},{2,3},{3,2},{4,5},{5,4},{6,7},{7,6},{8,9},{9,8},{10,11... | collective-permute-start | bytes 2359304 | tf_op jit(solution)/shard_map/ppermute | solution.py:38
  (52 other events, 1032.6 us)
Sparse Core Ops, SparseCore 0:
  14.2 95.6 all-gather.4
  290.9 93.8 reduce-scatter.1
  504.2 76.9 all-gather.6

commit v4 on v3

--- a/solution.py
+++ b/solution.py
@@ -17,6 +17,8 @@
 PLANE = 16
 SEGMENTS = 3
 AUX = 16
+LANES = 256
+MORE = 128
 
 EPS = 1e-06
 ROPE_BASE = 10000.0
@@ -46,10 +48,6 @@
     count = lax.axis_size("dp")
     first, last = (max(0, -steps), min(count, count - steps))
     return lax.ppermute(value, "dp", [(s, s + steps) for s in range(first, last)])
-
-
-def to_all(array):
-    return lax.all_to_all(array, "dp", 0, 0, tiled=True)
 
 
 def rope_tables(count, dp_size):
@@ -204,6 +202,28 @@
     )(q, grad, log_total, cosine, sine, *blocks)
 
 
+def pack_weights_kernel(gate_ref, up_ref, down_ref, out_ref):
+    hidden = gate_ref.shape[1]
+    out_ref[:, :hidden] = gate_ref[...]
+    out_ref[:, hidden : 2 * hidden] = up_ref[...]
+    out_ref[:, 2 * hidden :] = jnp.transpose(down_ref[...].astype(F32)).astype(BF16)
+
+
+def pack_weights(gate, up, down):
+    width, hidden = gate.shape
+    thin = pl.BlockSpec((LANES, hidden), lambda i: (i, 0))
+    return pl.pallas_call(
+        pack_weights_kernel,
+        grid=(width // LANES,),
+        in_specs=[thin, thin, pl.BlockSpec((hidden, LANES), lambda i: (0, i))],
+        out_specs=pl.BlockSpec((LANES, 3 * hidden), lambda i: (i, 0)),
+        out_shape=jax.ShapeDtypeStruct((width, 3 * hidden), BF16),
+        cost_estimate=pl.CostEstimate(
+            flops=width * hidden, bytes_accessed=12 * width * hidden, transcendentals=0
+        ),
+    )(gate, up, down)
+
+
 def expert_kernel(x_ref, g_ref, own_ref, peer_ref, dx_ref, own_acts, peer_acts):
     width = x_ref.shape[-1]
     rows, grads = (x_ref[...].reshape(-1, width), g_ref[...].reshape(-1, width))
@@ -332,86 +352,75 @@
     )(own, *peers)
 
 
-def weight_grads_kernel(normed_ref, qkv_ref, attended_ref, branch_ref, out_ref):
+def weight_grads_kernel(normed_ref, qkv_ref, attended_ref, branch_ref, extra_ref, out_ref):
     width = branch_ref.shape[1]
+    columns = width + qkv_ref.shape[0]
     out_ref[:, :width] = contract(attended_ref[...], branch_ref[...], NN).astype(BF16)
-    out_ref[:, width:] = contract(normed_ref[...], qkv_ref[...], ((0,), (1,))).astype(BF16)
-
-
-def weight_grads(normed, grad_qkv, attended, branch):
+    out_ref[:, width:columns] = contract(normed_ref[...], qkv_ref[...], ((0,), (1,))).astype(BF16)
+    out_ref[:, columns:] = jnp.transpose(extra_ref[...]).astype(BF16)
+
+
+def weight_grads(normed, grad_qkv, attended, branch, extra):
     tok, model = normed.shape
     width, columns = (attended.shape[0], grad_qkv.shape[0])
-    half = width // 256
+    half = width // LANES
+    every = width + columns + MORE
     return pl.pallas_call(
         weight_grads_kernel,
-        grid=(model // 256,),
+        grid=(model // LANES,),
         in_specs=[
-            pl.BlockSpec((tok, 256), lambda i: (0, i)),
+            pl.BlockSpec((tok, LANES), lambda i: (0, i)),
             pl.BlockSpec((columns, tok), lambda i: (0, 0)),
-            pl.BlockSpec((256, tok), lambda i: (i % half, 0)),
+            pl.BlockSpec((LANES, tok), lambda i: (i % half, 0)),
             pl.BlockSpec((tok, width), lambda i: (0, i // half)),
+            pl.BlockSpec((MORE, LANES), lambda i: (0, i)),
         ],
-        out_specs=pl.BlockSpec((256, width + columns), lambda i: (i, 0)),
-        out_shape=jax.ShapeDtypeStruct((model, width + columns), BF16),
-        cost_estimate=pl.CostEstimate(
-            flops=2 * tok * model * (width + columns),
-            bytes_accessed=2 * model * (width + columns) + 4 * tok * model,
+        out_specs=pl.BlockSpec((LANES, every), lambda i: (i, 0)),
+        out_shape=jax.ShapeDtypeStruct((model, every), BF16),
+        cost_estimate=pl.CostEstimate(
+            flops=2 * tok * model * every,
+            bytes_accessed=2 * model * every + 4 * tok * model,
             transcendentals=0,
         ),
-    )(normed, grad_qkv, attended, branch)
+    )(normed, grad_qkv, attended, branch, extra)
 
 
 def unpack_kernel(
     in_ref, query_ref, key_ref, sq_ref, sk_ref,
     wo_ref, wq_ref, wk_ref, wv_ref, sum_ref, cq_ref, ck_ref,
 ):
-    step = pl.program_id(0)
-    chunks, lines, _ = in_ref.shape
-    for c in range(chunks):
-        here, at = (slice(c * lines, (c + 1) * lines), 0)
-        for target in (wo_ref, wq_ref, wk_ref, wv_ref):
-            size = target.shape[1]
-            target[here, :] = in_ref[c, :, at : at + size].astype(F32)
-            at += size
-    total = jnp.sum(in_ref[:, :, at:].astype(F32), axis=0)
+    at = 0
+    for target in (wo_ref, wq_ref, wk_ref, wv_ref):
+        size = target.shape[1]
+        target[...] = in_ref[:, at : at + size].astype(F32)
+        at += size
+    sum_ref[...] = jnp.transpose(in_ref[:, at:].astype(F32))[: sum_ref.shape[0]]
     cq_ref[...] = (query_ref[...].astype(F32) * sq_ref[...]).astype(BF16)
     ck_ref[...] = (key_ref[...].astype(F32) * sk_ref[...]).astype(BF16)
 
-    @pl.when(step == 0)
-    def _():
-        sum_ref[...] = total
-
-    @pl.when(step > 0)
-    def _():
-        sum_ref[...] = sum_ref[...] + total
-
-
-def unpack(gathered, w_query, w_key, scale_query, scale_key):
-    parts, lines, every = gathered.shape
+
+def unpack(summed, w_query, w_key, scale_query, scale_key):
+    total, every = summed.shape
     width, narrow = (w_query.shape[1], w_key.shape[1])
-    steps = 16
-    per = parts // steps
-    rows = per * lines
-    total = parts * lines
-    extra = (lines, every - 2 * width - 2 * narrow)
-    wide = pl.BlockSpec((rows, width), lambda i: (i, 0))
-    thin = pl.BlockSpec((rows, narrow), lambda i: (i, 0))
+    steps = total // LANES
+    wide = pl.BlockSpec((LANES, width), lambda i: (i, 0))
+    thin = pl.BlockSpec((LANES, narrow), lambda i: (i, 0))
     return pl.pallas_call(
         unpack_kernel,
         grid=(steps,),
         in_specs=[
-            pl.BlockSpec((per, lines, every), lambda i: (i, 0, 0)),
+            pl.BlockSpec((LANES, every), lambda i: (i, 0)),
             wide,
             thin,
             pl.BlockSpec((1, width), lambda i: (0, 0)),
             pl.BlockSpec((1, narrow), lambda i: (0, 0)),
         ],
         out_specs=[
-            pl.BlockSpec((rows, width), lambda i: (i % (steps // 2), i // (steps // 2))),
+            pl.BlockSpec((LANES, width), lambda i: (i % (steps // 2), i // (steps // 2))),
             wide,
             thin,
             thin,
-            pl.BlockSpec(extra, lambda i: (0, 0)),
+            pl.BlockSpec((8, LANES), lambda i: (0, i)),
             wide,
             thin,
         ],
@@ -420,7 +429,7 @@
             jax.ShapeDtypeStruct((total, width), F32),
             jax.ShapeDtypeStruct((total, narrow), F32),
             jax.ShapeDtypeStruct((total, narrow), F32),
-            jax.ShapeDtypeStruct(extra, F32),
+            jax.ShapeDtypeStruct((8, total), F32),
             jax.ShapeDtypeStruct((total, width), BF16),
             jax.ShapeDtypeStruct((total, narrow), BF16),
         ],
@@ -428,7 +437,7 @@
         cost_estimate=pl.CostEstimate(
             flops=total * every, bytes_accessed=8 * total * every, transcendentals=0
         ),
-    )(gathered, w_query, w_key, scale_query, scale_key)
+    )(summed, w_query, w_key, scale_query, scale_key)
 
 
 def rms_scale(values):
@@ -472,7 +481,7 @@
     plane_groups = [list(range(at, at + PLANE)) for at in range(0, dp_size, PLANE)]
     column_groups = [list(range(at, dp_size, PLANE)) for at in range(PLANE)]
 
-    packed_w = jnp.concatenate([w_gate[0], w_up[0], w_down[0].T], axis=1)
+    packed_w = pack_weights(w_gate[0], w_up[0], w_down[0])
     own = lax.all_gather(packed_w, "dp", axis=0, axis_index_groups=column_groups)
 
     picks = route_ids.T
@@ -560,10 +569,6 @@
     grad_key_pre = rotate(kv_total[:kv_rows], cosine, -sine).astype(BF16)
     grad_value = kv_total[kv_rows:].astype(BF16)
 
-    grad_qkv = jnp.concatenate([grad_query_pre, grad_key_pre, grad_value])
-    parts = weight_grads(normed1, grad_qkv, attended, grad_branch)
-    parts = to_all(after(parts, expert_out).reshape(dp_size, -1, parts.shape[1]))
-    summed = jnp.sum(parts.astype(F32), axis=0).astype(BF16)
     grad_norm1_part = (
         contract(grad_query_pre, w_query, ((0,), (1,)))
         + contract(grad_key_pre, w_key, ((0,), (1,)))
@@ -573,39 +578,28 @@
     grad_normed1 = grad_norm1_part.astype(F32) + swapped(grad_norm1_part).astype(F32)
     grad_from_norm1, grad_gain1 = norm_back(grad_normed1, x_float, inverse1, norm1_gain)
     input_grad = grad_hidden1 + grad_from_norm1
-    width = w_query.shape[1]
     peak = jnp.max(peaks, axis=1)
-    peak_high = peak.astype(BF16)
-    peak_low = (peak - peak_high.astype(F32)).astype(BF16)
-    third = model_width // dp_size
-    more = width - 2 * kv_rows
-    extra = jnp.concatenate(
-        [
-            grad_gain1.astype(BF16).reshape(-1, more),
-            grad_gain2.astype(BF16).reshape(-1, more),
-            jnp.pad(jnp.stack([peak_high, peak_low]), ((0, 0), (0, more - local_heads))),
-        ]
-    )
-    gain_rows = model_width // more
-    extra = jnp.pad(extra, ((0, third - len(extra)), (0, 0)))
-    packed = jnp.concatenate([summed, extra], axis=1)
-    packed, sums, expert_out = lax.optimization_barrier((packed, sums, expert_out))
-    gathered = lax.all_gather(packed, "dp", axis=0)
+    peak_high = peak.astype(BF16).astype(F32)
+    places = jnp.arange(dp_size)[:, None] == lax.axis_index("dp")
+    peak_row = jnp.where(places, jnp.concatenate([peak_high, peak - peak_high])[None], 0.0)
+    extra = jnp.stack([grad_gain1, grad_gain2, peak_row.reshape(-1)])
+    extra = jnp.pad(extra, ((0, MORE - len(extra)), (0, 0)))
+    grad_qkv = jnp.concatenate([grad_query_pre, grad_key_pre, grad_value])
+    parts = weight_grads(normed1, grad_qkv, attended, grad_branch, extra)
+    parts, sums, expert_out = lax.optimization_barrier((parts, sums, expert_out))
+    summed = lax.psum(parts, "dp")
     output = (hidden1 + combined(gated, expert_out)).astype(BF16)
     grad_gate, grad_up, grad_down = jnp.split(sums[0].astype(F32), 3, axis=1)
     grad_down = grad_down.T
-    high = gathered[:, 2 * gain_rows, -more : local_heads - more].astype(F32)
-    low = gathered[:, 2 * gain_rows + 1, -more : local_heads - more].astype(F32)
-    head_peaks = jnp.max(high + low, axis=0)
+    all_peaks = summed[:, 2 - MORE].astype(F32).reshape(dp_size, 2 * local_heads)
+    head_peaks = jnp.max(all_peaks[:, :local_heads] + all_peaks[:, local_heads:], axis=0)
     factor = clip_limit / jnp.maximum(head_peaks, clip_limit)
     key_factor = jnp.min(factor.reshape(local_kv, group), axis=1)
     scale_query = jnp.repeat(jnp.sqrt(factor), HD)[None, :]
     scale_key = jnp.repeat(jnp.sqrt(key_factor), HD)[None, :]
     grad_wo, grad_wq, grad_wk, grad_wv, totals, clipped_query, clipped_key = unpack(
-        gathered, w_query, w_key, scale_query, scale_key
-    )
-    grad_gain1 = totals[:gain_rows].reshape(-1)
-    grad_gain2 = totals[gain_rows : 2 * gain_rows].reshape(-1)
+        summed, w_query, w_key, scale_query, scale_key
+    )
     return (
         output,
         input_grad,
@@ -613,8 +607,8 @@
         grad_wk,
         grad_wv,
         grad_wo,
-        grad_gain1,
-        grad_gain2,
+        totals[0],
+        totals[1],
         grad_gate[None],
         grad_up[None],
         grad_down[None],

time: 614 us -> 570 us (0.928); the launches traced: 604 us -> 568 us
  starting transfers between devices: 104 us -> 60.5 us
  waiting for transfers between devices: 232 us -> 256 us
  local copies, waits for them, and re-layouts: 34 us -> 21.6 us
    psum x0 -> x1, waiting for transfers between devices: none -> 160 us  [shards(): summed = lax.psum(parts, 'dp')]
    all_to_all x1 -> x0, waiting for transfers between devices: 78.4 us -> none  [to_all(): return lax.all_to_all(array, 'dp', 0, 0, tiled=True)]
    all_gather x1 -> x0, waiting for transfers between devices: 59.8 us -> none  [shards(): gathered = lax.all_gather(packed, 'dp', axis=0)]
    all_to_all x1 -> x0, starting transfers between devices: 41.3 us -> none  [to_all(): return lax.all_to_all(array, 'dp', 0, 0, tiled=True)]
    all_gather x1 -> x0, local copies, waits for them, and re-layouts: 12.6 us -> none  [shards(): lax.all_gather(packed_w, 'dp', axis=0, axis_index_groups=column_groups)]
    pallas_call x2 -> x3, Pallas kernels: 15.6 us -> 18.5 us  [the longest x1 7.48 us: weight_grads(): pl.pallas_call(weight_grads_kernel, grid=(model // LANES,), in_specs=[pl....]
    unnamed x109 -> x113, local copies, waits for them, and re-layouts: 14.3 us -> 13.7 us
  transfers between devices with their start and end apart: 23 -> 22, of which waited for: 12 -> 11; matrix products, arithmetic and copies ran while one was open for 10% -> 10% of each run, Pallas kernels for 11% -> 11%
where the time goes in v4:
time: 570 us; the launch traced here: 568 us
  waiting for transfers between devices  256 us (45%)
  Pallas kernels  93.7 us (16%)
  blocking collectives  69 us (12%)
  starting transfers between devices  60.5 us (11%)
  other arithmetic  27.3 us (5%)
  matrix products  25.8 us (5%)
  local copies, waits for them, and re-layouts  21.6 us (4%)
  between operations  14.6 us (3%)
    psum x1, waiting for transfers between devices, shards(): summed = lax.psum(parts, 'dp')  160 us
    all_to_all x1, blocking collectives, in_plane(): lax.all_to_all(rows, 'dp', 0, 0, tiled=True, axis_index_groups=plane_groups)  69 us
    all_to_all x3, waiting for transfers between devices, in_plane(): lax.all_to_all(rows, 'dp', 0, 0, tiled=True, axis_index_groups=plane_groups)  41.8 us
    ppermute x8, waiting for transfers between devices, passed_along(): lax.ppermute(value, 'dp', [(s, s + steps) for s in range(first, last)])  37.1 us
    dot_general x13, matrix products, contract(): lax.dot_general(left, right, (dims, ((), ())), preferred_element_type=F32)  25.8 us
    all_to_all x3, starting transfers between devices, in_plane(): lax.all_to_all(rows, 'dp', 0, 0, tiled=True, axis_index_groups=plane_groups)  22.4 us
    ppermute x8, starting transfers between devices, passed_along(): lax.ppermute(value, 'dp', [(s, s + steps) for s in range(first, last)])  21.7 us
    pallas_call x1, Pallas kernels, expert_sums(): pl.pallas_call(expert_sums_kernel, grid=(segments,), in_specs=[wide, wide...  18.3 us
  transfers between devices with their start and end apart: 22, of which 11 were waited for; matrix products, arithmetic and copies ran while one was open for 10% of the time, Pallas kernels for 11%

profile of v4, /device:TPU:1, one launch (start us, length us, event | category | flops | bytes accessed | tf_op | source)
XLA Modules:
  0.0 568.5 jit_solution(15794784284584663265)
XLA Ops:
  7.2 5.4 shard_map.300
  24.1 5.7 collective-permute-start.1
  38.2 4.9 fusion
  43.8 11.5 %all-to-all-start = ((bf16[16,96,1536]{2,1,0:T(8,128)(2,1)}), bf16[16,96,1536]{2,1,0:T(8,128)(2,1)}, u32[]{:S(2)}, u32[]{:S(2)}) async-start(bf16[16,96,1536]{2,1,0:T(8,128)(2,1)} %bitcast.70), calls=%async_computation | async-start | bytes 9437184 | tf_op jit(solution)/shard_map/all_to_all | solution.py:509
  62.7 11.3 %shard_map.299 = (bf16[768,256]{1,0:T(8,128)(2,1)S(1)}, f32[12,256]{1,0:T(8,128)S(1)}, f32[12,256]{1,0:T(8,128)S(1)}) custom-call(bf16[768,256]{1,0:T(8,128)(2,1)S(1)} %bitcast.67, bf16[528,256]{1,0:T(8,128)(2,1)S(1)} %collective-permute-done.k4, bf16[528,256]{1,0:T(8,128)(2,1)S(1)} %copy-done.15, bf16[528,256]{1,0:T(8,128)(2,1)} %collective-permute-done.2.k2, ...), custom_call_target="tpu_custom_call" | custom-call | flops 1006632960 | bytes 2138112 | tf_op jit(solution)/shard_map/pallas_call | solution.py:125
  85.0 28.1 %all-to-all-done.g_ref = bf16[16,96,1536]{2,1,0:T(8,128)(2,1)} async-done(((bf16[16,96,1536]{2,1,0:T(8,128)(2,1)}), bf16[16,96,1536]{2,1,0:T(8,128)(2,1)}, u32[]{:S(2)}, u32[]{:S(2)}) %all-to-all-start) | async-done | bytes 4718624 | tf_op jit(solution)/shard_map/all_to_all | solution.py:509
  113.0 4.6 collective-permute-start.5
  117.6 69.0 %all_to_all.20.x_ref = bf16[16,96,1536]{2,1,0:T(8,128)(2,1)} all-to-all(bf16[16,96,1536]{2,1,0:T(8,128)(2,1)} %bitcast.69), channel_id=1, replica_groups={{0,2,4,6,8,10,12,14,16,18,20,22,24,26,28,30},{32,34,36,38,40,42,44,46,4..., dimensions={0} | all-to-all | bytes 9437184 | tf_op jit(solution)/shard_map/all_to_all | solution.py:509
  186.7 18.0 %shard_map.301 = (bf16[16,96,1536]{2,1,0:T(8,128)(2,1)}, bf16[3,512,768]{2,1,0:T(8,128)(2,1)}, bf16[3,512,768]{2,1,0:T(8,128)(2,1)}) custom-call(bf16[16,96,1536]{2,1,0:T(8,128)(2,1)} %all_to_all.20.x_ref, bf16[16,96,1536]{2,1,0:T(8,128)(2,1)} %all-to-all-done.g_ref, bf16[4,1536,768]{2,1,0:T(8,128)(2,1)} %bitcast.85, ...), custom_call_target="tpu_custom_call" | custom-call | flops 12683575296 | bytes 28311552 | tf_op jit(solution)/shard_map/pallas_call | solution.py:254
  204.7 4.6 all-to-all-start.2
  209.3 18.3 %shard_map.302 = (bf16[3,1536,768]{2,1,0:T(8,128)(2,1)}, bf16[3,1536,256]{2,1,0:T(8,128)(2,1)}, bf16[3,1536,256]{2,1,0:T(8,128)(2,1)}, bf16[3,1536,256]{2,1,0:T(8,128)(2,1)}, bf16[16,96,1536]{2,1,0:T(8,128)(2,1)}) custom-call(bf16[16,96,1536]{2,1,0:T(8,128)(2,1)} %all_to_all.20.x_ref, bf16[16,96,1536]{2,1,0:T(8,128)(2,1)} %all-to-all-done.g_ref, ...), custom_call_target="tpu_custom_call" | custom-call | flops 10871635968 | bytes 31850496 | tf_op jit(solution)/shard_map/pallas_call | solution.py:302
  241.1 11.9 %shard_map.303 = bf16[4,1536,768]{2,1,0:T(8,128)(2,1)} custom-call(bf16[3,1536,768]{2,1,0:T(8,128)(2,1)} %get-tuple-element.63.own_ref, bf16[3,1536,256]{2,1,0:T(8,128)(2,1)} %collective-permute-done.6.refs_0_, bf16[3,1536,256]{2,1,0:T(8,128)(2,1)} %collective-permute-done.7.refs_1_, bf16[3,1536,256]{2,1,0:T(8,128)(2,1)} %collective-permute-done.8.refs_2_), custom_call_target="tpu_custom_call" | custom-call | flops 4718592 | bytes 28311552 | tf_op jit(solution)/shard_map/pallas_call | solution.py:343
  253.0 13.7 %all-to-all-done.2 = bf16[16,96,1536]{2,1,0:T(8,128)(2,1)} async-done(((bf16[16,96,1536]{2,1,0:T(8,128)(2,1)}), bf16[16,96,1536]{2,1,0:T(8,128)(2,1)}, u32[]{:S(2)}, u32[]{:S(2)}) %all-to-all-start.2) | async-done | bytes 4718624 | tf_op jit(solution)/shard_map/all_to_all | solution.py:509
  266.7 4.6 convolution_convert_fusion.1
  271.4 5.3 collective-permute-start.9
  277.9 6.3 %all-to-all-start.3 = ((bf16[16,96,1536]{2,1,0:T(8,128)(2,1)}), bf16[16,96,1536]{2,1,0:T(8,128)(2,1)}, u32[]{:S(2)}, u32[]{:S(2)}) async-start(bf16[16,96,1536]{2,1,0:T(8,128)(2,1)} %get-tuple-element.77), calls=%async_computation.4 | async-start | bytes 9437184 | tf_op jit(solution)/shard_map/all_to_all | solution.py:509
  292.2 15.7 %shard_map.304 = (bf16[768,256]{1,0:T(8,128)(2,1)S(1)}, bf16[512,256]{1,0:T(8,128)(2,1)S(1)}, bf16[512,256]{1,0:T(8,128)(2,1)S(1)}, bf16[512,256]{1,0:T(8,128)(2...) custom-call(bf16[768,256]{1,0:T(8,128)(2,1)S(1)} %bitcast.68, bf16[768,256]{1,0:T(8,128)(2,1)S(1)} %fusion.13.g_ref, ...), custom_call_target="tpu_custom_call" | custom-call | flops 251658240000 | bytes 3883008 | tf_op jit(solution)/shard_map/pallas_call | solution.py:188
  314.0 30.4 %collective-permute-done.10 = bf16[512,256]{1,0:T(8,128)(2,1)S(1)} collective-permute-done((bf16[512,256]{1,0:T(8,128)(2,1)S(1)}, bf16[512,256]{1,0:T(8,128)(2,1)S(1)}, u32[]{:S(2)}, u32[]{:S(2)}) %collective-permute-start.10) | collective-permute-done | bytes 262176 | tf_op jit(solution)/shard_map/ppermute | solution.py:50
  346.6 4.5 collective-permute-done.12
  359.6 7.5 %shard_map.305 = bf16[1536,2176]{1,0:T(8,128)(2,1)} custom-call(bf16[256,1536]{1,0:T(8,128)(2,1)} %copy-done.22, bf16[1280,256]{1,0:T(8,128)(2,1)} %pad_maximum_fusion.qkv_ref, bf16[768,256]{1,0:T(8,128)(2,1)} %copy-done.7, bf16[256,1536]{1,0:T(8,128)(2,1)} %copy-done.23, f32[128,1536]{1,0:T(8,128)} %select_maximum_fusion.extra_ref), custom_call_target="tpu_custom_call" | custom-call | flops 1711276032 | bytes 8257536 | tf_op jit(solution)/shard_map/pallas_call | solution.py:368
  367.1 4.6 reduce-scatter.2.cloned.1.call-done
  375.4 4.8 convolution_convert_fusion.2
  389.2 159.8 %all-reduce.3.cloned.1.call-done.in_ref = bf16[1536,2176]{1,0:T(8,128)(2,1)} async-done(((bf16[1536,2176]{1,0:T(8,128)(2,1)}), bf16[1536,2176]{1,0:T(8,128)(2,1)}) %all-reduce.3.cloned.1.call-update) | async-done | bytes 6684688 | tf_op jit(solution)/shard_map/psum | solution.py:590
  555.6 5.7 %shard_map.306 = (f32[768,1536]{1,0:T(8,128)}, f32[1536,768]{1,0:T(8,128)}, f32[1536,256]{1,0:T(8,128)}, f32[1536,256]{1,0:T(8,128)}, f32[8,1536]{1,0:T(8,128)S(...) custom-call(bf16[1536,2176]{1,0:T(8,128)(2,1)S(1)} %copy-done.4, bf16[1536,768]{1,0:T(8,128)(2,1)S(1)} %copy-done.3, ...), custom_call_target="tpu_custom_call" | custom-call | flops 3342336 | bytes 26738688 | tf_op jit(solution)/shard_map/pallas_call | solution.py:408
  (226 shorter events, 97.7 us)
Async XLA Ops:
  7.2 105.8 %all-gather.3.cloned.1.call-start = ((), (), s32[]{:S(2)}) async-start(), calls=%async_computation.7 | async-start | bytes 11796480 | tf_op jit(solution)/shard_map/all_gather | solution.py:485
  20.2 22.9 %collective-permute-start = (bf16[528,256]{1,0:T(8,128)(2,1)S(1)}, bf16[528,256]{1,0:T(8,128)(2,1)S(1)}, u32[]{:S(2)}, u32[]{:S(2)}) collective-permute-start(bf16[528,256]{1,0:T(8,128)(2,1)S(1)} %concatenate.25.k0), channel_id=1, source_target_pairs={{0,8},{2,10},{4,12},{6,14},{8,16},{10,18},{12,20},{14,22},{16,24},... | collective-permute-start | bytes 811016 | tf_op jit(solution)/shard_map/ppermute | solution.py:50
  24.1 18.9 %collective-permute-start.1 = (bf16[528,256]{1,0:T(8,128)(2,1)S(1)}, bf16[528,256]{1,0:T(8,128)(2,1)S(1)}, u32[]{:S(2)}, u32[]{:S(2)}) collective-permute-start(bf16[528,256]{1,0:T(8,128)(2,1)S(1)} %concatenate.25.k0), channel_id=1, source_target_pairs={{0,6},{2,8},{4,10},{6,12},{8,14},{10,16},{12,18},{14,20},{16,22},{... | collective-permute-start | bytes 811016 | tf_op jit(solution)/shard_map/ppermute | solution.py:50
  29.8 13.3 %collective-permute-start.2 = (bf16[528,256]{1,0:T(8,128)(2,1)S(1)}, bf16[528,256]{1,0:T(8,128)(2,1)}, u32[]{:S(2)}, u32[]{:S(2)}) collective-permute-start(bf16[528,256]{1,0:T(8,128)(2,1)S(1)} %concatenate.25.k0), channel_id=1, source_target_pairs={{0,4},{2,6},{4,8},{6,10},{8,12},{10,14},{12,16},{14,18},{16,20},{1... | collective-permute-start | bytes 811016 | tf_op jit(solution)/shard_map/ppermute | solution.py:50
  33.0 10.1 %collective-permute-start.3 = (bf16[528,256]{1,0:T(8,128)(2,1)S(1)}, bf16[528,256]{1,0:T(8,128)(2,1)}, u32[]{:S(2)}, u32[]{:S(2)}) collective-permute-start(bf16[528,256]{1,0:T(8,128)(2,1)S(1)} %concatenate.25.k0), channel_id=1, source_target_pairs={{0,2},{2,4},{4,6},{6,8},{8,10},{10,12},{12,14},{14,16},{16,18},{18... | collective-permute-start | bytes 811016 | tf_op jit(solution)/shard_map/ppermute | solution.py:50
  36.7 193.7 %copy-start.47 = (f32[32]{0:T(128)}, f32[32]{0:T(128)S(1)}, u32[]{:S(2)}) copy-start(f32[32]{0:T(128)S(1)} %add_convert_fusion.4) | copy-start | bytes 388
  37.3 193.0 %copy-start.31 = (f32[48,256]{1,0:T(8,128)}, f32[48,256]{1,0:T(8,128)S(1)}, u32[]{:S(2)}) copy-start(f32[48,256]{1,0:T(8,128)S(1)} %convolution_select_fusion) | copy-start | bytes 147460
  43.8 69.2 %all-to-all-start = ((bf16[16,96,1536]{2,1,0:T(8,128)(2,1)}), bf16[16,96,1536]{2,1,0:T(8,128)(2,1)}, u32[]{:S(2)}, u32[]{:S(2)}) async-start(bf16[16,96,1536]{2,1,0:T(8,128)(2,1)} %bitcast.70), calls=%async_computation | async-start | bytes 9437184 | tf_op jit(solution)/shard_map/all_to_all | solution.py:509
  74.8 4.9 collective-permute-start.4
  113.0 73.6 %collective-permute-start.5 = (bf16[4,1536,768]{2,1,0:T(8,128)(2,1)}, bf16[4,1536,768]{2,1,0:T(8,128)(2,1)}, u32[]{:S(2)}, u32[]{:S(2)}) collective-permute-start(bf16[4,1536,768]{2,1,0:T(8,128)(2,1)} %bitcast.84), channel_id=1, source_target_pairs={{0,1},{1,0},{2,3},{3,2},{4,5},{5,4},{6,7},{7,6},{8,9},{9,8},{10,11... | collective-permute-start | bytes 28311560 | tf_op jit(solution)/shard_map/ppermute | solution.py:40
  204.7 62.0 %all-to-all-start.2 = ((bf16[16,96,1536]{2,1,0:T(8,128)(2,1)}), bf16[16,96,1536]{2,1,0:T(8,128)(2,1)}, u32[]{:S(2)}, u32[]{:S(2)}) async-start(bf16[16,96,1536]{2,1,0:T(8,128)(2,1)} %get-tuple-element.60), calls=%async_computation.2 | async-start | bytes 9437184 | tf_op jit(solution)/shard_map/all_to_all | solution.py:509
  209.3 162.5 %reduce-scatter.2.cloned.1.call-start = ((), (), s32[]{:S(2)}) async-start(), calls=%async_computation.5 | async-start | bytes 11796480 | tf_op jit(solution)/shard_map/reduce_scatter | solution.py:550
  227.6 6.8 %collective-permute-start.6 = (bf16[3,1536,256]{2,1,0:T(8,128)(2,1)}, bf16[3,1536,256]{2,1,0:T(8,128)(2,1)}, u32[]{:S(2)}, u32[]{:S(2)}) collective-permute-start(bf16[3,1536,256]{2,1,0:T(8,128)(2,1)} %get-tuple-element.64), channel_id=1, source_target_pairs={{0,1},{1,0},{2,3},{3,2},{4,5},{5,4},{6,7},{7,6},{8,9},{9,8},{10,11... | collective-permute-start | bytes 7077896 | tf_op jit(solution)/shard_map/ppermute | solution.py:40
  229.9 7.9 %collective-permute-start.7 = (bf16[3,1536,256]{2,1,0:T(8,128)(2,1)}, bf16[3,1536,256]{2,1,0:T(8,128)(2,1)}, u32[]{:S(2)}, u32[]{:S(2)}) collective-permute-start(bf16[3,1536,256]{2,1,0:T(8,128)(2,1)} %get-tuple-element.65), channel_id=1, source_target_pairs={{0,1},{1,0},{2,3},{3,2},{4,5},{5,4},{6,7},{7,6},{8,9},{9,8},{10,11... | collective-permute-start | bytes 7077896 | tf_op jit(solution)/shard_map/ppermute | solution.py:40
  229.9 11.2 %collective-permute-start.8 = (bf16[3,1536,256]{2,1,0:T(8,128)(2,1)}, bf16[3,1536,256]{2,1,0:T(8,128)(2,1)}, u32[]{:S(2)}, u32[]{:S(2)}) collective-permute-start(bf16[3,1536,256]{2,1,0:T(8,128)(2,1)} %get-tuple-element.66), channel_id=1, source_target_pairs={{0,1},{1,0},{2,3},{3,2},{4,5},{5,4},{6,7},{7,6},{8,9},{9,8},{10,11... | collective-permute-start | bytes 7077896 | tf_op jit(solution)/shard_map/ppermute | solution.py:40
  271.4 13.1 %collective-permute-start.9 = (bf16[256,1536]{1,0:T(8,128)(2,1)}, bf16[256,1536]{1,0:T(8,128)(2,1)}, u32[]{:S(2)}, u32[]{:S(2)}) collective-permute-start(bf16[256,1536]{1,0:T(8,128)(2,1)} %convolution_convert_fusion.1), channel_id=1, source_target_pairs={{0,1},{1,0},{2,3},{3,2},{4,5},{5,4},{6,7},{7,6},{8,9},{9,8},{10,11... | collective-permute-start | bytes 2359304 | tf_op jit(solution)/shard_map/ppermute | solution.py:40
  277.9 89.3 %all-to-all-start.3 = ((bf16[16,96,1536]{2,1,0:T(8,128)(2,1)}), bf16[16,96,1536]{2,1,0:T(8,128)(2,1)}, u32[]{:S(2)}, u32[]{:S(2)}) async-start(bf16[16,96,1536]{2,1,0:T(8,128)(2,1)} %get-tuple-element.77), calls=%async_computation.4 | async-start | bytes 9437184 | tf_op jit(solution)/shard_map/all_to_all | solution.py:509
  284.2 264.8 %all-reduce.3.cloned.1.call-start = ((), (), s32[]{:S(2)}) async-start(), calls=%async_computation.6 | async-start | bytes 13369344 | tf_op jit(solution)/shard_map/psum | solution.py:590
  307.9 36.5 %collective-permute-start.10 = (bf16[512,256]{1,0:T(8,128)(2,1)S(1)}, bf16[512,256]{1,0:T(8,128)(2,1)S(1)}, u32[]{:S(2)}, u32[]{:S(2)}) collective-permute-start(bf16[512,256]{1,0:T(8,128)(2,1)S(1)} %get-tuple-element.71), channel_id=1, source_target_pairs={{8,0},{10,2},{12,4},{14,6},{16,8},{18,10},{20,12},{22,14},{24,16},... | collective-permute-start | bytes 786440 | tf_op jit(solution)/shard_map/ppermute | solution.py:50
  309.2 37.3 %collective-permute-start.11 = (bf16[512,256]{1,0:T(8,128)(2,1)S(1)}, bf16[512,256]{1,0:T(8,128)(2,1)S(1)}, u32[]{:S(2)}, u32[]{:S(2)}) collective-permute-start(bf16[512,256]{1,0:T(8,128)(2,1)S(1)} %get-tuple-element.72), channel_id=1, source_target_pairs={{6,0},{8,2},{10,4},{12,6},{14,8},{16,10},{18,12},{20,14},{22,16},{... | collective-permute-start | bytes 786440 | tf_op jit(solution)/shard_map/ppermute | solution.py:50
  310.5 40.5 %collective-permute-start.12 = (bf16[512,256]{1,0:T(8,128)(2,1)S(1)}, bf16[512,256]{1,0:T(8,128)(2,1)S(1)}, u32[]{:S(2)}, u32[]{:S(2)}) collective-permute-start(bf16[512,256]{1,0:T(8,128)(2,1)S(1)} %get-tuple-element.73), channel_id=1, source_target_pairs={{4,0},{6,2},{8,4},{10,6},{12,8},{14,10},{16,12},{18,14},{20,16},{2... | collective-permute-start | bytes 786440 | tf_op jit(solution)/shard_map/ppermute | solution.py:50
  311.8 39.2 %collective-permute-start.13 = (bf16[512,256]{1,0:T(8,128)(2,1)S(1)}, bf16[512,256]{1,0:T(8,128)(2,1)S(1)}, u32[]{:S(2)}, u32[]{:S(2)}) collective-permute-start(bf16[512,256]{1,0:T(8,128)(2,1)S(1)} %get-tuple-element.74), channel_id=1, source_target_pairs={{2,0},{4,2},{6,4},{8,6},{10,8},{12,10},{14,12},{16,14},{18,16},{20... | collective-permute-start | bytes 786440 | tf_op jit(solution)/shard_map/ppermute | solution.py:50
  354.0 2.9 collective-permute-start.14
  380.2 6.4 %collective-permute-start.15 = (bf16[256,1536]{1,0:T(8,128)(2,1)}, bf16[256,1536]{1,0:T(8,128)(2,1)}, u32[]{:S(2)}, u32[]{:S(2)}) collective-permute-start(bf16[256,1536]{1,0:T(8,128)(2,1)} %convolution_convert_fusion.2), channel_id=1, source_target_pairs={{0,1},{1,0},{2,3},{3,2},{4,5},{5,4},{6,7},{7,6},{8,9},{9,8},{10,11... | collective-permute-start | bytes 2359304 | tf_op jit(solution)/shard_map/ppermute | solution.py:40
  (54 other events, 594.6 us)
Sparse Core Ops, SparseCore 0:
  12.8 95.6 all-gather.2
  278.0 93.7 reduce-scatter.1
  376.7 172.2 all-reduce.2

commit v5 on v4

--- a/solution.py
+++ b/solution.py
@@ -16,6 +16,7 @@
 RANK_ROWS = 32
 PLANE = 16
 SEGMENTS = 3
+EARLY = 2
 AUX = 16
 LANES = 256
 MORE = 128
@@ -195,7 +196,7 @@
         scratch_shapes=[pltpu.VMEM((len(blocks) * tok, tok), F32)],
         compiler_params=pltpu.CompilerParams(vmem_limit_bytes=48 << 20),
         cost_estimate=pl.CostEstimate(
-            flops=1000 * rows * tok * tok * len(blocks),
+            flops=500 * rows * tok * tok * len(blocks),
             bytes_accessed=6 * rows * tok + 4 * len(blocks) * 528 * tok,
             transcendentals=rows // HD * tok * tok * len(blocks),
         ),
@@ -274,7 +275,8 @@
     width = x_ref.shape[-1]
     rows, grads = (x_ref[...].reshape(-1, width), g_ref[...].reshape(-1, width))
     hidden = own_ref.shape[-1]
-    out_ref = outs[-1]
+    early_ref, late_ref = outs[3:]
+    segment = pl.program_id(0)
     out = None
     for side, (acts, weights) in enumerate(((own_acts, own_ref), (peer_acts, peer_ref))):
         first = contract(rows, acts[0, :, : 2 * hidden], TN).astype(BF16)
@@ -288,7 +290,15 @@
             outs[2][0] = second
         part = contract(acts[0, :, 2 * hidden :], weights[0], NT)
         out = part if out is None else out + part
-    out_ref[...] = out.astype(BF16).reshape(out_ref.shape)
+    out = out.astype(BF16).reshape(x_ref.shape)
+
+    @pl.when(segment < EARLY)
+    def _():
+        early_ref[...] = out
+
+    @pl.when(segment >= EARLY)
+    def _():
+        late_ref[...] = out
 
 
 def expert_sums(rows, grads, own_acts, peer_acts, own, peer):
@@ -296,7 +306,8 @@
     segments, triple = (lines // RANK_ROWS, own.shape[-1])
     hidden = triple // 3
     count = sources * RANK_ROWS
-    wide = pl.BlockSpec((sources, RANK_ROWS, width), lambda s: (0, s, 0))
+    block = (sources, RANK_ROWS, width)
+    wide = pl.BlockSpec(block, lambda s: (0, s, 0))
     down = pl.BlockSpec((1, width, hidden), lambda s: (s, 0, 2))
     act = pl.BlockSpec((1, count, triple), lambda s: (s, 0, 0))
     return pl.pallas_call(
@@ -305,10 +316,16 @@
         in_specs=[wide, wide, act, act, down, down],
         out_specs=[pl.BlockSpec((1, width, triple), lambda s: (s, 0, 0))]
         + [pl.BlockSpec((1, width, hidden), lambda s: (s, 0, 0))] * 3
-        + [wide],
+        + [
+            pl.BlockSpec(block, lambda s: (0, jnp.minimum(s, EARLY - 1), 0)),
+            pl.BlockSpec(block, lambda s: (0, jnp.maximum(s - EARLY, 0), 0)),
+        ],
         out_shape=[jax.ShapeDtypeStruct((segments, width, triple), BF16)]
         + [jax.ShapeDtypeStruct((segments, width, hidden), BF16)] * 3
-        + [jax.ShapeDtypeStruct(rows.shape, BF16)],
+        + [
+            jax.ShapeDtypeStruct((sources, EARLY * RANK_ROWS, width), BF16),
+            jax.ShapeDtypeStruct((sources, (segments - EARLY) * RANK_ROWS, width), BF16),
+        ],
         compiler_params=pltpu.CompilerParams(vmem_limit_bytes=60 << 20),
         cost_estimate=pl.CostEstimate(
             flops=6 * sources * lines * width * triple,
@@ -433,7 +450,7 @@
             jax.ShapeDtypeStruct((total, width), BF16),
             jax.ShapeDtypeStruct((total, narrow), BF16),
         ],
-        compiler_params=pltpu.CompilerParams(vmem_limit_bytes=32 << 20),
+        compiler_params=pltpu.CompilerParams(vmem_limit_bytes=60 << 20),
         cost_estimate=pl.CostEstimate(
             flops=total * every, bytes_accessed=8 * total * every, transcendentals=0
         ),
@@ -481,8 +498,6 @@
     plane_groups = [list(range(at, at + PLANE)) for at in range(0, dp_size, PLANE)]
     column_groups = [list(range(at, dp_size, PLANE)) for at in range(PLANE)]
 
-    packed_w = pack_weights(w_gate[0], w_up[0], w_down[0])
-    own = lax.all_gather(packed_w, "dp", axis=0, axis_index_groups=column_groups)
 
     picks = route_ids.T
     logits = route_logits.T
@@ -524,6 +539,8 @@
     block = jnp.concatenate([key, value, side])
     blocks = tuple(passed_along(block, hop) for hop in range(HOPS, 0, -1)) + (block,)
     blocks, grad_rows = lax.optimization_barrier((blocks, grad_rows))
+    packed_w = pack_weights(w_gate[0], w_up[0], w_down[0])
+    own = lax.all_gather(packed_w, "dp", axis=0, axis_index_groups=column_groups)
     grad_rows = in_plane(grad_rows)
     attended, log_total, peaks = attend(query, blocks, group)
     attn_part = contract(attended, w_out, TN)
@@ -542,10 +559,10 @@
         part = contract(weights, rows.reshape(-1, model_width), TN).astype(BF16)
         return part.astype(F32) + swapped(part).astype(F32)
 
-    sum_own, *sum_peer, expert_out = expert_sums(rows_in, grad_rows, own_acts, peer_acts, own, peer)
+    sum_own, *sum_peer, out_early, out_late = expert_sums(rows_in, grad_rows, own_acts, peer_acts, own, peer)
     sums = both_cores(sum_own, [swapped(part) for part in sum_peer], dp_size // PLANE)
     back = in_plane(back)
-    expert_out = in_plane(after(expert_out, back))
+    out_early = in_plane(after(out_early, back))
     grad_normed2 = combined(pick, after(back, sums))
     sums = lax.psum_scatter(
         sums, "dp", scatter_dimension=0, tiled=True, axis_index_groups=column_groups
@@ -562,6 +579,7 @@
     returned = [
         passed_along(grad_blocks[number], -hop) for number, hop in enumerate(range(HOPS, 0, -1))
     ]
+    out_late = in_plane(after(out_late, (returned, out_early)))
     kv_total = grad_blocks[-1]
     for part in returned:
         kv_total = kv_total + part.astype(F32)
@@ -586,8 +604,9 @@
     extra = jnp.pad(extra, ((0, MORE - len(extra)), (0, 0)))
     grad_qkv = jnp.concatenate([grad_query_pre, grad_key_pre, grad_value])
     parts = weight_grads(normed1, grad_qkv, attended, grad_branch, extra)
-    parts, sums, expert_out = lax.optimization_barrier((parts, sums, expert_out))
+    parts, sums, out_early, out_late = lax.optimization_barrier((parts, sums, out_early, out_late))
     summed = lax.psum(parts, "dp")
+    expert_out = jnp.concatenate([out_early, out_late], axis=1)
     output = (hidden1 + combined(gated, expert_out)).astype(BF16)
     grad_gate, grad_up, grad_down = jnp.split(sums[0].astype(F32), 3, axis=1)
     grad_down = grad_down.T

time: 570 us -> 561 us (0.984)
  waiting for transfers between devices: 256 us -> 224 us
  starting transfers between devices: 60.5 us -> 86.9 us
    all_to_all x3 -> x4, starting transfers between devices: 22.4 us -> 48.1 us  [in_plane(): lax.all_to_all(rows, 'dp', 0, 0, tiled=True, axis_index_groups=plane_groups)]
    psum x1, waiting for transfers between devices: 160 us -> 135 us  [shards(): summed = lax.psum(parts, 'dp')]
    ppermute x8, waiting for transfers between devices: 37.1 us -> 22.6 us  [passed_along(): lax.ppermute(value, 'dp', [(s, s + steps) for s in range(first, last)])]
    all_to_all x3 -> x4, waiting for transfers between devices: 41.8 us -> 51.9 us  [in_plane(): lax.all_to_all(rows, 'dp', 0, 0, tiled=True, axis_index_groups=plane_groups)]
    unnamed x113 -> x83, local copies, waits for them, and re-layouts: 13.7 us -> 9.15 us
  transfers between devices with their start and end apart: 22 -> 23, of which waited for: 11 -> 10; matrix products, arithmetic and copies ran while one was open for 10% -> 10% of each run, Pallas kernels for 11% -> 12%
where the time goes in v5:
time: 561 us; the launch traced here: 560 us
  waiting for transfers between devices  224 us (40%)
  Pallas kernels  99 us (18%)
  starting transfers between devices  86.9 us (15%)
  blocking collectives  69 us (12%)
  other arithmetic  24.7 us (4%)
  matrix products  22.7 us (4%)
  local copies, waits for them, and re-layouts  19.1 us (3%)
  between operations  14.6 us (3%)
    psum x1, waiting for transfers between devices, shards(): summed = lax.psum(parts, 'dp')  135 us
    all_to_all x1, blocking collectives, in_plane(): lax.all_to_all(rows, 'dp', 0, 0, tiled=True, axis_index_groups=plane_groups)  69 us
    all_to_all x4, waiting for transfers between devices, in_plane(): lax.all_to_all(rows, 'dp', 0, 0, tiled=True, axis_index_groups=plane_groups)  51.9 us
    all_to_all x4, starting transfers between devices, in_plane(): lax.all_to_all(rows, 'dp', 0, 0, tiled=True, axis_index_groups=plane_groups)  48.1 us
    dot_general x13, matrix products, contract(): lax.dot_general(left, right, (dims, ((), ())), preferred_element_type=F32)  22.7 us
    ppermute x8, waiting for transfers between devices, passed_along(): lax.ppermute(value, 'dp', [(s, s + steps) for s in range(first, last)])  22.6 us
    ppermute x8, starting transfers between devices, passed_along(): lax.ppermute(value, 'dp', [(s, s + steps) for s in range(first, last)])  21.6 us
    pallas_call x1, Pallas kernels, expert_sums(): pl.pallas_call(expert_sums_kernel, grid=(segments,), in_specs=[wide, wide...  19.3 us
  transfers between devices with their start and end apart: 23, of which 10 were waited for; matrix products, arithmetic and copies ran while one was open for 10% of the time, Pallas kernels for 12%

profile of v5, /device:TPU:1, one launch (start us, length us, event | category | flops | bytes accessed | tf_op | source)
XLA Modules:
  0.0 559.6 jit_solution(5509815497125434893)
XLA Ops:
  7.2 5.4 shard_map.300
  21.9 5.7 %collective-permute-start.1 = (bf16[528,256]{1,0:T(8,128)(2,1)S(1)}, bf16[528,256]{1,0:T(8,128)(2,1)S(1)}, u32[]{:S(2)}, u32[]{:S(2)}) collective-permute-start(bf16[528,256]{1,0:T(8,128)(2,1)S(1)} %concatenate.28.k0), channel_id=1, source_target_pairs={{0,6},{2,8},{4,10},{6,12},{8,14},{10,16},{12,18},{14,20},{16,22},{... | collective-permute-start | bytes 811016 | tf_op jit(solution)/shard_map/ppermute | solution.py:51
  35.9 4.9 fusion
  41.5 11.7 %all-to-all-start = ((bf16[16,96,1536]{2,1,0:T(8,128)(2,1)}), bf16[16,96,1536]{2,1,0:T(8,128)(2,1)}, u32[]{:S(2)}, u32[]{:S(2)}) async-start(bf16[16,96,1536]{2,1,0:T(8,128)(2,1)} %bitcast.70), calls=%async_computation | async-start | bytes 9437184 | tf_op jit(solution)/shard_map/all_to_all | solution.py:524
  60.5 11.3 %shard_map.299 = (bf16[768,256]{1,0:T(8,128)(2,1)S(1)}, f32[12,256]{1,0:T(8,128)S(1)}, f32[12,256]{1,0:T(8,128)S(1)}) custom-call(bf16[768,256]{1,0:T(8,128)(2,1)S(1)} %bitcast.67, bf16[528,256]{1,0:T(8,128)(2,1)S(1)} %collective-permute-done.k4, bf16[528,256]{1,0:T(8,128)(2,1)S(1)} %copy-done.4, bf16[528,256]{1,0:T(8,128)(2,1)} %collective-permute-done.2.k2, ...), custom_call_target="tpu_custom_call" | custom-call | flops 1006632960 | bytes 2138112 | tf_op jit(solution)/shard_map/pallas_call | solution.py:126
  82.7 28.1 %all-to-all-done.g_ref = bf16[16,96,1536]{2,1,0:T(8,128)(2,1)} async-done(((bf16[16,96,1536]{2,1,0:T(8,128)(2,1)}), bf16[16,96,1536]{2,1,0:T(8,128)(2,1)}, u32[]{:S(2)}, u32[]{:S(2)}) %all-to-all-start) | async-done | bytes 4718624 | tf_op jit(solution)/shard_map/all_to_all | solution.py:524
  110.8 4.6 collective-permute-start.5
  115.4 69.0 %all_to_all.25.x_ref = bf16[16,96,1536]{2,1,0:T(8,128)(2,1)} all-to-all(bf16[16,96,1536]{2,1,0:T(8,128)(2,1)} %bitcast.69), channel_id=1, replica_groups={{0,2,4,6,8,10,12,14,16,18,20,22,24,26,28,30},{32,34,36,38,40,42,44,46,4..., dimensions={0} | all-to-all | bytes 9437184 | tf_op jit(solution)/shard_map/all_to_all | solution.py:524
  184.5 18.0 %shard_map.301 = (bf16[16,96,1536]{2,1,0:T(8,128)(2,1)}, bf16[3,512,768]{2,1,0:T(8,128)(2,1)}, bf16[3,512,768]{2,1,0:T(8,128)(2,1)}) custom-call(bf16[16,96,1536]{2,1,0:T(8,128)(2,1)} %all_to_all.25.x_ref, bf16[16,96,1536]{2,1,0:T(8,128)(2,1)} %all-to-all-done.g_ref, bf16[4,1536,768]{2,1,0:T(8,128)(2,1)} %bitcast.86, ...), custom_call_target="tpu_custom_call" | custom-call | flops 12683575296 | bytes 28311552 | tf_op jit(solution)/shard_map/pallas_call | solution.py:255
  202.5 4.6 all-to-all-start.2
  207.1 19.3 %shard_map.302 = (bf16[3,1536,768]{2,1,0:T(8,128)(2,1)}, bf16[3,1536,256]{2,1,0:T(8,128)(2,1)}, bf16[3,1536,256]{2,1,0:T(8,128)(2,1)}, bf16[3,1536,256]{2,1,0:T(...) custom-call(bf16[16,96,1536]{2,1,0:T(8,128)(2,1)} %all_to_all.25.x_ref, ...), custom_call_target="tpu_custom_call" | custom-call | flops 10871635968 | bytes 31850496 | tf_op jit(solution)/shard_map/pallas_call | solution.py:313
  240.1 11.9 %shard_map.303 = bf16[4,1536,768]{2,1,0:T(8,128)(2,1)} custom-call(bf16[3,1536,768]{2,1,0:T(8,128)(2,1)} %get-tuple-element.66.own_ref, bf16[3,1536,256]{2,1,0:T(8,128)(2,1)} %collective-permute-done.6.refs_0_, bf16[3,1536,256]{2,1,0:T(8,128)(2,1)} %collective-permute-done.7.refs_1_, bf16[3,1536,256]{2,1,0:T(8,128)(2,1)} %collective-permute-done.8.refs_2_), custom_call_target="tpu_custom_call" | custom-call | flops 4718592 | bytes 28311552 | tf_op jit(solution)/shard_map/pallas_call | solution.py:360
  253.0 11.5 %all-to-all-done.2 = bf16[16,96,1536]{2,1,0:T(8,128)(2,1)} async-done(((bf16[16,96,1536]{2,1,0:T(8,128)(2,1)}), bf16[16,96,1536]{2,1,0:T(8,128)(2,1)}, u32[]{:S(2)}, u32[]{:S(2)}) %all-to-all-start.2) | async-done | bytes 4718624 | tf_op jit(solution)/shard_map/all_to_all | solution.py:524
  264.6 4.9 convolution_convert_fusion.1
  269.5 5.2 collective-permute-start.9
  274.8 6.1 %all-to-all-start.3 = ((bf16[16,64,1536]{2,1,0:T(8,128)(2,1)}), bf16[16,64,1536]{2,1,0:T(8,128)(2,1)}, u32[]{:S(2)}, u32[]{:S(2)}) async-start(bf16[16,64,1536]{2,1,0:T(8,128)(2,1)} %get-tuple-element.80), calls=%async_computation.4 | async-start | bytes 6291456 | tf_op jit(solution)/shard_map/all_to_all | solution.py:524
  287.8 15.6 %shard_map.304 = (bf16[768,256]{1,0:T(8,128)(2,1)S(1)}, bf16[512,256]{1,0:T(8,128)(2,1)S(1)}, bf16[512,256]{1,0:T(8,128)(2,1)S(1)}, bf16[512,256]{1,0:T(8,128)(2...) custom-call(bf16[768,256]{1,0:T(8,128)(2,1)S(1)} %bitcast.68, bf16[768,256]{1,0:T(8,128)(2,1)S(1)} %fusion.13.g_ref, ...), custom_call_target="tpu_custom_call" | custom-call | flops 125829120000 | bytes 3883008 | tf_op jit(solution)/shard_map/pallas_call | solution.py:189
  309.5 13.3 %collective-permute-done.10 = bf16[512,256]{1,0:T(8,128)(2,1)S(1)} collective-permute-done((bf16[512,256]{1,0:T(8,128)(2,1)S(1)}, bf16[512,256]{1,0:T(8,128)(2,1)S(1)}, u32[]{:S(2)}, u32[]{:S(2)}) %collective-permute-start.10) | collective-permute-done | bytes 262176 | tf_op jit(solution)/shard_map/ppermute | solution.py:51
  322.8 9.3 %collective-permute-done.11 = bf16[512,256]{1,0:T(8,128)(2,1)S(1)} collective-permute-done((bf16[512,256]{1,0:T(8,128)(2,1)S(1)}, bf16[512,256]{1,0:T(8,128)(2,1)S(1)}, u32[]{:S(2)}, u32[]{:S(2)}) %collective-permute-start.11) | collective-permute-done | bytes 262176 | tf_op jit(solution)/shard_map/ppermute | solution.py:51
  335.4 25.8 %all-to-all-start.4 = ((bf16[16,32,1536]{2,1,0:T(8,128)(2,1)}), bf16[16,32,1536]{2,1,0:T(8,128)(2,1)}, u32[]{:S(2)}, u32[]{:S(2)}) async-start(bf16[16,32,1536]{2,1,0:T(8,128)(2,1)} %get-tuple-element.82), calls=%async_computation.5 | async-start | bytes 3145728 | tf_op jit(solution)/shard_map/all_to_all | solution.py:524
  365.2 7.4 %shard_map.305 = bf16[1536,2176]{1,0:T(8,128)(2,1)} custom-call(bf16[256,1536]{1,0:T(8,128)(2,1)} %copy-done.12, bf16[1280,256]{1,0:T(8,128)(2,1)} %pad_maximum_fusion.1.qkv_ref, bf16[768,256]{1,0:T(8,128)(2,1)} %copy-done.2, bf16[256,1536]{1,0:T(8,128)(2,1)} %copy-done.16, f32[128,1536]{1,0:T(8,128)} %select_maximum_fusion.extra_ref), custom_call_target="tpu_custom_call" | custom-call | flops 1711276032 | bytes 8257536 | tf_op jit(solution)/shard_map/pallas_call | solution.py:385
  372.6 12.3 %all-to-all-done.4 = bf16[16,32,1536]{2,1,0:T(8,128)(2,1)} async-done(((bf16[16,32,1536]{2,1,0:T(8,128)(2,1)}), bf16[16,32,1536]{2,1,0:T(8,128)(2,1)}, u32[]{:S(2)}, u32[]{:S(2)}) %all-to-all-start.4) | async-done | bytes 1572896 | tf_op jit(solution)/shard_map/all_to_all | solution.py:524
  403.0 135.3 %all-reduce.3.cloned.1.call-done.in_ref = bf16[1536,2176]{1,0:T(8,128)(2,1)} async-done(((bf16[1536,2176]{1,0:T(8,128)(2,1)}), bf16[1536,2176]{1,0:T(8,128)(2,1)}) %all-reduce.3.cloned.1.call-update) | async-done | bytes 6684688 | tf_op jit(solution)/shard_map/psum | solution.py:608
  541.5 10.0 %shard_map.306 = (f32[768,1536]{1,0:T(8,128)}, f32[1536,768]{1,0:T(8,128)}, f32[1536,256]{1,0:T(8,128)}, f32[1536,256]{1,0:T(8,128)}, f32[8,1536]{1,0:T(8,128)},...) custom-call(bf16[1536,2176]{1,0:T(8,128)(2,1)} %all-reduce.3.cloned.1.call-done.in_ref, ...), custom_call_target="tpu_custom_call" | custom-call | flops 3342336 | bytes 26738688 | tf_op jit(solution)/shard_map/pallas_call | solution.py:425
  (199 shorter events, 93.8 us)
Async XLA Ops:
  7.2 103.6 %all-gather.3.cloned.1.call-start = ((), (), s32[]{:S(2)}) async-start(), calls=%async_computation.8 | async-start | bytes 11796480 | tf_op jit(solution)/shard_map/all_gather | solution.py:543
  18.0 22.8 %collective-permute-start = (bf16[528,256]{1,0:T(8,128)(2,1)S(1)}, bf16[528,256]{1,0:T(8,128)(2,1)S(1)}, u32[]{:S(2)}, u32[]{:S(2)}) collective-permute-start(bf16[528,256]{1,0:T(8,128)(2,1)S(1)} %concatenate.28.k0), channel_id=1, source_target_pairs={{0,8},{2,10},{4,12},{6,14},{8,16},{10,18},{12,20},{14,22},{16,24},... | collective-permute-start | bytes 811016 | tf_op jit(solution)/shard_map/ppermute | solution.py:51
  21.9 18.9 %collective-permute-start.1 = (bf16[528,256]{1,0:T(8,128)(2,1)S(1)}, bf16[528,256]{1,0:T(8,128)(2,1)S(1)}, u32[]{:S(2)}, u32[]{:S(2)}) collective-permute-start(bf16[528,256]{1,0:T(8,128)(2,1)S(1)} %concatenate.28.k0), channel_id=1, source_target_pairs={{0,6},{2,8},{4,10},{6,12},{8,14},{10,16},{12,18},{14,20},{16,22},{... | collective-permute-start | bytes 811016 | tf_op jit(solution)/shard_map/ppermute | solution.py:51
  27.6 13.2 %collective-permute-start.2 = (bf16[528,256]{1,0:T(8,128)(2,1)S(1)}, bf16[528,256]{1,0:T(8,128)(2,1)}, u32[]{:S(2)}, u32[]{:S(2)}) collective-permute-start(bf16[528,256]{1,0:T(8,128)(2,1)S(1)} %concatenate.28.k0), channel_id=1, source_target_pairs={{0,4},{2,6},{4,8},{6,10},{8,12},{10,14},{12,16},{14,18},{16,20},{1... | collective-permute-start | bytes 811016 | tf_op jit(solution)/shard_map/ppermute | solution.py:51
  30.8 10.0 %collective-permute-start.3 = (bf16[528,256]{1,0:T(8,128)(2,1)S(1)}, bf16[528,256]{1,0:T(8,128)(2,1)}, u32[]{:S(2)}, u32[]{:S(2)}) collective-permute-start(bf16[528,256]{1,0:T(8,128)(2,1)S(1)} %concatenate.28.k0), channel_id=1, source_target_pairs={{0,2},{2,4},{4,6},{6,8},{8,10},{10,12},{12,14},{14,16},{16,18},{18... | collective-permute-start | bytes 811016 | tf_op jit(solution)/shard_map/ppermute | solution.py:51
  41.5 69.3 %all-to-all-start = ((bf16[16,96,1536]{2,1,0:T(8,128)(2,1)}), bf16[16,96,1536]{2,1,0:T(8,128)(2,1)}, u32[]{:S(2)}, u32[]{:S(2)}) async-start(bf16[16,96,1536]{2,1,0:T(8,128)(2,1)} %bitcast.70), calls=%async_computation | async-start | bytes 9437184 | tf_op jit(solution)/shard_map/all_to_all | solution.py:524
  72.7 4.9 collective-permute-start.4
  110.8 73.6 %collective-permute-start.5 = (bf16[4,1536,768]{2,1,0:T(8,128)(2,1)}, bf16[4,1536,768]{2,1,0:T(8,128)(2,1)}, u32[]{:S(2)}, u32[]{:S(2)}) collective-permute-start(bf16[4,1536,768]{2,1,0:T(8,128)(2,1)} %bitcast.85), channel_id=1, source_target_pairs={{0,1},{1,0},{2,3},{3,2},{4,5},{5,4},{6,7},{7,6},{8,9},{9,8},{10,11... | collective-permute-start | bytes 28311560 | tf_op jit(solution)/shard_map/ppermute | solution.py:41
  202.5 62.0 %all-to-all-start.2 = ((bf16[16,96,1536]{2,1,0:T(8,128)(2,1)}), bf16[16,96,1536]{2,1,0:T(8,128)(2,1)}, u32[]{:S(2)}, u32[]{:S(2)}) async-start(bf16[16,96,1536]{2,1,0:T(8,128)(2,1)} %get-tuple-element.63), calls=%async_computation.2 | async-start | bytes 9437184 | tf_op jit(solution)/shard_map/all_to_all | solution.py:524
  207.1 177.8 %reduce-scatter.2.cloned.1.call-start = ((), (), s32[]{:S(2)}) async-start(), calls=%async_computation.6 | async-start | bytes 11796480 | tf_op jit(solution)/shard_map/reduce_scatter | solution.py:567
  226.5 6.9 %collective-permute-start.6 = (bf16[3,1536,256]{2,1,0:T(8,128)(2,1)}, bf16[3,1536,256]{2,1,0:T(8,128)(2,1)}, u32[]{:S(2)}, u32[]{:S(2)}) collective-permute-start(bf16[3,1536,256]{2,1,0:T(8,128)(2,1)} %get-tuple-element.67), channel_id=1, source_target_pairs={{0,1},{1,0},{2,3},{3,2},{4,5},{5,4},{6,7},{7,6},{8,9},{9,8},{10,11... | collective-permute-start | bytes 7077896 | tf_op jit(solution)/shard_map/ppermute | solution.py:41
  228.8 7.9 %collective-permute-start.7 = (bf16[3,1536,256]{2,1,0:T(8,128)(2,1)}, bf16[3,1536,256]{2,1,0:T(8,128)(2,1)}, u32[]{:S(2)}, u32[]{:S(2)}) collective-permute-start(bf16[3,1536,256]{2,1,0:T(8,128)(2,1)} %get-tuple-element.68), channel_id=1, source_target_pairs={{0,1},{1,0},{2,3},{3,2},{4,5},{5,4},{6,7},{7,6},{8,9},{9,8},{10,11... | collective-permute-start | bytes 7077896 | tf_op jit(solution)/shard_map/ppermute | solution.py:41
  228.9 11.2 %collective-permute-start.8 = (bf16[3,1536,256]{2,1,0:T(8,128)(2,1)}, bf16[3,1536,256]{2,1,0:T(8,128)(2,1)}, u32[]{:S(2)}, u32[]{:S(2)}) collective-permute-start(bf16[3,1536,256]{2,1,0:T(8,128)(2,1)} %get-tuple-element.69), channel_id=1, source_target_pairs={{0,1},{1,0},{2,3},{3,2},{4,5},{5,4},{6,7},{7,6},{8,9},{9,8},{10,11... | collective-permute-start | bytes 7077896 | tf_op jit(solution)/shard_map/ppermute | solution.py:41
  269.5 11.5 %collective-permute-start.9 = (bf16[256,1536]{1,0:T(8,128)(2,1)}, bf16[256,1536]{1,0:T(8,128)(2,1)}, u32[]{:S(2)}, u32[]{:S(2)}) collective-permute-start(bf16[256,1536]{1,0:T(8,128)(2,1)} %convolution_convert_fusion.1), channel_id=1, source_target_pairs={{0,1},{1,0},{2,3},{3,2},{4,5},{5,4},{6,7},{7,6},{8,9},{9,8},{10,11... | collective-permute-start | bytes 2359304 | tf_op jit(solution)/shard_map/ppermute | solution.py:41
  274.8 60.6 %all-to-all-start.3 = ((bf16[16,64,1536]{2,1,0:T(8,128)(2,1)}), bf16[16,64,1536]{2,1,0:T(8,128)(2,1)}, u32[]{:S(2)}, u32[]{:S(2)}) async-start(bf16[16,64,1536]{2,1,0:T(8,128)(2,1)} %get-tuple-element.80), calls=%async_computation.4 | async-start | bytes 6291456 | tf_op jit(solution)/shard_map/all_to_all | solution.py:524
  303.5 19.3 %collective-permute-start.10 = (bf16[512,256]{1,0:T(8,128)(2,1)S(1)}, bf16[512,256]{1,0:T(8,128)(2,1)S(1)}, u32[]{:S(2)}, u32[]{:S(2)}) collective-permute-start(bf16[512,256]{1,0:T(8,128)(2,1)S(1)} %get-tuple-element.74), channel_id=1, source_target_pairs={{8,0},{10,2},{12,4},{14,6},{16,8},{18,10},{20,12},{22,14},{24,16},... | collective-permute-start | bytes 786440 | tf_op jit(solution)/shard_map/ppermute | solution.py:51
  304.8 27.3 %collective-permute-start.11 = (bf16[512,256]{1,0:T(8,128)(2,1)S(1)}, bf16[512,256]{1,0:T(8,128)(2,1)S(1)}, u32[]{:S(2)}, u32[]{:S(2)}) collective-permute-start(bf16[512,256]{1,0:T(8,128)(2,1)S(1)} %get-tuple-element.75), channel_id=1, source_target_pairs={{6,0},{8,2},{10,4},{12,6},{14,8},{16,10},{18,12},{20,14},{22,16},{... | collective-permute-start | bytes 786440 | tf_op jit(solution)/shard_map/ppermute | solution.py:51
  306.1 26.0 %collective-permute-start.12 = (bf16[512,256]{1,0:T(8,128)(2,1)S(1)}, bf16[512,256]{1,0:T(8,128)(2,1)S(1)}, u32[]{:S(2)}, u32[]{:S(2)}) collective-permute-start(bf16[512,256]{1,0:T(8,128)(2,1)S(1)} %get-tuple-element.76), channel_id=1, source_target_pairs={{4,0},{6,2},{8,4},{10,6},{12,8},{14,10},{16,12},{18,14},{20,16},{2... | collective-permute-start | bytes 786440 | tf_op jit(solution)/shard_map/ppermute | solution.py:51
  307.4 24.7 %collective-permute-start.13 = (bf16[512,256]{1,0:T(8,128)(2,1)S(1)}, bf16[512,256]{1,0:T(8,128)(2,1)S(1)}, u32[]{:S(2)}, u32[]{:S(2)}) collective-permute-start(bf16[512,256]{1,0:T(8,128)(2,1)S(1)} %get-tuple-element.77), channel_id=1, source_target_pairs={{2,0},{4,2},{6,4},{8,6},{10,8},{12,10},{14,12},{16,14},{18,16},{20... | collective-permute-start | bytes 786440 | tf_op jit(solution)/shard_map/ppermute | solution.py:51
  335.0 28.5 %collective-permute-start.14 = (bf16[256,1536]{1,0:T(8,128)(2,1)S(1)}, bf16[256,1536]{1,0:T(8,128)(2,1)S(1)}, u32[]{:S(2)}, u32[]{:S(2)}) collective-permute-start(bf16[256,1536]{1,0:T(8,128)(2,1)S(1)} %fusion.1), channel_id=1, source_target_pairs={{0,1},{1,0},{2,3},{3,2},{4,5},{5,4},{6,7},{7,6},{8,9},{9,8},{10,11... | collective-permute-start | bytes 2359304 | tf_op jit(solution)/shard_map/ppermute | solution.py:41
  335.4 49.5 %all-to-all-start.4 = ((bf16[16,32,1536]{2,1,0:T(8,128)(2,1)}), bf16[16,32,1536]{2,1,0:T(8,128)(2,1)}, u32[]{:S(2)}, u32[]{:S(2)}) async-start(bf16[16,32,1536]{2,1,0:T(8,128)(2,1)} %get-tuple-element.82), calls=%async_computation.5 | async-start | bytes 3145728 | tf_op jit(solution)/shard_map/all_to_all | solution.py:524
  361.2 177.1 %all-reduce.3.cloned.1.call-start = ((), (), s32[]{:S(2)}) async-start(), calls=%async_computation.7 | async-start | bytes 13369344 | tf_op jit(solution)/shard_map/psum | solution.py:608
  392.5 8.2 %collective-permute-start.15 = (bf16[256,1536]{1,0:T(8,128)(2,1)S(1)}, bf16[256,1536]{1,0:T(8,128)(2,1)}, u32[]{:S(2)}, u32[]{:S(2)}) collective-permute-start(bf16[256,1536]{1,0:T(8,128)(2,1)S(1)} %convolution_convert_fusion.2), channel_id=1, source_target_pairs={{0,1},{1,0},{2,3},{3,2},{4,5},{5,4},{6,7},{7,6},{8,9},{9,8},{10,11... | collective-permute-start | bytes 2359304 | tf_op jit(solution)/shard_map/ppermute | solution.py:41
  400.7 139.0 %copy-start.38 = (f32[12]{0:T(128)S(1)}, f32[12]{0:T(128)}, u32[]{:S(2)}) copy-start(f32[12]{0:T(128)} %param.35) | copy-start | bytes 148
  (40 other events, 268.2 us)
Sparse Core Ops, SparseCore 0:
  12.8 95.1 all-gather.2
  252.1 94.8 reduce-scatter.1
  385.1 153.1 all-reduce.2

commit v6 on v5

--- a/solution.py
+++ b/solution.py
@@ -16,7 +16,7 @@
 RANK_ROWS = 32
 PLANE = 16
 SEGMENTS = 3
-EARLY = 2
+EARLY = 1
 AUX = 16
 LANES = 256
 MORE = 128
@@ -225,6 +225,41 @@
     )(gate, up, down)
 
 
+def expert_first_kernel(x_ref, own_ref, peer_ref, out_ref):
+    width = x_ref.shape[-1]
+    rows = x_ref[...].reshape(-1, width)
+    hidden = own_ref.shape[-1] // 3
+    out = None
+    for weights in (own_ref, peer_ref):
+        both = contract(rows, weights[0, :, : 2 * hidden], NN)
+        gate_act, up_act = (both[:, :hidden], both[:, hidden:])
+        inner = gate_act * (1.0 / (1.0 + jnp.exp(-gate_act))) * up_act
+        part = contract(inner.astype(BF16), weights[0, :, 2 * hidden :], NT)
+        out = part if out is None else out + part
+    out_ref[...] = out.astype(BF16).reshape(out_ref.shape)
+
+
+def expert_first(rows, own, peer):
+    sources, _, width = rows.shape
+    triple = own.shape[-1]
+    step = sources // 2
+    part = pl.BlockSpec((step, RANK_ROWS, width), lambda s, j: (j, s, 0))
+    weight = pl.BlockSpec((1, width, triple), lambda s, j: (s, 0, 0))
+    return pl.pallas_call(
+        expert_first_kernel,
+        grid=(EARLY, 2),
+        in_specs=[part, weight, weight],
+        out_specs=part,
+        out_shape=jax.ShapeDtypeStruct((sources, EARLY * RANK_ROWS, width), BF16),
+        compiler_params=pltpu.CompilerParams(vmem_limit_bytes=56 << 20),
+        cost_estimate=pl.CostEstimate(
+            flops=4 * sources * EARLY * RANK_ROWS * width * triple,
+            bytes_accessed=4 * sources * EARLY * RANK_ROWS * width + 4 * EARLY * width * triple,
+            transcendentals=sources * EARLY * RANK_ROWS * triple * 2 // 3,
+        ),
+    )(rows, own, peer)
+
+
 def expert_kernel(x_ref, g_ref, own_ref, peer_ref, dx_ref, own_acts, peer_acts):
     width = x_ref.shape[-1]
     rows, grads = (x_ref[...].reshape(-1, width), g_ref[...].reshape(-1, width))
@@ -275,10 +310,9 @@
     width = x_ref.shape[-1]
     rows, grads = (x_ref[...].reshape(-1, width), g_ref[...].reshape(-1, width))
     hidden = own_ref.shape[-1]
-    early_ref, late_ref = outs[3:]
+    late_ref = outs[3]
     segment = pl.program_id(0)
-    out = None
-    for side, (acts, weights) in enumerate(((own_acts, own_ref), (peer_acts, peer_ref))):
+    for side, acts in enumerate((own_acts, peer_acts)):
         first = contract(rows, acts[0, :, : 2 * hidden], TN).astype(BF16)
         second = contract(grads, acts[0, :, 2 * hidden :], TN).astype(BF16)
         if side == 0:
@@ -288,17 +322,12 @@
             outs[0][0] = first[:, :hidden]
             outs[1][0] = first[:, hidden:]
             outs[2][0] = second
-        part = contract(acts[0, :, 2 * hidden :], weights[0], NT)
-        out = part if out is None else out + part
-    out = out.astype(BF16).reshape(x_ref.shape)
-
-    @pl.when(segment < EARLY)
-    def _():
-        early_ref[...] = out
 
     @pl.when(segment >= EARLY)
     def _():
-        late_ref[...] = out
+        out = contract(own_acts[0, :, 2 * hidden :], own_ref[0], NT)
+        out = out + contract(peer_acts[0, :, 2 * hidden :], peer_ref[0], NT)
+        late_ref[...] = out.astype(BF16).reshape(x_ref.shape)
 
 
 def expert_sums(rows, grads, own_acts, peer_acts, own, peer):
@@ -316,16 +345,10 @@
         in_specs=[wide, wide, act, act, down, down],
         out_specs=[pl.BlockSpec((1, width, triple), lambda s: (s, 0, 0))]
         + [pl.BlockSpec((1, width, hidden), lambda s: (s, 0, 0))] * 3
-        + [
-            pl.BlockSpec(block, lambda s: (0, jnp.minimum(s, EARLY - 1), 0)),
-            pl.BlockSpec(block, lambda s: (0, jnp.maximum(s - EARLY, 0), 0)),
-        ],
+        + [pl.BlockSpec(block, lambda s: (0, jnp.maximum(s - EARLY, 0), 0))],
         out_shape=[jax.ShapeDtypeStruct((segments, width, triple), BF16)]
         + [jax.ShapeDtypeStruct((segments, width, hidden), BF16)] * 3
-        + [
-            jax.ShapeDtypeStruct((sources, EARLY * RANK_ROWS, width), BF16),
-            jax.ShapeDtypeStruct((sources, (segments - EARLY) * RANK_ROWS, width), BF16),
-        ],
+        + [jax.ShapeDtypeStruct((sources, (segments - EARLY) * RANK_ROWS, width), BF16)],
         compiler_params=pltpu.CompilerParams(vmem_limit_bytes=60 << 20),
         cost_estimate=pl.CostEstimate(
             flops=6 * sources * lines * width * triple,
@@ -553,16 +576,17 @@
     own = after(own, rows_out)
     peer = swapped(own)
     rows_in = in_plane(rows_out)
+    out_early = in_plane(expert_first(rows_in, own, peer))
     back, own_acts, peer_acts = expert_back(rows_in, grad_rows, own, peer)
 
     def combined(weights, rows):
         part = contract(weights, rows.reshape(-1, model_width), TN).astype(BF16)
         return part.astype(F32) + swapped(part).astype(F32)
 
-    sum_own, *sum_peer, out_early, out_late = expert_sums(rows_in, grad_rows, own_acts, peer_acts, own, peer)
+    sum_own, *sum_peer, out_late = expert_sums(rows_in, grad_rows, own_acts, peer_acts, own, peer)
     sums = both_cores(sum_own, [swapped(part) for part in sum_peer], dp_size // PLANE)
-    back = in_plane(back)
-    out_early = in_plane(after(out_early, back))
+    back = in_plane(after(back, out_early))
+    out_late = in_plane(after(out_late, back))
     grad_normed2 = combined(pick, after(back, sums))
     sums = lax.psum_scatter(
         sums, "dp", scatter_dimension=0, tiled=True, axis_index_groups=column_groups
@@ -579,7 +603,6 @@
     returned = [
         passed_along(grad_blocks[number], -hop) for number, hop in enumerate(range(HOPS, 0, -1))
     ]
-    out_late = in_plane(after(out_late, (returned, out_early)))
     kv_total = grad_blocks[-1]
     for part in returned:
         kv_total = kv_total + part.astype(F32)

time: 561 us -> 556 us (level)
  starting transfers between devices: 86.9 us -> 69.9 us
  waiting for transfers between devices: 224 us -> 232 us
    psum x1, waiting for transfers between devices: 135 us -> 157 us  [shards(): summed = lax.psum(parts, 'dp')]
    all_to_all x4, starting transfers between devices: 48.1 us -> 26.1 us  [in_plane(): lax.all_to_all(rows, 'dp', 0, 0, tiled=True, axis_index_groups=plane_groups)]
    all_to_all x4, waiting for transfers between devices: 51.9 us -> 37.9 us  [in_plane(): lax.all_to_all(rows, 'dp', 0, 0, tiled=True, axis_index_groups=plane_groups)]
    pallas_call x0 -> x1, Pallas kernels: none -> 6.51 us  [expert_first(): pl.pallas_call(expert_first_kernel, grid=(EARLY, 2), in_specs=[part, weig...]
  transfers between devices with their start and end apart: 23 -> 23, of which waited for: 10 -> 11; matrix products, arithmetic and copies ran while one was open for 10% -> 10% of each run, Pallas kernels for 12% -> 15%
where the time goes in v6:
time: 556 us; the launch traced here: 554 us
  waiting for transfers between devices  232 us (42%)
  Pallas kernels  103 us (19%)
  starting transfers between devices  69.9 us (13%)
  blocking collectives  69 us (12%)
  other arithmetic  24.8 us (4%)
  matrix products  22.6 us (4%)
  local copies, waits for them, and re-layouts  18.6 us (3%)
  between operations  14.6 us (3%)
    psum x1, waiting for transfers between devices, shards(): summed = lax.psum(parts, 'dp')  157 us
    all_to_all x1, blocking collectives, in_plane(): lax.all_to_all(rows, 'dp', 0, 0, tiled=True, axis_index_groups=plane_groups)  69 us
    all_to_all x4, waiting for transfers between devices, in_plane(): lax.all_to_all(rows, 'dp', 0, 0, tiled=True, axis_index_groups=plane_groups)  37.9 us
    all_to_all x4, starting transfers between devices, in_plane(): lax.all_to_all(rows, 'dp', 0, 0, tiled=True, axis_index_groups=plane_groups)  26.1 us
    dot_general x13, matrix products, contract(): lax.dot_general(left, right, (dims, ((), ())), preferred_element_type=F32)  22.6 us
    ppermute x8, waiting for transfers between devices, passed_along(): lax.ppermute(value, 'dp', [(s, s + steps) for s in range(first, last)])  22.3 us
    ppermute x8, starting transfers between devices, swapped(): return lax.ppermute(array, 'tensor', [(0, 1), (1, 0)])  21.8 us
    ppermute x8, starting transfers between devices, passed_along(): lax.ppermute(value, 'dp', [(s, s + steps) for s in range(first, last)])  21.6 us
  transfers between devices with their start and end apart: 23, of which 11 were waited for; matrix products, arithmetic and copies ran while one was open for 10% of the time, Pallas kernels for 15%

profile of v6, /device:TPU:1, one launch (start us, length us, event | category | flops | bytes accessed | tf_op | source)
XLA Modules:
  0.0 554.3 jit_solution(10350190668999430526)
XLA Ops:
  7.2 5.4 shard_map.300
  21.9 5.7 %collective-permute-start.1 = (bf16[528,256]{1,0:T(8,128)(2,1)S(1)}, bf16[528,256]{1,0:T(8,128)(2,1)S(1)}, u32[]{:S(2)}, u32[]{:S(2)}) collective-permute-start(bf16[528,256]{1,0:T(8,128)(2,1)S(1)} %concatenate.28.k0), channel_id=1, source_target_pairs={{0,6},{2,8},{4,10},{6,12},{8,14},{10,16},{12,18},{14,20},{16,22},{... | collective-permute-start | bytes 811016 | tf_op jit(solution)/shard_map/ppermute | solution.py:51
  35.9 4.9 fusion
  41.5 11.6 %all-to-all-start = ((bf16[16,96,1536]{2,1,0:T(8,128)(2,1)}), bf16[16,96,1536]{2,1,0:T(8,128)(2,1)}, u32[]{:S(2)}, u32[]{:S(2)}) async-start(bf16[16,96,1536]{2,1,0:T(8,128)(2,1)} %bitcast.74), calls=%async_computation | async-start | bytes 9437184 | tf_op jit(solution)/shard_map/all_to_all | solution.py:547
  60.5 11.3 %shard_map.299 = (bf16[768,256]{1,0:T(8,128)(2,1)S(1)}, f32[12,256]{1,0:T(8,128)S(1)}, f32[12,256]{1,0:T(8,128)S(1)}) custom-call(bf16[768,256]{1,0:T(8,128)(2,1)S(1)} %bitcast.67, bf16[528,256]{1,0:T(8,128)(2,1)S(1)} %collective-permute-done.k4, bf16[528,256]{1,0:T(8,128)(2,1)S(1)} %copy-done.4, bf16[528,256]{1,0:T(8,128)(2,1)} %collective-permute-done.2.k2, ...), custom_call_target="tpu_custom_call" | custom-call | flops 1006632960 | bytes 2138112 | tf_op jit(solution)/shard_map/pallas_call | solution.py:126
  82.7 28.1 %all-to-all-done.g_ref = bf16[16,96,1536]{2,1,0:T(8,128)(2,1)} async-done(((bf16[16,96,1536]{2,1,0:T(8,128)(2,1)}), bf16[16,96,1536]{2,1,0:T(8,128)(2,1)}, u32[]{:S(2)}, u32[]{:S(2)}) %all-to-all-start) | async-done | bytes 4718624 | tf_op jit(solution)/shard_map/all_to_all | solution.py:547
  110.8 4.6 collective-permute-start.5
  115.4 69.0 %all_to_all.25.x_ref = bf16[16,96,1536]{2,1,0:T(8,128)(2,1)} all-to-all(bf16[16,96,1536]{2,1,0:T(8,128)(2,1)} %bitcast.69), channel_id=1, replica_groups={{0,2,4,6,8,10,12,14,16,18,20,22,24,26,28,30},{32,34,36,38,40,42,44,46,4..., dimensions={0} | all-to-all | bytes 9437184 | tf_op jit(solution)/shard_map/all_to_all | solution.py:547
  184.5 6.5 %shard_map.302 = bf16[16,32,1536]{2,1,0:T(8,128)(2,1)} custom-call(bf16[16,96,1536]{2,1,0:T(8,128)(2,1)} %all_to_all.25.x_ref, bf16[4,1536,768]{2,1,0:T(8,128)(2,1)} %bitcast.71, bf16[4,1536,768]{2,1,0:T(8,128)(2,1)} %collective-permute-done.5.peer_ref), custom_call_target="tpu_custom_call" | custom-call | flops 2415919104 | bytes 7864320 | tf_op jit(solution)/shard_map/pallas_call | solution.py:248
  191.0 4.5 all-to-all-start.2
  195.5 18.1 %shard_map.301 = (bf16[16,96,1536]{2,1,0:T(8,128)(2,1)}, bf16[3,512,768]{2,1,0:T(8,128)(2,1)}, bf16[3,512,768]{2,1,0:T(8,128)(2,1)}) custom-call(bf16[16,96,1536]{2,1,0:T(8,128)(2,1)} %all_to_all.25.x_ref, bf16[16,96,1536]{2,1,0:T(8,128)(2,1)} %all-to-all-done.g_ref, bf16[4,1536,768]{2,1,0:T(8,128)(2,1)} %bitcast.72, ...), custom_call_target="tpu_custom_call" | custom-call | flops 12683575296 | bytes 28311552 | tf_op jit(solution)/shard_map/pallas_call | solution.py:290
  215.9 4.7 all-to-all-start.3
  220.7 16.4 %shard_map.303 = (bf16[3,1536,768]{2,1,0:T(8,128)(2,1)}, bf16[3,1536,256]{2,1,0:T(8,128)(2,1)}, bf16[3,1536,256]{2,1,0:T(8,128)(2,1)}, bf16[3,1536,256]{2,1,0:T(8,128)(2,1)}, bf16[16,64,1536]{2,1,0:T(8,128)(2,1)}) custom-call(bf16[16,96,1536]{2,1,0:T(8,128)(2,1)} %all_to_all.25.x_ref, bf16[16,96,1536]{2,1,0:T(8,128)(2,1)} %all-to-all-done.g_ref, ...), custom_call_target="tpu_custom_call" | custom-call | flops 10871635968 | bytes 31850496 | tf_op jit(solution)/shard_map/pallas_call | solution.py:342
  252.4 11.9 %shard_map.304 = bf16[4,1536,768]{2,1,0:T(8,128)(2,1)} custom-call(bf16[3,1536,768]{2,1,0:T(8,128)(2,1)} %get-tuple-element.66.own_ref, bf16[3,1536,256]{2,1,0:T(8,128)(2,1)} %collective-permute-done.6.refs_0_, bf16[3,1536,256]{2,1,0:T(8,128)(2,1)} %collective-permute-done.7.refs_1_, bf16[3,1536,256]{2,1,0:T(8,128)(2,1)} %collective-permute-done.8.refs_2_), custom_call_target="tpu_custom_call" | custom-call | flops 4718592 | bytes 28311552 | tf_op jit(solution)/shard_map/pallas_call | solution.py:383
  265.4 7.5 %all-to-all-done.3 = bf16[16,96,1536]{2,1,0:T(8,128)(2,1)} async-done(((bf16[16,96,1536]{2,1,0:T(8,128)(2,1)}), bf16[16,96,1536]{2,1,0:T(8,128)(2,1)}, u32[]{:S(2)}, u32[]{:S(2)}) %all-to-all-start.3) | async-done | bytes 4718624 | tf_op jit(solution)/shard_map/all_to_all | solution.py:547
  272.9 4.8 convolution_convert_fusion.1
  277.7 9.5 %collective-permute-start.9 = (bf16[256,1536]{1,0:T(8,128)(2,1)}, bf16[256,1536]{1,0:T(8,128)(2,1)}, u32[]{:S(2)}, u32[]{:S(2)}) collective-permute-start(bf16[256,1536]{1,0:T(8,128)(2,1)} %convolution_convert_fusion.1), channel_id=1, source_target_pairs={{0,1},{1,0},{2,3},{3,2},{4,5},{5,4},{6,7},{7,6},{8,9},{9,8},{10,11... | collective-permute-start | bytes 2359304 | tf_op jit(solution)/shard_map/ppermute | solution.py:41
  287.3 5.2 all-to-all-start.4
  299.7 15.6 %shard_map.305 = (bf16[768,256]{1,0:T(8,128)(2,1)S(1)}, bf16[512,256]{1,0:T(8,128)(2,1)S(1)}, bf16[512,256]{1,0:T(8,128)(2,1)S(1)}, bf16[512,256]{1,0:T(8,128)(2...) custom-call(bf16[768,256]{1,0:T(8,128)(2,1)S(1)} %bitcast.68, bf16[768,256]{1,0:T(8,128)(2,1)S(1)} %fusion.13.g_ref, ...), custom_call_target="tpu_custom_call" | custom-call | flops 125829120000 | bytes 3883008 | tf_op jit(solution)/shard_map/pallas_call | solution.py:189
  321.4 13.0 %collective-permute-done.10 = bf16[512,256]{1,0:T(8,128)(2,1)S(1)} collective-permute-done((bf16[512,256]{1,0:T(8,128)(2,1)S(1)}, bf16[512,256]{1,0:T(8,128)(2,1)S(1)}, u32[]{:S(2)}, u32[]{:S(2)}) %collective-permute-start.10) | collective-permute-done | bytes 262176 | tf_op jit(solution)/shard_map/ppermute | solution.py:51
  334.4 9.3 %collective-permute-done.11 = bf16[512,256]{1,0:T(8,128)(2,1)S(1)} collective-permute-done((bf16[512,256]{1,0:T(8,128)(2,1)S(1)}, bf16[512,256]{1,0:T(8,128)(2,1)S(1)}, u32[]{:S(2)}, u32[]{:S(2)}) %collective-permute-start.11) | collective-permute-done | bytes 262176 | tf_op jit(solution)/shard_map/ppermute | solution.py:51
  350.9 7.4 %shard_map.306 = bf16[1536,2176]{1,0:T(8,128)(2,1)} custom-call(bf16[256,1536]{1,0:T(8,128)(2,1)} %copy-done.12, bf16[1280,256]{1,0:T(8,128)(2,1)} %pad_maximum_fusion.1.qkv_ref, bf16[768,256]{1,0:T(8,128)(2,1)} %copy-done.2, bf16[256,1536]{1,0:T(8,128)(2,1)} %copy-done.16, f32[128,1536]{1,0:T(8,128)} %select_maximum_fusion.extra_ref), custom_call_target="tpu_custom_call" | custom-call | flops 1711276032 | bytes 8257536 | tf_op jit(solution)/shard_map/pallas_call | solution.py:408
  375.7 157.3 %all-reduce.3.cloned.1.call-done.in_ref = bf16[1536,2176]{1,0:T(8,128)(2,1)} async-done(((bf16[1536,2176]{1,0:T(8,128)(2,1)}), bf16[1536,2176]{1,0:T(8,128)(2,1)}) %all-reduce.3.cloned.1.call-update) | async-done | bytes 6684688 | tf_op jit(solution)/shard_map/psum | solution.py:631
  536.2 10.0 %shard_map.307 = (f32[768,1536]{1,0:T(8,128)}, f32[1536,768]{1,0:T(8,128)}, f32[1536,256]{1,0:T(8,128)}, f32[1536,256]{1,0:T(8,128)}, f32[8,1536]{1,0:T(8,128)},...) custom-call(bf16[1536,2176]{1,0:T(8,128)(2,1)} %all-reduce.3.cloned.1.call-done.in_ref, ...), custom_call_target="tpu_custom_call" | custom-call | flops 3342336 | bytes 26738688 | tf_op jit(solution)/shard_map/pallas_call | solution.py:448
  (200 shorter events, 97.4 us)
Async XLA Ops:
  7.2 103.6 %all-gather.3.cloned.1.call-start = ((), (), s32[]{:S(2)}) async-start(), calls=%async_computation.8 | async-start | bytes 11796480 | tf_op jit(solution)/shard_map/all_gather | solution.py:566
  18.0 22.8 %collective-permute-start = (bf16[528,256]{1,0:T(8,128)(2,1)S(1)}, bf16[528,256]{1,0:T(8,128)(2,1)S(1)}, u32[]{:S(2)}, u32[]{:S(2)}) collective-permute-start(bf16[528,256]{1,0:T(8,128)(2,1)S(1)} %concatenate.28.k0), channel_id=1, source_target_pairs={{0,8},{2,10},{4,12},{6,14},{8,16},{10,18},{12,20},{14,22},{16,24},... | collective-permute-start | bytes 811016 | tf_op jit(solution)/shard_map/ppermute | solution.py:51
  21.9 18.9 %collective-permute-start.1 = (bf16[528,256]{1,0:T(8,128)(2,1)S(1)}, bf16[528,256]{1,0:T(8,128)(2,1)S(1)}, u32[]{:S(2)}, u32[]{:S(2)}) collective-permute-start(bf16[528,256]{1,0:T(8,128)(2,1)S(1)} %concatenate.28.k0), channel_id=1, source_target_pairs={{0,6},{2,8},{4,10},{6,12},{8,14},{10,16},{12,18},{14,20},{16,22},{... | collective-permute-start | bytes 811016 | tf_op jit(solution)/shard_map/ppermute | solution.py:51
  27.6 13.2 %collective-permute-start.2 = (bf16[528,256]{1,0:T(8,128)(2,1)S(1)}, bf16[528,256]{1,0:T(8,128)(2,1)}, u32[]{:S(2)}, u32[]{:S(2)}) collective-permute-start(bf16[528,256]{1,0:T(8,128)(2,1)S(1)} %concatenate.28.k0), channel_id=1, source_target_pairs={{0,4},{2,6},{4,8},{6,10},{8,12},{10,14},{12,16},{14,18},{16,20},{1... | collective-permute-start | bytes 811016 | tf_op jit(solution)/shard_map/ppermute | solution.py:51
  30.8 10.0 %collective-permute-start.3 = (bf16[528,256]{1,0:T(8,128)(2,1)S(1)}, bf16[528,256]{1,0:T(8,128)(2,1)}, u32[]{:S(2)}, u32[]{:S(2)}) collective-permute-start(bf16[528,256]{1,0:T(8,128)(2,1)S(1)} %concatenate.28.k0), channel_id=1, source_target_pairs={{0,2},{2,4},{4,6},{6,8},{8,10},{10,12},{12,14},{14,16},{16,18},{18... | collective-permute-start | bytes 811016 | tf_op jit(solution)/shard_map/ppermute | solution.py:51
  41.5 69.3 %all-to-all-start = ((bf16[16,96,1536]{2,1,0:T(8,128)(2,1)}), bf16[16,96,1536]{2,1,0:T(8,128)(2,1)}, u32[]{:S(2)}, u32[]{:S(2)}) async-start(bf16[16,96,1536]{2,1,0:T(8,128)(2,1)} %bitcast.74), calls=%async_computation | async-start | bytes 9437184 | tf_op jit(solution)/shard_map/all_to_all | solution.py:547
  72.7 4.9 collective-permute-start.4
  110.8 73.6 %collective-permute-start.5 = (bf16[4,1536,768]{2,1,0:T(8,128)(2,1)}, bf16[4,1536,768]{2,1,0:T(8,128)(2,1)}, u32[]{:S(2)}, u32[]{:S(2)}) collective-permute-start(bf16[4,1536,768]{2,1,0:T(8,128)(2,1)} %bitcast.70), channel_id=1, source_target_pairs={{0,1},{1,0},{2,3},{3,2},{4,5},{5,4},{6,7},{7,6},{8,9},{9,8},{10,11... | collective-permute-start | bytes 28311560 | tf_op jit(solution)/shard_map/ppermute | solution.py:41
  191.0 24.9 %all-to-all-start.2 = ((bf16[16,32,1536]{2,1,0:T(8,128)(2,1)}), bf16[16,32,1536]{2,1,0:T(8,128)(2,1)}, u32[]{:S(2)}, u32[]{:S(2)}) async-start(bf16[16,32,1536]{2,1,0:T(8,128)(2,1)} %shard_map.302), calls=%async_computation.2 | async-start | bytes 3145728 | tf_op jit(solution)/shard_map/all_to_all | solution.py:547
  215.9 57.0 %all-to-all-start.3 = ((bf16[16,96,1536]{2,1,0:T(8,128)(2,1)}), bf16[16,96,1536]{2,1,0:T(8,128)(2,1)}, u32[]{:S(2)}, u32[]{:S(2)}) async-start(bf16[16,96,1536]{2,1,0:T(8,128)(2,1)} %get-tuple-element.63), calls=%async_computation.3 | async-start | bytes 9437184 | tf_op jit(solution)/shard_map/all_to_all | solution.py:547
  220.6 138.5 %reduce-scatter.2.cloned.1.call-start = ((), (), s32[]{:S(2)}) async-start(), calls=%async_computation.6 | async-start | bytes 11796480 | tf_op jit(solution)/shard_map/reduce_scatter | solution.py:591
  237.0 8.6 %collective-permute-start.6 = (bf16[3,1536,256]{2,1,0:T(8,128)(2,1)}, bf16[3,1536,256]{2,1,0:T(8,128)(2,1)}, u32[]{:S(2)}, u32[]{:S(2)}) collective-permute-start(bf16[3,1536,256]{2,1,0:T(8,128)(2,1)} %get-tuple-element.67), channel_id=1, source_target_pairs={{0,1},{1,0},{2,3},{3,2},{4,5},{5,4},{6,7},{7,6},{8,9},{9,8},{10,11... | collective-permute-start | bytes 7077896 | tf_op jit(solution)/shard_map/ppermute | solution.py:41
  241.2 7.9 %collective-permute-start.7 = (bf16[3,1536,256]{2,1,0:T(8,128)(2,1)}, bf16[3,1536,256]{2,1,0:T(8,128)(2,1)}, u32[]{:S(2)}, u32[]{:S(2)}) collective-permute-start(bf16[3,1536,256]{2,1,0:T(8,128)(2,1)} %get-tuple-element.68), channel_id=1, source_target_pairs={{0,1},{1,0},{2,3},{3,2},{4,5},{5,4},{6,7},{7,6},{8,9},{9,8},{10,11... | collective-permute-start | bytes 7077896 | tf_op jit(solution)/shard_map/ppermute | solution.py:41
  241.3 11.2 %collective-permute-start.8 = (bf16[3,1536,256]{2,1,0:T(8,128)(2,1)}, bf16[3,1536,256]{2,1,0:T(8,128)(2,1)}, u32[]{:S(2)}, u32[]{:S(2)}) collective-permute-start(bf16[3,1536,256]{2,1,0:T(8,128)(2,1)} %get-tuple-element.69), channel_id=1, source_target_pairs={{0,1},{1,0},{2,3},{3,2},{4,5},{5,4},{6,7},{7,6},{8,9},{9,8},{10,11... | collective-permute-start | bytes 7077896 | tf_op jit(solution)/shard_map/ppermute | solution.py:41
  277.7 15.1 %collective-permute-start.9 = (bf16[256,1536]{1,0:T(8,128)(2,1)}, bf16[256,1536]{1,0:T(8,128)(2,1)}, u32[]{:S(2)}, u32[]{:S(2)}) collective-permute-start(bf16[256,1536]{1,0:T(8,128)(2,1)} %convolution_convert_fusion.1), channel_id=1, source_target_pairs={{0,1},{1,0},{2,3},{3,2},{4,5},{5,4},{6,7},{7,6},{8,9},{9,8},{10,11... | collective-permute-start | bytes 2359304 | tf_op jit(solution)/shard_map/ppermute | solution.py:41
  287.3 71.1 %all-to-all-start.4 = ((bf16[16,64,1536]{2,1,0:T(8,128)(2,1)}), bf16[16,64,1536]{2,1,0:T(8,128)(2,1)}, u32[]{:S(2)}, u32[]{:S(2)}) async-start(bf16[16,64,1536]{2,1,0:T(8,128)(2,1)} %get-tuple-element.80), calls=%async_computation.5 | async-start | bytes 6291456 | tf_op jit(solution)/shard_map/all_to_all | solution.py:547
  292.5 240.5 %all-reduce.3.cloned.1.call-start = ((), (), s32[]{:S(2)}) async-start(), calls=%async_computation.7 | async-start | bytes 13369344 | tf_op jit(solution)/shard_map/psum | solution.py:631
  315.3 19.1 %collective-permute-start.10 = (bf16[512,256]{1,0:T(8,128)(2,1)S(1)}, bf16[512,256]{1,0:T(8,128)(2,1)S(1)}, u32[]{:S(2)}, u32[]{:S(2)}) collective-permute-start(bf16[512,256]{1,0:T(8,128)(2,1)S(1)} %get-tuple-element.74), channel_id=1, source_target_pairs={{8,0},{10,2},{12,4},{14,6},{16,8},{18,10},{20,12},{22,14},{24,16},... | collective-permute-start | bytes 786440 | tf_op jit(solution)/shard_map/ppermute | solution.py:51
  316.6 27.1 %collective-permute-start.11 = (bf16[512,256]{1,0:T(8,128)(2,1)S(1)}, bf16[512,256]{1,0:T(8,128)(2,1)S(1)}, u32[]{:S(2)}, u32[]{:S(2)}) collective-permute-start(bf16[512,256]{1,0:T(8,128)(2,1)S(1)} %get-tuple-element.75), channel_id=1, source_target_pairs={{6,0},{8,2},{10,4},{12,6},{14,8},{16,10},{18,12},{20,14},{22,16},{... | collective-permute-start | bytes 786440 | tf_op jit(solution)/shard_map/ppermute | solution.py:51
  317.9 25.8 %collective-permute-start.12 = (bf16[512,256]{1,0:T(8,128)(2,1)S(1)}, bf16[512,256]{1,0:T(8,128)(2,1)S(1)}, u32[]{:S(2)}, u32[]{:S(2)}) collective-permute-start(bf16[512,256]{1,0:T(8,128)(2,1)S(1)} %get-tuple-element.76), channel_id=1, source_target_pairs={{4,0},{6,2},{8,4},{10,6},{12,8},{14,10},{16,12},{18,14},{20,16},{2... | collective-permute-start | bytes 786440 | tf_op jit(solution)/shard_map/ppermute | solution.py:51
  319.2 24.5 %collective-permute-start.13 = (bf16[512,256]{1,0:T(8,128)(2,1)S(1)}, bf16[512,256]{1,0:T(8,128)(2,1)S(1)}, u32[]{:S(2)}, u32[]{:S(2)}) collective-permute-start(bf16[512,256]{1,0:T(8,128)(2,1)S(1)} %get-tuple-element.77), channel_id=1, source_target_pairs={{2,0},{4,2},{6,4},{8,6},{10,8},{12,10},{14,12},{16,14},{18,16},{20... | collective-permute-start | bytes 786440 | tf_op jit(solution)/shard_map/ppermute | solution.py:51
  346.6 2.6 collective-permute-start.14
  366.9 6.5 %collective-permute-start.15 = (bf16[256,1536]{1,0:T(8,128)(2,1)S(1)}, bf16[256,1536]{1,0:T(8,128)(2,1)}, u32[]{:S(2)}, u32[]{:S(2)}) collective-permute-start(bf16[256,1536]{1,0:T(8,128)(2,1)S(1)} %convolution_convert_fusion.2), channel_id=1, source_target_pairs={{0,1},{1,0},{2,3},{3,2},{4,5},{5,4},{6,7},{7,6},{8,9},{9,8},{10,11... | collective-permute-start | bytes 2359304 | tf_op jit(solution)/shard_map/ppermute | solution.py:41
  373.4 161.1 %copy-start.38 = (f32[12]{0:T(128)S(1)}, f32[12]{0:T(128)}, u32[]{:S(2)}) copy-start(f32[12]{0:T(128)} %param.35) | copy-start | bytes 148
  (40 other events, 244.3 us)
Sparse Core Ops, SparseCore 0:
  12.8 95.1 all-gather.2
  264.4 94.6 reduce-scatter.1
  364.1 168.8 all-reduce.2

commit v7 on v6

--- a/solution.py
+++ b/solution.py
@@ -212,12 +212,13 @@
 
 def pack_weights(gate, up, down):
     width, hidden = gate.shape
-    thin = pl.BlockSpec((LANES, hidden), lambda i: (i, 0))
+    rows = width // 2
+    thin = pl.BlockSpec((rows, hidden), lambda i: (i, 0))
     return pl.pallas_call(
         pack_weights_kernel,
-        grid=(width // LANES,),
-        in_specs=[thin, thin, pl.BlockSpec((hidden, LANES), lambda i: (0, i))],
-        out_specs=pl.BlockSpec((LANES, 3 * hidden), lambda i: (i, 0)),
+        grid=(2,),
+        in_specs=[thin, thin, pl.BlockSpec((hidden, rows), lambda i: (0, i))],
+        out_specs=pl.BlockSpec((rows, 3 * hidden), lambda i: (i, 0)),
         out_shape=jax.ShapeDtypeStruct((width, 3 * hidden), BF16),
         cost_estimate=pl.CostEstimate(
             flops=width * hidden, bytes_accessed=12 * width * hidden, transcendentals=0
@@ -260,9 +261,15 @@
     )(rows, own, peer)
 
 
-def expert_kernel(x_ref, g_ref, own_ref, peer_ref, dx_ref, own_acts, peer_acts):
+def of_segment(early_ref, late_ref):
+    width = early_ref.shape[-1]
+    chosen = jnp.where(pl.program_id(0) < EARLY, early_ref[...], late_ref[...])
+    return chosen.reshape(-1, width)
+
+
+def expert_kernel(x_ref, g1_ref, g2_ref, own_ref, peer_ref, dx_ref, own_acts, peer_acts):
     width = x_ref.shape[-1]
-    rows, grads = (x_ref[...].reshape(-1, width), g_ref[...].reshape(-1, width))
+    rows, grads = (x_ref[...].reshape(-1, width), of_segment(g1_ref, g2_ref))
     hidden = own_ref.shape[-1] // 3
     back = None
     for weights, acts in ((own_ref, own_acts), (peer_ref, peer_acts)):
@@ -280,17 +287,26 @@
     dx_ref[...] = back.astype(BF16).reshape(dx_ref.shape)
 
 
+def segment_specs(block):
+    return [
+        pl.BlockSpec(block, lambda s: (0, s, 0)),
+        pl.BlockSpec(block, lambda s: (0, jnp.minimum(s, EARLY - 1), 0)),
+        pl.BlockSpec(block, lambda s: (0, jnp.maximum(s - EARLY, 0), 0)),
+    ]
+
+
 def expert_back(rows, grads, own, peer):
     sources, lines, width = rows.shape
     segments, triple = (lines // RANK_ROWS, own.shape[-1])
     count = sources * RANK_ROWS
-    wide = pl.BlockSpec((sources, RANK_ROWS, width), lambda s: (0, s, 0))
+    specs = segment_specs((sources, RANK_ROWS, width))
+    wide = specs[0]
     weight = pl.BlockSpec((1, width, triple), lambda s: (s, 0, 0))
     act = pl.BlockSpec((1, count, triple), lambda s: (s, 0, 0))
     return pl.pallas_call(
         expert_kernel,
         grid=(segments,),
-        in_specs=[wide, wide, weight, weight],
+        in_specs=[*specs, weight, weight],
         out_specs=[wide, act, act],
         out_shape=[
             jax.ShapeDtypeStruct(rows.shape, BF16),
@@ -303,12 +319,12 @@
             bytes_accessed=6 * sources * lines * width + 4 * segments * width * triple,
             transcendentals=2 * sources * lines * triple // 3,
         ),
-    )(rows, grads, own, peer)
-
-
-def expert_sums_kernel(x_ref, g_ref, own_acts, peer_acts, own_ref, peer_ref, sum_own, *outs):
+    )(rows, *grads, own, peer)
+
+
+def expert_sums_kernel(x_ref, g1_ref, g2_ref, own_acts, peer_acts, own_ref, peer_ref, sum_own, *outs):
     width = x_ref.shape[-1]
-    rows, grads = (x_ref[...].reshape(-1, width), g_ref[...].reshape(-1, width))
+    rows, grads = (x_ref[...].reshape(-1, width), of_segment(g1_ref, g2_ref))
     hidden = own_ref.shape[-1]
     late_ref = outs[3]
     segment = pl.program_id(0)
@@ -336,13 +352,12 @@
     hidden = triple // 3
     count = sources * RANK_ROWS
     block = (sources, RANK_ROWS, width)
-    wide = pl.BlockSpec(block, lambda s: (0, s, 0))
     down = pl.BlockSpec((1, width, hidden), lambda s: (s, 0, 2))
     act = pl.BlockSpec((1, count, triple), lambda s: (s, 0, 0))
     return pl.pallas_call(
         expert_sums_kernel,
         grid=(segments,),
-        in_specs=[wide, wide, act, act, down, down],
+        in_specs=[*segment_specs(block), act, act, down, down],
         out_specs=[pl.BlockSpec((1, width, triple), lambda s: (s, 0, 0))]
         + [pl.BlockSpec((1, width, hidden), lambda s: (s, 0, 0))] * 3
         + [pl.BlockSpec(block, lambda s: (0, jnp.maximum(s - EARLY, 0), 0))],
@@ -355,7 +370,7 @@
             bytes_accessed=6 * sources * lines * width + 5 * segments * width * triple,
             transcendentals=0,
         ),
-    )(rows, grads, own_acts, peer_acts, own, peer)
+    )(rows, *grads, own_acts, peer_acts, own, peer)
 
 
 def both_cores_kernel(own_ref, *refs):
@@ -392,68 +407,116 @@
     )(own, *peers)
 
 
-def weight_grads_kernel(normed_ref, qkv_ref, attended_ref, branch_ref, extra_ref, out_ref):
+def first_grads_kernel(normed_ref, query_ref, attended_ref, branch_ref, out_ref):
     width = branch_ref.shape[1]
-    columns = width + qkv_ref.shape[0]
     out_ref[:, :width] = contract(attended_ref[...], branch_ref[...], NN).astype(BF16)
-    out_ref[:, width:columns] = contract(normed_ref[...], qkv_ref[...], ((0,), (1,))).astype(BF16)
-    out_ref[:, columns:] = jnp.transpose(extra_ref[...]).astype(BF16)
-
-
-def weight_grads(normed, grad_qkv, attended, branch, extra):
+    out_ref[:, width:] = contract(normed_ref[...], query_ref[...], ((0,), (1,))).astype(BF16)
+
+
+def last_grads_kernel(normed_ref, kv_ref, extra_ref, _, out_ref):
+    columns = kv_ref.shape[0]
+    out_ref[:, :columns] = contract(normed_ref[...], kv_ref[...], ((0,), (1,))).astype(BF16)
+    out_ref[:, columns : columns + MORE] = jnp.transpose(extra_ref[...]).astype(BF16)
+    out_ref[:, columns + MORE :] = jnp.zeros((out_ref.shape[0], MORE), BF16)
+
+
+def first_grads(normed, grad_query, attended, branch, every):
     tok, model = normed.shape
-    width, columns = (attended.shape[0], grad_qkv.shape[0])
+    width = attended.shape[0]
     half = width // LANES
-    every = width + columns + MORE
-    return pl.pallas_call(
-        weight_grads_kernel,
+    return pl.pallas_call(
+        first_grads_kernel,
+        grid=(model // LANES,),
+        in_specs=[
+            pl.BlockSpec((tok, LANES), lambda i: (0, i)),
+            pl.BlockSpec((width, tok), lambda i: (0, 0)),
+            pl.BlockSpec((LANES, tok), lambda i: (i % half, 0)),
+            pl.BlockSpec((tok, width), lambda i: (0, i // half)),
+        ],
+        out_specs=pl.BlockSpec((LANES, 2 * width), lambda i: (i, 0)),
+        out_shape=jax.ShapeDtypeStruct((model, every), BF16),
+        cost_estimate=pl.CostEstimate(
+            flops=4 * tok * model * width, bytes_accessed=4 * model * width, transcendentals=0
+        ),
+    )(normed, grad_query, attended, branch)
+
+
+def last_grads(normed, grad_kv, extra, parts):
+    tok, model = normed.shape
+    columns = grad_kv.shape[0]
+    every = parts.shape[1]
+    size = columns + 2 * MORE
+    return pl.pallas_call(
+        last_grads_kernel,
         grid=(model // LANES,),
         in_specs=[
             pl.BlockSpec((tok, LANES), lambda i: (0, i)),
             pl.BlockSpec((columns, tok), lambda i: (0, 0)),
-            pl.BlockSpec((LANES, tok), lambda i: (i % half, 0)),
-            pl.BlockSpec((tok, width), lambda i: (0, i // half)),
             pl.BlockSpec((MORE, LANES), lambda i: (0, i)),
+            pl.BlockSpec(memory_space=pl.ANY),
         ],
-        out_specs=pl.BlockSpec((LANES, every), lambda i: (i, 0)),
-        out_shape=jax.ShapeDtypeStruct((model, every), BF16),
-        cost_estimate=pl.CostEstimate(
-            flops=2 * tok * model * every,
-            bytes_accessed=2 * model * every + 4 * tok * model,
-            transcendentals=0,
-        ),
-    )(normed, grad_qkv, attended, branch, extra)
+        out_specs=pl.BlockSpec((LANES, size), lambda i: (i, (every - size) // size)),
+        out_shape=jax.ShapeDtypeStruct(parts.shape, BF16),
+        input_output_aliases={3: 0},
+        cost_estimate=pl.CostEstimate(
+            flops=2 * tok * model * columns, bytes_accessed=2 * model * size, transcendentals=0
+        ),
+    )(normed, grad_kv, extra, parts)
 
 
 def unpack_kernel(
-    in_ref, query_ref, key_ref, sq_ref, sk_ref,
-    wo_ref, wq_ref, wk_ref, wv_ref, sum_ref, cq_ref, ck_ref,
+    devices, in_ref, query_ref, key_ref, clip_ref,
+    wo_ref, wq_ref, wk_ref, wv_ref, sum_ref, cq_ref, ck_ref, peak_ref, sq_ref, sk_ref,
 ):
     at = 0
+    group = cq_ref.shape[1] // ck_ref.shape[1]
+    heads = cq_ref.shape[1] // HD
+    start = 2 * (wo_ref.shape[1] + wk_ref.shape[1])
+
+    @pl.when(pl.program_id(0) == 0)
+    def _():
+        lines = in_ref[:devices, start : start + MORE].astype(F32)
+        high, low = (lines[:, 2 : 2 + heads], lines[:, 2 + heads : 2 + 2 * heads])
+        peak = jnp.max(high + low, axis=0, keepdims=True)
+        clip = clip_ref[...]
+        scale = jnp.sqrt(clip / jnp.maximum(peak, clip))
+        peak_ref[...] = peak
+        each = lax.broadcasted_iota(jnp.int32, sq_ref.shape, 1) // HD
+        of_key = lax.broadcasted_iota(jnp.int32, sk_ref.shape, 1) // HD
+        query_scale, key_scale = (jnp.zeros(sq_ref.shape, F32), jnp.zeros(sk_ref.shape, F32))
+        for h in range(heads):
+            query_scale = jnp.where(each == h, scale[:, h : h + 1], query_scale)
+        for g in range(heads // group):
+            least = jnp.min(scale[:, g * group : (g + 1) * group], axis=1, keepdims=True)
+            key_scale = jnp.where(of_key == g, least, key_scale)
+        sq_ref[...] = query_scale
+        sk_ref[...] = key_scale
+
     for target in (wo_ref, wq_ref, wk_ref, wv_ref):
         size = target.shape[1]
         target[...] = in_ref[:, at : at + size].astype(F32)
         at += size
-    sum_ref[...] = jnp.transpose(in_ref[:, at:].astype(F32))[: sum_ref.shape[0]]
+    sum_ref[...] = jnp.transpose(in_ref[:, at : at + MORE].astype(F32))[: sum_ref.shape[0]]
     cq_ref[...] = (query_ref[...].astype(F32) * sq_ref[...]).astype(BF16)
     ck_ref[...] = (key_ref[...].astype(F32) * sk_ref[...]).astype(BF16)
 
 
-def unpack(summed, w_query, w_key, scale_query, scale_key):
+def unpack(summed, w_query, w_key, clip_limit, devices):
     total, every = summed.shape
     width, narrow = (w_query.shape[1], w_key.shape[1])
     steps = total // LANES
     wide = pl.BlockSpec((LANES, width), lambda i: (i, 0))
     thin = pl.BlockSpec((LANES, narrow), lambda i: (i, 0))
-    return pl.pallas_call(
-        unpack_kernel,
+    heads = width // HD
+    line = pl.BlockSpec((1, heads), lambda i: (0, 0))
+    return pl.pallas_call(
+        functools.partial(unpack_kernel, devices),
         grid=(steps,),
         in_specs=[
             pl.BlockSpec((LANES, every), lambda i: (i, 0)),
             wide,
             thin,
-            pl.BlockSpec((1, width), lambda i: (0, 0)),
-            pl.BlockSpec((1, narrow), lambda i: (0, 0)),
+            line,
         ],
         out_specs=[
             pl.BlockSpec((LANES, width), lambda i: (i % (steps // 2), i // (steps // 2))),
@@ -463,7 +526,9 @@
             pl.BlockSpec((8, LANES), lambda i: (0, i)),
             wide,
             thin,
+            line,
         ],
+        scratch_shapes=[pltpu.VMEM((1, width), F32), pltpu.VMEM((1, narrow), F32)],
         out_shape=[
             jax.ShapeDtypeStruct((total // 2, 2 * width), F32),
             jax.ShapeDtypeStruct((total, width), F32),
@@ -472,12 +537,13 @@
             jax.ShapeDtypeStruct((8, total), F32),
             jax.ShapeDtypeStruct((total, width), BF16),
             jax.ShapeDtypeStruct((total, narrow), BF16),
+            jax.ShapeDtypeStruct((1, heads), F32),
         ],
         compiler_params=pltpu.CompilerParams(vmem_limit_bytes=60 << 20),
         cost_estimate=pl.CostEstimate(
             flops=total * every, bytes_accessed=8 * total * every, transcendentals=0
         ),
-    )(summed, w_query, w_key, scale_query, scale_key)
+    )(summed, w_query, w_key, clip_limit.reshape(1, heads))
 
 
 def rms_scale(values):
@@ -546,7 +612,14 @@
         rows = rows.reshape(PLANE, -1, model_width)
         return lax.all_to_all(rows, "dp", 0, 0, tiled=True, axis_index_groups=plane_groups)
 
-    grad_rows = (contract(pick, out_grad, NN) * slot_gate).astype(BF16)
+    def grads_for(first, last):
+        shape = (PLANE, SEGMENTS * RANK_ROWS, -1)
+        part = pick.reshape(shape)[:, first * RANK_ROWS : last * RANK_ROWS].reshape(-1, tok_dev)
+        gate = slot_gate.reshape(shape)[:, first * RANK_ROWS : last * RANK_ROWS].reshape(-1, 1)
+        return (contract(part, out_grad, NN) * gate).astype(BF16)
+
+    grads_early = in_plane(grads_for(0, EARLY))
+    grads_late = grads_for(EARLY, SEGMENTS)
 
     cosine, sine = rope_tables(tok_dev, dp_size)
     x_float = tokens.astype(F32)
@@ -561,10 +634,10 @@
     ).astype(BF16)
     block = jnp.concatenate([key, value, side])
     blocks = tuple(passed_along(block, hop) for hop in range(HOPS, 0, -1)) + (block,)
-    blocks, grad_rows = lax.optimization_barrier((blocks, grad_rows))
+    blocks, grads_early, grads_late = lax.optimization_barrier((blocks, grads_early, grads_late))
     packed_w = pack_weights(w_gate[0], w_up[0], w_down[0])
     own = lax.all_gather(packed_w, "dp", axis=0, axis_index_groups=column_groups)
-    grad_rows = in_plane(grad_rows)
+    grad_rows = (grads_early, in_plane(grads_late))
     attended, log_total, peaks = attend(query, blocks, group)
     attn_part = contract(attended, w_out, TN)
     hidden1 = x_float + (attn_part + swapped(attn_part))
@@ -572,7 +645,7 @@
     normed2 = (hidden1 * inverse2 * norm2_gain).astype(BF16)
 
     rows_out = contract(pick, normed2, NN).astype(BF16)
-    rows_out = after(rows_out, grad_rows)
+    rows_out = after(rows_out, grad_rows[1])
     own = after(own, rows_out)
     peer = swapped(own)
     rows_in = in_plane(rows_out)
@@ -600,9 +673,12 @@
     grad_query_pre, *grad_blocks = attend_back(
         query, grad_attended, log_total, cosine, sine, blocks, group
     )
+    every = 2 * w_query.shape[1] + 2 * w_key.shape[1] + 2 * MORE
+    parts = first_grads(normed1, grad_query_pre, attended, grad_branch, every)
     returned = [
         passed_along(grad_blocks[number], -hop) for number, hop in enumerate(range(HOPS, 0, -1))
     ]
+    returned = after(returned, parts)
     kv_total = grad_blocks[-1]
     for part in returned:
         kv_total = kv_total + part.astype(F32)
@@ -621,26 +697,20 @@
     input_grad = grad_hidden1 + grad_from_norm1
     peak = jnp.max(peaks, axis=1)
     peak_high = peak.astype(BF16).astype(F32)
-    places = jnp.arange(dp_size)[:, None] == lax.axis_index("dp")
-    peak_row = jnp.where(places, jnp.concatenate([peak_high, peak - peak_high])[None], 0.0)
-    extra = jnp.stack([grad_gain1, grad_gain2, peak_row.reshape(-1)])
+    peak_pair = jnp.concatenate([peak_high, peak - peak_high])
+    places = jnp.arange(model_width)[None] == lax.axis_index("dp")
+    peak_rows = jnp.where(places, peak_pair[:, None], 0.0)
+    extra = jnp.concatenate([grad_gain1[None], grad_gain2[None], peak_rows])
     extra = jnp.pad(extra, ((0, MORE - len(extra)), (0, 0)))
-    grad_qkv = jnp.concatenate([grad_query_pre, grad_key_pre, grad_value])
-    parts = weight_grads(normed1, grad_qkv, attended, grad_branch, extra)
+    parts = last_grads(normed1, jnp.concatenate([grad_key_pre, grad_value]), extra, parts)
     parts, sums, out_early, out_late = lax.optimization_barrier((parts, sums, out_early, out_late))
     summed = lax.psum(parts, "dp")
     expert_out = jnp.concatenate([out_early, out_late], axis=1)
     output = (hidden1 + combined(gated, expert_out)).astype(BF16)
     grad_gate, grad_up, grad_down = jnp.split(sums[0].astype(F32), 3, axis=1)
     grad_down = grad_down.T
-    all_peaks = summed[:, 2 - MORE].astype(F32).reshape(dp_size, 2 * local_heads)
-    head_peaks = jnp.max(all_peaks[:, :local_heads] + all_peaks[:, local_heads:], axis=0)
-    factor = clip_limit / jnp.maximum(head_peaks, clip_limit)
-    key_factor = jnp.min(factor.reshape(local_kv, group), axis=1)
-    scale_query = jnp.repeat(jnp.sqrt(factor), HD)[None, :]
-    scale_key = jnp.repeat(jnp.sqrt(key_factor), HD)[None, :]
-    grad_wo, grad_wq, grad_wk, grad_wv, totals, clipped_query, clipped_key = unpack(
-        summed, w_query, w_key, scale_query, scale_key
+    grad_wo, grad_wq, grad_wk, grad_wv, totals, clipped_query, clipped_key, head_peaks = unpack(
+        summed, w_query, w_key, clip_limit, dp_size
     )
     return (
         output,
@@ -656,7 +726,7 @@
         grad_down[None],
         clipped_query,
         clipped_key,
-        head_peaks,
+        head_peaks.reshape(-1),
     )
 
 

time: 556 us -> 562 us (1.011); the launches traced: 554 us -> 552 us
  waiting for transfers between devices: 232 us -> 196 us
  starting transfers between devices: 69.9 us -> 95.8 us
    all_to_all x4 -> x5, waiting for transfers between devices: 37.9 us -> 20.3 us  [in_plane(): lax.all_to_all(rows, 'dp', 0, 0, tiled=True, axis_index_groups=plane_groups)]
    ppermute x8, waiting for transfers between devices: 22.3 us -> 8.52 us  [passed_along(): lax.ppermute(value, 'dp', [(s, s + steps) for s in range(first, last)])]
    all_to_all x4 -> x5, starting transfers between devices: 26.1 us -> 39.3 us  [in_plane(): lax.all_to_all(rows, 'dp', 0, 0, tiled=True, axis_index_groups=plane_groups)]
    psum x1, starting transfers between devices: 0.26 us -> 9.42 us  [shards(): summed = lax.psum(parts, 'dp')]
    pallas_call x5 -> x6, Pallas kernels: 57.3 us -> 60.9 us  [the longest x1 18.5 us: expert_back(): pl.pallas_call(expert_kernel, grid=(segments,), in_specs=[*specs, weight,...]
    dot_general x13 -> x14, matrix products: 22.6 us -> 24.4 us  [contract(): lax.dot_general(left, right, (dims, ((), ())), preferred_element_type=F32)]
  transfers between devices with their start and end apart: 23 -> 24, of which waited for: 11 -> 12; matrix products, arithmetic and copies ran while one was open for 10% -> 11% of each run, Pallas kernels for 15% -> 16%
where the time goes in v7:
time: 562 us; the launch traced here: 552 us
  waiting for transfers between devices  196 us (35%)
  Pallas kernels  106 us (19%)
  starting transfers between devices  95.8 us (17%)
  blocking collectives  69.9 us (12%)
  other arithmetic  26.7 us (5%)
  matrix products  24.4 us (4%)
  local copies, waits for them, and re-layouts  18.1 us (3%)
  between operations  14.7 us (3%)
    psum x1, waiting for transfers between devices, shards(): summed = lax.psum(parts, 'dp')  152 us
    all_to_all x1, blocking collectives, in_plane(): lax.all_to_all(rows, 'dp', 0, 0, tiled=True, axis_index_groups=plane_groups)  69.9 us
    all_to_all x5, starting transfers between devices, in_plane(): lax.all_to_all(rows, 'dp', 0, 0, tiled=True, axis_index_groups=plane_groups)  39.3 us
    ppermute x8, starting transfers between devices, swapped(): return lax.ppermute(array, 'tensor', [(0, 1), (1, 0)])  27.1 us
    dot_general x14, matrix products, contract(): lax.dot_general(left, right, (dims, ((), ())), preferred_element_type=F32)  24.4 us
    all_to_all x5, waiting for transfers between devices, in_plane(): lax.all_to_all(rows, 'dp', 0, 0, tiled=True, axis_index_groups=plane_groups)  20.3 us
    ppermute x8, starting transfers between devices, passed_along(): lax.ppermute(value, 'dp', [(s, s + steps) for s in range(first, last)])  20 us
    pallas_call x1, Pallas kernels, expert_back(): pl.pallas_call(expert_kernel, grid=(segments,), in_specs=[*specs, weight,...  18.5 us
  transfers between devices with their start and end apart: 24, of which 12 were waited for; matrix products, arithmetic and copies ran while one was open for 11% of the time, Pallas kernels for 16%

profile of v7, /device:TPU:1, one launch (start us, length us, event | category | flops | bytes accessed | tf_op | source)
XLA Modules:
  0.0 552.2 jit_solution(13761434932335057401)
XLA Ops:
  15.5 8.6 %all-to-all-start = ((bf16[16,32,1536]{2,1,0:T(8,128)(2,1)}), bf16[16,32,1536]{2,1,0:T(8,128)(2,1)}, u32[]{:S(2)}, u32[]{:S(2)}) async-start(bf16[16,32,1536]{2,1,0:T(8,128)(2,1)} %bitcast.90), calls=%async_computation | async-start | bytes 3145728 | tf_op jit(solution)/shard_map/all_to_all | solution.py:613
  32.1 5.0 collective-permute-start.1
  55.7 15.7 %all-to-all-start.1 = ((bf16[16,64,1536]{2,1,0:T(8,128)(2,1)}), bf16[16,64,1536]{2,1,0:T(8,128)(2,1)}, u32[]{:S(2)}, u32[]{:S(2)}) async-start(bf16[16,64,1536]{2,1,0:T(8,128)(2,1)} %bitcast.92), calls=%async_computation.1 | async-start | bytes 6291456 | tf_op jit(solution)/shard_map/all_to_all | solution.py:613
  71.4 11.4 %shard_map.299 = (bf16[768,256]{1,0:T(8,128)(2,1)S(1)}, f32[12,256]{1,0:T(8,128)S(1)}, f32[12,256]{1,0:T(8,128)S(1)}) custom-call(bf16[768,256]{1,0:T(8,128)(2,1)S(1)} %bitcast.82, bf16[528,256]{1,0:T(8,128)(2,1)S(1)} %collective-permute-done.k4, bf16[528,256]{1,0:T(8,128)(2,1)} %collective-permute-done.1.k3, bf16[528,256]{1,0:T(8,128)(2,1)} %collective-permute-done.2.k2, ...), custom_call_target="tpu_custom_call" | custom-call | flops 1006632960 | bytes 2138112 | tf_op jit(solution)/shard_map/pallas_call | solution.py:126
  97.4 11.3 %all-to-all-done.1.g2_ref = bf16[16,64,1536]{2,1,0:T(8,128)(2,1)} async-done(((bf16[16,64,1536]{2,1,0:T(8,128)(2,1)}), bf16[16,64,1536]{2,1,0:T(8,128)(2,1)}, u32[]{:S(2)}, u32[]{:S(2)}) %all-to-all-start.1) | async-done | bytes 3145760 | tf_op jit(solution)/shard_map/all_to_all | solution.py:613
  108.6 6.5 %collective-permute-start.5 = (bf16[4,1536,768]{2,1,0:T(8,128)(2,1)}, bf16[4,1536,768]{2,1,0:T(8,128)(2,1)}, u32[]{:S(2)}, u32[]{:S(2)}) collective-permute-start(bf16[4,1536,768]{2,1,0:T(8,128)(2,1)} %bitcast.85), channel_id=1, source_target_pairs={{0,1},{1,0},{2,3},{3,2},{4,5},{5,4},{6,7},{7,6},{8,9},{9,8},{10,11... | collective-permute-start | bytes 28311560 | tf_op jit(solution)/shard_map/ppermute | solution.py:41
  115.2 69.9 %all_to_all.30.x_ref = bf16[16,96,1536]{2,1,0:T(8,128)(2,1)} all-to-all(bf16[16,96,1536]{2,1,0:T(8,128)(2,1)} %bitcast.84), channel_id=1, replica_groups={{0,2,4,6,8,10,12,14,16,18,20,22,24,26,28,30},{32,34,36,38,40,42,44,46,4..., dimensions={0} | all-to-all | bytes 9437184 | tf_op jit(solution)/shard_map/all_to_all | solution.py:613
  185.1 6.5 %shard_map.302 = bf16[16,32,1536]{2,1,0:T(8,128)(2,1)} custom-call(bf16[16,96,1536]{2,1,0:T(8,128)(2,1)} %all_to_all.30.x_ref, bf16[4,1536,768]{2,1,0:T(8,128)(2,1)} %bitcast.86, bf16[4,1536,768]{2,1,0:T(8,128)(2,1)} %collective-permute-done.5.peer_ref), custom_call_target="tpu_custom_call" | custom-call | flops 2415919104 | bytes 7864320 | tf_op jit(solution)/shard_map/pallas_call | solution.py:249
  191.6 5.0 all-to-all-start.3
  196.6 18.5 %shard_map.301 = (bf16[16,96,1536]{2,1,0:T(8,128)(2,1)}, bf16[3,512,768]{2,1,0:T(8,128)(2,1)}, bf16[3,512,768]{2,1,0:T(8,128)(2,1)}) custom-call(bf16[16,96,1536]{2,1,0:T(8,128)(2,1)} %all_to_all.30.x_ref, bf16[16,32,1536]{2,1,0:T(8,128)(2,1)} %all-to-all-done.g1_ref, bf16[16,64,1536]{2,1,0:T(8,128)(2,1)} %all-to-all-done.1.g2_ref, ...), custom_call_target="tpu_custom_call" | custom-call | flops 12683575296 | bytes 28311552 | tf_op jit(solution)/shard_map/pallas_call | solution.py:306
  217.1 4.6 all-to-all-start.4
  221.8 16.8 %shard_map.303 = (bf16[3,1536,768]{2,1,0:T(8,128)(2,1)}, bf16[3,1536,256]{2,1,0:T(8,128)(2,1)}, bf16[3,1536,256]{2,1,0:T(8,128)(2,1)}, bf16[3,1536,256]{2,1,0:T(8,128)(2,1)}, bf16[16,64,1536]{2,1,0:T(8,128)(2,1)}) custom-call(bf16[16,96,1536]{2,1,0:T(8,128)(2,1)} %all_to_all.30.x_ref, bf16[16,32,1536]{2,1,0:T(8,128)(2,1)} %all-to-all-done.g1_ref, ...), custom_call_target="tpu_custom_call" | custom-call | flops 10871635968 | bytes 31850496 | tf_op jit(solution)/shard_map/pallas_call | solution.py:357
  254.1 11.8 %shard_map.304 = bf16[4,1536,768]{2,1,0:T(8,128)(2,1)} custom-call(bf16[3,1536,768]{2,1,0:T(8,128)(2,1)} %get-tuple-element.73.own_ref, bf16[3,1536,256]{2,1,0:T(8,128)(2,1)} %collective-permute-done.6.refs_0_, bf16[3,1536,256]{2,1,0:T(8,128)(2,1)} %collective-permute-done.7.refs_1_, bf16[3,1536,256]{2,1,0:T(8,128)(2,1)} %collective-permute-done.8.refs_2_), custom_call_target="tpu_custom_call" | custom-call | flops 4718592 | bytes 28311552 | tf_op jit(solution)/shard_map/pallas_call | solution.py:398
  267.0 7.0 %all-to-all-done.4 = bf16[16,96,1536]{2,1,0:T(8,128)(2,1)} async-done(((bf16[16,96,1536]{2,1,0:T(8,128)(2,1)}), bf16[16,96,1536]{2,1,0:T(8,128)(2,1)}, u32[]{:S(2)}, u32[]{:S(2)}) %all-to-all-start.4) | async-done | bytes 4718624 | tf_op jit(solution)/shard_map/all_to_all | solution.py:613
  274.0 4.8 convolution_convert_fusion.1
  278.8 9.5 %collective-permute-start.9 = (bf16[256,1536]{1,0:T(8,128)(2,1)}, bf16[256,1536]{1,0:T(8,128)(2,1)}, u32[]{:S(2)}, u32[]{:S(2)}) collective-permute-start(bf16[256,1536]{1,0:T(8,128)(2,1)} %convolution_convert_fusion.1), channel_id=1, source_target_pairs={{0,1},{1,0},{2,3},{3,2},{4,5},{5,4},{6,7},{7,6},{8,9},{9,8},{10,11... | collective-permute-start | bytes 2359304 | tf_op jit(solution)/shard_map/ppermute | solution.py:41
  288.3 5.3 all-to-all-start.5
  293.7 9.4 %all-reduce.3.cloned.1.call-start = ((), (), s32[]{:S(2)}) async-start(), calls=%async_computation.8 | async-start | bytes 14155776 | tf_op jit(solution)/shard_map/psum | solution.py:707
  309.8 15.8 %shard_map.305 = (bf16[768,256]{1,0:T(8,128)(2,1)S(1)}, bf16[512,256]{1,0:T(8,128)(2,1)S(1)}, bf16[512,256]{1,0:T(8,128)(2,1)S(1)}, bf16[512,256]{1,0:T(8,128)(2...) custom-call(bf16[768,256]{1,0:T(8,128)(2,1)S(1)} %bitcast.83, bf16[768,256]{1,0:T(8,128)(2,1)S(1)} %fusion.13.g_ref, ...), custom_call_target="tpu_custom_call" | custom-call | flops 125829120000 | bytes 3883008 | tf_op jit(solution)/shard_map/pallas_call | solution.py:189
  332.8 6.7 %shard_map.306._ = bf16[1536,2304]{1,0:T(8,128)(2,1)} custom-call(bf16[256,1536]{1,0:T(8,128)(2,1)} %copy-done.7, bf16[768,256]{1,0:T(8,128)(2,1)} %copy-done.3, bf16[768,256]{1,0:T(8,128)(2,1)} %copy-done.2, bf16[256,1536]{1,0:T(8,128)(2,1)} %copy-done.14), custom_call_target="tpu_custom_call" | custom-call | flops 1207959552 | bytes 4718592 | tf_op jit(solution)/shard_map/pallas_call | solution.py:427
  339.5 6.7 %collective-permute-done.11 = bf16[512,256]{1,0:T(8,128)(2,1)S(1)} collective-permute-done((bf16[512,256]{1,0:T(8,128)(2,1)S(1)}, bf16[512,256]{1,0:T(8,128)(2,1)S(1)}, u32[]{:S(2)}, u32[]{:S(2)}) %collective-permute-start.11) | collective-permute-done | bytes 262176 | tf_op jit(solution)/shard_map/ppermute | solution.py:51
  358.5 5.7 %shard_map.307 = bf16[1536,2304]{1,0:T(8,128)(2,1)} custom-call(bf16[256,1536]{1,0:T(8,128)(2,1)} %copy-done.7, bf16[512,256]{1,0:T(8,128)(2,1)} %pad_maximum_fusion.1.kv_ref, f32[128,1536]{1,0:T(8,128)} %select_maximum_fusion.extra_ref, bf16[1536,2304]{1,0:T(8,128)(2,1)} %shard_map.306._), custom_call_target="tpu_custom_call", output_to_operand_aliasing={{}: (3, {})} | custom-call | flops 402653184 | bytes 2359296 | tf_op jit(solution)/shard_map/pallas_call | solution.py:449
  381.2 152.5 %all-reduce.3.cloned.1.call-done.in_ref = bf16[1536,2304]{1,0:T(8,128)(2,1)} async-done(((bf16[1536,2304]{1,0:T(8,128)(2,1)}), bf16[1536,2304]{1,0:T(8,128)(2,1)}) %all-reduce.3.cloned.1.call-update) | async-done | bytes 7077904 | tf_op jit(solution)/shard_map/psum | solution.py:707
  533.7 10.2 %shard_map.308 = (f32[768,1536]{1,0:T(8,128)}, f32[1536,768]{1,0:T(8,128)}, f32[1536,256]{1,0:T(8,128)}, f32[1536,256]{1,0:T(8,128)}, f32[8,1536]{1,0:T(8,128)},...) custom-call(bf16[1536,2304]{1,0:T(8,128)(2,1)} %all-reduce.3.cloned.1.call-done.in_ref, ...), custom_call_target="tpu_custom_call" | custom-call | flops 3538944 | bytes 28311552 | tf_op jit(solution)/shard_map/pallas_call | solution.py:512
  (206 shorter events, 112.2 us)
Async XLA Ops:
  7.2 101.4 %all-gather.3.cloned.1.call-start = ((), (), s32[]{:S(2)}) async-start(), calls=%async_computation.9 | async-start | bytes 11796480 | tf_op jit(solution)/shard_map/all_gather | solution.py:639
  15.5 40.1 %all-to-all-start = ((bf16[16,32,1536]{2,1,0:T(8,128)(2,1)}), bf16[16,32,1536]{2,1,0:T(8,128)(2,1)}, u32[]{:S(2)}, u32[]{:S(2)}) async-start(bf16[16,32,1536]{2,1,0:T(8,128)(2,1)} %bitcast.90), calls=%async_computation | async-start | bytes 3145728 | tf_op jit(solution)/shard_map/all_to_all | solution.py:613
  28.9 25.0 %collective-permute-start = (bf16[528,256]{1,0:T(8,128)(2,1)S(1)}, bf16[528,256]{1,0:T(8,128)(2,1)S(1)}, u32[]{:S(2)}, u32[]{:S(2)}) collective-permute-start(bf16[528,256]{1,0:T(8,128)(2,1)S(1)} %concatenate.31.k0), channel_id=1, source_target_pairs={{0,8},{2,10},{4,12},{6,14},{8,16},{10,18},{12,20},{14,22},{16,24},... | collective-permute-start | bytes 811016 | tf_op jit(solution)/shard_map/ppermute | solution.py:51
  32.1 23.4 %collective-permute-start.1 = (bf16[528,256]{1,0:T(8,128)(2,1)S(1)}, bf16[528,256]{1,0:T(8,128)(2,1)}, u32[]{:S(2)}, u32[]{:S(2)}) collective-permute-start(bf16[528,256]{1,0:T(8,128)(2,1)S(1)} %concatenate.31.k0), channel_id=1, source_target_pairs={{0,6},{2,8},{4,10},{6,12},{8,14},{10,16},{12,18},{14,20},{16,22},{... | collective-permute-start | bytes 811016 | tf_op jit(solution)/shard_map/ppermute | solution.py:51
  37.1 18.5 %collective-permute-start.2 = (bf16[528,256]{1,0:T(8,128)(2,1)S(1)}, bf16[528,256]{1,0:T(8,128)(2,1)}, u32[]{:S(2)}, u32[]{:S(2)}) collective-permute-start(bf16[528,256]{1,0:T(8,128)(2,1)S(1)} %concatenate.31.k0), channel_id=1, source_target_pairs={{0,4},{2,6},{4,8},{6,10},{8,12},{10,14},{12,16},{14,18},{16,20},{1... | collective-permute-start | bytes 811016 | tf_op jit(solution)/shard_map/ppermute | solution.py:51
  41.1 14.5 %collective-permute-start.3 = (bf16[528,256]{1,0:T(8,128)(2,1)S(1)}, bf16[528,256]{1,0:T(8,128)(2,1)}, u32[]{:S(2)}, u32[]{:S(2)}) collective-permute-start(bf16[528,256]{1,0:T(8,128)(2,1)S(1)} %concatenate.31.k0), channel_id=1, source_target_pairs={{0,2},{2,4},{4,6},{6,8},{8,10},{10,12},{12,14},{14,16},{16,18},{18... | collective-permute-start | bytes 811016 | tf_op jit(solution)/shard_map/ppermute | solution.py:51
  55.7 52.9 %all-to-all-start.1 = ((bf16[16,64,1536]{2,1,0:T(8,128)(2,1)}), bf16[16,64,1536]{2,1,0:T(8,128)(2,1)}, u32[]{:S(2)}, u32[]{:S(2)}) async-start(bf16[16,64,1536]{2,1,0:T(8,128)(2,1)} %bitcast.92), calls=%async_computation.1 | async-start | bytes 6291456 | tf_op jit(solution)/shard_map/all_to_all | solution.py:613
  84.8 5.4 collective-permute-start.4
  108.6 76.5 %collective-permute-start.5 = (bf16[4,1536,768]{2,1,0:T(8,128)(2,1)}, bf16[4,1536,768]{2,1,0:T(8,128)(2,1)}, u32[]{:S(2)}, u32[]{:S(2)}) collective-permute-start(bf16[4,1536,768]{2,1,0:T(8,128)(2,1)} %bitcast.85), channel_id=1, source_target_pairs={{0,1},{1,0},{2,3},{3,2},{4,5},{5,4},{6,7},{7,6},{8,9},{9,8},{10,11... | collective-permute-start | bytes 28311560 | tf_op jit(solution)/shard_map/ppermute | solution.py:41
  191.6 25.5 %all-to-all-start.3 = ((bf16[16,32,1536]{2,1,0:T(8,128)(2,1)}), bf16[16,32,1536]{2,1,0:T(8,128)(2,1)}, u32[]{:S(2)}, u32[]{:S(2)}) async-start(bf16[16,32,1536]{2,1,0:T(8,128)(2,1)} %shard_map.302), calls=%async_computation.3 | async-start | bytes 3145728 | tf_op jit(solution)/shard_map/all_to_all | solution.py:613
  217.1 56.8 %all-to-all-start.4 = ((bf16[16,96,1536]{2,1,0:T(8,128)(2,1)}), bf16[16,96,1536]{2,1,0:T(8,128)(2,1)}, u32[]{:S(2)}, u32[]{:S(2)}) async-start(bf16[16,96,1536]{2,1,0:T(8,128)(2,1)} %get-tuple-element.70), calls=%async_computation.4 | async-start | bytes 9437184 | tf_op jit(solution)/shard_map/all_to_all | solution.py:613
  221.8 142.5 %reduce-scatter.2.cloned.1.call-start = ((), (), s32[]{:S(2)}) async-start(), calls=%async_computation.7 | async-start | bytes 11796480 | tf_op jit(solution)/shard_map/reduce_scatter | solution.py:664
  238.6 8.7 %collective-permute-start.6 = (bf16[3,1536,256]{2,1,0:T(8,128)(2,1)}, bf16[3,1536,256]{2,1,0:T(8,128)(2,1)}, u32[]{:S(2)}, u32[]{:S(2)}) collective-permute-start(bf16[3,1536,256]{2,1,0:T(8,128)(2,1)} %get-tuple-element.74), channel_id=1, source_target_pairs={{0,1},{1,0},{2,3},{3,2},{4,5},{5,4},{6,7},{7,6},{8,9},{9,8},{10,11... | collective-permute-start | bytes 7077896 | tf_op jit(solution)/shard_map/ppermute | solution.py:41
  242.8 7.9 %collective-permute-start.7 = (bf16[3,1536,256]{2,1,0:T(8,128)(2,1)}, bf16[3,1536,256]{2,1,0:T(8,128)(2,1)}, u32[]{:S(2)}, u32[]{:S(2)}) collective-permute-start(bf16[3,1536,256]{2,1,0:T(8,128)(2,1)} %get-tuple-element.75), channel_id=1, source_target_pairs={{0,1},{1,0},{2,3},{3,2},{4,5},{5,4},{6,7},{7,6},{8,9},{9,8},{10,11... | collective-permute-start | bytes 7077896 | tf_op jit(solution)/shard_map/ppermute | solution.py:41
  242.9 11.2 %collective-permute-start.8 = (bf16[3,1536,256]{2,1,0:T(8,128)(2,1)}, bf16[3,1536,256]{2,1,0:T(8,128)(2,1)}, u32[]{:S(2)}, u32[]{:S(2)}) collective-permute-start(bf16[3,1536,256]{2,1,0:T(8,128)(2,1)} %get-tuple-element.76), channel_id=1, source_target_pairs={{0,1},{1,0},{2,3},{3,2},{4,5},{5,4},{6,7},{7,6},{8,9},{9,8},{10,11... | collective-permute-start | bytes 7077896 | tf_op jit(solution)/shard_map/ppermute | solution.py:41
  278.8 24.4 %collective-permute-start.9 = (bf16[256,1536]{1,0:T(8,128)(2,1)}, bf16[256,1536]{1,0:T(8,128)(2,1)}, u32[]{:S(2)}, u32[]{:S(2)}) collective-permute-start(bf16[256,1536]{1,0:T(8,128)(2,1)} %convolution_convert_fusion.1), channel_id=1, source_target_pairs={{0,1},{1,0},{2,3},{3,2},{4,5},{5,4},{6,7},{7,6},{8,9},{9,8},{10,11... | collective-permute-start | bytes 2359304 | tf_op jit(solution)/shard_map/ppermute | solution.py:41
  288.3 75.9 %all-to-all-start.5 = ((bf16[16,64,1536]{2,1,0:T(8,128)(2,1)}), bf16[16,64,1536]{2,1,0:T(8,128)(2,1)}, u32[]{:S(2)}, u32[]{:S(2)}) async-start(bf16[16,64,1536]{2,1,0:T(8,128)(2,1)} %get-tuple-element.91), calls=%async_computation.6 | async-start | bytes 6291456 | tf_op jit(solution)/shard_map/all_to_all | solution.py:613
  293.7 240.0 %all-reduce.3.cloned.1.call-start = ((), (), s32[]{:S(2)}) async-start(), calls=%async_computation.8 | async-start | bytes 14155776 | tf_op jit(solution)/shard_map/psum | solution.py:707
  325.6 13.9 %collective-permute-start.10 = (bf16[512,256]{1,0:T(8,128)(2,1)S(1)}, bf16[512,256]{1,0:T(8,128)(2,1)S(1)}, u32[]{:S(2)}, u32[]{:S(2)}) collective-permute-start(bf16[512,256]{1,0:T(8,128)(2,1)S(1)} %get-tuple-element.80), channel_id=1, source_target_pairs={{8,0},{10,2},{12,4},{14,6},{16,8},{18,10},{20,12},{22,14},{24,16},... | collective-permute-start | bytes 786440 | tf_op jit(solution)/shard_map/ppermute | solution.py:51
  326.9 19.3 %collective-permute-start.11 = (bf16[512,256]{1,0:T(8,128)(2,1)S(1)}, bf16[512,256]{1,0:T(8,128)(2,1)S(1)}, u32[]{:S(2)}, u32[]{:S(2)}) collective-permute-start(bf16[512,256]{1,0:T(8,128)(2,1)S(1)} %get-tuple-element.81), channel_id=1, source_target_pairs={{6,0},{8,2},{10,4},{12,6},{14,8},{16,10},{18,12},{20,14},{22,16},{... | collective-permute-start | bytes 786440 | tf_op jit(solution)/shard_map/ppermute | solution.py:51
  328.2 18.0 %collective-permute-start.12 = (bf16[512,256]{1,0:T(8,128)(2,1)S(1)}, bf16[512,256]{1,0:T(8,128)(2,1)S(1)}, u32[]{:S(2)}, u32[]{:S(2)}) collective-permute-start(bf16[512,256]{1,0:T(8,128)(2,1)S(1)} %get-tuple-element.82), channel_id=1, source_target_pairs={{4,0},{6,2},{8,4},{10,6},{12,8},{14,10},{16,12},{18,14},{20,16},{2... | collective-permute-start | bytes 786440 | tf_op jit(solution)/shard_map/ppermute | solution.py:51
  329.5 16.7 %collective-permute-start.13 = (bf16[512,256]{1,0:T(8,128)(2,1)S(1)}, bf16[512,256]{1,0:T(8,128)(2,1)S(1)}, u32[]{:S(2)}, u32[]{:S(2)}) collective-permute-start(bf16[512,256]{1,0:T(8,128)(2,1)S(1)} %get-tuple-element.83), channel_id=1, source_target_pairs={{2,0},{4,2},{6,4},{8,6},{10,8},{12,10},{14,12},{16,14},{18,16},{20... | collective-permute-start | bytes 786440 | tf_op jit(solution)/shard_map/ppermute | solution.py:51
  351.0 5.8 %collective-permute-start.14 = (bf16[256,1536]{1,0:T(8,128)(2,1)S(1)}, bf16[256,1536]{1,0:T(8,128)(2,1)S(1)}, u32[]{:S(2)}, u32[]{:S(2)}) collective-permute-start(bf16[256,1536]{1,0:T(8,128)(2,1)S(1)} %fusion.1), channel_id=1, source_target_pairs={{0,1},{1,0},{2,3},{3,2},{4,5},{5,4},{6,7},{7,6},{8,9},{9,8},{10,11... | collective-permute-start | bytes 2359304 | tf_op jit(solution)/shard_map/ppermute | solution.py:41
  372.7 6.2 %collective-permute-start.15 = (bf16[256,1536]{1,0:T(8,128)(2,1)S(1)}, bf16[256,1536]{1,0:T(8,128)(2,1)}, u32[]{:S(2)}, u32[]{:S(2)}) collective-permute-start(bf16[256,1536]{1,0:T(8,128)(2,1)S(1)} %convolution_convert_fusion.2), channel_id=1, source_target_pairs={{0,1},{1,0},{2,3},{3,2},{4,5},{5,4},{6,7},{7,6},{8,9},{9,8},{10,11... | collective-permute-start | bytes 2359304 | tf_op jit(solution)/shard_map/ppermute | solution.py:41
  (44 other events, 741.5 us)
Sparse Core Ops, SparseCore 0:
  10.4 97.0 all-gather.2
  266.1 91.4 reduce-scatter.1
  364.4 169.2 all-reduce.2

commit v8 on v7

--- a/solution.py
+++ b/solution.py
@@ -267,9 +267,8 @@
     return chosen.reshape(-1, width)
 
 
-def expert_kernel(x_ref, g1_ref, g2_ref, own_ref, peer_ref, dx_ref, own_acts, peer_acts):
-    width = x_ref.shape[-1]
-    rows, grads = (x_ref[...].reshape(-1, width), of_segment(g1_ref, g2_ref))
+def expert_kernel(x1_ref, x2_ref, g1_ref, g2_ref, own_ref, peer_ref, dx_ref, own_acts, peer_acts):
+    rows, grads = (of_segment(x1_ref, x2_ref), of_segment(g1_ref, g2_ref))
     hidden = own_ref.shape[-1] // 3
     back = None
     for weights, acts in ((own_ref, own_acts), (peer_ref, peer_acts)):
@@ -296,8 +295,9 @@
 
 
 def expert_back(rows, grads, own, peer):
-    sources, lines, width = rows.shape
-    segments, triple = (lines // RANK_ROWS, own.shape[-1])
+    sources, _, width = rows[0].shape
+    segments, triple = (SEGMENTS, own.shape[-1])
+    lines = segments * RANK_ROWS
     count = sources * RANK_ROWS
     specs = segment_specs((sources, RANK_ROWS, width))
     wide = specs[0]
@@ -306,10 +306,10 @@
     return pl.pallas_call(
         expert_kernel,
         grid=(segments,),
-        in_specs=[*specs, weight, weight],
+        in_specs=[*specs[1:], *specs[1:], weight, weight],
         out_specs=[wide, act, act],
         out_shape=[
-            jax.ShapeDtypeStruct(rows.shape, BF16),
+            jax.ShapeDtypeStruct((sources, lines, width), BF16),
             jax.ShapeDtypeStruct((segments, count, triple), BF16),
             jax.ShapeDtypeStruct((segments, count, triple), BF16),
         ],
@@ -319,12 +319,13 @@
             bytes_accessed=6 * sources * lines * width + 4 * segments * width * triple,
             transcendentals=2 * sources * lines * triple // 3,
         ),
-    )(rows, *grads, own, peer)
-
-
-def expert_sums_kernel(x_ref, g1_ref, g2_ref, own_acts, peer_acts, own_ref, peer_ref, sum_own, *outs):
-    width = x_ref.shape[-1]
-    rows, grads = (x_ref[...].reshape(-1, width), of_segment(g1_ref, g2_ref))
+    )(*rows, *grads, own, peer)
+
+
+def expert_sums_kernel(
+    x1_ref, x2_ref, g1_ref, g2_ref, own_acts, peer_acts, own_ref, peer_ref, sum_own, *outs
+):
+    rows, grads = (of_segment(x1_ref, x2_ref), of_segment(g1_ref, g2_ref))
     hidden = own_ref.shape[-1]
     late_ref = outs[3]
     segment = pl.program_id(0)
@@ -343,12 +344,13 @@
     def _():
         out = contract(own_acts[0, :, 2 * hidden :], own_ref[0], NT)
         out = out + contract(peer_acts[0, :, 2 * hidden :], peer_ref[0], NT)
-        late_ref[...] = out.astype(BF16).reshape(x_ref.shape)
+        late_ref[...] = out.astype(BF16).reshape(late_ref.shape)
 
 
 def expert_sums(rows, grads, own_acts, peer_acts, own, peer):
-    sources, lines, width = rows.shape
-    segments, triple = (lines // RANK_ROWS, own.shape[-1])
+    sources, _, width = rows[0].shape
+    segments, triple = (SEGMENTS, own.shape[-1])
+    lines = segments * RANK_ROWS
     hidden = triple // 3
     count = sources * RANK_ROWS
     block = (sources, RANK_ROWS, width)
@@ -357,7 +359,7 @@
     return pl.pallas_call(
         expert_sums_kernel,
         grid=(segments,),
-        in_specs=[*segment_specs(block), act, act, down, down],
+        in_specs=[*segment_specs(block)[1:] * 2, act, act, down, down],
         out_specs=[pl.BlockSpec((1, width, triple), lambda s: (s, 0, 0))]
         + [pl.BlockSpec((1, width, hidden), lambda s: (s, 0, 0))] * 3
         + [pl.BlockSpec(block, lambda s: (0, jnp.maximum(s - EARLY, 0), 0))],
@@ -370,7 +372,7 @@
             bytes_accessed=6 * sources * lines * width + 5 * segments * width * triple,
             transcendentals=0,
         ),
-    )(rows, *grads, own_acts, peer_acts, own, peer)
+    )(*rows, *grads, own_acts, peer_acts, own, peer)
 
 
 def both_cores_kernel(own_ref, *refs):
@@ -612,14 +614,21 @@
         rows = rows.reshape(PLANE, -1, model_width)
         return lax.all_to_all(rows, "dp", 0, 0, tiled=True, axis_index_groups=plane_groups)
 
-    def grads_for(first, last):
-        shape = (PLANE, SEGMENTS * RANK_ROWS, -1)
-        part = pick.reshape(shape)[:, first * RANK_ROWS : last * RANK_ROWS].reshape(-1, tok_dev)
-        gate = slot_gate.reshape(shape)[:, first * RANK_ROWS : last * RANK_ROWS].reshape(-1, 1)
-        return (contract(part, out_grad, NN) * gate).astype(BF16)
-
-    grads_early = in_plane(grads_for(0, EARLY))
-    grads_late = grads_for(EARLY, SEGMENTS)
+    shape = (PLANE, SEGMENTS * RANK_ROWS, -1)
+    picks_of = tuple(
+        pick.reshape(shape)[:, first * RANK_ROWS : last * RANK_ROWS].reshape(-1, tok_dev)
+        for first, last in ((0, EARLY), (EARLY, SEGMENTS))
+    )
+    gates_of = tuple(
+        slot_gate.reshape(shape)[:, first * RANK_ROWS : last * RANK_ROWS].reshape(-1, 1)
+        for first, last in ((0, EARLY), (EARLY, SEGMENTS))
+    )
+
+    def grads_for(part):
+        return (contract(picks_of[part], out_grad, NN) * gates_of[part]).astype(BF16)
+
+    grads_early = in_plane(grads_for(0))
+    grads_late = grads_for(1)
 
     cosine, sine = rope_tables(tok_dev, dp_size)
     x_float = tokens.astype(F32)
@@ -644,12 +653,14 @@
     inverse2 = rms_scale(hidden1)
     normed2 = (hidden1 * inverse2 * norm2_gain).astype(BF16)
 
-    rows_out = contract(pick, normed2, NN).astype(BF16)
-    rows_out = after(rows_out, grad_rows[1])
-    own = after(own, rows_out)
+    rows_early, rows_late = (contract(part, normed2, NN).astype(BF16) for part in picks_of)
+    rows_early, rows_late, *_ = lax.optimization_barrier((rows_early, rows_late, grad_rows[1]))
+    rows_early = in_plane(rows_early)
+    own = after(own, rows_early)
     peer = swapped(own)
-    rows_in = in_plane(rows_out)
-    out_early = in_plane(expert_first(rows_in, own, peer))
+    rows_late = in_plane(after(rows_late, rows_early))
+    rows_in = (rows_early, rows_late)
+    out_early = in_plane(after(expert_first(rows_early, own, peer), rows_late))
     back, own_acts, peer_acts = expert_back(rows_in, grad_rows, own, peer)
 
     def combined(weights, rows):

time: 562 us -> 564 us (level)
  waiting for transfers between devices: 196 us -> 250 us
  blocking collectives: 69.9 us -> 24.1 us
  starting transfers between devices: 95.8 us -> 89.6 us
    all_to_all x1, blocking collectives: 69.9 us -> 24.1 us  [in_plane(): lax.all_to_all(rows, 'dp', 0, 0, tiled=True, axis_index_groups=plane_groups)]
    all_to_all x5 -> x6, waiting for transfers between devices: 20.3 us -> 51.3 us  [in_plane(): lax.all_to_all(rows, 'dp', 0, 0, tiled=True, axis_index_groups=plane_groups)]
    ppermute x8, waiting for transfers between devices: 14.7 us -> 24.8 us  [swapped(): return lax.ppermute(array, 'tensor', [(0, 1), (1, 0)])]
    all_to_all x5 -> x6, starting transfers between devices: 39.3 us -> 49.1 us  [in_plane(): lax.all_to_all(rows, 'dp', 0, 0, tiled=True, axis_index_groups=plane_groups)]
    psum x1, starting transfers between devices: 9.42 us -> 0.04 us  [shards(): summed = lax.psum(parts, 'dp')]
    ppermute x8, waiting for transfers between devices: 8.52 us -> 16 us  [passed_along(): lax.ppermute(value, 'dp', [(s, s + steps) for s in range(first, last)])]
    ppermute x8, starting transfers between devices: 27.1 us -> 20.4 us  [swapped(): return lax.ppermute(array, 'tensor', [(0, 1), (1, 0)])]
    dot_general x14 -> x15, matrix products: 24.4 us -> 24.6 us  [contract(): lax.dot_general(left, right, (dims, ((), ())), preferred_element_type=F32)]
  transfers between devices with their start and end apart: 24 -> 25, of which waited for: 12 -> 15; matrix products, arithmetic and copies ran while one was open for 11% -> 11% of each run, Pallas kernels for 16% -> 17%
where the time goes in v8:
time: 564 us; the launch traced here: 554 us
  waiting for transfers between devices  250 us (44%)
  Pallas kernels  107 us (19%)
  starting transfers between devices  89.6 us (16%)
  matrix products  24.6 us (4%)
  other arithmetic  24.4 us (4%)
  blocking collectives  24.1 us (4%)
  local copies, waits for them, and re-layouts  18.6 us (3%)
  between operations  15 us (3%)
    psum x1, waiting for transfers between devices, shards(): summed = lax.psum(parts, 'dp')  158 us
    all_to_all x6, waiting for transfers between devices, in_plane(): lax.all_to_all(rows, 'dp', 0, 0, tiled=True, axis_index_groups=plane_groups)  51.3 us
    all_to_all x6, starting transfers between devices, in_plane(): lax.all_to_all(rows, 'dp', 0, 0, tiled=True, axis_index_groups=plane_groups)  49.1 us
    ppermute x8, waiting for transfers between devices, swapped(): return lax.ppermute(array, 'tensor', [(0, 1), (1, 0)])  24.8 us
    dot_general x15, matrix products, contract(): lax.dot_general(left, right, (dims, ((), ())), preferred_element_type=F32)  24.6 us
    all_to_all x1, blocking collectives, in_plane(): lax.all_to_all(rows, 'dp', 0, 0, tiled=True, axis_index_groups=plane_groups)  24.1 us
    ppermute x8, starting transfers between devices, swapped(): return lax.ppermute(array, 'tensor', [(0, 1), (1, 0)])  20.4 us
    ppermute x8, starting transfers between devices, passed_along(): lax.ppermute(value, 'dp', [(s, s + steps) for s in range(first, last)])  20 us
  transfers between devices with their start and end apart: 25, of which 15 were waited for; matrix products, arithmetic and copies ran while one was open for 11% of the time, Pallas kernels for 17%

profile of v8, /device:TPU:1, one launch (start us, length us, event | category | flops | bytes accessed | tf_op | source)
XLA Modules:
  0.0 553.6 jit_solution(1489840088079477192)
XLA Ops:
  15.5 8.6 %all-to-all-start = ((bf16[16,32,1536]{2,1,0:T(8,128)(2,1)}), bf16[16,32,1536]{2,1,0:T(8,128)(2,1)}, u32[]{:S(2)}, u32[]{:S(2)}) async-start(bf16[16,32,1536]{2,1,0:T(8,128)(2,1)} %bitcast.91), calls=%async_computation | async-start | bytes 3145728 | tf_op jit(solution)/shard_map/all_to_all | solution.py:615
  55.7 15.7 %all-to-all-start.1 = ((bf16[16,64,1536]{2,1,0:T(8,128)(2,1)}), bf16[16,64,1536]{2,1,0:T(8,128)(2,1)}, u32[]{:S(2)}, u32[]{:S(2)}) async-start(bf16[16,64,1536]{2,1,0:T(8,128)(2,1)} %bitcast.93), calls=%async_computation.1 | async-start | bytes 6291456 | tf_op jit(solution)/shard_map/all_to_all | solution.py:615
  71.4 11.4 %shard_map.299 = (bf16[768,256]{1,0:T(8,128)(2,1)S(1)}, f32[12,256]{1,0:T(8,128)S(1)}, f32[12,256]{1,0:T(8,128)S(1)}) custom-call(bf16[768,256]{1,0:T(8,128)(2,1)S(1)} %bitcast.82, bf16[528,256]{1,0:T(8,128)(2,1)S(1)} %collective-permute-done.k4, bf16[528,256]{1,0:T(8,128)(2,1)} %collective-permute-done.1.k3, bf16[528,256]{1,0:T(8,128)(2,1)} %collective-permute-done.2.k2, ...), custom_call_target="tpu_custom_call" | custom-call | flops 1006632960 | bytes 2138112 | tf_op jit(solution)/shard_map/pallas_call | solution.py:126
  93.8 14.8 %all-to-all-done.1.g2_ref = bf16[16,64,1536]{2,1,0:T(8,128)(2,1)} async-done(((bf16[16,64,1536]{2,1,0:T(8,128)(2,1)}), bf16[16,64,1536]{2,1,0:T(8,128)(2,1)}, u32[]{:S(2)}, u32[]{:S(2)}) %all-to-all-start.1) | async-done | bytes 3145760 | tf_op jit(solution)/shard_map/all_to_all | solution.py:615
  108.6 24.1 %all_to_all.35.x1_ref.x_ref = bf16[16,32,1536]{2,1,0:T(8,128)(2,1)} all-to-all(bf16[16,32,1536]{2,1,0:T(8,128)(2,1)} %bitcast.89), channel_id=1, replica_groups={{0,2,4,6,8,10,12,14,16,18,20,22,24,26,28,30},{32,34,36,38,40,42,44,46,4..., dimensions={0} | all-to-all | bytes 3145728 | tf_op jit(solution)/shard_map/all_to_all | solution.py:615
  132.7 5.7 %collective-permute-start.5 = (bf16[4,1536,768]{2,1,0:T(8,128)(2,1)}, bf16[4,1536,768]{2,1,0:T(8,128)(2,1)}, u32[]{:S(2)}, u32[]{:S(2)}) collective-permute-start(bf16[4,1536,768]{2,1,0:T(8,128)(2,1)} %bitcast.85), channel_id=1, source_target_pairs={{0,1},{1,0},{2,3},{3,2},{4,5},{5,4},{6,7},{7,6},{8,9},{9,8},{10,11... | collective-permute-start | bytes 28311560 | tf_op jit(solution)/shard_map/ppermute | solution.py:41
  142.9 10.1 %collective-permute-done.5.peer_ref = bf16[4,1536,768]{2,1,0:T(8,128)(2,1)} collective-permute-done((bf16[4,1536,768]{2,1,0:T(8,128)(2,1)}, bf16[4,1536,768]{2,1,0:T(8,128)(2,1)}, u32[]{:S(2)}, u32[]{:S(2)}) %collective-permute-start.5) | collective-permute-done | bytes 9437216 | tf_op jit(solution)/shard_map/ppermute | solution.py:41
  153.1 6.5 %shard_map.302 = bf16[16,32,1536]{2,1,0:T(8,128)(2,1)} custom-call(bf16[16,32,1536]{2,1,0:T(8,128)(2,1)} %all_to_all.35.x1_ref.x_ref, bf16[4,1536,768]{2,1,0:T(8,128)(2,1)} %bitcast.86, bf16[4,1536,768]{2,1,0:T(8,128)(2,1)} %collective-permute-done.5.peer_ref), custom_call_target="tpu_custom_call" | custom-call | flops 2415919104 | bytes 7864320 | tf_op jit(solution)/shard_map/pallas_call | solution.py:249
  159.6 26.1 %all-to-all-done.3.x2_ref = bf16[16,64,1536]{2,1,0:T(8,128)(2,1)} async-done(((bf16[16,64,1536]{2,1,0:T(8,128)(2,1)}), bf16[16,64,1536]{2,1,0:T(8,128)(2,1)}, u32[]{:S(2)}, u32[]{:S(2)}) %all-to-all-start.3) | async-done | bytes 3145760 | tf_op jit(solution)/shard_map/all_to_all | solution.py:615
  185.7 10.6 %all-to-all-start.4 = ((bf16[16,32,1536]{2,1,0:T(8,128)(2,1)}), bf16[16,32,1536]{2,1,0:T(8,128)(2,1)}, u32[]{:S(2)}, u32[]{:S(2)}) async-start(bf16[16,32,1536]{2,1,0:T(8,128)(2,1)} %shard_map.302), calls=%async_computation.4 | async-start | bytes 3145728 | tf_op jit(solution)/shard_map/all_to_all | solution.py:615
  196.2 18.9 %shard_map.301 = (bf16[16,96,1536]{2,1,0:T(8,128)(2,1)}, bf16[3,512,768]{2,1,0:T(8,128)(2,1)}, bf16[3,512,768]{2,1,0:T(8,128)(2,1)}) custom-call(bf16[16,32,1536]{2,1,0:T(8,128)(2,1)} %all_to_all.35.x1_ref.x_ref, bf16[16,64,1536]{2,1,0:T(8,128)(2,1)} %all-to-all-done.3.x2_ref, bf16[16,32,1536]{2,1,0:T(8,128)(2,1)} %all-to-all-done.g1_ref, ...), custom_call_target="tpu_custom_call" | custom-call | flops 12683575296 | bytes 28311552 | tf_op jit(solution)/shard_map/pallas_call | solution.py:306
  216.8 5.2 all-to-all-start.5
  222.1 17.3 %shard_map.303 = (bf16[3,1536,768]{2,1,0:T(8,128)(2,1)}, bf16[3,1536,256]{2,1,0:T(8,128)(2,1)}, bf16[3,1536,256]{2,1,0:T(8,128)(2,1)}, bf16[3,1536,256]{2,1,0:T(8,128)(2,1)}, bf16[16,64,1536]{2,1,0:T(8,128)(2,1)}) custom-call(bf16[16,32,1536]{2,1,0:T(8,128)(2,1)} %all_to_all.35.x1_ref.x_ref, bf16[16,64,1536]{2,1,0:T(8,128)(2,1)} %all-to-all-done.3.x2_ref, ...), custom_call_target="tpu_custom_call" | custom-call | flops 10871635968 | bytes 31850496 | tf_op jit(solution)/shard_map/pallas_call | solution.py:359
  254.2 11.8 %shard_map.304 = bf16[4,1536,768]{2,1,0:T(8,128)(2,1)} custom-call(bf16[3,1536,768]{2,1,0:T(8,128)(2,1)} %get-tuple-element.79.own_ref, bf16[3,1536,256]{2,1,0:T(8,128)(2,1)} %collective-permute-done.6.refs_0_, bf16[3,1536,256]{2,1,0:T(8,128)(2,1)} %collective-permute-done.7.refs_1_, bf16[3,1536,256]{2,1,0:T(8,128)(2,1)} %collective-permute-done.8.refs_2_), custom_call_target="tpu_custom_call" | custom-call | flops 4718592 | bytes 28311552 | tf_op jit(solution)/shard_map/pallas_call | solution.py:400
  267.9 8.7 %all-to-all-done.5 = bf16[16,96,1536]{2,1,0:T(8,128)(2,1)} async-done(((bf16[16,96,1536]{2,1,0:T(8,128)(2,1)}), bf16[16,96,1536]{2,1,0:T(8,128)(2,1)}, u32[]{:S(2)}, u32[]{:S(2)}) %all-to-all-start.5) | async-done | bytes 4718624 | tf_op jit(solution)/shard_map/all_to_all | solution.py:615
  276.6 5.2 convolution_convert_fusion.2
  281.8 7.4 %collective-permute-start.9 = (bf16[256,1536]{1,0:T(8,128)(2,1)}, bf16[256,1536]{1,0:T(8,128)(2,1)}, u32[]{:S(2)}, u32[]{:S(2)}) collective-permute-start(bf16[256,1536]{1,0:T(8,128)(2,1)} %convolution_convert_fusion.2), channel_id=1, source_target_pairs={{0,1},{1,0},{2,3},{3,2},{4,5},{5,4},{6,7},{7,6},{8,9},{9,8},{10,11... | collective-permute-start | bytes 2359304 | tf_op jit(solution)/shard_map/ppermute | solution.py:41
  300.5 15.7 %shard_map.305 = (bf16[768,256]{1,0:T(8,128)(2,1)S(1)}, bf16[512,256]{1,0:T(8,128)(2,1)S(1)}, bf16[512,256]{1,0:T(8,128)(2,1)S(1)}, bf16[512,256]{1,0:T(8,128)(2...) custom-call(bf16[768,256]{1,0:T(8,128)(2,1)S(1)} %bitcast.83, bf16[768,256]{1,0:T(8,128)(2,1)S(1)} %fusion.13.g_ref, ...), custom_call_target="tpu_custom_call" | custom-call | flops 125829120000 | bytes 3883008 | tf_op jit(solution)/shard_map/pallas_call | solution.py:189
  323.5 6.8 %shard_map.306._ = bf16[1536,2304]{1,0:T(8,128)(2,1)} custom-call(bf16[256,1536]{1,0:T(8,128)(2,1)} %copy-done.7, bf16[768,256]{1,0:T(8,128)(2,1)} %copy-done.3, bf16[768,256]{1,0:T(8,128)(2,1)} %copy-done.2, bf16[256,1536]{1,0:T(8,128)(2,1)} %copy-done.15), custom_call_target="tpu_custom_call" | custom-call | flops 1207959552 | bytes 4718592 | tf_op jit(solution)/shard_map/pallas_call | solution.py:429
  330.2 6.3 %collective-permute-done.10 = bf16[512,256]{1,0:T(8,128)(2,1)S(1)} collective-permute-done((bf16[512,256]{1,0:T(8,128)(2,1)S(1)}, bf16[512,256]{1,0:T(8,128)(2,1)S(1)}, u32[]{:S(2)}, u32[]{:S(2)}) %collective-permute-start.10) | collective-permute-done | bytes 262176 | tf_op jit(solution)/shard_map/ppermute | solution.py:51
  336.5 8.7 %collective-permute-done.11 = bf16[512,256]{1,0:T(8,128)(2,1)S(1)} collective-permute-done((bf16[512,256]{1,0:T(8,128)(2,1)S(1)}, bf16[512,256]{1,0:T(8,128)(2,1)S(1)}, u32[]{:S(2)}, u32[]{:S(2)}) %collective-permute-start.11) | collective-permute-done | bytes 262176 | tf_op jit(solution)/shard_map/ppermute | solution.py:51
  354.4 5.7 %shard_map.307 = bf16[1536,2304]{1,0:T(8,128)(2,1)} custom-call(bf16[256,1536]{1,0:T(8,128)(2,1)} %copy-done.7, bf16[512,256]{1,0:T(8,128)(2,1)} %pad_maximum_fusion.1.kv_ref, f32[128,1536]{1,0:T(8,128)} %select_maximum_fusion.extra_ref, bf16[1536,2304]{1,0:T(8,128)(2,1)} %shard_map.306._), custom_call_target="tpu_custom_call", output_to_operand_aliasing={{}: (3, {})} | custom-call | flops 402653184 | bytes 2359296 | tf_op jit(solution)/shard_map/pallas_call | solution.py:451
  377.0 157.9 %all-reduce.3.cloned.1.call-done.in_ref = bf16[1536,2304]{1,0:T(8,128)(2,1)} async-done(((bf16[1536,2304]{1,0:T(8,128)(2,1)}), bf16[1536,2304]{1,0:T(8,128)(2,1)}) %all-reduce.3.cloned.1.call-update) | async-done | bytes 7077904 | tf_op jit(solution)/shard_map/psum | solution.py:718
  534.9 10.2 %shard_map.308 = (f32[768,1536]{1,0:T(8,128)}, f32[1536,768]{1,0:T(8,128)}, f32[1536,256]{1,0:T(8,128)}, f32[1536,256]{1,0:T(8,128)}, f32[8,1536]{1,0:T(8,128)},...) custom-call(bf16[1536,2304]{1,0:T(8,128)(2,1)} %all-reduce.3.cloned.1.call-done.in_ref, ...), custom_call_target="tpu_custom_call" | custom-call | flops 3538944 | bytes 28311552 | tf_op jit(solution)/shard_map/pallas_call | solution.py:514
  (215 shorter events, 119.1 us)
Async XLA Ops:
  7.2 125.5 %all-gather.3.cloned.1.call-start = ((), (), s32[]{:S(2)}) async-start(), calls=%async_computation.10 | async-start | bytes 11796480 | tf_op jit(solution)/shard_map/all_gather | solution.py:648
  15.5 40.1 %all-to-all-start = ((bf16[16,32,1536]{2,1,0:T(8,128)(2,1)}), bf16[16,32,1536]{2,1,0:T(8,128)(2,1)}, u32[]{:S(2)}, u32[]{:S(2)}) async-start(bf16[16,32,1536]{2,1,0:T(8,128)(2,1)} %bitcast.91), calls=%async_computation | async-start | bytes 3145728 | tf_op jit(solution)/shard_map/all_to_all | solution.py:615
  28.9 25.8 %collective-permute-start = (bf16[528,256]{1,0:T(8,128)(2,1)S(1)}, bf16[528,256]{1,0:T(8,128)(2,1)S(1)}, u32[]{:S(2)}, u32[]{:S(2)}) collective-permute-start(bf16[528,256]{1,0:T(8,128)(2,1)S(1)} %concatenate.31.k0), channel_id=1, source_target_pairs={{0,8},{2,10},{4,12},{6,14},{8,16},{10,18},{12,20},{14,22},{16,24},... | collective-permute-start | bytes 811016 | tf_op jit(solution)/shard_map/ppermute | solution.py:51
  32.1 23.4 %collective-permute-start.1 = (bf16[528,256]{1,0:T(8,128)(2,1)S(1)}, bf16[528,256]{1,0:T(8,128)(2,1)}, u32[]{:S(2)}, u32[]{:S(2)}) collective-permute-start(bf16[528,256]{1,0:T(8,128)(2,1)S(1)} %concatenate.31.k0), channel_id=1, source_target_pairs={{0,6},{2,8},{4,10},{6,12},{8,14},{10,16},{12,18},{14,20},{16,22},{... | collective-permute-start | bytes 811016 | tf_op jit(solution)/shard_map/ppermute | solution.py:51
  37.1 18.5 %collective-permute-start.2 = (bf16[528,256]{1,0:T(8,128)(2,1)S(1)}, bf16[528,256]{1,0:T(8,128)(2,1)}, u32[]{:S(2)}, u32[]{:S(2)}) collective-permute-start(bf16[528,256]{1,0:T(8,128)(2,1)S(1)} %concatenate.31.k0), channel_id=1, source_target_pairs={{0,4},{2,6},{4,8},{6,10},{8,12},{10,14},{12,16},{14,18},{16,20},{1... | collective-permute-start | bytes 811016 | tf_op jit(solution)/shard_map/ppermute | solution.py:51
  41.1 14.5 %collective-permute-start.3 = (bf16[528,256]{1,0:T(8,128)(2,1)S(1)}, bf16[528,256]{1,0:T(8,128)(2,1)}, u32[]{:S(2)}, u32[]{:S(2)}) collective-permute-start(bf16[528,256]{1,0:T(8,128)(2,1)S(1)} %concatenate.31.k0), channel_id=1, source_target_pairs={{0,2},{2,4},{4,6},{6,8},{8,10},{10,12},{12,14},{14,16},{16,18},{18... | collective-permute-start | bytes 811016 | tf_op jit(solution)/shard_map/ppermute | solution.py:51
  55.7 53.0 %all-to-all-start.1 = ((bf16[16,64,1536]{2,1,0:T(8,128)(2,1)}), bf16[16,64,1536]{2,1,0:T(8,128)(2,1)}, u32[]{:S(2)}, u32[]{:S(2)}) async-start(bf16[16,64,1536]{2,1,0:T(8,128)(2,1)} %bitcast.93), calls=%async_computation.1 | async-start | bytes 6291456 | tf_op jit(solution)/shard_map/all_to_all | solution.py:615
  83.7 5.1 collective-permute-start.4
  132.7 20.4 %collective-permute-start.5 = (bf16[4,1536,768]{2,1,0:T(8,128)(2,1)}, bf16[4,1536,768]{2,1,0:T(8,128)(2,1)}, u32[]{:S(2)}, u32[]{:S(2)}) collective-permute-start(bf16[4,1536,768]{2,1,0:T(8,128)(2,1)} %bitcast.85), channel_id=1, source_target_pairs={{0,1},{1,0},{2,3},{3,2},{4,5},{5,4},{6,7},{7,6},{8,9},{9,8},{10,11... | collective-permute-start | bytes 28311560 | tf_op jit(solution)/shard_map/ppermute | solution.py:41
  138.4 47.2 %all-to-all-start.3 = ((bf16[16,64,1536]{2,1,0:T(8,128)(2,1)}), bf16[16,64,1536]{2,1,0:T(8,128)(2,1)}, u32[]{:S(2)}, u32[]{:S(2)}) async-start(bf16[16,64,1536]{2,1,0:T(8,128)(2,1)} %bitcast.84), calls=%async_computation.3 | async-start | bytes 6291456 | tf_op jit(solution)/shard_map/all_to_all | solution.py:615
  185.7 31.2 %all-to-all-start.4 = ((bf16[16,32,1536]{2,1,0:T(8,128)(2,1)}), bf16[16,32,1536]{2,1,0:T(8,128)(2,1)}, u32[]{:S(2)}, u32[]{:S(2)}) async-start(bf16[16,32,1536]{2,1,0:T(8,128)(2,1)} %shard_map.302), calls=%async_computation.4 | async-start | bytes 3145728 | tf_op jit(solution)/shard_map/all_to_all | solution.py:615
  216.8 59.8 %all-to-all-start.5 = ((bf16[16,96,1536]{2,1,0:T(8,128)(2,1)}), bf16[16,96,1536]{2,1,0:T(8,128)(2,1)}, u32[]{:S(2)}, u32[]{:S(2)}) async-start(bf16[16,96,1536]{2,1,0:T(8,128)(2,1)} %get-tuple-element.76), calls=%async_computation.5 | async-start | bytes 9437184 | tf_op jit(solution)/shard_map/all_to_all | solution.py:615
  222.0 138.1 %reduce-scatter.2.cloned.1.call-start = ((), (), s32[]{:S(2)}) async-start(), calls=%async_computation.8 | async-start | bytes 11796480 | tf_op jit(solution)/shard_map/reduce_scatter | solution.py:675
  239.4 8.1 %collective-permute-start.6 = (bf16[3,1536,256]{2,1,0:T(8,128)(2,1)}, bf16[3,1536,256]{2,1,0:T(8,128)(2,1)}, u32[]{:S(2)}, u32[]{:S(2)}) collective-permute-start(bf16[3,1536,256]{2,1,0:T(8,128)(2,1)} %get-tuple-element.80), channel_id=1, source_target_pairs={{0,1},{1,0},{2,3},{3,2},{4,5},{5,4},{6,7},{7,6},{8,9},{9,8},{10,11... | collective-permute-start | bytes 7077896 | tf_op jit(solution)/shard_map/ppermute | solution.py:41
  243.0 7.9 %collective-permute-start.7 = (bf16[3,1536,256]{2,1,0:T(8,128)(2,1)}, bf16[3,1536,256]{2,1,0:T(8,128)(2,1)}, u32[]{:S(2)}, u32[]{:S(2)}) collective-permute-start(bf16[3,1536,256]{2,1,0:T(8,128)(2,1)} %get-tuple-element.81), channel_id=1, source_target_pairs={{0,1},{1,0},{2,3},{3,2},{4,5},{5,4},{6,7},{7,6},{8,9},{9,8},{10,11... | collective-permute-start | bytes 7077896 | tf_op jit(solution)/shard_map/ppermute | solution.py:41
  243.1 11.2 %collective-permute-start.8 = (bf16[3,1536,256]{2,1,0:T(8,128)(2,1)}, bf16[3,1536,256]{2,1,0:T(8,128)(2,1)}, u32[]{:S(2)}, u32[]{:S(2)}) collective-permute-start(bf16[3,1536,256]{2,1,0:T(8,128)(2,1)} %get-tuple-element.82), channel_id=1, source_target_pairs={{0,1},{1,0},{2,3},{3,2},{4,5},{5,4},{6,7},{7,6},{8,9},{9,8},{10,11... | collective-permute-start | bytes 7077896 | tf_op jit(solution)/shard_map/ppermute | solution.py:41
  281.8 12.1 %collective-permute-start.9 = (bf16[256,1536]{1,0:T(8,128)(2,1)}, bf16[256,1536]{1,0:T(8,128)(2,1)}, u32[]{:S(2)}, u32[]{:S(2)}) collective-permute-start(bf16[256,1536]{1,0:T(8,128)(2,1)} %convolution_convert_fusion.2), channel_id=1, source_target_pairs={{0,1},{1,0},{2,3},{3,2},{4,5},{5,4},{6,7},{7,6},{8,9},{9,8},{10,11... | collective-permute-start | bytes 2359304 | tf_op jit(solution)/shard_map/ppermute | solution.py:41
  289.3 70.8 %all-to-all-start.6 = ((bf16[16,64,1536]{2,1,0:T(8,128)(2,1)}), bf16[16,64,1536]{2,1,0:T(8,128)(2,1)}, u32[]{:S(2)}, u32[]{:S(2)}) async-start(bf16[16,64,1536]{2,1,0:T(8,128)(2,1)} %get-tuple-element.97), calls=%async_computation.7 | async-start | bytes 6291456 | tf_op jit(solution)/shard_map/all_to_all | solution.py:615
  293.8 241.1 %all-reduce.3.cloned.1.call-start = ((), (), s32[]{:S(2)}) async-start(), calls=%async_computation.9 | async-start | bytes 14155776 | tf_op jit(solution)/shard_map/psum | solution.py:718
  316.3 20.2 %collective-permute-start.10 = (bf16[512,256]{1,0:T(8,128)(2,1)S(1)}, bf16[512,256]{1,0:T(8,128)(2,1)S(1)}, u32[]{:S(2)}, u32[]{:S(2)}) collective-permute-start(bf16[512,256]{1,0:T(8,128)(2,1)S(1)} %get-tuple-element.86), channel_id=1, source_target_pairs={{8,0},{10,2},{12,4},{14,6},{16,8},{18,10},{20,12},{22,14},{24,16},... | collective-permute-start | bytes 786440 | tf_op jit(solution)/shard_map/ppermute | solution.py:51
  317.6 27.7 %collective-permute-start.11 = (bf16[512,256]{1,0:T(8,128)(2,1)S(1)}, bf16[512,256]{1,0:T(8,128)(2,1)S(1)}, u32[]{:S(2)}, u32[]{:S(2)}) collective-permute-start(bf16[512,256]{1,0:T(8,128)(2,1)S(1)} %get-tuple-element.87), channel_id=1, source_target_pairs={{6,0},{8,2},{10,4},{12,6},{14,8},{16,10},{18,12},{20,14},{22,16},{... | collective-permute-start | bytes 786440 | tf_op jit(solution)/shard_map/ppermute | solution.py:51
  318.9 26.4 %collective-permute-start.12 = (bf16[512,256]{1,0:T(8,128)(2,1)S(1)}, bf16[512,256]{1,0:T(8,128)(2,1)S(1)}, u32[]{:S(2)}, u32[]{:S(2)}) collective-permute-start(bf16[512,256]{1,0:T(8,128)(2,1)S(1)} %get-tuple-element.88), channel_id=1, source_target_pairs={{4,0},{6,2},{8,4},{10,6},{12,8},{14,10},{16,12},{18,14},{20,16},{2... | collective-permute-start | bytes 786440 | tf_op jit(solution)/shard_map/ppermute | solution.py:51
  320.2 25.1 %collective-permute-start.13 = (bf16[512,256]{1,0:T(8,128)(2,1)S(1)}, bf16[512,256]{1,0:T(8,128)(2,1)S(1)}, u32[]{:S(2)}, u32[]{:S(2)}) collective-permute-start(bf16[512,256]{1,0:T(8,128)(2,1)S(1)} %get-tuple-element.89), channel_id=1, source_target_pairs={{2,0},{4,2},{6,4},{8,6},{10,8},{12,10},{14,12},{16,14},{18,16},{20... | collective-permute-start | bytes 786440 | tf_op jit(solution)/shard_map/ppermute | solution.py:51
  368.6 6.1 %collective-permute-start.15 = (bf16[256,1536]{1,0:T(8,128)(2,1)S(1)}, bf16[256,1536]{1,0:T(8,128)(2,1)}, u32[]{:S(2)}, u32[]{:S(2)}) collective-permute-start(bf16[256,1536]{1,0:T(8,128)(2,1)S(1)} %convolution_convert_fusion.3), channel_id=1, source_target_pairs={{0,1},{1,0},{2,3},{3,2},{4,5},{5,4},{6,7},{7,6},{8,9},{9,8},{10,11... | collective-permute-start | bytes 2359304 | tf_op jit(solution)/shard_map/ppermute | solution.py:41
  (49 other events, 513.6 us)
Sparse Core Ops, SparseCore 0:
  10.4 97.0 all-gather.2
  266.2 92.5 reduce-scatter.1
  363.7 171.1 all-reduce.2

commit v9 on v7

--- a/solution.py
+++ b/solution.py
@@ -100,24 +100,22 @@
     fill_bias(blocks, bias)
     kv_rows = (k0.shape[0] - AUX) // 2
 
-    def one_group(g, _):
-        at = pl.multiple_of(g * HD, HD)
+    def one_head(head, _):
+        at = pl.multiple_of(head // group * HD, HD)
         keys = all_keys(blocks, at)
         values = all_keys(blocks, kv_rows + at)
-        for j in range(group):
-            head = g * group + j
-            here = pl.ds(pl.multiple_of(head * HD, HD), HD)
-            scores = contract(keys, q_ref[here, :], TN) + bias[...]
-            peak = jnp.max(scores, axis=0, keepdims=True)
-            weight = jnp.exp(scores - peak)
-            total = jnp.sum(weight, axis=0, keepdims=True)
-            mixed = contract(values, weight.astype(BF16), NN) * (1.0 / total)
-            out_ref[here, :] = mixed.astype(BF16)
-            log_ref[pl.ds(head, 1), :] = peak + jnp.log(total)
-            peak_ref[pl.ds(head, 1), :] = peak
+        here = pl.ds(pl.multiple_of(head * HD, HD), HD)
+        scores = contract(keys, q_ref[here, :], TN) + bias[...]
+        peak = jnp.max(scores, axis=0, keepdims=True)
+        weight = jnp.exp(scores - peak)
+        total = jnp.sum(weight, axis=0, keepdims=True)
+        mixed = contract(values, weight.astype(BF16), NN) * (1.0 / total)
+        out_ref[here, :] = mixed.astype(BF16)
+        log_ref[pl.ds(head, 1), :] = peak + jnp.log(total)
+        peak_ref[pl.ds(head, 1), :] = peak
         return 0
 
-    lax.fori_loop(0, kv_rows // HD, one_group, 0)
+    lax.fori_loop(0, group * kv_rows // HD, one_head, 0)
 
 
 def attend(q, blocks, group):
@@ -155,9 +153,8 @@
         at = pl.multiple_of(g * HD, HD)
         keys = all_keys(blocks, at)
         values = all_keys(blocks, kv_rows + at)
-        key_sum = value_sum = None
-        for j in range(group):
-            head = g * group + j
+
+        def one_head(head, sums):
             start = pl.multiple_of(head * HD, HD)
             query, grad = (q_ref[pl.ds(start, HD), :], g_ref[pl.ds(start, HD), :])
             scores = contract(keys, query, TN) + bias[...]
@@ -165,15 +162,18 @@
             grad_probs = contract(values, grad, TN)
             delta = jnp.sum(probs * grad_probs, axis=0, keepdims=True)
             grad_scores = (probs * (grad_probs - delta)).astype(BF16)
-            key_part = contract(query, grad_scores, NT)
-            value_part = contract(grad, probs.astype(BF16), NT)
-            key_sum = key_part if key_sum is None else key_sum + key_part
-            value_sum = value_part if value_sum is None else value_sum + value_part
             turned = contract(keys, grad_scores, NN) * (HD**-0.5)
             first, second = (turned[:half], turned[half:])
             cosine, sine = (cos_ref[...], sin_ref[...])
             dq_ref[pl.ds(start, half), :] = (first * cosine + second * sine).astype(BF16)
             dq_ref[pl.ds(start + half, half), :] = (second * cosine - first * sine).astype(BF16)
+            return (
+                sums[0] + contract(query, grad_scores, NT),
+                sums[1] + contract(grad, probs.astype(BF16), NT),
+            )
+
+        zero = jnp.zeros(keys.shape, F32)
+        key_sum, value_sum = lax.fori_loop(g * group, (g + 1) * group, one_head, (zero, zero))
         for number, grad_ref in enumerate(grads):
             piece = slice(number * tok, (number + 1) * tok)
             grad_ref[pl.ds(at, HD), :] = key_sum[:, piece].astype(grad_ref.dtype)
@@ -261,30 +261,39 @@
     )(rows, own, peer)
 
 
-def of_segment(early_ref, late_ref):
-    width = early_ref.shape[-1]
-    chosen = jnp.where(pl.program_id(0) < EARLY, early_ref[...], late_ref[...])
-    return chosen.reshape(-1, width)
+def of_segment(early_ref, late_ref, sources=slice(None), lanes=slice(None)):
+    early, late = (ref[sources, :, lanes] for ref in (early_ref, late_ref))
+    chosen = jnp.where(pl.program_id(0) < EARLY, early, late)
+    return chosen.reshape(-1, chosen.shape[-1])
 
 
 def expert_kernel(x_ref, g1_ref, g2_ref, own_ref, peer_ref, dx_ref, own_acts, peer_acts):
-    width = x_ref.shape[-1]
-    rows, grads = (x_ref[...].reshape(-1, width), of_segment(g1_ref, g2_ref))
     hidden = own_ref.shape[-1] // 3
-    back = None
-    for weights, acts in ((own_ref, own_acts), (peer_ref, peer_acts)):
-        both = contract(rows, weights[0, :, : 2 * hidden], NN)
-        grad_inner = contract(grads, weights[0, :, 2 * hidden :], NN)
-        gate_act, up_act = (both[:, :hidden], both[:, hidden:])
-        sigmoid = 1.0 / (1.0 + jnp.exp(-gate_act))
-        silu = gate_act * sigmoid
-        dgate = grad_inner * up_act * (sigmoid * (1.0 + gate_act * (1.0 - sigmoid)))
-        acts[0, :, :hidden] = dgate.astype(BF16)
-        acts[0, :, hidden : 2 * hidden] = (grad_inner * silu).astype(BF16)
-        acts[0, :, 2 * hidden :] = (silu * up_act).astype(BF16)
-        part = contract(acts[0, :, : 2 * hidden], weights[0, :, : 2 * hidden], NT)
-        back = part if back is None else back + part
-    dx_ref[...] = back.astype(BF16).reshape(dx_ref.shape)
+    sources = x_ref.shape[0] // 2
+    count = sources * RANK_ROWS
+
+    def one_half(half, _):
+        here = pl.ds(half * sources, sources)
+        there = pl.ds(pl.multiple_of(half * count, count), count)
+        rows = x_ref[here].reshape(count, -1)
+        grads = of_segment(g1_ref, g2_ref, here)
+        back = None
+        for weights, acts in ((own_ref, own_acts), (peer_ref, peer_acts)):
+            both = contract(rows, weights[0, :, : 2 * hidden], NN)
+            grad_inner = contract(grads, weights[0, :, 2 * hidden :], NN)
+            gate_act, up_act = (both[:, :hidden], both[:, hidden:])
+            sigmoid = 1.0 / (1.0 + jnp.exp(-gate_act))
+            silu = gate_act * sigmoid
+            dgate = grad_inner * up_act * (sigmoid * (1.0 + gate_act * (1.0 - sigmoid)))
+            acts[0, there, :hidden] = dgate.astype(BF16)
+            acts[0, there, hidden : 2 * hidden] = (grad_inner * silu).astype(BF16)
+            acts[0, there, 2 * hidden :] = (silu * up_act).astype(BF16)
+            part = contract(acts[0, there, : 2 * hidden], weights[0, :, : 2 * hidden], NT)
+            back = part if back is None else back + part
+        dx_ref[here] = back.astype(BF16).reshape(sources, RANK_ROWS, -1)
+        return 0
+
+    lax.fori_loop(0, 2, one_half, 0)
 
 
 def segment_specs(block):
@@ -324,26 +333,40 @@
 
 def expert_sums_kernel(x_ref, g1_ref, g2_ref, own_acts, peer_acts, own_ref, peer_ref, sum_own, *outs):
     width = x_ref.shape[-1]
-    rows, grads = (x_ref[...].reshape(-1, width), of_segment(g1_ref, g2_ref))
     hidden = own_ref.shape[-1]
     late_ref = outs[3]
-    segment = pl.program_id(0)
-    for side, acts in enumerate((own_acts, peer_acts)):
-        first = contract(rows, acts[0, :, : 2 * hidden], TN).astype(BF16)
-        second = contract(grads, acts[0, :, 2 * hidden :], TN).astype(BF16)
-        if side == 0:
-            sum_own[0, :, : 2 * hidden] = first
-            sum_own[0, :, 2 * hidden :] = second
-        else:
-            outs[0][0] = first[:, :hidden]
-            outs[1][0] = first[:, hidden:]
-            outs[2][0] = second
-
-    @pl.when(segment >= EARLY)
+    chunk = width // 3
+
+    def one_chunk(c, _):
+        lanes = pl.ds(pl.multiple_of(c * chunk, chunk), chunk)
+        rows = x_ref[:, :, lanes].reshape(-1, chunk)
+        grads = of_segment(g1_ref, g2_ref, slice(None), lanes)
+        for side, acts in enumerate((own_acts, peer_acts)):
+            first = contract(rows, acts[0, :, : 2 * hidden], TN).astype(BF16)
+            second = contract(grads, acts[0, :, 2 * hidden :], TN).astype(BF16)
+            if side == 0:
+                sum_own[0, lanes, : 2 * hidden] = first
+                sum_own[0, lanes, 2 * hidden :] = second
+            else:
+                outs[0][0, lanes, :] = first[:, :hidden]
+                outs[1][0, lanes, :] = first[:, hidden:]
+                outs[2][0, lanes, :] = second
+        return 0
+
+    lax.fori_loop(0, 3, one_chunk, 0)
+    sources = x_ref.shape[0] // 2
+    count = sources * RANK_ROWS
+
+    def one_half(half, _):
+        there = pl.ds(pl.multiple_of(half * count, count), count)
+        out = contract(own_acts[0, there, 2 * hidden :], own_ref[0], NT)
+        out = out + contract(peer_acts[0, there, 2 * hidden :], peer_ref[0], NT)
+        late_ref[pl.ds(half * sources, sources)] = out.astype(BF16).reshape(sources, RANK_ROWS, -1)
+        return 0
+
+    @pl.when(pl.program_id(0) >= EARLY)
     def _():
-        out = contract(own_acts[0, :, 2 * hidden :], own_ref[0], NT)
-        out = out + contract(peer_acts[0, :, 2 * hidden :], peer_ref[0], NT)
-        late_ref[...] = out.astype(BF16).reshape(x_ref.shape)
+        lax.fori_loop(0, 2, one_half, 0)
 
 
 def expert_sums(rows, grads, own_acts, peer_acts, own, peer):

time: 562 us -> 554 us (0.986); the launches traced: 552 us -> 552 us
  starting transfers between devices: 95.8 us -> 78.8 us
  waiting for transfers between devices: 196 us -> 207 us
  Pallas kernels: 106 us -> 113 us
    psum x1, starting transfers between devices: 9.42 us -> 0.04 us  [shards(): summed = lax.psum(parts, 'dp')]
    ppermute x8, starting transfers between devices: 27.1 us -> 19.3 us  [swapped(): return lax.ppermute(array, 'tensor', [(0, 1), (1, 0)])]
  transfers between devices with their start and end apart: 24 -> 24, of which waited for: 12 -> 13; matrix products, arithmetic and copies ran while one was open for 11% -> 11% of each run, Pallas kernels for 16% -> 17%
where the time goes in v9:
time: 554 us; the launch traced here: 552 us
  waiting for transfers between devices  207 us (37%)
  Pallas kernels  113 us (20%)
  starting transfers between devices  78.8 us (14%)
  blocking collectives  69.9 us (13%)
  other arithmetic  26.7 us (5%)
  matrix products  24.4 us (4%)
  local copies, waits for them, and re-layouts  18.2 us (3%)
  between operations  14.5 us (3%)
    psum x1, waiting for transfers between devices, shards(): summed = lax.psum(parts, 'dp')  156 us
    all_to_all x1, blocking collectives, in_plane(): lax.all_to_all(rows, 'dp', 0, 0, tiled=True, axis_index_groups=plane_groups)  69.9 us
    all_to_all x5, starting transfers between devices, in_plane(): lax.all_to_all(rows, 'dp', 0, 0, tiled=True, axis_index_groups=plane_groups)  39.2 us
    dot_general x14, matrix products, contract(): lax.dot_general(left, right, (dims, ((), ())), preferred_element_type=F32)  24.4 us
    all_to_all x5, waiting for transfers between devices, in_plane(): lax.all_to_all(rows, 'dp', 0, 0, tiled=True, axis_index_groups=plane_groups)  22.6 us
    ppermute x8, starting transfers between devices, passed_along(): lax.ppermute(value, 'dp', [(s, s + steps) for s in range(first, last)])  20.2 us
    pallas_call x1, Pallas kernels, expert_back(): pl.pallas_call(expert_kernel, grid=(segments,), in_specs=[*specs, weight,...  19.5 us
    ppermute x8, starting transfers between devices, swapped(): return lax.ppermute(array, 'tensor', [(0, 1), (1, 0)])  19.3 us
  transfers between devices with their start and end apart: 24, of which 13 were waited for; matrix products, arithmetic and copies ran while one was open for 11% of the time, Pallas kernels for 17%

profile of v9, /device:TPU:1, one launch (start us, length us, event | category | flops | bytes accessed | tf_op | source)
XLA Modules:
  0.0 552.3 jit_solution(13722064117840792029)
XLA Ops:
  15.5 8.6 %all-to-all-start = ((bf16[16,32,1536]{2,1,0:T(8,128)(2,1)}), bf16[16,32,1536]{2,1,0:T(8,128)(2,1)}, u32[]{:S(2)}, u32[]{:S(2)}) async-start(bf16[16,32,1536]{2,1,0:T(8,128)(2,1)} %bitcast.90), calls=%async_computation | async-start | bytes 3145728 | tf_op jit(solution)/shard_map/all_to_all | solution.py:636
  32.1 5.0 collective-permute-start.1
  37.1 4.1 collective-permute-start.2
  55.7 15.7 %all-to-all-start.1 = ((bf16[16,64,1536]{2,1,0:T(8,128)(2,1)}), bf16[16,64,1536]{2,1,0:T(8,128)(2,1)}, u32[]{:S(2)}, u32[]{:S(2)}) async-start(bf16[16,64,1536]{2,1,0:T(8,128)(2,1)} %bitcast.92), calls=%async_computation.1 | async-start | bytes 6291456 | tf_op jit(solution)/shard_map/all_to_all | solution.py:636
  71.4 12.3 %shard_map.299 = (bf16[768,256]{1,0:T(8,128)(2,1)S(1)}, f32[12,256]{1,0:T(8,128)S(1)}, f32[12,256]{1,0:T(8,128)S(1)}) custom-call(bf16[768,256]{1,0:T(8,128)(2,1)S(1)} %bitcast.82, bf16[528,256]{1,0:T(8,128)(2,1)S(1)} %collective-permute-done.k4, bf16[528,256]{1,0:T(8,128)(2,1)} %collective-permute-done.1.k3, bf16[528,256]{1,0:T(8,128)(2,1)} %collective-permute-done.2.k2, ...), custom_call_target="tpu_custom_call" | custom-call | flops 1006632960 | bytes 2138112 | tf_op jit(solution)/shard_map/pallas_call | solution.py:124
  98.2 10.4 %all-to-all-done.1.g2_ref = bf16[16,64,1536]{2,1,0:T(8,128)(2,1)} async-done(((bf16[16,64,1536]{2,1,0:T(8,128)(2,1)}), bf16[16,64,1536]{2,1,0:T(8,128)(2,1)}, u32[]{:S(2)}, u32[]{:S(2)}) %all-to-all-start.1) | async-done | bytes 3145760 | tf_op jit(solution)/shard_map/all_to_all | solution.py:636
  108.6 6.5 %collective-permute-start.5 = (bf16[4,1536,768]{2,1,0:T(8,128)(2,1)}, bf16[4,1536,768]{2,1,0:T(8,128)(2,1)}, u32[]{:S(2)}, u32[]{:S(2)}) collective-permute-start(bf16[4,1536,768]{2,1,0:T(8,128)(2,1)} %bitcast.85), channel_id=1, source_target_pairs={{0,1},{1,0},{2,3},{3,2},{4,5},{5,4},{6,7},{7,6},{8,9},{9,8},{10,11... | collective-permute-start | bytes 28311560 | tf_op jit(solution)/shard_map/ppermute | solution.py:41
  115.2 69.9 %all_to_all.30.x_ref = bf16[16,96,1536]{2,1,0:T(8,128)(2,1)} all-to-all(bf16[16,96,1536]{2,1,0:T(8,128)(2,1)} %bitcast.84), channel_id=1, replica_groups={{0,2,4,6,8,10,12,14,16,18,20,22,24,26,28,30},{32,34,36,38,40,42,44,46,4..., dimensions={0} | all-to-all | bytes 9437184 | tf_op jit(solution)/shard_map/all_to_all | solution.py:636
  185.1 6.5 %shard_map.302 = bf16[16,32,1536]{2,1,0:T(8,128)(2,1)} custom-call(bf16[16,96,1536]{2,1,0:T(8,128)(2,1)} %all_to_all.30.x_ref, bf16[4,1536,768]{2,1,0:T(8,128)(2,1)} %bitcast.86, bf16[4,1536,768]{2,1,0:T(8,128)(2,1)} %collective-permute-done.5.peer_ref), custom_call_target="tpu_custom_call" | custom-call | flops 2415919104 | bytes 7864320 | tf_op jit(solution)/shard_map/pallas_call | solution.py:249
  191.6 4.6 all-to-all-start.3
  196.2 19.5 %shard_map.301 = (bf16[16,96,1536]{2,1,0:T(8,128)(2,1)}, bf16[3,512,768]{2,1,0:T(8,128)(2,1)}, bf16[3,512,768]{2,1,0:T(8,128)(2,1)}) custom-call(bf16[16,96,1536]{2,1,0:T(8,128)(2,1)} %all_to_all.30.x_ref, bf16[16,32,1536]{2,1,0:T(8,128)(2,1)} %all-to-all-done.g1_ref, bf16[16,64,1536]{2,1,0:T(8,128)(2,1)} %all-to-all-done.1.g2_ref, ...), custom_call_target="tpu_custom_call" | custom-call | flops 12683575296 | bytes 28311552 | tf_op jit(solution)/shard_map/pallas_call | solution.py:315
  216.5 5.8 %all-to-all-start.4 = ((bf16[16,96,1536]{2,1,0:T(8,128)(2,1)}), bf16[16,96,1536]{2,1,0:T(8,128)(2,1)}, u32[]{:S(2)}, u32[]{:S(2)}) async-start(bf16[16,96,1536]{2,1,0:T(8,128)(2,1)} %get-tuple-element.70), calls=%async_computation.4 | async-start | bytes 9437184 | tf_op jit(solution)/shard_map/all_to_all | solution.py:636
  222.3 17.8 %shard_map.303 = (bf16[3,1536,768]{2,1,0:T(8,128)(2,1)}, bf16[3,1536,256]{2,1,0:T(8,128)(2,1)}, bf16[3,1536,256]{2,1,0:T(8,128)(2,1)}, bf16[3,1536,256]{2,1,0:T(8,128)(2,1)}, bf16[16,64,1536]{2,1,0:T(8,128)(2,1)}) custom-call(bf16[16,96,1536]{2,1,0:T(8,128)(2,1)} %all_to_all.30.x_ref, bf16[16,32,1536]{2,1,0:T(8,128)(2,1)} %all-to-all-done.g1_ref, ...), custom_call_target="tpu_custom_call" | custom-call | flops 10871635968 | bytes 31850496 | tf_op jit(solution)/shard_map/pallas_call | solution.py:380
  254.4 11.8 %shard_map.304 = bf16[4,1536,768]{2,1,0:T(8,128)(2,1)} custom-call(bf16[3,1536,768]{2,1,0:T(8,128)(2,1)} %get-tuple-element.73.own_ref, bf16[3,1536,256]{2,1,0:T(8,128)(2,1)} %collective-permute-done.6.refs_0_, bf16[3,1536,256]{2,1,0:T(8,128)(2,1)} %collective-permute-done.7.refs_1_, bf16[3,1536,256]{2,1,0:T(8,128)(2,1)} %collective-permute-done.8.refs_2_), custom_call_target="tpu_custom_call" | custom-call | flops 4718592 | bytes 28311552 | tf_op jit(solution)/shard_map/pallas_call | solution.py:421
  267.3 11.4 %all-to-all-done.4 = bf16[16,96,1536]{2,1,0:T(8,128)(2,1)} async-done(((bf16[16,96,1536]{2,1,0:T(8,128)(2,1)}), bf16[16,96,1536]{2,1,0:T(8,128)(2,1)}, u32[]{:S(2)}, u32[]{:S(2)}) %all-to-all-start.4) | async-done | bytes 4718624 | tf_op jit(solution)/shard_map/all_to_all | solution.py:636
  278.7 4.8 convolution_convert_fusion.1
  283.5 6.5 %collective-permute-start.9 = (bf16[256,1536]{1,0:T(8,128)(2,1)}, bf16[256,1536]{1,0:T(8,128)(2,1)}, u32[]{:S(2)}, u32[]{:S(2)}) collective-permute-start(bf16[256,1536]{1,0:T(8,128)(2,1)} %convolution_convert_fusion.1), channel_id=1, source_target_pairs={{0,1},{1,0},{2,3},{3,2},{4,5},{5,4},{6,7},{7,6},{8,9},{9,8},{10,11... | collective-permute-start | bytes 2359304 | tf_op jit(solution)/shard_map/ppermute | solution.py:41
  290.1 4.5 all-to-all-start.5
  301.3 19.3 %shard_map.305 = (bf16[768,256]{1,0:T(8,128)(2,1)S(1)}, bf16[512,256]{1,0:T(8,128)(2,1)S(1)}, bf16[512,256]{1,0:T(8,128)(2,1)S(1)}, bf16[512,256]{1,0:T(8,128)(2...) custom-call(bf16[768,256]{1,0:T(8,128)(2,1)S(1)} %bitcast.83, bf16[768,256]{1,0:T(8,128)(2,1)S(1)} %fusion.13.g_ref, ...), custom_call_target="tpu_custom_call" | custom-call | flops 125829120000 | bytes 3883008 | tf_op jit(solution)/shard_map/pallas_call | solution.py:189
  328.0 6.7 %shard_map.306._ = bf16[1536,2304]{1,0:T(8,128)(2,1)} custom-call(bf16[256,1536]{1,0:T(8,128)(2,1)} %copy-done.7, bf16[768,256]{1,0:T(8,128)(2,1)} %copy-done.3, bf16[768,256]{1,0:T(8,128)(2,1)} %copy-done.2, bf16[256,1536]{1,0:T(8,128)(2,1)} %copy-done.14), custom_call_target="tpu_custom_call" | custom-call | flops 1207959552 | bytes 4718592 | tf_op jit(solution)/shard_map/pallas_call | solution.py:450
  337.3 8.7 %collective-permute-done.11 = bf16[512,256]{1,0:T(8,128)(2,1)S(1)} collective-permute-done((bf16[512,256]{1,0:T(8,128)(2,1)S(1)}, bf16[512,256]{1,0:T(8,128)(2,1)S(1)}, u32[]{:S(2)}, u32[]{:S(2)}) %collective-permute-start.11) | collective-permute-done | bytes 262176 | tf_op jit(solution)/shard_map/ppermute | solution.py:51
  355.0 5.7 %shard_map.307 = bf16[1536,2304]{1,0:T(8,128)(2,1)} custom-call(bf16[256,1536]{1,0:T(8,128)(2,1)} %copy-done.7, bf16[512,256]{1,0:T(8,128)(2,1)} %pad_maximum_fusion.1.kv_ref, f32[128,1536]{1,0:T(8,128)} %select_maximum_fusion.extra_ref, bf16[1536,2304]{1,0:T(8,128)(2,1)} %shard_map.306._), custom_call_target="tpu_custom_call", output_to_operand_aliasing={{}: (3, {})} | custom-call | flops 402653184 | bytes 2359296 | tf_op jit(solution)/shard_map/pallas_call | solution.py:472
  377.7 156.3 %all-reduce.3.cloned.1.call-done.in_ref = bf16[1536,2304]{1,0:T(8,128)(2,1)} async-done(((bf16[1536,2304]{1,0:T(8,128)(2,1)}), bf16[1536,2304]{1,0:T(8,128)(2,1)}) %all-reduce.3.cloned.1.call-update) | async-done | bytes 7077904 | tf_op jit(solution)/shard_map/psum | solution.py:730
  534.1 10.2 %shard_map.308 = (f32[768,1536]{1,0:T(8,128)}, f32[1536,768]{1,0:T(8,128)}, f32[1536,256]{1,0:T(8,128)}, f32[1536,256]{1,0:T(8,128)}, f32[8,1536]{1,0:T(8,128)},...) custom-call(bf16[1536,2304]{1,0:T(8,128)(2,1)} %all-reduce.3.cloned.1.call-done.in_ref, ...), custom_call_target="tpu_custom_call" | custom-call | flops 3538944 | bytes 28311552 | tf_op jit(solution)/shard_map/pallas_call | solution.py:535
  (206 shorter events, 105.1 us)
Async XLA Ops:
  7.2 101.4 %all-gather.3.cloned.1.call-start = ((), (), s32[]{:S(2)}) async-start(), calls=%async_computation.9 | async-start | bytes 11796480 | tf_op jit(solution)/shard_map/all_gather | solution.py:662
  15.5 40.1 %all-to-all-start = ((bf16[16,32,1536]{2,1,0:T(8,128)(2,1)}), bf16[16,32,1536]{2,1,0:T(8,128)(2,1)}, u32[]{:S(2)}, u32[]{:S(2)}) async-start(bf16[16,32,1536]{2,1,0:T(8,128)(2,1)} %bitcast.90), calls=%async_computation | async-start | bytes 3145728 | tf_op jit(solution)/shard_map/all_to_all | solution.py:636
  28.9 25.0 %collective-permute-start = (bf16[528,256]{1,0:T(8,128)(2,1)S(1)}, bf16[528,256]{1,0:T(8,128)(2,1)S(1)}, u32[]{:S(2)}, u32[]{:S(2)}) collective-permute-start(bf16[528,256]{1,0:T(8,128)(2,1)S(1)} %concatenate.31.k0), channel_id=1, source_target_pairs={{0,8},{2,10},{4,12},{6,14},{8,16},{10,18},{12,20},{14,22},{16,24},... | collective-permute-start | bytes 811016 | tf_op jit(solution)/shard_map/ppermute | solution.py:51
  32.1 23.4 %collective-permute-start.1 = (bf16[528,256]{1,0:T(8,128)(2,1)S(1)}, bf16[528,256]{1,0:T(8,128)(2,1)}, u32[]{:S(2)}, u32[]{:S(2)}) collective-permute-start(bf16[528,256]{1,0:T(8,128)(2,1)S(1)} %concatenate.31.k0), channel_id=1, source_target_pairs={{0,6},{2,8},{4,10},{6,12},{8,14},{10,16},{12,18},{14,20},{16,22},{... | collective-permute-start | bytes 811016 | tf_op jit(solution)/shard_map/ppermute | solution.py:51
  37.1 18.5 %collective-permute-start.2 = (bf16[528,256]{1,0:T(8,128)(2,1)S(1)}, bf16[528,256]{1,0:T(8,128)(2,1)}, u32[]{:S(2)}, u32[]{:S(2)}) collective-permute-start(bf16[528,256]{1,0:T(8,128)(2,1)S(1)} %concatenate.31.k0), channel_id=1, source_target_pairs={{0,4},{2,6},{4,8},{6,10},{8,12},{10,14},{12,16},{14,18},{16,20},{1... | collective-permute-start | bytes 811016 | tf_op jit(solution)/shard_map/ppermute | solution.py:51
  41.1 14.5 %collective-permute-start.3 = (bf16[528,256]{1,0:T(8,128)(2,1)S(1)}, bf16[528,256]{1,0:T(8,128)(2,1)}, u32[]{:S(2)}, u32[]{:S(2)}) collective-permute-start(bf16[528,256]{1,0:T(8,128)(2,1)S(1)} %concatenate.31.k0), channel_id=1, source_target_pairs={{0,2},{2,4},{4,6},{6,8},{8,10},{10,12},{12,14},{14,16},{16,18},{18... | collective-permute-start | bytes 811016 | tf_op jit(solution)/shard_map/ppermute | solution.py:51
  55.7 53.0 %all-to-all-start.1 = ((bf16[16,64,1536]{2,1,0:T(8,128)(2,1)}), bf16[16,64,1536]{2,1,0:T(8,128)(2,1)}, u32[]{:S(2)}, u32[]{:S(2)}) async-start(bf16[16,64,1536]{2,1,0:T(8,128)(2,1)} %bitcast.92), calls=%async_computation.1 | async-start | bytes 6291456 | tf_op jit(solution)/shard_map/all_to_all | solution.py:636
  85.6 5.4 collective-permute-start.4
  108.6 76.5 %collective-permute-start.5 = (bf16[4,1536,768]{2,1,0:T(8,128)(2,1)}, bf16[4,1536,768]{2,1,0:T(8,128)(2,1)}, u32[]{:S(2)}, u32[]{:S(2)}) collective-permute-start(bf16[4,1536,768]{2,1,0:T(8,128)(2,1)} %bitcast.85), channel_id=1, source_target_pairs={{0,1},{1,0},{2,3},{3,2},{4,5},{5,4},{6,7},{7,6},{8,9},{9,8},{10,11... | collective-permute-start | bytes 28311560 | tf_op jit(solution)/shard_map/ppermute | solution.py:41
  191.6 24.9 %all-to-all-start.3 = ((bf16[16,32,1536]{2,1,0:T(8,128)(2,1)}), bf16[16,32,1536]{2,1,0:T(8,128)(2,1)}, u32[]{:S(2)}, u32[]{:S(2)}) async-start(bf16[16,32,1536]{2,1,0:T(8,128)(2,1)} %shard_map.302), calls=%async_computation.3 | async-start | bytes 3145728 | tf_op jit(solution)/shard_map/all_to_all | solution.py:636
  216.5 62.3 %all-to-all-start.4 = ((bf16[16,96,1536]{2,1,0:T(8,128)(2,1)}), bf16[16,96,1536]{2,1,0:T(8,128)(2,1)}, u32[]{:S(2)}, u32[]{:S(2)}) async-start(bf16[16,96,1536]{2,1,0:T(8,128)(2,1)} %get-tuple-element.70), calls=%async_computation.4 | async-start | bytes 9437184 | tf_op jit(solution)/shard_map/all_to_all | solution.py:636
  222.3 138.5 %reduce-scatter.2.cloned.1.call-start = ((), (), s32[]{:S(2)}) async-start(), calls=%async_computation.7 | async-start | bytes 11796480 | tf_op jit(solution)/shard_map/reduce_scatter | solution.py:687
  240.2 7.5 %collective-permute-start.6 = (bf16[3,1536,256]{2,1,0:T(8,128)(2,1)}, bf16[3,1536,256]{2,1,0:T(8,128)(2,1)}, u32[]{:S(2)}, u32[]{:S(2)}) collective-permute-start(bf16[3,1536,256]{2,1,0:T(8,128)(2,1)} %get-tuple-element.74), channel_id=1, source_target_pairs={{0,1},{1,0},{2,3},{3,2},{4,5},{5,4},{6,7},{7,6},{8,9},{9,8},{10,11... | collective-permute-start | bytes 7077896 | tf_op jit(solution)/shard_map/ppermute | solution.py:41
  243.2 7.9 %collective-permute-start.7 = (bf16[3,1536,256]{2,1,0:T(8,128)(2,1)}, bf16[3,1536,256]{2,1,0:T(8,128)(2,1)}, u32[]{:S(2)}, u32[]{:S(2)}) collective-permute-start(bf16[3,1536,256]{2,1,0:T(8,128)(2,1)} %get-tuple-element.75), channel_id=1, source_target_pairs={{0,1},{1,0},{2,3},{3,2},{4,5},{5,4},{6,7},{7,6},{8,9},{9,8},{10,11... | collective-permute-start | bytes 7077896 | tf_op jit(solution)/shard_map/ppermute | solution.py:41
  243.2 11.2 %collective-permute-start.8 = (bf16[3,1536,256]{2,1,0:T(8,128)(2,1)}, bf16[3,1536,256]{2,1,0:T(8,128)(2,1)}, u32[]{:S(2)}, u32[]{:S(2)}) collective-permute-start(bf16[3,1536,256]{2,1,0:T(8,128)(2,1)} %get-tuple-element.76), channel_id=1, source_target_pairs={{0,1},{1,0},{2,3},{3,2},{4,5},{5,4},{6,7},{7,6},{8,9},{9,8},{10,11... | collective-permute-start | bytes 7077896 | tf_op jit(solution)/shard_map/ppermute | solution.py:41
  283.5 11.2 %collective-permute-start.9 = (bf16[256,1536]{1,0:T(8,128)(2,1)}, bf16[256,1536]{1,0:T(8,128)(2,1)}, u32[]{:S(2)}, u32[]{:S(2)}) collective-permute-start(bf16[256,1536]{1,0:T(8,128)(2,1)} %convolution_convert_fusion.1), channel_id=1, source_target_pairs={{0,1},{1,0},{2,3},{3,2},{4,5},{5,4},{6,7},{7,6},{8,9},{9,8},{10,11... | collective-permute-start | bytes 2359304 | tf_op jit(solution)/shard_map/ppermute | solution.py:41
  290.1 70.6 %all-to-all-start.5 = ((bf16[16,64,1536]{2,1,0:T(8,128)(2,1)}), bf16[16,64,1536]{2,1,0:T(8,128)(2,1)}, u32[]{:S(2)}, u32[]{:S(2)}) async-start(bf16[16,64,1536]{2,1,0:T(8,128)(2,1)} %get-tuple-element.91), calls=%async_computation.6 | async-start | bytes 6291456 | tf_op jit(solution)/shard_map/all_to_all | solution.py:636
  294.6 239.4 %all-reduce.3.cloned.1.call-start = ((), (), s32[]{:S(2)}) async-start(), calls=%async_computation.8 | async-start | bytes 14155776 | tf_op jit(solution)/shard_map/psum | solution.py:730
  320.6 16.6 %collective-permute-start.10 = (bf16[512,256]{1,0:T(8,128)(2,1)S(1)}, bf16[512,256]{1,0:T(8,128)(2,1)S(1)}, u32[]{:S(2)}, u32[]{:S(2)}) collective-permute-start(bf16[512,256]{1,0:T(8,128)(2,1)S(1)} %get-tuple-element.80), channel_id=1, source_target_pairs={{8,0},{10,2},{12,4},{14,6},{16,8},{18,10},{20,12},{22,14},{24,16},... | collective-permute-start | bytes 786440 | tf_op jit(solution)/shard_map/ppermute | solution.py:51
  321.9 24.1 %collective-permute-start.11 = (bf16[512,256]{1,0:T(8,128)(2,1)S(1)}, bf16[512,256]{1,0:T(8,128)(2,1)S(1)}, u32[]{:S(2)}, u32[]{:S(2)}) collective-permute-start(bf16[512,256]{1,0:T(8,128)(2,1)S(1)} %get-tuple-element.81), channel_id=1, source_target_pairs={{6,0},{8,2},{10,4},{12,6},{14,8},{16,10},{18,12},{20,14},{22,16},{... | collective-permute-start | bytes 786440 | tf_op jit(solution)/shard_map/ppermute | solution.py:51
  323.2 22.8 %collective-permute-start.12 = (bf16[512,256]{1,0:T(8,128)(2,1)S(1)}, bf16[512,256]{1,0:T(8,128)(2,1)S(1)}, u32[]{:S(2)}, u32[]{:S(2)}) collective-permute-start(bf16[512,256]{1,0:T(8,128)(2,1)S(1)} %get-tuple-element.82), channel_id=1, source_target_pairs={{4,0},{6,2},{8,4},{10,6},{12,8},{14,10},{16,12},{18,14},{20,16},{2... | collective-permute-start | bytes 786440 | tf_op jit(solution)/shard_map/ppermute | solution.py:51
  324.5 21.5 %collective-permute-start.13 = (bf16[512,256]{1,0:T(8,128)(2,1)S(1)}, bf16[512,256]{1,0:T(8,128)(2,1)S(1)}, u32[]{:S(2)}, u32[]{:S(2)}) collective-permute-start(bf16[512,256]{1,0:T(8,128)(2,1)S(1)} %get-tuple-element.83), channel_id=1, source_target_pairs={{2,0},{4,2},{6,4},{8,6},{10,8},{12,10},{14,12},{16,14},{18,16},{20... | collective-permute-start | bytes 786440 | tf_op jit(solution)/shard_map/ppermute | solution.py:51
  350.9 2.4 collective-permute-start.14
  369.2 6.2 %collective-permute-start.15 = (bf16[256,1536]{1,0:T(8,128)(2,1)S(1)}, bf16[256,1536]{1,0:T(8,128)(2,1)}, u32[]{:S(2)}, u32[]{:S(2)}) collective-permute-start(bf16[256,1536]{1,0:T(8,128)(2,1)S(1)} %convolution_convert_fusion.2), channel_id=1, source_target_pairs={{0,1},{1,0},{2,3},{3,2},{4,5},{5,4},{6,7},{7,6},{8,9},{9,8},{10,11... | collective-permute-start | bytes 2359304 | tf_op jit(solution)/shard_map/ppermute | solution.py:41
  (44 other events, 741.1 us)
Sparse Core Ops, SparseCore 0:
  10.4 97.0 all-gather.2
  266.4 91.4 reduce-scatter.1
  362.8 171.2 all-reduce.2

commit v10 on v9

--- a/solution.py
+++ b/solution.py
@@ -201,6 +201,115 @@
             transcendentals=rows // HD * tok * tok * len(blocks),
         ),
     )(q, grad, log_total, cosine, sine, *blocks)
+
+
+def dispatch_kernel(pick_ref, rows_ref, *refs):
+    rows = contract(pick_ref[...], rows_ref[...], NN)
+    for gate_ref in refs[:-1]:
+        rows = rows * jnp.sum(gate_ref[...], axis=1, keepdims=True)
+    refs[-1][...] = rows.astype(BF16)
+
+
+def dispatch(pick, rows, *gates):
+    slots, tok = pick.shape
+    width = rows.shape[1]
+    return pl.pallas_call(
+        dispatch_kernel,
+        grid=(slots // LANES,),
+        in_specs=[
+            pl.BlockSpec((LANES, tok), lambda i: (i, 0)),
+            pl.BlockSpec((tok, width), lambda i: (0, 0)),
+        ]
+        + [pl.BlockSpec((LANES, tok), lambda i: (i, 0))] * len(gates),
+        out_specs=pl.BlockSpec((LANES, width), lambda i: (i, 0)),
+        out_shape=jax.ShapeDtypeStruct((slots, width), BF16),
+        cost_estimate=pl.CostEstimate(
+            flops=2 * slots * tok * width, bytes_accessed=2 * slots * (width + tok), transcendentals=0
+        ),
+    )(pick, rows, *gates)
+
+
+def combine_kernel(weight_ref, rows_ref, out_ref):
+    rows = rows_ref[...].reshape(weight_ref.shape[0], -1)
+    out_ref[...] = contract(weight_ref[...], rows, TN).astype(BF16)
+
+
+def combine(weights, rows):
+    sources, lines, width = rows.shape
+    slots, tok = weights.shape
+    part = 512
+    return pl.pallas_call(
+        combine_kernel,
+        grid=(width // part,),
+        in_specs=[
+            pl.BlockSpec((slots, tok), lambda i: (0, 0)),
+            pl.BlockSpec((sources, lines, part), lambda i: (0, 0, i)),
+        ],
+        out_specs=pl.BlockSpec((tok, part), lambda i: (0, i)),
+        out_shape=jax.ShapeDtypeStruct((tok, width), BF16),
+        cost_estimate=pl.CostEstimate(
+            flops=2 * slots * tok * width, bytes_accessed=2 * slots * (width + tok), transcendentals=0
+        ),
+    )(weights, rows)
+
+
+def project_kernel(
+    x_ref, gain_ref, wq_ref, wk_ref, wv_ref, cos_ref, sin_ref, side_ref,
+    normed_ref, inverse_ref, q_ref, block_ref,
+):
+    x = x_ref[...].astype(F32)
+    inverse = lax.rsqrt(jnp.mean(x * x, axis=-1, keepdims=True) + EPS)
+    inverse_ref[...] = inverse
+    normed_ref[...] = (x * inverse * gain_ref[...]).astype(BF16)
+    kv = wk_ref.shape[1]
+    step, half = (2 * HD, HD // 2)
+    block_ref[2 * kv :, :] = side_ref[...]
+
+    def columns(weight_ref, c):
+        lanes = pl.ds(pl.multiple_of(c * step, step), step)
+        return contract(weight_ref[:, lanes], normed_ref[...], ((0,), (1,)))
+
+    def rotated(weight_ref, out_ref, scale):
+        def one(c, _):
+            both = columns(weight_ref, c)
+            cosine, sine = (cos_ref[...] * scale, sin_ref[...] * scale)
+            for head in range(2):
+                first, second = (both[head * HD : head * HD + half], both[head * HD + half : (head + 1) * HD])
+                at = pl.multiple_of(c * step + head * HD, HD)
+                out_ref[pl.ds(at, half), :] = (first * cosine - second * sine).astype(BF16)
+                out_ref[pl.ds(at + half, half), :] = (second * cosine + first * sine).astype(BF16)
+            return 0
+
+        lax.fori_loop(0, weight_ref.shape[1] // step, one, 0)
+
+    def one_value(c, _):
+        at = pl.multiple_of(kv + c * step, step)
+        block_ref[pl.ds(at, step), :] = columns(wv_ref, c).astype(BF16)
+        return 0
+
+    rotated(wk_ref, block_ref, 1.0)
+    lax.fori_loop(0, kv // step, one_value, 0)
+    rotated(wq_ref, q_ref, HD**-0.5)
+
+
+def project(tokens, gain, w_query, w_key, w_value, cosine, sine, side):
+    tok, model = tokens.shape
+    width, kv = (w_query.shape[1], w_key.shape[1])
+    return pl.pallas_call(
+        project_kernel,
+        out_shape=(
+            jax.ShapeDtypeStruct((tok, model), BF16),
+            jax.ShapeDtypeStruct((tok, 1), F32),
+            jax.ShapeDtypeStruct((width, tok), BF16),
+            jax.ShapeDtypeStruct((2 * kv + AUX, tok), BF16),
+        ),
+        compiler_params=pltpu.CompilerParams(vmem_limit_bytes=40 << 20),
+        cost_estimate=pl.CostEstimate(
+            flops=2 * tok * model * (width + 2 * kv),
+            bytes_accessed=2 * model * (width + 2 * kv + 3 * tok),
+            transcendentals=0,
+        ),
+    )(tokens, gain, w_query, w_key, w_value, cosine, sine, side)
 
 
 def pack_weights_kernel(gate_ref, up_ref, down_ref, out_ref):
@@ -628,8 +737,7 @@
     chosen = rank[:, None, :] == wanted[None, :, None]
     pick = chosen.astype(BF16).reshape(-1, tok_dev)
     gated = jnp.where(chosen, gate_of[:, None, :], 0.0)
-    slot_gate = jnp.sum(gated, axis=2).reshape(-1, 1)
-    gated = gated.astype(BF16).reshape(-1, tok_dev)
+    gated = gated.reshape(-1, tok_dev)
 
     def in_plane(rows):
         rows = rows.reshape(PLANE, -1, model_width)
@@ -638,24 +746,20 @@
     def grads_for(first, last):
         shape = (PLANE, SEGMENTS * RANK_ROWS, -1)
         part = pick.reshape(shape)[:, first * RANK_ROWS : last * RANK_ROWS].reshape(-1, tok_dev)
-        gate = slot_gate.reshape(shape)[:, first * RANK_ROWS : last * RANK_ROWS].reshape(-1, 1)
-        return (contract(part, out_grad, NN) * gate).astype(BF16)
+        gate = gated.reshape(shape)[:, first * RANK_ROWS : last * RANK_ROWS].reshape(-1, tok_dev)
+        return dispatch(part, out_grad, gate)
 
     grads_early = in_plane(grads_for(0, EARLY))
     grads_late = grads_for(EARLY, SEGMENTS)
 
     cosine, sine = rope_tables(tok_dev, dp_size)
     x_float = tokens.astype(F32)
-    inverse1 = rms_scale(x_float)
-    normed1 = (x_float * inverse1 * norm1_gain).astype(BF16)
-    query = rotate(contract(w_query, normed1, ((0,), (1,))), cosine, sine)
-    query = (query * (HD**-0.5)).astype(BF16)
-    key = rotate(contract(w_key, normed1, ((0,), (1,))), cosine, sine).astype(BF16)
-    value = contract(w_value, normed1, ((0,), (1,))).astype(BF16)
     side = jnp.concatenate(
         [(seq_ids + 1)[None], piece_ids[None], jnp.zeros((AUX - 2, tok_dev), jnp.int32)]
     ).astype(BF16)
-    block = jnp.concatenate([key, value, side])
+    normed1, inverse1, query, block = project(
+        tokens, norm1_gain[None], w_query, w_key, w_value, cosine, sine, side
+    )
     blocks = tuple(passed_along(block, hop) for hop in range(HOPS, 0, -1)) + (block,)
     blocks, grads_early, grads_late = lax.optimization_barrier((blocks, grads_early, grads_late))
     packed_w = pack_weights(w_gate[0], w_up[0], w_down[0])
@@ -667,7 +771,7 @@
     inverse2 = rms_scale(hidden1)
     normed2 = (hidden1 * inverse2 * norm2_gain).astype(BF16)
 
-    rows_out = contract(pick, normed2, NN).astype(BF16)
+    rows_out = dispatch(pick, normed2)
     rows_out = after(rows_out, grad_rows[1])
     own = after(own, rows_out)
     peer = swapped(own)
@@ -676,7 +780,7 @@
     back, own_acts, peer_acts = expert_back(rows_in, grad_rows, own, peer)
 
     def combined(weights, rows):
-        part = contract(weights, rows.reshape(-1, model_width), TN).astype(BF16)
+        part = combine(weights, rows)
         return part.astype(F32) + swapped(part).astype(F32)
 
     sum_own, *sum_peer, out_late = expert_sums(rows_in, grad_rows, own_acts, peer_acts, own, peer)
@@ -729,7 +833,7 @@
     parts, sums, out_early, out_late = lax.optimization_barrier((parts, sums, out_early, out_late))
     summed = lax.psum(parts, "dp")
     expert_out = jnp.concatenate([out_early, out_late], axis=1)
-    output = (hidden1 + combined(gated, expert_out)).astype(BF16)
+    output = (hidden1 + combined(gated.astype(BF16), expert_out)).astype(BF16)
     grad_gate, grad_up, grad_down = jnp.split(sums[0].astype(F32), 3, axis=1)
     grad_down = grad_down.T
     grad_wo, grad_wq, grad_wk, grad_wv, totals, clipped_query, clipped_key, head_peaks = unpack(

time: 554 us -> 554 us (level)
  Pallas kernels: 113 us -> 142 us
  matrix products: 24.4 us -> 5.71 us
  waiting for transfers between devices: 207 us -> 196 us
    pallas_call x0 -> x6, Pallas kernels: none -> 29 us  [the longest x3 14 us: dispatch(): pl.pallas_call(dispatch_kernel, grid=(slots // LANES,), in_specs=[pl.Bloc...]
    dot_general x14 -> x6, matrix products: 24.4 us -> 5.71 us  [contract(): lax.dot_general(left, right, (dims, ((), ())), preferred_element_type=F32)]
    unnamed x87 -> x97, local copies, waits for them, and re-layouts: 10.4 us -> 14.1 us
  transfers between devices with their start and end apart: 24 -> 24, of which waited for: 13 -> 12; matrix products, arithmetic and copies ran while one was open for 11% -> 7% of each run, Pallas kernels for 17% -> 22%
where the time goes in v10:
time: 554 us; the launch traced here: 552 us
  waiting for transfers between devices  196 us (35%)
  Pallas kernels  142 us (26%)
  starting transfers between devices  78.2 us (14%)
  blocking collectives  67.8 us (12%)
  other arithmetic  25.4 us (5%)
  local copies, waits for them, and re-layouts  22.7 us (4%)
  between operations  14.4 us (3%)
  matrix products  5.71 us (1%)
    psum x1, waiting for transfers between devices, shards(): summed = lax.psum(parts, 'dp')  152 us
    all_to_all x1, blocking collectives, in_plane(): lax.all_to_all(rows, 'dp', 0, 0, tiled=True, axis_index_groups=plane_groups)  67.8 us
    all_to_all x5, starting transfers between devices, in_plane(): lax.all_to_all(rows, 'dp', 0, 0, tiled=True, axis_index_groups=plane_groups)  38.3 us
    ppermute x8, starting transfers between devices, passed_along(): lax.ppermute(value, 'dp', [(s, s + steps) for s in range(first, last)])  20.1 us
    ppermute x8, starting transfers between devices, swapped(): return lax.ppermute(array, 'tensor', [(0, 1), (1, 0)])  19.5 us
    pallas_call x1, Pallas kernels, attend_back(): pl.pallas_call(functools.partial(attend_back_kernel, group), out_shape=(j...  19.5 us
    pallas_call x1, Pallas kernels, expert_back(): pl.pallas_call(expert_kernel, grid=(segments,), in_specs=[*specs, weight,...  19.5 us
    all_to_all x5, waiting for transfers between devices, in_plane(): lax.all_to_all(rows, 'dp', 0, 0, tiled=True, axis_index_groups=plane_groups)  18.7 us
  transfers between devices with their start and end apart: 24, of which 12 were waited for; matrix products, arithmetic and copies ran while one was open for 7% of the time, Pallas kernels for 22%

profile of v10, /device:TPU:1, one launch (start us, length us, event | category | flops | bytes accessed | tf_op | source)
XLA Modules:
  0.0 552.4 jit_solution(7358862790135540137)
XLA Ops:
  17.6 8.6 %all-to-all-start = ((bf16[16,32,1536]{2,1,0:T(8,128)(2,1)}), bf16[16,32,1536]{2,1,0:T(8,128)(2,1)}, u32[]{:S(2)}, u32[]{:S(2)}) async-start(bf16[16,32,1536]{2,1,0:T(8,128)(2,1)} %bitcast.74), calls=%async_computation | async-start | bytes 3145728 | tf_op jit(solution)/shard_map/all_to_all | solution.py:744
  40.9 5.0 collective-permute-start.1
  58.7 14.8 %all-to-all-start.1 = ((bf16[16,64,1536]{2,1,0:T(8,128)(2,1)}), bf16[16,64,1536]{2,1,0:T(8,128)(2,1)}, u32[]{:S(2)}, u32[]{:S(2)}) async-start(bf16[16,64,1536]{2,1,0:T(8,128)(2,1)} %bitcast.69), calls=%async_computation.1 | async-start | bytes 6291456 | tf_op jit(solution)/shard_map/all_to_all | solution.py:744
  74.6 12.5 %shard_map.302 = (bf16[768,256]{1,0:T(8,128)(2,1)S(1)}, f32[12,256]{1,0:T(8,128)S(1)}, f32[12,256]{1,0:T(8,128)S(1)}) custom-call(bf16[768,256]{1,0:T(8,128)(2,1)S(1)} %copy-done.14, bf16[528,256]{1,0:T(8,128)(2,1)} %collective-permute-done.k4, bf16[528,256]{1,0:T(8,128)(2,1)} %collective-permute-done.1.k3, bf16[528,256]{1,0:T(8,128)(2,1)} %collective-permute-done.2.k2, ...), custom_call_target="tpu_custom_call" | custom-call | flops 1006632960 | bytes 2138112 | tf_op jit(solution)/shard_map/pallas_call | solution.py:124
  98.8 6.2 %shard_map.303 = bf16[1536,1536]{1,0:T(8,128)(2,1)} custom-call(bf16[1536,256]{1,0:T(8,128)(2,1)} %fusion.8.pick_ref.weight_ref, bf16[256,1536]{1,0:T(8,128)(2,1)} %multiply_convert_fusion.rows_ref), custom_call_target="tpu_custom_call" | custom-call | flops 1207959552 | bytes 5505024 | tf_op jit(solution)/shard_map/pallas_call | solution.py:216
  105.1 5.8 %all-to-all-done.1.g2_ref = bf16[16,64,1536]{2,1,0:T(8,128)(2,1)} async-done(((bf16[16,64,1536]{2,1,0:T(8,128)(2,1)}), bf16[16,64,1536]{2,1,0:T(8,128)(2,1)}, u32[]{:S(2)}, u32[]{:S(2)}) %all-to-all-start.1) | async-done | bytes 3145760 | tf_op jit(solution)/shard_map/all_to_all | solution.py:744
  110.8 6.5 %collective-permute-start.5 = (bf16[4,1536,768]{2,1,0:T(8,128)(2,1)}, bf16[4,1536,768]{2,1,0:T(8,128)(2,1)}, u32[]{:S(2)}, u32[]{:S(2)}) collective-permute-start(bf16[4,1536,768]{2,1,0:T(8,128)(2,1)} %bitcast.70), channel_id=1, source_target_pairs={{0,1},{1,0},{2,3},{3,2},{4,5},{5,4},{6,7},{7,6},{8,9},{9,8},{10,11... | collective-permute-start | bytes 28311560 | tf_op jit(solution)/shard_map/ppermute | solution.py:41
  117.3 67.8 %all_to_all.30.x_ref = bf16[16,96,1536]{2,1,0:T(8,128)(2,1)} all-to-all(bf16[16,96,1536]{2,1,0:T(8,128)(2,1)} %bitcast.66), channel_id=1, replica_groups={{0,2,4,6,8,10,12,14,16,18,20,22,24,26,28,30},{32,34,36,38,40,42,44,46,4..., dimensions={0} | all-to-all | bytes 9437184 | tf_op jit(solution)/shard_map/all_to_all | solution.py:744
  185.1 6.5 %shard_map.306 = bf16[16,32,1536]{2,1,0:T(8,128)(2,1)} custom-call(bf16[16,96,1536]{2,1,0:T(8,128)(2,1)} %all_to_all.30.x_ref, bf16[4,1536,768]{2,1,0:T(8,128)(2,1)} %bitcast.71, bf16[4,1536,768]{2,1,0:T(8,128)(2,1)} %collective-permute-done.5.peer_ref), custom_call_target="tpu_custom_call" | custom-call | flops 2415919104 | bytes 7864320 | tf_op jit(solution)/shard_map/pallas_call | solution.py:358
  196.1 19.5 %shard_map.305 = (bf16[16,96,1536]{2,1,0:T(8,128)(2,1)}, bf16[3,512,768]{2,1,0:T(8,128)(2,1)}, bf16[3,512,768]{2,1,0:T(8,128)(2,1)}) custom-call(bf16[16,96,1536]{2,1,0:T(8,128)(2,1)} %all_to_all.30.x_ref, bf16[16,32,1536]{2,1,0:T(8,128)(2,1)} %all-to-all-done.g1_ref, bf16[16,64,1536]{2,1,0:T(8,128)(2,1)} %all-to-all-done.1.g2_ref, ...), custom_call_target="tpu_custom_call" | custom-call | flops 12683575296 | bytes 28311552 | tf_op jit(solution)/shard_map/pallas_call | solution.py:424
  216.4 5.8 %all-to-all-start.4 = ((bf16[16,96,1536]{2,1,0:T(8,128)(2,1)}), bf16[16,96,1536]{2,1,0:T(8,128)(2,1)}, u32[]{:S(2)}, u32[]{:S(2)}) async-start(bf16[16,96,1536]{2,1,0:T(8,128)(2,1)} %get-tuple-element.77), calls=%async_computation.4 | async-start | bytes 9437184 | tf_op jit(solution)/shard_map/all_to_all | solution.py:744
  222.4 17.9 %shard_map.307 = (bf16[3,1536,768]{2,1,0:T(8,128)(2,1)}, bf16[3,1536,256]{2,1,0:T(8,128)(2,1)}, bf16[3,1536,256]{2,1,0:T(8,128)(2,1)}, bf16[3,1536,256]{2,1,0:T(8,128)(2,1)}, bf16[16,64,1536]{2,1,0:T(8,128)(2,1)}) custom-call(bf16[16,96,1536]{2,1,0:T(8,128)(2,1)} %all_to_all.30.x_ref, bf16[16,32,1536]{2,1,0:T(8,128)(2,1)} %all-to-all-done.g1_ref, ...), custom_call_target="tpu_custom_call" | custom-call | flops 10871635968 | bytes 31850496 | tf_op jit(solution)/shard_map/pallas_call | solution.py:489
  254.6 11.8 %shard_map.308 = bf16[4,1536,768]{2,1,0:T(8,128)(2,1)} custom-call(bf16[3,1536,768]{2,1,0:T(8,128)(2,1)} %get-tuple-element.80.own_ref, bf16[3,1536,256]{2,1,0:T(8,128)(2,1)} %collective-permute-done.6.refs_0_, bf16[3,1536,256]{2,1,0:T(8,128)(2,1)} %collective-permute-done.7.refs_1_, bf16[3,1536,256]{2,1,0:T(8,128)(2,1)} %collective-permute-done.8.refs_2_), custom_call_target="tpu_custom_call" | custom-call | flops 4718592 | bytes 28311552 | tf_op jit(solution)/shard_map/pallas_call | solution.py:530
  266.4 12.1 %all-to-all-done.4.rows_ref = bf16[16,96,1536]{2,1,0:T(8,128)(2,1)} async-done(((bf16[16,96,1536]{2,1,0:T(8,128)(2,1)}), bf16[16,96,1536]{2,1,0:T(8,128)(2,1)}, u32[]{:S(2)}, u32[]{:S(2)}) %all-to-all-start.4) | async-done | bytes 4718624 | tf_op jit(solution)/shard_map/all_to_all | solution.py:744
  278.5 5.1 shard_map.309
  283.7 6.4 %collective-permute-start.9 = (bf16[256,1536]{1,0:T(8,128)(2,1)}, bf16[256,1536]{1,0:T(8,128)(2,1)}, u32[]{:S(2)}, u32[]{:S(2)}) collective-permute-start(bf16[256,1536]{1,0:T(8,128)(2,1)} %shard_map.309), channel_id=1, source_target_pairs={{0,1},{1,0},{2,3},{3,2},{4,5},{5,4},{6,7},{7,6},{8,9},{9,8},{10,11... | collective-permute-start | bytes 2359304 | tf_op jit(solution)/shard_map/ppermute | solution.py:41
  302.1 19.5 %shard_map.310 = (bf16[768,256]{1,0:T(8,128)(2,1)S(1)}, bf16[512,256]{1,0:T(8,128)(2,1)S(1)}, bf16[512,256]{1,0:T(8,128)(2,1)S(1)}, bf16[512,256]{1,0:T(8,128)(2...) custom-call(bf16[768,256]{1,0:T(8,128)(2,1)S(1)} %copy-done.15, bf16[768,256]{1,0:T(8,128)(2,1)S(1)} %fusion.12.g_ref, ...), custom_call_target="tpu_custom_call" | custom-call | flops 125829120000 | bytes 3883008 | tf_op jit(solution)/shard_map/pallas_call | solution.py:189
  328.8 6.7 %shard_map.311._ = bf16[1536,2304]{1,0:T(8,128)(2,1)} custom-call(bf16[256,1536]{1,0:T(8,128)(2,1)} %copy-done.8, bf16[768,256]{1,0:T(8,128)(2,1)} %copy-done.12, bf16[768,256]{1,0:T(8,128)(2,1)} %copy-done.11, bf16[256,1536]{1,0:T(8,128)(2,1)} %copy-done.25), custom_call_target="tpu_custom_call" | custom-call | flops 1207959552 | bytes 4718592 | tf_op jit(solution)/shard_map/pallas_call | solution.py:559
  338.2 8.7 %collective-permute-done.11 = bf16[512,256]{1,0:T(8,128)(2,1)S(1)} collective-permute-done((bf16[512,256]{1,0:T(8,128)(2,1)S(1)}, bf16[512,256]{1,0:T(8,128)(2,1)S(1)}, u32[]{:S(2)}, u32[]{:S(2)}) %collective-permute-start.11) | collective-permute-done | bytes 262176 | tf_op jit(solution)/shard_map/ppermute | solution.py:51
  354.5 5.7 %shard_map.312 = bf16[1536,2304]{1,0:T(8,128)(2,1)} custom-call(bf16[256,1536]{1,0:T(8,128)(2,1)} %copy-done.8, bf16[512,256]{1,0:T(8,128)(2,1)} %pad_maximum_fusion.1.kv_ref, f32[128,1536]{1,0:T(8,128)} %select_maximum_fusion.extra_ref, bf16[1536,2304]{1,0:T(8,128)(2,1)} %shard_map.311._), custom_call_target="tpu_custom_call", output_to_operand_aliasing={{}: (3, {})} | custom-call | flops 402653184 | bytes 2359296 | tf_op jit(solution)/shard_map/pallas_call | solution.py:581
  365.0 5.0 pad_maximum_fusion.rows_ref
  370.0 5.2 shard_map.313
  382.5 151.6 %all-reduce.3.cloned.1.call-done.in_ref = bf16[1536,2304]{1,0:T(8,128)(2,1)} async-done(((bf16[1536,2304]{1,0:T(8,128)(2,1)}), bf16[1536,2304]{1,0:T(8,128)(2,1)}) %all-reduce.3.cloned.1.call-update) | async-done | bytes 7077904 | tf_op jit(solution)/shard_map/psum | solution.py:834
  534.1 10.2 %shard_map.314 = (f32[768,1536]{1,0:T(8,128)}, f32[1536,768]{1,0:T(8,128)}, f32[1536,256]{1,0:T(8,128)}, f32[1536,256]{1,0:T(8,128)}, f32[8,1536]{1,0:T(8,128)},...) custom-call(bf16[1536,2304]{1,0:T(8,128)(2,1)} %all-reduce.3.cloned.1.call-done.in_ref, ...), custom_call_target="tpu_custom_call" | custom-call | flops 3538944 | bytes 28311552 | tf_op jit(solution)/shard_map/pallas_call | solution.py:644
  (207 shorter events, 113.1 us)
Async XLA Ops:
  7.2 103.6 %all-gather.3.cloned.1.call-start = ((), (), s32[]{:S(2)}) async-start(), calls=%async_computation.9 | async-start | bytes 11796480 | tf_op jit(solution)/shard_map/all_gather | solution.py:766
  17.6 41.2 %all-to-all-start = ((bf16[16,32,1536]{2,1,0:T(8,128)(2,1)}), bf16[16,32,1536]{2,1,0:T(8,128)(2,1)}, u32[]{:S(2)}, u32[]{:S(2)}) async-start(bf16[16,32,1536]{2,1,0:T(8,128)(2,1)} %bitcast.74), calls=%async_computation | async-start | bytes 3145728 | tf_op jit(solution)/shard_map/all_to_all | solution.py:744
  36.8 21.7 %collective-permute-start = (bf16[528,256]{1,0:T(8,128)(2,1)}, bf16[528,256]{1,0:T(8,128)(2,1)}, u32[]{:S(2)}, u32[]{:S(2)}) collective-permute-start(bf16[528,256]{1,0:T(8,128)(2,1)} %get-tuple-element.69.k0), channel_id=1, source_target_pairs={{0,8},{2,10},{4,12},{6,14},{8,16},{10,18},{12,20},{14,22},{16,24},... | collective-permute-start | bytes 811016 | tf_op jit(solution)/shard_map/ppermute | solution.py:51
  40.9 17.7 %collective-permute-start.1 = (bf16[528,256]{1,0:T(8,128)(2,1)}, bf16[528,256]{1,0:T(8,128)(2,1)}, u32[]{:S(2)}, u32[]{:S(2)}) collective-permute-start(bf16[528,256]{1,0:T(8,128)(2,1)} %get-tuple-element.69.k0), channel_id=1, source_target_pairs={{0,6},{2,8},{4,10},{6,12},{8,14},{10,16},{12,18},{14,20},{16,22},{... | collective-permute-start | bytes 811016 | tf_op jit(solution)/shard_map/ppermute | solution.py:51
  45.9 12.7 %collective-permute-start.2 = (bf16[528,256]{1,0:T(8,128)(2,1)}, bf16[528,256]{1,0:T(8,128)(2,1)}, u32[]{:S(2)}, u32[]{:S(2)}) collective-permute-start(bf16[528,256]{1,0:T(8,128)(2,1)} %get-tuple-element.69.k0), channel_id=1, source_target_pairs={{0,4},{2,6},{4,8},{6,10},{8,12},{10,14},{12,16},{14,18},{16,20},{1... | collective-permute-start | bytes 811016 | tf_op jit(solution)/shard_map/ppermute | solution.py:51
  49.3 9.4 %collective-permute-start.3 = (bf16[528,256]{1,0:T(8,128)(2,1)}, bf16[528,256]{1,0:T(8,128)(2,1)}, u32[]{:S(2)}, u32[]{:S(2)}) collective-permute-start(bf16[528,256]{1,0:T(8,128)(2,1)} %get-tuple-element.69.k0), channel_id=1, source_target_pairs={{0,2},{2,4},{4,6},{6,8},{8,10},{10,12},{12,14},{14,16},{16,18},{18... | collective-permute-start | bytes 811016 | tf_op jit(solution)/shard_map/ppermute | solution.py:51
  58.7 52.1 %all-to-all-start.1 = ((bf16[16,64,1536]{2,1,0:T(8,128)(2,1)}), bf16[16,64,1536]{2,1,0:T(8,128)(2,1)}, u32[]{:S(2)}, u32[]{:S(2)}) async-start(bf16[16,64,1536]{2,1,0:T(8,128)(2,1)} %bitcast.69), calls=%async_computation.1 | async-start | bytes 6291456 | tf_op jit(solution)/shard_map/all_to_all | solution.py:744
  89.0 5.4 collective-permute-start.4
  110.8 74.3 %collective-permute-start.5 = (bf16[4,1536,768]{2,1,0:T(8,128)(2,1)}, bf16[4,1536,768]{2,1,0:T(8,128)(2,1)}, u32[]{:S(2)}, u32[]{:S(2)}) collective-permute-start(bf16[4,1536,768]{2,1,0:T(8,128)(2,1)} %bitcast.70), channel_id=1, source_target_pairs={{0,1},{1,0},{2,3},{3,2},{4,5},{5,4},{6,7},{7,6},{8,9},{9,8},{10,11... | collective-permute-start | bytes 28311560 | tf_op jit(solution)/shard_map/ppermute | solution.py:41
  191.6 24.7 %all-to-all-start.3 = ((bf16[16,32,1536]{2,1,0:T(8,128)(2,1)}), bf16[16,32,1536]{2,1,0:T(8,128)(2,1)}, u32[]{:S(2)}, u32[]{:S(2)}) async-start(bf16[16,32,1536]{2,1,0:T(8,128)(2,1)} %shard_map.306), calls=%async_computation.3 | async-start | bytes 3145728 | tf_op jit(solution)/shard_map/all_to_all | solution.py:744
  216.4 62.2 %all-to-all-start.4 = ((bf16[16,96,1536]{2,1,0:T(8,128)(2,1)}), bf16[16,96,1536]{2,1,0:T(8,128)(2,1)}, u32[]{:S(2)}, u32[]{:S(2)}) async-start(bf16[16,96,1536]{2,1,0:T(8,128)(2,1)} %get-tuple-element.77), calls=%async_computation.4 | async-start | bytes 9437184 | tf_op jit(solution)/shard_map/all_to_all | solution.py:744
  222.2 138.1 %reduce-scatter.2.cloned.1.call-start = ((), (), s32[]{:S(2)}) async-start(), calls=%async_computation.7 | async-start | bytes 11796480 | tf_op jit(solution)/shard_map/reduce_scatter | solution.py:791
  240.3 7.6 %collective-permute-start.6 = (bf16[3,1536,256]{2,1,0:T(8,128)(2,1)}, bf16[3,1536,256]{2,1,0:T(8,128)(2,1)}, u32[]{:S(2)}, u32[]{:S(2)}) collective-permute-start(bf16[3,1536,256]{2,1,0:T(8,128)(2,1)} %get-tuple-element.81), channel_id=1, source_target_pairs={{0,1},{1,0},{2,3},{3,2},{4,5},{5,4},{6,7},{7,6},{8,9},{9,8},{10,11... | collective-permute-start | bytes 7077896 | tf_op jit(solution)/shard_map/ppermute | solution.py:41
  243.3 7.9 %collective-permute-start.7 = (bf16[3,1536,256]{2,1,0:T(8,128)(2,1)}, bf16[3,1536,256]{2,1,0:T(8,128)(2,1)}, u32[]{:S(2)}, u32[]{:S(2)}) collective-permute-start(bf16[3,1536,256]{2,1,0:T(8,128)(2,1)} %get-tuple-element.82), channel_id=1, source_target_pairs={{0,1},{1,0},{2,3},{3,2},{4,5},{5,4},{6,7},{7,6},{8,9},{9,8},{10,11... | collective-permute-start | bytes 7077896 | tf_op jit(solution)/shard_map/ppermute | solution.py:41
  243.4 11.2 %collective-permute-start.8 = (bf16[3,1536,256]{2,1,0:T(8,128)(2,1)}, bf16[3,1536,256]{2,1,0:T(8,128)(2,1)}, u32[]{:S(2)}, u32[]{:S(2)}) collective-permute-start(bf16[3,1536,256]{2,1,0:T(8,128)(2,1)} %get-tuple-element.83), channel_id=1, source_target_pairs={{0,1},{1,0},{2,3},{3,2},{4,5},{5,4},{6,7},{7,6},{8,9},{9,8},{10,11... | collective-permute-start | bytes 7077896 | tf_op jit(solution)/shard_map/ppermute | solution.py:41
  283.7 11.9 %collective-permute-start.9 = (bf16[256,1536]{1,0:T(8,128)(2,1)}, bf16[256,1536]{1,0:T(8,128)(2,1)}, u32[]{:S(2)}, u32[]{:S(2)}) collective-permute-start(bf16[256,1536]{1,0:T(8,128)(2,1)} %shard_map.309), channel_id=1, source_target_pairs={{0,1},{1,0},{2,3},{3,2},{4,5},{5,4},{6,7},{7,6},{8,9},{9,8},{10,11... | collective-permute-start | bytes 2359304 | tf_op jit(solution)/shard_map/ppermute | solution.py:41
  290.9 69.4 %all-to-all-start.5 = ((bf16[16,64,1536]{2,1,0:T(8,128)(2,1)}), bf16[16,64,1536]{2,1,0:T(8,128)(2,1)}, u32[]{:S(2)}, u32[]{:S(2)}) async-start(bf16[16,64,1536]{2,1,0:T(8,128)(2,1)} %get-tuple-element.99), calls=%async_computation.6 | async-start | bytes 6291456 | tf_op jit(solution)/shard_map/all_to_all | solution.py:744
  295.5 238.7 %all-reduce.3.cloned.1.call-start = ((), (), s32[]{:S(2)}) async-start(), calls=%async_computation.8 | async-start | bytes 14155776 | tf_op jit(solution)/shard_map/psum | solution.py:834
  321.6 16.6 %collective-permute-start.10 = (bf16[512,256]{1,0:T(8,128)(2,1)S(1)}, bf16[512,256]{1,0:T(8,128)(2,1)S(1)}, u32[]{:S(2)}, u32[]{:S(2)}) collective-permute-start(bf16[512,256]{1,0:T(8,128)(2,1)S(1)} %get-tuple-element.87), channel_id=1, source_target_pairs={{8,0},{10,2},{12,4},{14,6},{16,8},{18,10},{20,12},{22,14},{24,16},... | collective-permute-start | bytes 786440 | tf_op jit(solution)/shard_map/ppermute | solution.py:51
  322.9 24.1 %collective-permute-start.11 = (bf16[512,256]{1,0:T(8,128)(2,1)S(1)}, bf16[512,256]{1,0:T(8,128)(2,1)S(1)}, u32[]{:S(2)}, u32[]{:S(2)}) collective-permute-start(bf16[512,256]{1,0:T(8,128)(2,1)S(1)} %get-tuple-element.88), channel_id=1, source_target_pairs={{6,0},{8,2},{10,4},{12,6},{14,8},{16,10},{18,12},{20,14},{22,16},{... | collective-permute-start | bytes 786440 | tf_op jit(solution)/shard_map/ppermute | solution.py:51
  324.2 22.8 %collective-permute-start.12 = (bf16[512,256]{1,0:T(8,128)(2,1)S(1)}, bf16[512,256]{1,0:T(8,128)(2,1)S(1)}, u32[]{:S(2)}, u32[]{:S(2)}) collective-permute-start(bf16[512,256]{1,0:T(8,128)(2,1)S(1)} %get-tuple-element.89), channel_id=1, source_target_pairs={{4,0},{6,2},{8,4},{10,6},{12,8},{14,10},{16,12},{18,14},{20,16},{2... | collective-permute-start | bytes 786440 | tf_op jit(solution)/shard_map/ppermute | solution.py:51
  325.5 21.5 %collective-permute-start.13 = (bf16[512,256]{1,0:T(8,128)(2,1)S(1)}, bf16[512,256]{1,0:T(8,128)(2,1)S(1)}, u32[]{:S(2)}, u32[]{:S(2)}) collective-permute-start(bf16[512,256]{1,0:T(8,128)(2,1)S(1)} %get-tuple-element.90), channel_id=1, source_target_pairs={{2,0},{4,2},{6,4},{8,6},{10,8},{12,10},{14,12},{16,14},{18,16},{20... | collective-permute-start | bytes 786440 | tf_op jit(solution)/shard_map/ppermute | solution.py:51
  350.2 2.6 collective-permute-start.14
  375.2 6.2 %collective-permute-start.15 = (bf16[256,1536]{1,0:T(8,128)(2,1)}, bf16[256,1536]{1,0:T(8,128)(2,1)S(1)}, u32[]{:S(2)}, u32[]{:S(2)}) collective-permute-start(bf16[256,1536]{1,0:T(8,128)(2,1)} %shard_map.313), channel_id=1, source_target_pairs={{0,1},{1,0},{2,3},{3,2},{4,5},{5,4},{6,7},{7,6},{8,9},{9,8},{10,11... | collective-permute-start | bytes 2359304 | tf_op jit(solution)/shard_map/ppermute | solution.py:41
  (48 other events, 405.1 us)
Sparse Core Ops, SparseCore 0:
  10.4 97.0 all-gather.2
  266.5 91.4 reduce-scatter.1
  362.9 171.1 all-reduce.2

commit v11 on v10

--- a/solution.py
+++ b/solution.py
@@ -230,19 +230,19 @@
 
 
 def combine_kernel(weight_ref, rows_ref, out_ref):
-    rows = rows_ref[...].reshape(weight_ref.shape[0], -1)
-    out_ref[...] = contract(weight_ref[...], rows, TN).astype(BF16)
+    rows = rows_ref[...].reshape(weight_ref.shape[1], -1)
+    out_ref[...] = contract(weight_ref[...], rows, NN).astype(BF16)
 
 
 def combine(weights, rows):
     sources, lines, width = rows.shape
-    slots, tok = weights.shape
+    tok, slots = weights.shape
     part = 512
     return pl.pallas_call(
         combine_kernel,
         grid=(width // part,),
         in_specs=[
-            pl.BlockSpec((slots, tok), lambda i: (0, 0)),
+            pl.BlockSpec((tok, slots), lambda i: (0, 0)),
             pl.BlockSpec((sources, lines, part), lambda i: (0, 0, i)),
         ],
         out_specs=pl.BlockSpec((tok, part), lambda i: (0, i)),
@@ -545,11 +545,15 @@
     out_ref[:, width:] = contract(normed_ref[...], query_ref[...], ((0,), (1,))).astype(BF16)
 
 
-def last_grads_kernel(normed_ref, kv_ref, extra_ref, _, out_ref):
-    columns = kv_ref.shape[0]
-    out_ref[:, :columns] = contract(normed_ref[...], kv_ref[...], ((0,), (1,))).astype(BF16)
-    out_ref[:, columns : columns + MORE] = jnp.transpose(extra_ref[...]).astype(BF16)
-    out_ref[:, columns + MORE :] = jnp.zeros((out_ref.shape[0], MORE), BF16)
+def key_grads_kernel(normed_ref, kv_ref, _, out_ref):
+    out_ref[...] = contract(normed_ref[...], kv_ref[...], ((0,), (1,))).astype(BF16)
+
+
+def gain_rows_kernel(gain_ref, extra_ref, _, out_ref):
+    line = lax.broadcasted_iota(jnp.int32, extra_ref.shape, 0)
+    lines = jnp.where(line == 0, gain_ref[...], extra_ref[...])
+    out_ref[:, :MORE] = jnp.transpose(lines).astype(BF16)
+    out_ref[:, MORE:] = jnp.zeros((out_ref.shape[0], MORE), BF16)
 
 
 def first_grads(normed, grad_query, attended, branch, every):
@@ -573,32 +577,52 @@
     )(normed, grad_query, attended, branch)
 
 
-def last_grads(normed, grad_kv, extra, parts):
+def key_grads(normed, grad_kv, parts):
     tok, model = normed.shape
     columns = grad_kv.shape[0]
-    every = parts.shape[1]
-    size = columns + 2 * MORE
-    return pl.pallas_call(
-        last_grads_kernel,
-        grid=(model // LANES,),
+    rows = 2 * LANES
+    at = (parts.shape[1] - columns - 2 * MORE) // columns
+    return pl.pallas_call(
+        key_grads_kernel,
+        grid=(model // rows,),
         in_specs=[
-            pl.BlockSpec((tok, LANES), lambda i: (0, i)),
+            pl.BlockSpec((tok, rows), lambda i: (0, i)),
             pl.BlockSpec((columns, tok), lambda i: (0, 0)),
-            pl.BlockSpec((MORE, LANES), lambda i: (0, i)),
             pl.BlockSpec(memory_space=pl.ANY),
         ],
-        out_specs=pl.BlockSpec((LANES, size), lambda i: (i, (every - size) // size)),
+        out_specs=pl.BlockSpec((rows, columns), lambda i: (i, at)),
         out_shape=jax.ShapeDtypeStruct(parts.shape, BF16),
-        input_output_aliases={3: 0},
-        cost_estimate=pl.CostEstimate(
-            flops=2 * tok * model * columns, bytes_accessed=2 * model * size, transcendentals=0
-        ),
-    )(normed, grad_kv, extra, parts)
+        input_output_aliases={2: 0},
+        cost_estimate=pl.CostEstimate(
+            flops=2 * tok * model * columns, bytes_accessed=2 * model * columns, transcendentals=0
+        ),
+    )(normed, grad_kv, parts)
+
+
+def gain_rows(gain, extra, parts):
+    model = gain.shape[1]
+    rows = 2 * LANES
+    at = parts.shape[1] // (2 * MORE) - 1
+    return pl.pallas_call(
+        gain_rows_kernel,
+        grid=(model // rows,),
+        in_specs=[
+            pl.BlockSpec((1, rows), lambda i: (0, i)),
+            pl.BlockSpec((MORE, rows), lambda i: (0, i)),
+            pl.BlockSpec(memory_space=pl.ANY),
+        ],
+        out_specs=pl.BlockSpec((rows, 2 * MORE), lambda i: (i, at)),
+        out_shape=jax.ShapeDtypeStruct(parts.shape, BF16),
+        input_output_aliases={2: 0},
+        cost_estimate=pl.CostEstimate(
+            flops=model * MORE, bytes_accessed=8 * model * MORE, transcendentals=0
+        ),
+    )(gain, extra, parts)
 
 
 def unpack_kernel(
     devices, in_ref, query_ref, key_ref, clip_ref,
-    wo_ref, wq_ref, wk_ref, wv_ref, sum_ref, cq_ref, ck_ref, peak_ref, sq_ref, sk_ref,
+    wo_ref, wq_ref, wk_ref, wv_ref, gain1_ref, gain2_ref, cq_ref, ck_ref, peak_ref, sq_ref, sk_ref,
 ):
     at = 0
     group = cq_ref.shape[1] // ck_ref.shape[1]
@@ -628,7 +652,9 @@
         size = target.shape[1]
         target[...] = in_ref[:, at : at + size].astype(F32)
         at += size
-    sum_ref[...] = jnp.transpose(in_ref[:, at : at + MORE].astype(F32))[: sum_ref.shape[0]]
+    lines = jnp.transpose(in_ref[:, at : at + MORE].astype(F32))
+    gain1_ref[...] = lines[0:1, :]
+    gain2_ref[...] = lines[1:2, :]
     cq_ref[...] = (query_ref[...].astype(F32) * sq_ref[...]).astype(BF16)
     ck_ref[...] = (key_ref[...].astype(F32) * sk_ref[...]).astype(BF16)
 
@@ -655,7 +681,8 @@
             wide,
             thin,
             thin,
-            pl.BlockSpec((8, LANES), lambda i: (0, i)),
+            pl.BlockSpec((1, LANES), lambda i: (0, i)),
+            pl.BlockSpec((1, LANES), lambda i: (0, i)),
             wide,
             thin,
             line,
@@ -666,7 +693,8 @@
             jax.ShapeDtypeStruct((total, width), F32),
             jax.ShapeDtypeStruct((total, narrow), F32),
             jax.ShapeDtypeStruct((total, narrow), F32),
-            jax.ShapeDtypeStruct((8, total), F32),
+            jax.ShapeDtypeStruct((1, total), F32),
+            jax.ShapeDtypeStruct((1, total), F32),
             jax.ShapeDtypeStruct((total, width), BF16),
             jax.ShapeDtypeStruct((total, narrow), BF16),
             jax.ShapeDtypeStruct((1, heads), F32),
@@ -738,6 +766,7 @@
     pick = chosen.astype(BF16).reshape(-1, tok_dev)
     gated = jnp.where(chosen, gate_of[:, None, :], 0.0)
     gated = gated.reshape(-1, tok_dev)
+    pick_back, gated_back = (pick.T, gated.astype(BF16).T)
 
     def in_plane(rows):
         rows = rows.reshape(PLANE, -1, model_width)
@@ -787,7 +816,7 @@
     sums = both_cores(sum_own, [swapped(part) for part in sum_peer], dp_size // PLANE)
     back = in_plane(after(back, out_early))
     out_late = in_plane(after(out_late, back))
-    grad_normed2 = combined(pick, after(back, sums))
+    grad_normed2 = combined(pick_back, after(back, sums))
     sums = lax.psum_scatter(
         sums, "dp", scatter_dimension=0, tiled=True, axis_index_groups=column_groups
     )
@@ -827,16 +856,17 @@
     peak_pair = jnp.concatenate([peak_high, peak - peak_high])
     places = jnp.arange(model_width)[None] == lax.axis_index("dp")
     peak_rows = jnp.where(places, peak_pair[:, None], 0.0)
-    extra = jnp.concatenate([grad_gain1[None], grad_gain2[None], peak_rows])
+    extra = jnp.concatenate([jnp.zeros((1, model_width), F32), grad_gain2[None], peak_rows])
     extra = jnp.pad(extra, ((0, MORE - len(extra)), (0, 0)))
-    parts = last_grads(normed1, jnp.concatenate([grad_key_pre, grad_value]), extra, parts)
+    parts = key_grads(normed1, jnp.concatenate([grad_key_pre, grad_value]), parts)
+    parts = gain_rows(grad_gain1[None], extra, parts)
     parts, sums, out_early, out_late = lax.optimization_barrier((parts, sums, out_early, out_late))
     summed = lax.psum(parts, "dp")
     expert_out = jnp.concatenate([out_early, out_late], axis=1)
-    output = (hidden1 + combined(gated.astype(BF16), expert_out)).astype(BF16)
+    output = (hidden1 + combined(gated_back, expert_out)).astype(BF16)
     grad_gate, grad_up, grad_down = jnp.split(sums[0].astype(F32), 3, axis=1)
     grad_down = grad_down.T
-    grad_wo, grad_wq, grad_wk, grad_wv, totals, clipped_query, clipped_key, head_peaks = unpack(
+    grad_wo, grad_wq, grad_wk, grad_wv, sum1, sum2, clipped_query, clipped_key, head_peaks = unpack(
         summed, w_query, w_key, clip_limit, dp_size
     )
     return (
@@ -846,8 +876,8 @@
         grad_wk,
         grad_wv,
         grad_wo,
-        totals[0],
-        totals[1],
+        sum1.reshape(-1),
+        sum2.reshape(-1),
         grad_gate[None],
         grad_up[None],
         grad_down[None],

time: 554 us -> 556 us (level)
  waiting for transfers between devices: 196 us -> 180 us
  other arithmetic: 25.4 us -> 36.4 us
  local copies, waits for them, and re-layouts: 22.7 us -> 28.4 us
    all_to_all x5, waiting for transfers between devices: 18.7 us -> 11.3 us  [in_plane(): lax.all_to_all(rows, 'dp', 0, 0, tiled=True, axis_index_groups=plane_groups)]
    unnamed x97 -> x93, local copies, waits for them, and re-layouts: 14.1 us -> 13.5 us
  transfers between devices with their start and end apart: 24 -> 24, of which waited for: 12 -> 9; matrix products, arithmetic and copies ran while one was open for 7% -> 10% of each run, Pallas kernels for 22% -> 22%
where the time goes in v11:
time: 556 us; the launch traced here: 554 us
  waiting for transfers between devices  180 us (32%)
  Pallas kernels  144 us (26%)
  starting transfers between devices  78.1 us (14%)
  blocking collectives  67.3 us (12%)
  other arithmetic  36.4 us (7%)
  local copies, waits for them, and re-layouts  28.4 us (5%)
  between operations  14.4 us (3%)
    psum x1, waiting for transfers between devices, shards(): summed = lax.psum(parts, 'dp')  148 us
    all_to_all x1, blocking collectives, in_plane(): lax.all_to_all(rows, 'dp', 0, 0, tiled=True, axis_index_groups=plane_groups)  67.3 us
    all_to_all x5, starting transfers between devices, in_plane(): lax.all_to_all(rows, 'dp', 0, 0, tiled=True, axis_index_groups=plane_groups)  38.6 us
    pallas_call x1, Pallas kernels, attend_back(): pl.pallas_call(functools.partial(attend_back_kernel, group), out_shape=(j...  20.2 us
    ppermute x8, starting transfers between devices, passed_along(): lax.ppermute(value, 'dp', [(s, s + steps) for s in range(first, last)])  20.2 us
    pallas_call x1, Pallas kernels, expert_back(): pl.pallas_call(expert_kernel, grid=(segments,), in_specs=[*specs, weight,...  19.5 us
    ppermute x8, starting transfers between devices, swapped(): return lax.ppermute(array, 'tensor', [(0, 1), (1, 0)])  19.2 us
    pallas_call x1, Pallas kernels, expert_sums(): pl.pallas_call(expert_sums_kernel, grid=(segments,), in_specs=[*segment_s...  17.8 us
  transfers between devices with their start and end apart: 24, of which 9 were waited for; matrix products, arithmetic and copies ran while one was open for 10% of the time, Pallas kernels for 22%

profile of v11, /device:TPU:1, one launch (start us, length us, event | category | flops | bytes accessed | tf_op | source)
XLA Modules:
  0.0 553.6 jit_solution(7121292894892780764)
XLA Ops:
  18.1 8.6 %all-to-all-start = ((bf16[16,32,1536]{2,1,0:T(8,128)(2,1)}), bf16[16,32,1536]{2,1,0:T(8,128)(2,1)}, u32[]{:S(2)}, u32[]{:S(2)}) async-start(bf16[16,32,1536]{2,1,0:T(8,128)(2,1)} %bitcast.74), calls=%async_computation | async-start | bytes 3145728 | tf_op jit(solution)/shard_map/all_to_all | solution.py:773
  32.5 4.7 shard_map.299
  41.3 5.1 collective-permute-start.1
  54.2 4.9 shard_map.301
  59.1 14.9 %all-to-all-start.1 = ((bf16[16,64,1536]{2,1,0:T(8,128)(2,1)}), bf16[16,64,1536]{2,1,0:T(8,128)(2,1)}, u32[]{:S(2)}, u32[]{:S(2)}) async-start(bf16[16,64,1536]{2,1,0:T(8,128)(2,1)} %bitcast.69), calls=%async_computation.1 | async-start | bytes 6291456 | tf_op jit(solution)/shard_map/all_to_all | solution.py:773
  75.1 12.5 %shard_map.302 = (bf16[768,256]{1,0:T(8,128)(2,1)S(1)}, f32[12,256]{1,0:T(8,128)S(1)}, f32[12,256]{1,0:T(8,128)S(1)}) custom-call(bf16[768,256]{1,0:T(8,128)(2,1)S(1)} %copy-done.17, bf16[528,256]{1,0:T(8,128)(2,1)} %collective-permute-done.k4, bf16[528,256]{1,0:T(8,128)(2,1)} %collective-permute-done.1.k3, bf16[528,256]{1,0:T(8,128)(2,1)} %collective-permute-done.2.k2, ...), custom_call_target="tpu_custom_call" | custom-call | flops 1006632960 | bytes 2138112 | tf_op jit(solution)/shard_map/pallas_call | solution.py:124
  105.4 6.2 %shard_map.303 = bf16[1536,1536]{1,0:T(8,128)(2,1)} custom-call(bf16[1536,256]{1,0:T(8,128)(2,1)} %copy.49.pick_ref, bf16[256,1536]{1,0:T(8,128)(2,1)} %multiply_convert_fusion.rows_ref), custom_call_target="tpu_custom_call" | custom-call | flops 1207959552 | bytes 5505024 | tf_op jit(solution)/shard_map/pallas_call | solution.py:216
  111.6 6.2 %collective-permute-start.5 = (bf16[4,1536,768]{2,1,0:T(8,128)(2,1)}, bf16[4,1536,768]{2,1,0:T(8,128)(2,1)}, u32[]{:S(2)}, u32[]{:S(2)}) collective-permute-start(bf16[4,1536,768]{2,1,0:T(8,128)(2,1)} %bitcast.70), channel_id=1, source_target_pairs={{0,1},{1,0},{2,3},{3,2},{4,5},{5,4},{6,7},{7,6},{8,9},{9,8},{10,11... | collective-permute-start | bytes 28311560 | tf_op jit(solution)/shard_map/ppermute | solution.py:41
  117.8 67.3 %all_to_all.30.x_ref = bf16[16,96,1536]{2,1,0:T(8,128)(2,1)} all-to-all(bf16[16,96,1536]{2,1,0:T(8,128)(2,1)} %bitcast.66), channel_id=1, replica_groups={{0,2,4,6,8,10,12,14,16,18,20,22,24,26,28,30},{32,34,36,38,40,42,44,46,4..., dimensions={0} | all-to-all | bytes 9437184 | tf_op jit(solution)/shard_map/all_to_all | solution.py:773
  185.1 6.5 %shard_map.306 = bf16[16,32,1536]{2,1,0:T(8,128)(2,1)} custom-call(bf16[16,96,1536]{2,1,0:T(8,128)(2,1)} %all_to_all.30.x_ref, bf16[4,1536,768]{2,1,0:T(8,128)(2,1)} %bitcast.71, bf16[4,1536,768]{2,1,0:T(8,128)(2,1)} %collective-permute-done.5.peer_ref), custom_call_target="tpu_custom_call" | custom-call | flops 2415919104 | bytes 7864320 | tf_op jit(solution)/shard_map/pallas_call | solution.py:358
  196.0 19.5 %shard_map.305 = (bf16[16,96,1536]{2,1,0:T(8,128)(2,1)}, bf16[3,512,768]{2,1,0:T(8,128)(2,1)}, bf16[3,512,768]{2,1,0:T(8,128)(2,1)}) custom-call(bf16[16,96,1536]{2,1,0:T(8,128)(2,1)} %all_to_all.30.x_ref, bf16[16,32,1536]{2,1,0:T(8,128)(2,1)} %all-to-all-done.g1_ref, bf16[16,64,1536]{2,1,0:T(8,128)(2,1)} %all-to-all-done.1.g2_ref, ...), custom_call_target="tpu_custom_call" | custom-call | flops 12683575296 | bytes 28311552 | tf_op jit(solution)/shard_map/pallas_call | solution.py:424
  216.4 6.0 %all-to-all-start.4 = ((bf16[16,96,1536]{2,1,0:T(8,128)(2,1)}), bf16[16,96,1536]{2,1,0:T(8,128)(2,1)}, u32[]{:S(2)}, u32[]{:S(2)}) async-start(bf16[16,96,1536]{2,1,0:T(8,128)(2,1)} %get-tuple-element.77), calls=%async_computation.4 | async-start | bytes 9437184 | tf_op jit(solution)/shard_map/all_to_all | solution.py:773
  222.4 17.8 %shard_map.307 = (bf16[3,1536,768]{2,1,0:T(8,128)(2,1)}, bf16[3,1536,256]{2,1,0:T(8,128)(2,1)}, bf16[3,1536,256]{2,1,0:T(8,128)(2,1)}, bf16[3,1536,256]{2,1,0:T(8,128)(2,1)}, bf16[16,64,1536]{2,1,0:T(8,128)(2,1)}) custom-call(bf16[16,96,1536]{2,1,0:T(8,128)(2,1)} %all_to_all.30.x_ref, bf16[16,32,1536]{2,1,0:T(8,128)(2,1)} %all-to-all-done.g1_ref, ...), custom_call_target="tpu_custom_call" | custom-call | flops 10871635968 | bytes 31850496 | tf_op jit(solution)/shard_map/pallas_call | solution.py:489
  254.5 11.8 %shard_map.308 = bf16[4,1536,768]{2,1,0:T(8,128)(2,1)} custom-call(bf16[3,1536,768]{2,1,0:T(8,128)(2,1)} %get-tuple-element.80.own_ref, bf16[3,1536,256]{2,1,0:T(8,128)(2,1)} %collective-permute-done.6.refs_0_, bf16[3,1536,256]{2,1,0:T(8,128)(2,1)} %collective-permute-done.7.refs_1_, bf16[3,1536,256]{2,1,0:T(8,128)(2,1)} %collective-permute-done.8.refs_2_), custom_call_target="tpu_custom_call" | custom-call | flops 4718592 | bytes 28311552 | tf_op jit(solution)/shard_map/pallas_call | solution.py:530
  268.3 10.5 %all-to-all-done.4.rows_ref = bf16[16,96,1536]{2,1,0:T(8,128)(2,1)} async-done(((bf16[16,96,1536]{2,1,0:T(8,128)(2,1)}), bf16[16,96,1536]{2,1,0:T(8,128)(2,1)}, u32[]{:S(2)}, u32[]{:S(2)}) %all-to-all-start.4) | async-done | bytes 4718624 | tf_op jit(solution)/shard_map/all_to_all | solution.py:773
  278.7 5.0 shard_map.309
  283.7 6.5 %collective-permute-start.9 = (bf16[256,1536]{1,0:T(8,128)(2,1)}, bf16[256,1536]{1,0:T(8,128)(2,1)}, u32[]{:S(2)}, u32[]{:S(2)}) collective-permute-start(bf16[256,1536]{1,0:T(8,128)(2,1)} %shard_map.309), channel_id=1, source_target_pairs={{0,1},{1,0},{2,3},{3,2},{4,5},{5,4},{6,7},{7,6},{8,9},{9,8},{10,11... | collective-permute-start | bytes 2359304 | tf_op jit(solution)/shard_map/ppermute | solution.py:41
  302.7 20.2 %shard_map.310 = (bf16[768,256]{1,0:T(8,128)(2,1)S(1)}, bf16[512,256]{1,0:T(8,128)(2,1)}, bf16[512,256]{1,0:T(8,128)(2,1)}, bf16[512,256]{1,0:T(8,128)(2,1)S(1)}...) custom-call(bf16[768,256]{1,0:T(8,128)(2,1)S(1)} %copy-done.18, bf16[768,256]{1,0:T(8,128)(2,1)S(1)} %fusion.10.g_ref, ...), custom_call_target="tpu_custom_call" | custom-call | flops 125829120000 | bytes 3883008 | tf_op jit(solution)/shard_map/pallas_call | solution.py:189
  329.6 6.9 %shard_map.311._ = bf16[1536,2304]{1,0:T(8,128)(2,1)} custom-call(bf16[256,1536]{1,0:T(8,128)(2,1)} %copy-done.10, bf16[768,256]{1,0:T(8,128)(2,1)} %copy-done.12, bf16[768,256]{1,0:T(8,128)(2,1)} %copy-done.11, bf16[256,1536]{1,0:T(8,128)(2,1)} %copy-done.29), custom_call_target="tpu_custom_call" | custom-call | flops 1207959552 | bytes 4718592 | tf_op jit(solution)/shard_map/pallas_call | solution.py:563
  338.4 8.5 %collective-permute-done.11 = bf16[512,256]{1,0:T(8,128)(2,1)} collective-permute-done((bf16[512,256]{1,0:T(8,128)(2,1)}, bf16[512,256]{1,0:T(8,128)(2,1)}, u32[]{:S(2)}, u32[]{:S(2)}) %collective-permute-start.11) | collective-permute-done | bytes 262176 | tf_op jit(solution)/shard_map/ppermute | solution.py:51
  368.9 5.0 pad_maximum_fusion.rows_ref
  373.9 5.1 shard_map.314
  385.7 148.5 %all-reduce.3.cloned.1.call-done.in_ref = bf16[1536,2304]{1,0:T(8,128)(2,1)} async-done(((bf16[1536,2304]{1,0:T(8,128)(2,1)}), bf16[1536,2304]{1,0:T(8,128)(2,1)}) %all-reduce.3.cloned.1.call-update) | async-done | bytes 7077904 | tf_op jit(solution)/shard_map/psum | solution.py:864
  534.1 10.3 %shard_map.315 = (f32[768,1536]{1,0:T(8,128)}, f32[1536,768]{1,0:T(8,128)}, f32[1536,256]{1,0:T(8,128)}, f32[1536,256]{1,0:T(8,128)}, f32[1,1536]{1,0:T(1,128)},...) custom-call(bf16[1536,2304]{1,0:T(8,128)(2,1)} %all-reduce.3.cloned.1.call-done.in_, ...), custom_call_target="tpu_custom_call" | custom-call | flops 3538944 | bytes 28311552 | tf_op jit(solution)/shard_map/pallas_call | solution.py:670
  (211 shorter events, 120.9 us)
Async XLA Ops:
  7.2 104.4 %all-gather.3.cloned.1.call-start = ((), (), s32[]{:S(2)}) async-start(), calls=%async_computation.9 | async-start | bytes 11796480 | tf_op jit(solution)/shard_map/all_gather | solution.py:795
  18.1 41.0 %all-to-all-start = ((bf16[16,32,1536]{2,1,0:T(8,128)(2,1)}), bf16[16,32,1536]{2,1,0:T(8,128)(2,1)}, u32[]{:S(2)}, u32[]{:S(2)}) async-start(bf16[16,32,1536]{2,1,0:T(8,128)(2,1)} %bitcast.74), calls=%async_computation | async-start | bytes 3145728 | tf_op jit(solution)/shard_map/all_to_all | solution.py:773
  37.3 21.8 %collective-permute-start = (bf16[528,256]{1,0:T(8,128)(2,1)}, bf16[528,256]{1,0:T(8,128)(2,1)}, u32[]{:S(2)}, u32[]{:S(2)}) collective-permute-start(bf16[528,256]{1,0:T(8,128)(2,1)} %get-tuple-element.70.k0), channel_id=1, source_target_pairs={{0,8},{2,10},{4,12},{6,14},{8,16},{10,18},{12,20},{14,22},{16,24},... | collective-permute-start | bytes 811016 | tf_op jit(solution)/shard_map/ppermute | solution.py:51
  41.3 17.7 %collective-permute-start.1 = (bf16[528,256]{1,0:T(8,128)(2,1)}, bf16[528,256]{1,0:T(8,128)(2,1)}, u32[]{:S(2)}, u32[]{:S(2)}) collective-permute-start(bf16[528,256]{1,0:T(8,128)(2,1)} %get-tuple-element.70.k0), channel_id=1, source_target_pairs={{0,6},{2,8},{4,10},{6,12},{8,14},{10,16},{12,18},{14,20},{16,22},{... | collective-permute-start | bytes 811016 | tf_op jit(solution)/shard_map/ppermute | solution.py:51
  46.4 12.7 %collective-permute-start.2 = (bf16[528,256]{1,0:T(8,128)(2,1)}, bf16[528,256]{1,0:T(8,128)(2,1)}, u32[]{:S(2)}, u32[]{:S(2)}) collective-permute-start(bf16[528,256]{1,0:T(8,128)(2,1)} %get-tuple-element.70.k0), channel_id=1, source_target_pairs={{0,4},{2,6},{4,8},{6,10},{8,12},{10,14},{12,16},{14,18},{16,20},{1... | collective-permute-start | bytes 811016 | tf_op jit(solution)/shard_map/ppermute | solution.py:51
  49.7 9.4 %collective-permute-start.3 = (bf16[528,256]{1,0:T(8,128)(2,1)}, bf16[528,256]{1,0:T(8,128)(2,1)}, u32[]{:S(2)}, u32[]{:S(2)}) collective-permute-start(bf16[528,256]{1,0:T(8,128)(2,1)} %get-tuple-element.70.k0), channel_id=1, source_target_pairs={{0,2},{2,4},{4,6},{6,8},{8,10},{10,12},{12,14},{14,16},{16,18},{18... | collective-permute-start | bytes 811016 | tf_op jit(solution)/shard_map/ppermute | solution.py:51
  59.1 52.5 %all-to-all-start.1 = ((bf16[16,64,1536]{2,1,0:T(8,128)(2,1)}), bf16[16,64,1536]{2,1,0:T(8,128)(2,1)}, u32[]{:S(2)}, u32[]{:S(2)}) async-start(bf16[16,64,1536]{2,1,0:T(8,128)(2,1)} %bitcast.69), calls=%async_computation.1 | async-start | bytes 6291456 | tf_op jit(solution)/shard_map/all_to_all | solution.py:773
  89.5 10.1 %collective-permute-start.4 = (f32[256,1536]{1,0:T(8,128)}, f32[256,1536]{1,0:T(8,128)}, u32[]{:S(2)}, u32[]{:S(2)}) collective-permute-start(f32[256,1536]{1,0:T(8,128)} %fusion.22), channel_id=1, source_target_pairs={{0,1},{1,0},{2,3},{3,2},{4,5},{5,4},{6,7},{7,6},{8,9},{9,8},{10,11... | collective-permute-start | bytes 4718600 | tf_op jit(solution)/shard_map/ppermute | solution.py:41
  111.6 73.5 %collective-permute-start.5 = (bf16[4,1536,768]{2,1,0:T(8,128)(2,1)}, bf16[4,1536,768]{2,1,0:T(8,128)(2,1)}, u32[]{:S(2)}, u32[]{:S(2)}) collective-permute-start(bf16[4,1536,768]{2,1,0:T(8,128)(2,1)} %bitcast.70), channel_id=1, source_target_pairs={{0,1},{1,0},{2,3},{3,2},{4,5},{5,4},{6,7},{7,6},{8,9},{9,8},{10,11... | collective-permute-start | bytes 28311560 | tf_op jit(solution)/shard_map/ppermute | solution.py:41
  191.6 24.8 %all-to-all-start.3 = ((bf16[16,32,1536]{2,1,0:T(8,128)(2,1)}), bf16[16,32,1536]{2,1,0:T(8,128)(2,1)}, u32[]{:S(2)}, u32[]{:S(2)}) async-start(bf16[16,32,1536]{2,1,0:T(8,128)(2,1)} %shard_map.306), calls=%async_computation.3 | async-start | bytes 3145728 | tf_op jit(solution)/shard_map/all_to_all | solution.py:773
  216.4 62.4 %all-to-all-start.4 = ((bf16[16,96,1536]{2,1,0:T(8,128)(2,1)}), bf16[16,96,1536]{2,1,0:T(8,128)(2,1)}, u32[]{:S(2)}, u32[]{:S(2)}) async-start(bf16[16,96,1536]{2,1,0:T(8,128)(2,1)} %get-tuple-element.77), calls=%async_computation.4 | async-start | bytes 9437184 | tf_op jit(solution)/shard_map/all_to_all | solution.py:773
  222.4 138.9 %reduce-scatter.2.cloned.1.call-start = ((), (), s32[]{:S(2)}) async-start(), calls=%async_computation.7 | async-start | bytes 11796480 | tf_op jit(solution)/shard_map/reduce_scatter | solution.py:820
  240.2 7.5 %collective-permute-start.6 = (bf16[3,1536,256]{2,1,0:T(8,128)(2,1)}, bf16[3,1536,256]{2,1,0:T(8,128)(2,1)}, u32[]{:S(2)}, u32[]{:S(2)}) collective-permute-start(bf16[3,1536,256]{2,1,0:T(8,128)(2,1)} %get-tuple-element.81), channel_id=1, source_target_pairs={{0,1},{1,0},{2,3},{3,2},{4,5},{5,4},{6,7},{7,6},{8,9},{9,8},{10,11... | collective-permute-start | bytes 7077896 | tf_op jit(solution)/shard_map/ppermute | solution.py:41
  243.3 7.9 %collective-permute-start.7 = (bf16[3,1536,256]{2,1,0:T(8,128)(2,1)}, bf16[3,1536,256]{2,1,0:T(8,128)(2,1)}, u32[]{:S(2)}, u32[]{:S(2)}) collective-permute-start(bf16[3,1536,256]{2,1,0:T(8,128)(2,1)} %get-tuple-element.82), channel_id=1, source_target_pairs={{0,1},{1,0},{2,3},{3,2},{4,5},{5,4},{6,7},{7,6},{8,9},{9,8},{10,11... | collective-permute-start | bytes 7077896 | tf_op jit(solution)/shard_map/ppermute | solution.py:41
  243.4 11.2 %collective-permute-start.8 = (bf16[3,1536,256]{2,1,0:T(8,128)(2,1)}, bf16[3,1536,256]{2,1,0:T(8,128)(2,1)}, u32[]{:S(2)}, u32[]{:S(2)}) collective-permute-start(bf16[3,1536,256]{2,1,0:T(8,128)(2,1)} %get-tuple-element.83), channel_id=1, source_target_pairs={{0,1},{1,0},{2,3},{3,2},{4,5},{5,4},{6,7},{7,6},{8,9},{9,8},{10,11... | collective-permute-start | bytes 7077896 | tf_op jit(solution)/shard_map/ppermute | solution.py:41
  283.7 12.0 %collective-permute-start.9 = (bf16[256,1536]{1,0:T(8,128)(2,1)}, bf16[256,1536]{1,0:T(8,128)(2,1)}, u32[]{:S(2)}, u32[]{:S(2)}) collective-permute-start(bf16[256,1536]{1,0:T(8,128)(2,1)} %shard_map.309), channel_id=1, source_target_pairs={{0,1},{1,0},{2,3},{3,2},{4,5},{5,4},{6,7},{7,6},{8,9},{9,8},{10,11... | collective-permute-start | bytes 2359304 | tf_op jit(solution)/shard_map/ppermute | solution.py:41
  291.1 70.1 %all-to-all-start.5 = ((bf16[16,64,1536]{2,1,0:T(8,128)(2,1)}), bf16[16,64,1536]{2,1,0:T(8,128)(2,1)}, u32[]{:S(2)}, u32[]{:S(2)}) async-start(bf16[16,64,1536]{2,1,0:T(8,128)(2,1)} %get-tuple-element.100), calls=%async_computation.6 | async-start | bytes 6291456 | tf_op jit(solution)/shard_map/all_to_all | solution.py:773
  295.7 238.4 %all-reduce.3.cloned.1.call-start = ((), (), s32[]{:S(2)}) async-start(), calls=%async_computation.8 | async-start | bytes 14155776 | tf_op jit(solution)/shard_map/psum | solution.py:864
  324.4 14.1 %collective-permute-start.10 = (bf16[512,256]{1,0:T(8,128)(2,1)}, bf16[512,256]{1,0:T(8,128)(2,1)}, u32[]{:S(2)}, u32[]{:S(2)}) collective-permute-start(bf16[512,256]{1,0:T(8,128)(2,1)} %get-tuple-element.88), channel_id=1, source_target_pairs={{8,0},{10,2},{12,4},{14,6},{16,8},{18,10},{20,12},{22,14},{24,16},... | collective-permute-start | bytes 786440 | tf_op jit(solution)/shard_map/ppermute | solution.py:51
  325.6 21.3 %collective-permute-start.11 = (bf16[512,256]{1,0:T(8,128)(2,1)}, bf16[512,256]{1,0:T(8,128)(2,1)}, u32[]{:S(2)}, u32[]{:S(2)}) collective-permute-start(bf16[512,256]{1,0:T(8,128)(2,1)} %get-tuple-element.89), channel_id=1, source_target_pairs={{6,0},{8,2},{10,4},{12,6},{14,8},{16,10},{18,12},{20,14},{22,16},{... | collective-permute-start | bytes 786440 | tf_op jit(solution)/shard_map/ppermute | solution.py:51
  326.9 20.0 %collective-permute-start.12 = (bf16[512,256]{1,0:T(8,128)(2,1)S(1)}, bf16[512,256]{1,0:T(8,128)(2,1)}, u32[]{:S(2)}, u32[]{:S(2)}) collective-permute-start(bf16[512,256]{1,0:T(8,128)(2,1)S(1)} %get-tuple-element.90), channel_id=1, source_target_pairs={{4,0},{6,2},{8,4},{10,6},{12,8},{14,10},{16,12},{18,14},{20,16},{2... | collective-permute-start | bytes 786440 | tf_op jit(solution)/shard_map/ppermute | solution.py:51
  328.2 18.7 %collective-permute-start.13 = (bf16[512,256]{1,0:T(8,128)(2,1)S(1)}, bf16[512,256]{1,0:T(8,128)(2,1)}, u32[]{:S(2)}, u32[]{:S(2)}) collective-permute-start(bf16[512,256]{1,0:T(8,128)(2,1)S(1)} %get-tuple-element.91), channel_id=1, source_target_pairs={{2,0},{4,2},{6,4},{8,6},{10,8},{12,10},{14,12},{16,14},{18,16},{20... | collective-permute-start | bytes 786440 | tf_op jit(solution)/shard_map/ppermute | solution.py:51
  350.1 6.7 %collective-permute-start.14 = (bf16[256,1536]{1,0:T(8,128)(2,1)S(1)}, bf16[256,1536]{1,0:T(8,128)(2,1)S(1)}, u32[]{:S(2)}, u32[]{:S(2)}) collective-permute-start(bf16[256,1536]{1,0:T(8,128)(2,1)S(1)} %fusion), channel_id=1, source_target_pairs={{0,1},{1,0},{2,3},{3,2},{4,5},{5,4},{6,7},{7,6},{8,9},{9,8},{10,11... | collective-permute-start | bytes 2359304 | tf_op jit(solution)/shard_map/ppermute | solution.py:41
  379.0 4.1 collective-permute-start.15
  (46 other events, 313.1 us)
Sparse Core Ops, SparseCore 0:
  10.4 97.0 all-gather.2
  266.5 91.4 reduce-scatter.1
  362.9 171.1 all-reduce.2

commit v12 on v10

--- a/solution.py
+++ b/solution.py
@@ -17,6 +17,7 @@
 PLANE = 16
 SEGMENTS = 3
 EARLY = 1
+FIRST = 2
 AUX = 16
 LANES = 256
 MORE = 128
@@ -153,8 +154,9 @@
         at = pl.multiple_of(g * HD, HD)
         keys = all_keys(blocks, at)
         values = all_keys(blocks, kv_rows + at)
-
-        def one_head(head, sums):
+        key_sum = value_sum = None
+        for j in range(group):
+            head = g * group + j
             start = pl.multiple_of(head * HD, HD)
             query, grad = (q_ref[pl.ds(start, HD), :], g_ref[pl.ds(start, HD), :])
             scores = contract(keys, query, TN) + bias[...]
@@ -162,18 +164,15 @@
             grad_probs = contract(values, grad, TN)
             delta = jnp.sum(probs * grad_probs, axis=0, keepdims=True)
             grad_scores = (probs * (grad_probs - delta)).astype(BF16)
+            key_part = contract(query, grad_scores, NT)
+            value_part = contract(grad, probs.astype(BF16), NT)
+            key_sum = key_part if key_sum is None else key_sum + key_part
+            value_sum = value_part if value_sum is None else value_sum + value_part
             turned = contract(keys, grad_scores, NN) * (HD**-0.5)
             first, second = (turned[:half], turned[half:])
             cosine, sine = (cos_ref[...], sin_ref[...])
             dq_ref[pl.ds(start, half), :] = (first * cosine + second * sine).astype(BF16)
             dq_ref[pl.ds(start + half, half), :] = (second * cosine - first * sine).astype(BF16)
-            return (
-                sums[0] + contract(query, grad_scores, NT),
-                sums[1] + contract(grad, probs.astype(BF16), NT),
-            )
-
-        zero = jnp.zeros(keys.shape, F32)
-        key_sum, value_sum = lax.fori_loop(g * group, (g + 1) * group, one_head, (zero, zero))
         for number, grad_ref in enumerate(grads):
             piece = slice(number * tok, (number + 1) * tok)
             grad_ref[pl.ds(at, HD), :] = key_sum[:, piece].astype(grad_ref.dtype)
@@ -357,35 +356,35 @@
     weight = pl.BlockSpec((1, width, triple), lambda s, j: (s, 0, 0))
     return pl.pallas_call(
         expert_first_kernel,
-        grid=(EARLY, 2),
+        grid=(FIRST, 2),
         in_specs=[part, weight, weight],
         out_specs=part,
-        out_shape=jax.ShapeDtypeStruct((sources, EARLY * RANK_ROWS, width), BF16),
+        out_shape=jax.ShapeDtypeStruct((sources, FIRST * RANK_ROWS, width), BF16),
         compiler_params=pltpu.CompilerParams(vmem_limit_bytes=56 << 20),
         cost_estimate=pl.CostEstimate(
-            flops=4 * sources * EARLY * RANK_ROWS * width * triple,
-            bytes_accessed=4 * sources * EARLY * RANK_ROWS * width + 4 * EARLY * width * triple,
-            transcendentals=sources * EARLY * RANK_ROWS * triple * 2 // 3,
+            flops=4 * sources * FIRST * RANK_ROWS * width * triple,
+            bytes_accessed=4 * sources * FIRST * RANK_ROWS * width + 4 * FIRST * width * triple,
+            transcendentals=sources * FIRST * RANK_ROWS * triple * 2 // 3,
         ),
     )(rows, own, peer)
 
 
-def of_segment(early_ref, late_ref, sources=slice(None), lanes=slice(None)):
+def of_segment(split, early_ref, late_ref, sources=slice(None), lanes=slice(None)):
     early, late = (ref[sources, :, lanes] for ref in (early_ref, late_ref))
-    chosen = jnp.where(pl.program_id(0) < EARLY, early, late)
+    chosen = jnp.where(pl.program_id(0) < split, early, late)
     return chosen.reshape(-1, chosen.shape[-1])
 
 
-def expert_kernel(x_ref, g1_ref, g2_ref, own_ref, peer_ref, dx_ref, own_acts, peer_acts):
+def expert_kernel(x1_ref, x2_ref, g1_ref, g2_ref, own_ref, peer_ref, dx_ref, own_acts, peer_acts):
     hidden = own_ref.shape[-1] // 3
-    sources = x_ref.shape[0] // 2
+    sources = dx_ref.shape[0] // 2
     count = sources * RANK_ROWS
 
     def one_half(half, _):
         here = pl.ds(half * sources, sources)
         there = pl.ds(pl.multiple_of(half * count, count), count)
-        rows = x_ref[here].reshape(count, -1)
-        grads = of_segment(g1_ref, g2_ref, here)
+        rows = of_segment(FIRST, x1_ref, x2_ref, here)
+        grads = of_segment(EARLY, g1_ref, g2_ref, here)
         back = None
         for weights, acts in ((own_ref, own_acts), (peer_ref, peer_acts)):
             both = contract(rows, weights[0, :, : 2 * hidden], NN)
@@ -405,20 +404,20 @@
     lax.fori_loop(0, 2, one_half, 0)
 
 
-def segment_specs(block):
+def segment_specs(block, split):
     return [
-        pl.BlockSpec(block, lambda s: (0, s, 0)),
-        pl.BlockSpec(block, lambda s: (0, jnp.minimum(s, EARLY - 1), 0)),
-        pl.BlockSpec(block, lambda s: (0, jnp.maximum(s - EARLY, 0), 0)),
+        pl.BlockSpec(block, lambda s: (0, jnp.minimum(s, split - 1), 0)),
+        pl.BlockSpec(block, lambda s: (0, jnp.maximum(s - split, 0), 0)),
     ]
 
 
 def expert_back(rows, grads, own, peer):
-    sources, lines, width = rows.shape
-    segments, triple = (lines // RANK_ROWS, own.shape[-1])
-    count = sources * RANK_ROWS
-    specs = segment_specs((sources, RANK_ROWS, width))
-    wide = specs[0]
+    sources, _, width = rows[0].shape
+    segments, triple = (SEGMENTS, own.shape[-1])
+    lines, count = (segments * RANK_ROWS, sources * RANK_ROWS)
+    block = (sources, RANK_ROWS, width)
+    specs = segment_specs(block, FIRST) + segment_specs(block, EARLY)
+    wide = pl.BlockSpec(block, lambda s: (0, s, 0))
     weight = pl.BlockSpec((1, width, triple), lambda s: (s, 0, 0))
     act = pl.BlockSpec((1, count, triple), lambda s: (s, 0, 0))
     return pl.pallas_call(
@@ -427,7 +426,7 @@
         in_specs=[*specs, weight, weight],
         out_specs=[wide, act, act],
         out_shape=[
-            jax.ShapeDtypeStruct(rows.shape, BF16),
+            jax.ShapeDtypeStruct((sources, lines, width), BF16),
             jax.ShapeDtypeStruct((segments, count, triple), BF16),
             jax.ShapeDtypeStruct((segments, count, triple), BF16),
         ],
@@ -437,19 +436,21 @@
             bytes_accessed=6 * sources * lines * width + 4 * segments * width * triple,
             transcendentals=2 * sources * lines * triple // 3,
         ),
-    )(rows, *grads, own, peer)
-
-
-def expert_sums_kernel(x_ref, g1_ref, g2_ref, own_acts, peer_acts, own_ref, peer_ref, sum_own, *outs):
-    width = x_ref.shape[-1]
+    )(*rows, *grads, own, peer)
+
+
+def expert_sums_kernel(
+    x1_ref, x2_ref, g1_ref, g2_ref, own_acts, peer_acts, own_ref, peer_ref, sum_own, *outs
+):
+    width = x1_ref.shape[-1]
     hidden = own_ref.shape[-1]
     late_ref = outs[3]
     chunk = width // 3
 
     def one_chunk(c, _):
         lanes = pl.ds(pl.multiple_of(c * chunk, chunk), chunk)
-        rows = x_ref[:, :, lanes].reshape(-1, chunk)
-        grads = of_segment(g1_ref, g2_ref, slice(None), lanes)
+        rows = of_segment(FIRST, x1_ref, x2_ref, slice(None), lanes)
+        grads = of_segment(EARLY, g1_ref, g2_ref, slice(None), lanes)
         for side, acts in enumerate((own_acts, peer_acts)):
             first = contract(rows, acts[0, :, : 2 * hidden], TN).astype(BF16)
             second = contract(grads, acts[0, :, 2 * hidden :], TN).astype(BF16)
@@ -463,7 +464,7 @@
         return 0
 
     lax.fori_loop(0, 3, one_chunk, 0)
-    sources = x_ref.shape[0] // 2
+    sources = x1_ref.shape[0] // 2
     count = sources * RANK_ROWS
 
     def one_half(half, _):
@@ -473,14 +474,15 @@
         late_ref[pl.ds(half * sources, sources)] = out.astype(BF16).reshape(sources, RANK_ROWS, -1)
         return 0
 
-    @pl.when(pl.program_id(0) >= EARLY)
+    @pl.when(pl.program_id(0) >= FIRST)
     def _():
         lax.fori_loop(0, 2, one_half, 0)
 
 
 def expert_sums(rows, grads, own_acts, peer_acts, own, peer):
-    sources, lines, width = rows.shape
-    segments, triple = (lines // RANK_ROWS, own.shape[-1])
+    sources, _, width = rows[0].shape
+    segments, triple = (SEGMENTS, own.shape[-1])
+    lines = segments * RANK_ROWS
     hidden = triple // 3
     count = sources * RANK_ROWS
     block = (sources, RANK_ROWS, width)
@@ -489,20 +491,20 @@
     return pl.pallas_call(
         expert_sums_kernel,
         grid=(segments,),
-        in_specs=[*segment_specs(block), act, act, down, down],
+        in_specs=[*segment_specs(block, FIRST), *segment_specs(block, EARLY), act, act, down, down],
         out_specs=[pl.BlockSpec((1, width, triple), lambda s: (s, 0, 0))]
         + [pl.BlockSpec((1, width, hidden), lambda s: (s, 0, 0))] * 3
-        + [pl.BlockSpec(block, lambda s: (0, jnp.maximum(s - EARLY, 0), 0))],
+        + [pl.BlockSpec(block, lambda s: (0, jnp.maximum(s - FIRST, 0), 0))],
         out_shape=[jax.ShapeDtypeStruct((segments, width, triple), BF16)]
         + [jax.ShapeDtypeStruct((segments, width, hidden), BF16)] * 3
-        + [jax.ShapeDtypeStruct((sources, (segments - EARLY) * RANK_ROWS, width), BF16)],
+        + [jax.ShapeDtypeStruct((sources, (segments - FIRST) * RANK_ROWS, width), BF16)],
         compiler_params=pltpu.CompilerParams(vmem_limit_bytes=60 << 20),
         cost_estimate=pl.CostEstimate(
             flops=6 * sources * lines * width * triple,
             bytes_accessed=6 * sources * lines * width + 5 * segments * width * triple,
             transcendentals=0,
         ),
-    )(rows, *grads, own_acts, peer_acts, own, peer)
+    )(*rows, *grads, own_acts, peer_acts, own, peer)
 
 
 def both_cores_kernel(own_ref, *refs):
@@ -771,12 +773,20 @@
     inverse2 = rms_scale(hidden1)
     normed2 = (hidden1 * inverse2 * norm2_gain).astype(BF16)
 
-    rows_out = dispatch(pick, normed2)
-    rows_out = after(rows_out, grad_rows[1])
-    own = after(own, rows_out)
+    shape = (PLANE, SEGMENTS * RANK_ROWS, -1)
+    first_pick, last_pick = (
+        pick.reshape(shape)[:, first * RANK_ROWS : last * RANK_ROWS].reshape(-1, tok_dev)
+        for first, last in ((0, FIRST), (FIRST, SEGMENTS))
+    )
+    rows_first, rows_last, *_ = lax.optimization_barrier(
+        (dispatch(first_pick, normed2), dispatch(last_pick, normed2), grad_rows[1])
+    )
+    rows_first = in_plane(rows_first)
+    own = after(own, rows_first)
     peer = swapped(own)
-    rows_in = in_plane(rows_out)
-    out_early = in_plane(expert_first(rows_in, own, peer))
+    rows_last = in_plane(after(rows_last, rows_first))
+    rows_in = (rows_first, rows_last)
+    out_early = in_plane(after(expert_first(rows_first, own, peer), rows_last))
     back, own_acts, peer_acts = expert_back(rows_in, grad_rows, own, peer)
 
     def combined(weights, rows):

time: 554 us -> 571 us (1.031)
  waiting for transfers between devices: 196 us -> 232 us
  blocking collectives: 67.8 us -> 40.8 us
    all_to_all x1, blocking collectives: 67.8 us -> 40.8 us  [in_plane(): lax.all_to_all(rows, 'dp', 0, 0, tiled=True, axis_index_groups=plane_groups)]
    all_to_all x5 -> x6, waiting for transfers between devices: 18.7 us -> 41 us  [in_plane(): lax.all_to_all(rows, 'dp', 0, 0, tiled=True, axis_index_groups=plane_groups)]
    ppermute x8, waiting for transfers between devices: 13.9 us -> 25 us  [swapped(): return lax.ppermute(array, 'tensor', [(0, 1), (1, 0)])]
    all_to_all x5 -> x6, starting transfers between devices: 38.3 us -> 44.5 us  [in_plane(): lax.all_to_all(rows, 'dp', 0, 0, tiled=True, axis_index_groups=plane_groups)]
    unnamed x97 -> x89, local copies, waits for them, and re-layouts: 14.1 us -> 11.4 us
    pallas_call x3 -> x4, Pallas kernels: 14 us -> 15.3 us  [dispatch(): pl.pallas_call(dispatch_kernel, grid=(slots // LANES,), in_specs=[pl.Bloc...]
  transfers between devices with their start and end apart: 24 -> 25, of which waited for: 12 -> 14; matrix products, arithmetic and copies ran while one was open for 7% -> 7% of each run, Pallas kernels for 22% -> 23%
where the time goes in v12:
time: 571 us; the launch traced here: 569 us
  waiting for transfers between devices  232 us (41%)
  Pallas kernels  146 us (26%)
  starting transfers between devices  83.8 us (15%)
  blocking collectives  40.8 us (7%)
  other arithmetic  29 us (5%)
  local copies, waits for them, and re-layouts  20.1 us (4%)
  between operations  14.4 us (3%)
    psum x1, waiting for transfers between devices, shards(): summed = lax.psum(parts, 'dp')  154 us
    all_to_all x6, starting transfers between devices, in_plane(): lax.all_to_all(rows, 'dp', 0, 0, tiled=True, axis_index_groups=plane_groups)  44.5 us
    all_to_all x6, waiting for transfers between devices, in_plane(): lax.all_to_all(rows, 'dp', 0, 0, tiled=True, axis_index_groups=plane_groups)  41 us
    all_to_all x1, blocking collectives, in_plane(): lax.all_to_all(rows, 'dp', 0, 0, tiled=True, axis_index_groups=plane_groups)  40.8 us
    ppermute x8, waiting for transfers between devices, swapped(): return lax.ppermute(array, 'tensor', [(0, 1), (1, 0)])  25 us
    ppermute x8, starting transfers between devices, passed_along(): lax.ppermute(value, 'dp', [(s, s + steps) for s in range(first, last)])  20.1 us
    pallas_call x1, Pallas kernels, expert_back(): pl.pallas_call(expert_kernel, grid=(segments,), in_specs=[*specs, weight,...  20 us
    ppermute x8, starting transfers between devices, swapped(): return lax.ppermute(array, 'tensor', [(0, 1), (1, 0)])  19 us
  transfers between devices with their start and end apart: 25, of which 14 were waited for; matrix products, arithmetic and copies ran while one was open for 7% of the time, Pallas kernels for 23%

profile of v12, /device:TPU:1, one launch (start us, length us, event | category | flops | bytes accessed | tf_op | source)
XLA Modules:
  0.0 569.3 jit_solution(9279745209904882704)
XLA Ops:
  18.3 8.6 %all-to-all-start = ((bf16[16,32,1536]{2,1,0:T(8,128)(2,1)}), bf16[16,32,1536]{2,1,0:T(8,128)(2,1)}, u32[]{:S(2)}, u32[]{:S(2)}) async-start(bf16[16,32,1536]{2,1,0:T(8,128)(2,1)} %bitcast.77), calls=%async_computation | async-start | bytes 3145728 | tf_op jit(solution)/shard_map/all_to_all | solution.py:746
  41.5 5.0 collective-permute-start.1
  59.5 14.9 %all-to-all-start.1 = ((bf16[16,64,1536]{2,1,0:T(8,128)(2,1)}), bf16[16,64,1536]{2,1,0:T(8,128)(2,1)}, u32[]{:S(2)}, u32[]{:S(2)}) async-start(bf16[16,64,1536]{2,1,0:T(8,128)(2,1)} %bitcast.72), calls=%async_computation.1 | async-start | bytes 6291456 | tf_op jit(solution)/shard_map/all_to_all | solution.py:746
  75.3 12.5 %shard_map.302 = (bf16[768,256]{1,0:T(8,128)(2,1)S(1)}, f32[12,256]{1,0:T(8,128)S(1)}, f32[12,256]{1,0:T(8,128)S(1)}) custom-call(bf16[768,256]{1,0:T(8,128)(2,1)S(1)} %copy-done.17, bf16[528,256]{1,0:T(8,128)(2,1)} %collective-permute-done.k4, bf16[528,256]{1,0:T(8,128)(2,1)} %collective-permute-done.1.k3, bf16[528,256]{1,0:T(8,128)(2,1)} %collective-permute-done.2.k2, ...), custom_call_target="tpu_custom_call" | custom-call | flops 1006632960 | bytes 2138112 | tf_op jit(solution)/shard_map/pallas_call | solution.py:125
  105.2 6.4 %all-to-all-done.1.g2_ref = bf16[16,64,1536]{2,1,0:T(8,128)(2,1)} async-done(((bf16[16,64,1536]{2,1,0:T(8,128)(2,1)}), bf16[16,64,1536]{2,1,0:T(8,128)(2,1)}, u32[]{:S(2)}, u32[]{:S(2)}) %all-to-all-start.1) | async-done | bytes 3145760 | tf_op jit(solution)/shard_map/all_to_all | solution.py:746
  111.5 40.8 %all_to_all.35.x1_ref.x_ref = bf16[16,64,1536]{2,1,0:T(8,128)(2,1)} all-to-all(bf16[16,64,1536]{2,1,0:T(8,128)(2,1)} %bitcast.71), channel_id=1, replica_groups={{0,2,4,6,8,10,12,14,16,18,20,22,24,26,28,30},{32,34,36,38,40,42,44,46,4..., dimensions={0} | all-to-all | bytes 6291456 | tf_op jit(solution)/shard_map/all_to_all | solution.py:746
  152.3 5.9 %collective-permute-start.5 = (bf16[4,1536,768]{2,1,0:T(8,128)(2,1)}, bf16[4,1536,768]{2,1,0:T(8,128)(2,1)}, u32[]{:S(2)}, u32[]{:S(2)}) collective-permute-start(bf16[4,1536,768]{2,1,0:T(8,128)(2,1)} %bitcast.73), channel_id=1, source_target_pairs={{0,1},{1,0},{2,3},{3,2},{4,5},{5,4},{6,7},{7,6},{8,9},{9,8},{10,11... | collective-permute-start | bytes 28311560 | tf_op jit(solution)/shard_map/ppermute | solution.py:42
  162.6 10.2 %collective-permute-done.5.peer_ref = bf16[4,1536,768]{2,1,0:T(8,128)(2,1)} collective-permute-done((bf16[4,1536,768]{2,1,0:T(8,128)(2,1)}, bf16[4,1536,768]{2,1,0:T(8,128)(2,1)}, u32[]{:S(2)}, u32[]{:S(2)}) %collective-permute-start.5) | collective-permute-done | bytes 9437216 | tf_op jit(solution)/shard_map/ppermute | solution.py:42
  172.8 11.2 %shard_map.307 = bf16[16,64,1536]{2,1,0:T(8,128)(2,1)} custom-call(bf16[16,64,1536]{2,1,0:T(8,128)(2,1)} %all_to_all.35.x1_ref.x_ref, bf16[4,1536,768]{2,1,0:T(8,128)(2,1)} %bitcast.74, bf16[4,1536,768]{2,1,0:T(8,128)(2,1)} %collective-permute-done.5.peer_ref), custom_call_target="tpu_custom_call" | custom-call | flops 4831838208 | bytes 15728640 | tf_op jit(solution)/shard_map/pallas_call | solution.py:357
  191.1 20.0 %shard_map.306 = (bf16[16,96,1536]{2,1,0:T(8,128)(2,1)}, bf16[3,512,768]{2,1,0:T(8,128)(2,1)}, bf16[3,512,768]{2,1,0:T(8,128)(2,1)}) custom-call(bf16[16,64,1536]{2,1,0:T(8,128)(2,1)} %all_to_all.35.x1_ref.x_ref, bf16[16,32,1536]{2,1,0:T(8,128)(2,1)} %all-to-all-done.3.x2_ref, bf16[16,32,1536]{2,1,0:T(8,128)(2,1)} %all-to-all-done.g1_ref, ...), custom_call_target="tpu_custom_call" | custom-call | flops 12683575296 | bytes 28311552 | tf_op jit(solution)/shard_map/pallas_call | solution.py:423
  211.2 20.4 %all-to-all-done.4 = bf16[16,64,1536]{2,1,0:T(8,128)(2,1)} async-done(((bf16[16,64,1536]{2,1,0:T(8,128)(2,1)}), bf16[16,64,1536]{2,1,0:T(8,128)(2,1)}, u32[]{:S(2)}, u32[]{:S(2)}) %all-to-all-start.4) | async-done | bytes 3145760 | tf_op jit(solution)/shard_map/all_to_all | solution.py:746
  231.6 7.2 %all-to-all-start.5 = ((bf16[16,96,1536]{2,1,0:T(8,128)(2,1)}), bf16[16,96,1536]{2,1,0:T(8,128)(2,1)}, u32[]{:S(2)}, u32[]{:S(2)}) async-start(bf16[16,96,1536]{2,1,0:T(8,128)(2,1)} %get-tuple-element.83), calls=%async_computation.5 | async-start | bytes 9437184 | tf_op jit(solution)/shard_map/all_to_all | solution.py:746
  239.0 17.9 %shard_map.308 = (bf16[3,1536,768]{2,1,0:T(8,128)(2,1)}, bf16[3,1536,256]{2,1,0:T(8,128)(2,1)}, bf16[3,1536,256]{2,1,0:T(8,128)(2,1)}, bf16[3,1536,256]{2,1,0:T(8,128)(2,1)}, bf16[16,32,1536]{2,1,0:T(8,128)(2,1)}) custom-call(bf16[16,64,1536]{2,1,0:T(8,128)(2,1)} %all_to_all.35.x1_ref.x_ref, bf16[16,32,1536]{2,1,0:T(8,128)(2,1)} %all-to-all-done.3.x2_ref, ...), custom_call_target="tpu_custom_call" | custom-call | flops 10871635968 | bytes 31850496 | tf_op jit(solution)/shard_map/pallas_call | solution.py:491
  270.8 11.8 %shard_map.309 = bf16[4,1536,768]{2,1,0:T(8,128)(2,1)} custom-call(bf16[3,1536,768]{2,1,0:T(8,128)(2,1)} %get-tuple-element.86.own_ref, bf16[3,1536,256]{2,1,0:T(8,128)(2,1)} %collective-permute-done.6.refs_0_, bf16[3,1536,256]{2,1,0:T(8,128)(2,1)} %collective-permute-done.7.refs_1_, bf16[3,1536,256]{2,1,0:T(8,128)(2,1)} %collective-permute-done.8.refs_2_), custom_call_target="tpu_custom_call" | custom-call | flops 4718592 | bytes 28311552 | tf_op jit(solution)/shard_map/pallas_call | solution.py:532
  283.9 12.0 %all-to-all-done.5.rows_ref = bf16[16,96,1536]{2,1,0:T(8,128)(2,1)} async-done(((bf16[16,96,1536]{2,1,0:T(8,128)(2,1)}), bf16[16,96,1536]{2,1,0:T(8,128)(2,1)}, u32[]{:S(2)}, u32[]{:S(2)}) %all-to-all-start.5) | async-done | bytes 4718624 | tf_op jit(solution)/shard_map/all_to_all | solution.py:746
  295.8 5.1 shard_map.310
  300.9 5.9 %collective-permute-start.9 = (bf16[256,1536]{1,0:T(8,128)(2,1)}, bf16[256,1536]{1,0:T(8,128)(2,1)}, u32[]{:S(2)}, u32[]{:S(2)}) collective-permute-start(bf16[256,1536]{1,0:T(8,128)(2,1)} %shard_map.310), channel_id=1, source_target_pairs={{0,1},{1,0},{2,3},{3,2},{4,5},{5,4},{6,7},{7,6},{8,9},{9,8},{10,11... | collective-permute-start | bytes 2359304 | tf_op jit(solution)/shard_map/ppermute | solution.py:42
  318.7 16.5 %shard_map.311 = (bf16[768,256]{1,0:T(8,128)(2,1)S(1)}, bf16[512,256]{1,0:T(8,128)(2,1)}, bf16[512,256]{1,0:T(8,128)(2,1)}, bf16[512,256]{1,0:T(8,128)(2,1)S(1)}...) custom-call(bf16[768,256]{1,0:T(8,128)(2,1)S(1)} %copy-done.18, bf16[768,256]{1,0:T(8,128)(2,1)S(1)} %fusion.12.g_ref, ...), custom_call_target="tpu_custom_call" | custom-call | flops 125829120000 | bytes 3883008 | tf_op jit(solution)/shard_map/pallas_call | solution.py:188
  341.9 6.9 %shard_map.312._ = bf16[1536,2304]{1,0:T(8,128)(2,1)} custom-call(bf16[256,1536]{1,0:T(8,128)(2,1)} %copy-done.8, bf16[768,256]{1,0:T(8,128)(2,1)} %copy-done.12, bf16[768,256]{1,0:T(8,128)(2,1)} %copy-done.11, bf16[256,1536]{1,0:T(8,128)(2,1)} %copy-done.25), custom_call_target="tpu_custom_call" | custom-call | flops 1207959552 | bytes 4718592 | tf_op jit(solution)/shard_map/pallas_call | solution.py:561
  364.2 5.8 %shard_map.313 = bf16[1536,2304]{1,0:T(8,128)(2,1)} custom-call(bf16[256,1536]{1,0:T(8,128)(2,1)} %copy-done.8, bf16[512,256]{1,0:T(8,128)(2,1)} %pad_maximum_fusion.1.kv_ref, f32[128,1536]{1,0:T(8,128)} %select_maximum_fusion.extra_ref, bf16[1536,2304]{1,0:T(8,128)(2,1)} %shard_map.312._), custom_call_target="tpu_custom_call", output_to_operand_aliasing={{}: (3, {})} | custom-call | flops 402653184 | bytes 2359296 | tf_op jit(solution)/shard_map/pallas_call | solution.py:583
  379.2 5.0 pad_maximum_fusion.rows_ref
  384.2 5.2 shard_map.314
  396.6 154.5 %all-reduce.3.cloned.1.call-done.in_ref = bf16[1536,2304]{1,0:T(8,128)(2,1)} async-done(((bf16[1536,2304]{1,0:T(8,128)(2,1)}), bf16[1536,2304]{1,0:T(8,128)(2,1)}) %all-reduce.3.cloned.1.call-update) | async-done | bytes 7077904 | tf_op jit(solution)/shard_map/psum | solution.py:844
  551.1 10.2 %shard_map.315 = (f32[768,1536]{1,0:T(8,128)}, f32[1536,768]{1,0:T(8,128)}, f32[1536,256]{1,0:T(8,128)}, f32[1536,256]{1,0:T(8,128)}, f32[8,1536]{1,0:T(8,128)},...) custom-call(bf16[1536,2304]{1,0:T(8,128)(2,1)} %all-reduce.3.cloned.1.call-done.in_ref, ...), custom_call_target="tpu_custom_call" | custom-call | flops 3538944 | bytes 28311552 | tf_op jit(solution)/shard_map/pallas_call | solution.py:646
  (202 shorter events, 135.3 us)
Async XLA Ops:
  7.2 145.1 %all-gather.3.cloned.1.call-start = ((), (), s32[]{:S(2)}) async-start(), calls=%async_computation.10 | async-start | bytes 11796480 | tf_op jit(solution)/shard_map/all_gather | solution.py:768
  18.3 41.1 %all-to-all-start = ((bf16[16,32,1536]{2,1,0:T(8,128)(2,1)}), bf16[16,32,1536]{2,1,0:T(8,128)(2,1)}, u32[]{:S(2)}, u32[]{:S(2)}) async-start(bf16[16,32,1536]{2,1,0:T(8,128)(2,1)} %bitcast.77), calls=%async_computation | async-start | bytes 3145728 | tf_op jit(solution)/shard_map/all_to_all | solution.py:746
  37.5 21.9 %collective-permute-start = (bf16[528,256]{1,0:T(8,128)(2,1)}, bf16[528,256]{1,0:T(8,128)(2,1)}, u32[]{:S(2)}, u32[]{:S(2)}) collective-permute-start(bf16[528,256]{1,0:T(8,128)(2,1)} %get-tuple-element.72.k0), channel_id=1, source_target_pairs={{0,8},{2,10},{4,12},{6,14},{8,16},{10,18},{12,20},{14,22},{16,24},... | collective-permute-start | bytes 811016 | tf_op jit(solution)/shard_map/ppermute | solution.py:52
  41.5 17.9 %collective-permute-start.1 = (bf16[528,256]{1,0:T(8,128)(2,1)}, bf16[528,256]{1,0:T(8,128)(2,1)}, u32[]{:S(2)}, u32[]{:S(2)}) collective-permute-start(bf16[528,256]{1,0:T(8,128)(2,1)} %get-tuple-element.72.k0), channel_id=1, source_target_pairs={{0,6},{2,8},{4,10},{6,12},{8,14},{10,16},{12,18},{14,20},{16,22},{... | collective-permute-start | bytes 811016 | tf_op jit(solution)/shard_map/ppermute | solution.py:52
  46.6 12.9 %collective-permute-start.2 = (bf16[528,256]{1,0:T(8,128)(2,1)}, bf16[528,256]{1,0:T(8,128)(2,1)}, u32[]{:S(2)}, u32[]{:S(2)}) collective-permute-start(bf16[528,256]{1,0:T(8,128)(2,1)} %get-tuple-element.72.k0), channel_id=1, source_target_pairs={{0,4},{2,6},{4,8},{6,10},{8,12},{10,14},{12,16},{14,18},{16,20},{1... | collective-permute-start | bytes 811016 | tf_op jit(solution)/shard_map/ppermute | solution.py:52
  49.9 9.5 %collective-permute-start.3 = (bf16[528,256]{1,0:T(8,128)(2,1)}, bf16[528,256]{1,0:T(8,128)(2,1)}, u32[]{:S(2)}, u32[]{:S(2)}) collective-permute-start(bf16[528,256]{1,0:T(8,128)(2,1)} %get-tuple-element.72.k0), channel_id=1, source_target_pairs={{0,2},{2,4},{4,6},{6,8},{8,10},{10,12},{12,14},{14,16},{16,18},{18... | collective-permute-start | bytes 811016 | tf_op jit(solution)/shard_map/ppermute | solution.py:52
  59.5 52.1 %all-to-all-start.1 = ((bf16[16,64,1536]{2,1,0:T(8,128)(2,1)}), bf16[16,64,1536]{2,1,0:T(8,128)(2,1)}, u32[]{:S(2)}, u32[]{:S(2)}) async-start(bf16[16,64,1536]{2,1,0:T(8,128)(2,1)} %bitcast.72), calls=%async_computation.1 | async-start | bytes 6291456 | tf_op jit(solution)/shard_map/all_to_all | solution.py:746
  88.6 5.1 collective-permute-start.4
  152.3 20.5 %collective-permute-start.5 = (bf16[4,1536,768]{2,1,0:T(8,128)(2,1)}, bf16[4,1536,768]{2,1,0:T(8,128)(2,1)}, u32[]{:S(2)}, u32[]{:S(2)}) collective-permute-start(bf16[4,1536,768]{2,1,0:T(8,128)(2,1)} %bitcast.73), channel_id=1, source_target_pairs={{0,1},{1,0},{2,3},{3,2},{4,5},{5,4},{6,7},{7,6},{8,9},{9,8},{10,11... | collective-permute-start | bytes 28311560 | tf_op jit(solution)/shard_map/ppermute | solution.py:42
  158.2 28.1 %all-to-all-start.3 = ((bf16[16,32,1536]{2,1,0:T(8,128)(2,1)}), bf16[16,32,1536]{2,1,0:T(8,128)(2,1)}, u32[]{:S(2)}, u32[]{:S(2)}) async-start(bf16[16,32,1536]{2,1,0:T(8,128)(2,1)} %bitcast.78), calls=%async_computation.3 | async-start | bytes 3145728 | tf_op jit(solution)/shard_map/all_to_all | solution.py:746
  186.3 45.3 %all-to-all-start.4 = ((bf16[16,64,1536]{2,1,0:T(8,128)(2,1)}), bf16[16,64,1536]{2,1,0:T(8,128)(2,1)}, u32[]{:S(2)}, u32[]{:S(2)}) async-start(bf16[16,64,1536]{2,1,0:T(8,128)(2,1)} %shard_map.307), calls=%async_computation.4 | async-start | bytes 6291456 | tf_op jit(solution)/shard_map/all_to_all | solution.py:746
  231.6 64.3 %all-to-all-start.5 = ((bf16[16,96,1536]{2,1,0:T(8,128)(2,1)}), bf16[16,96,1536]{2,1,0:T(8,128)(2,1)}, u32[]{:S(2)}, u32[]{:S(2)}) async-start(bf16[16,96,1536]{2,1,0:T(8,128)(2,1)} %get-tuple-element.83), calls=%async_computation.5 | async-start | bytes 9437184 | tf_op jit(solution)/shard_map/all_to_all | solution.py:746
  238.7 136.2 %reduce-scatter.2.cloned.1.call-start = ((), (), s32[]{:S(2)}) async-start(), calls=%async_computation.8 | async-start | bytes 11796480 | tf_op jit(solution)/shard_map/reduce_scatter | solution.py:801
  256.8 7.2 %collective-permute-start.6 = (bf16[3,1536,256]{2,1,0:T(8,128)(2,1)}, bf16[3,1536,256]{2,1,0:T(8,128)(2,1)}, u32[]{:S(2)}, u32[]{:S(2)}) collective-permute-start(bf16[3,1536,256]{2,1,0:T(8,128)(2,1)} %get-tuple-element.87), channel_id=1, source_target_pairs={{0,1},{1,0},{2,3},{3,2},{4,5},{5,4},{6,7},{7,6},{8,9},{9,8},{10,11... | collective-permute-start | bytes 7077896 | tf_op jit(solution)/shard_map/ppermute | solution.py:42
  259.5 7.9 %collective-permute-start.7 = (bf16[3,1536,256]{2,1,0:T(8,128)(2,1)}, bf16[3,1536,256]{2,1,0:T(8,128)(2,1)}, u32[]{:S(2)}, u32[]{:S(2)}) collective-permute-start(bf16[3,1536,256]{2,1,0:T(8,128)(2,1)} %get-tuple-element.88), channel_id=1, source_target_pairs={{0,1},{1,0},{2,3},{3,2},{4,5},{5,4},{6,7},{7,6},{8,9},{9,8},{10,11... | collective-permute-start | bytes 7077896 | tf_op jit(solution)/shard_map/ppermute | solution.py:42
  259.6 11.2 %collective-permute-start.8 = (bf16[3,1536,256]{2,1,0:T(8,128)(2,1)}, bf16[3,1536,256]{2,1,0:T(8,128)(2,1)}, u32[]{:S(2)}, u32[]{:S(2)}) collective-permute-start(bf16[3,1536,256]{2,1,0:T(8,128)(2,1)} %get-tuple-element.89), channel_id=1, source_target_pairs={{0,1},{1,0},{2,3},{3,2},{4,5},{5,4},{6,7},{7,6},{8,9},{9,8},{10,11... | collective-permute-start | bytes 7077896 | tf_op jit(solution)/shard_map/ppermute | solution.py:42
  300.9 10.8 %collective-permute-start.9 = (bf16[256,1536]{1,0:T(8,128)(2,1)}, bf16[256,1536]{1,0:T(8,128)(2,1)}, u32[]{:S(2)}, u32[]{:S(2)}) collective-permute-start(bf16[256,1536]{1,0:T(8,128)(2,1)} %shard_map.310), channel_id=1, source_target_pairs={{0,1},{1,0},{2,3},{3,2},{4,5},{5,4},{6,7},{7,6},{8,9},{9,8},{10,11... | collective-permute-start | bytes 2359304 | tf_op jit(solution)/shard_map/ppermute | solution.py:42
  307.1 62.9 %all-to-all-start.6 = ((bf16[16,32,1536]{2,1,0:T(8,128)(2,1)}), bf16[16,32,1536]{2,1,0:T(8,128)(2,1)}, u32[]{:S(2)}, u32[]{:S(2)}) async-start(bf16[16,32,1536]{2,1,0:T(8,128)(2,1)} %get-tuple-element.105), calls=%async_computation.7 | async-start | bytes 3145728 | tf_op jit(solution)/shard_map/all_to_all | solution.py:746
  311.7 239.4 %all-reduce.3.cloned.1.call-start = ((), (), s32[]{:S(2)}) async-start(), calls=%async_computation.9 | async-start | bytes 14155776 | tf_op jit(solution)/shard_map/psum | solution.py:844
  336.7 12.9 %collective-permute-start.10 = (bf16[512,256]{1,0:T(8,128)(2,1)}, bf16[512,256]{1,0:T(8,128)(2,1)}, u32[]{:S(2)}, u32[]{:S(2)}) collective-permute-start(bf16[512,256]{1,0:T(8,128)(2,1)} %get-tuple-element.93), channel_id=1, source_target_pairs={{8,0},{10,2},{12,4},{14,6},{16,8},{18,10},{20,12},{22,14},{24,16},... | collective-permute-start | bytes 786440 | tf_op jit(solution)/shard_map/ppermute | solution.py:52
  338.0 15.4 %collective-permute-start.11 = (bf16[512,256]{1,0:T(8,128)(2,1)}, bf16[512,256]{1,0:T(8,128)(2,1)}, u32[]{:S(2)}, u32[]{:S(2)}) collective-permute-start(bf16[512,256]{1,0:T(8,128)(2,1)} %get-tuple-element.94), channel_id=1, source_target_pairs={{6,0},{8,2},{10,4},{12,6},{14,8},{16,10},{18,12},{20,14},{22,16},{... | collective-permute-start | bytes 786440 | tf_op jit(solution)/shard_map/ppermute | solution.py:52
  339.3 16.9 %collective-permute-start.12 = (bf16[512,256]{1,0:T(8,128)(2,1)S(1)}, bf16[512,256]{1,0:T(8,128)(2,1)}, u32[]{:S(2)}, u32[]{:S(2)}) collective-permute-start(bf16[512,256]{1,0:T(8,128)(2,1)S(1)} %get-tuple-element.95), channel_id=1, source_target_pairs={{4,0},{6,2},{8,4},{10,6},{12,8},{14,10},{16,12},{18,14},{20,16},{2... | collective-permute-start | bytes 786440 | tf_op jit(solution)/shard_map/ppermute | solution.py:52
  340.6 15.6 %collective-permute-start.13 = (bf16[512,256]{1,0:T(8,128)(2,1)S(1)}, bf16[512,256]{1,0:T(8,128)(2,1)}, u32[]{:S(2)}, u32[]{:S(2)}) collective-permute-start(bf16[512,256]{1,0:T(8,128)(2,1)S(1)} %get-tuple-element.96), channel_id=1, source_target_pairs={{2,0},{4,2},{6,4},{8,6},{10,8},{12,10},{14,12},{16,14},{18,16},{20... | collective-permute-start | bytes 786440 | tf_op jit(solution)/shard_map/ppermute | solution.py:52
  389.3 4.7 collective-permute-start.15
  (45 other events, 599.2 us)
Sparse Core Ops, SparseCore 0:
  10.4 97.0 all-gather.2
  282.7 92.1 reduce-scatter.1
  379.8 171.1 all-reduce.2

commit v13 on v10

--- a/solution.py
+++ b/solution.py
@@ -578,16 +578,17 @@
     columns = grad_kv.shape[0]
     every = parts.shape[1]
     size = columns + 2 * MORE
+    rows = 2 * LANES
     return pl.pallas_call(
         last_grads_kernel,
-        grid=(model // LANES,),
+        grid=(model // rows,),
         in_specs=[
-            pl.BlockSpec((tok, LANES), lambda i: (0, i)),
+            pl.BlockSpec((tok, rows), lambda i: (0, i)),
             pl.BlockSpec((columns, tok), lambda i: (0, 0)),
-            pl.BlockSpec((MORE, LANES), lambda i: (0, i)),
+            pl.BlockSpec((MORE, rows), lambda i: (0, i)),
             pl.BlockSpec(memory_space=pl.ANY),
         ],
-        out_specs=pl.BlockSpec((LANES, size), lambda i: (i, (every - size) // size)),
+        out_specs=pl.BlockSpec((rows, size), lambda i: (i, (every - size) // size)),
         out_shape=jax.ShapeDtypeStruct(parts.shape, BF16),
         input_output_aliases={3: 0},
         cost_estimate=pl.CostEstimate(
@@ -598,7 +599,7 @@
 
 def unpack_kernel(
     devices, in_ref, query_ref, key_ref, clip_ref,
-    wo_ref, wq_ref, wk_ref, wv_ref, sum_ref, cq_ref, ck_ref, peak_ref, sq_ref, sk_ref,
+    wo_ref, wq_ref, wk_ref, wv_ref, gain1_ref, gain2_ref, cq_ref, ck_ref, peak_ref, sq_ref, sk_ref,
 ):
     at = 0
     group = cq_ref.shape[1] // ck_ref.shape[1]
@@ -628,7 +629,10 @@
         size = target.shape[1]
         target[...] = in_ref[:, at : at + size].astype(F32)
         at += size
-    sum_ref[...] = jnp.transpose(in_ref[:, at : at + MORE].astype(F32))[: sum_ref.shape[0]]
+    lines = jnp.transpose(in_ref[:, at : at + MORE].astype(F32))
+    here = pl.ds(pl.multiple_of(pl.program_id(0) * LANES, LANES), LANES)
+    gain1_ref[here] = lines[0]
+    gain2_ref[here] = lines[1]
     cq_ref[...] = (query_ref[...].astype(F32) * sq_ref[...]).astype(BF16)
     ck_ref[...] = (key_ref[...].astype(F32) * sk_ref[...]).astype(BF16)
 
@@ -655,7 +659,8 @@
             wide,
             thin,
             thin,
-            pl.BlockSpec((8, LANES), lambda i: (0, i)),
+            pl.BlockSpec((total,), lambda i: (0,)),
+            pl.BlockSpec((total,), lambda i: (0,)),
             wide,
             thin,
             line,
@@ -666,7 +671,8 @@
             jax.ShapeDtypeStruct((total, width), F32),
             jax.ShapeDtypeStruct((total, narrow), F32),
             jax.ShapeDtypeStruct((total, narrow), F32),
-            jax.ShapeDtypeStruct((8, total), F32),
+            jax.ShapeDtypeStruct((total,), F32),
+            jax.ShapeDtypeStruct((total,), F32),
             jax.ShapeDtypeStruct((total, width), BF16),
             jax.ShapeDtypeStruct((total, narrow), BF16),
             jax.ShapeDtypeStruct((1, heads), F32),
@@ -836,7 +842,7 @@
     output = (hidden1 + combined(gated.astype(BF16), expert_out)).astype(BF16)
     grad_gate, grad_up, grad_down = jnp.split(sums[0].astype(F32), 3, axis=1)
     grad_down = grad_down.T
-    grad_wo, grad_wq, grad_wk, grad_wv, totals, clipped_query, clipped_key, head_peaks = unpack(
+    grad_wo, grad_wq, grad_wk, grad_wv, sum1, sum2, clipped_query, clipped_key, head_peaks = unpack(
         summed, w_query, w_key, clip_limit, dp_size
     )
     return (
@@ -846,8 +852,8 @@
         grad_wk,
         grad_wv,
         grad_wo,
-        totals[0],
-        totals[1],
+        sum1,
+        sum2,
         grad_gate[None],
         grad_up[None],
         grad_down[None],

time: 554 us -> 553 us (level)
  transfers between devices with their start and end apart: 24 -> 24, of which waited for: 12 -> 12; matrix products, arithmetic and copies ran while one was open for 7% -> 8% of each run, Pallas kernels for 22% -> 22%
where the time goes in v13:
time: 553 us; the launch traced here: 551 us
  waiting for transfers between devices  197 us (36%)
  Pallas kernels  141 us (25%)
  starting transfers between devices  78.2 us (14%)
  blocking collectives  67.8 us (12%)
  other arithmetic  25.4 us (5%)
  local copies, waits for them, and re-layouts  21.2 us (4%)
  between operations  14.4 us (3%)
  matrix products  5.71 us (1%)
    psum x1, waiting for transfers between devices, shards(): summed = lax.psum(parts, 'dp')  153 us
    all_to_all x1, blocking collectives, in_plane(): lax.all_to_all(rows, 'dp', 0, 0, tiled=True, axis_index_groups=plane_groups)  67.8 us
    all_to_all x5, starting transfers between devices, in_plane(): lax.all_to_all(rows, 'dp', 0, 0, tiled=True, axis_index_groups=plane_groups)  38.3 us
    ppermute x8, starting transfers between devices, passed_along(): lax.ppermute(value, 'dp', [(s, s + steps) for s in range(first, last)])  20.1 us
    pallas_call x1, Pallas kernels, attend_back(): pl.pallas_call(functools.partial(attend_back_kernel, group), out_shape=(j...  19.5 us
    pallas_call x1, Pallas kernels, expert_back(): pl.pallas_call(expert_kernel, grid=(segments,), in_specs=[*specs, weight,...  19.5 us
    ppermute x8, starting transfers between devices, swapped(): return lax.ppermute(array, 'tensor', [(0, 1), (1, 0)])  19.4 us
    all_to_all x5, waiting for transfers between devices, in_plane(): lax.all_to_all(rows, 'dp', 0, 0, tiled=True, axis_index_groups=plane_groups)  18.8 us
  transfers between devices with their start and end apart: 24, of which 12 were waited for; matrix products, arithmetic and copies ran while one was open for 8% of the time, Pallas kernels for 22%

profile of v13, /device:TPU:1, one launch (start us, length us, event | category | flops | bytes accessed | tf_op | source)
XLA Modules:
  0.0 550.9 jit_solution(4764753077558290013)
XLA Ops:
  17.6 8.6 %all-to-all-start = ((bf16[16,32,1536]{2,1,0:T(8,128)(2,1)}), bf16[16,32,1536]{2,1,0:T(8,128)(2,1)}, u32[]{:S(2)}, u32[]{:S(2)}) async-start(bf16[16,32,1536]{2,1,0:T(8,128)(2,1)} %bitcast.74), calls=%async_computation | async-start | bytes 3145728 | tf_op jit(solution)/shard_map/all_to_all | solution.py:750
  40.9 5.0 collective-permute-start.1
  53.7 4.9 shard_map.301
  58.7 14.8 %all-to-all-start.1 = ((bf16[16,64,1536]{2,1,0:T(8,128)(2,1)}), bf16[16,64,1536]{2,1,0:T(8,128)(2,1)}, u32[]{:S(2)}, u32[]{:S(2)}) async-start(bf16[16,64,1536]{2,1,0:T(8,128)(2,1)} %bitcast.69), calls=%async_computation.1 | async-start | bytes 6291456 | tf_op jit(solution)/shard_map/all_to_all | solution.py:750
  74.6 12.5 %shard_map.302 = (bf16[768,256]{1,0:T(8,128)(2,1)S(1)}, f32[12,256]{1,0:T(8,128)S(1)}, f32[12,256]{1,0:T(8,128)S(1)}) custom-call(bf16[768,256]{1,0:T(8,128)(2,1)S(1)} %copy-done.14, bf16[528,256]{1,0:T(8,128)(2,1)} %collective-permute-done.k4, bf16[528,256]{1,0:T(8,128)(2,1)} %collective-permute-done.1.k3, bf16[528,256]{1,0:T(8,128)(2,1)} %collective-permute-done.2.k2, ...), custom_call_target="tpu_custom_call" | custom-call | flops 1006632960 | bytes 2138112 | tf_op jit(solution)/shard_map/pallas_call | solution.py:124
  98.8 6.2 %shard_map.303 = bf16[1536,1536]{1,0:T(8,128)(2,1)} custom-call(bf16[1536,256]{1,0:T(8,128)(2,1)} %fusion.8.pick_ref.weight_ref, bf16[256,1536]{1,0:T(8,128)(2,1)} %multiply_convert_fusion.rows_ref), custom_call_target="tpu_custom_call" | custom-call | flops 1207959552 | bytes 5505024 | tf_op jit(solution)/shard_map/pallas_call | solution.py:216
  105.0 5.8 %all-to-all-done.1.g2_ref = bf16[16,64,1536]{2,1,0:T(8,128)(2,1)} async-done(((bf16[16,64,1536]{2,1,0:T(8,128)(2,1)}), bf16[16,64,1536]{2,1,0:T(8,128)(2,1)}, u32[]{:S(2)}, u32[]{:S(2)}) %all-to-all-start.1) | async-done | bytes 3145760 | tf_op jit(solution)/shard_map/all_to_all | solution.py:750
  110.8 6.5 %collective-permute-start.5 = (bf16[4,1536,768]{2,1,0:T(8,128)(2,1)}, bf16[4,1536,768]{2,1,0:T(8,128)(2,1)}, u32[]{:S(2)}, u32[]{:S(2)}) collective-permute-start(bf16[4,1536,768]{2,1,0:T(8,128)(2,1)} %bitcast.70), channel_id=1, source_target_pairs={{0,1},{1,0},{2,3},{3,2},{4,5},{5,4},{6,7},{7,6},{8,9},{9,8},{10,11... | collective-permute-start | bytes 28311560 | tf_op jit(solution)/shard_map/ppermute | solution.py:41
  117.3 67.8 %all_to_all.30.x_ref = bf16[16,96,1536]{2,1,0:T(8,128)(2,1)} all-to-all(bf16[16,96,1536]{2,1,0:T(8,128)(2,1)} %bitcast.66), channel_id=1, replica_groups={{0,2,4,6,8,10,12,14,16,18,20,22,24,26,28,30},{32,34,36,38,40,42,44,46,4..., dimensions={0} | all-to-all | bytes 9437184 | tf_op jit(solution)/shard_map/all_to_all | solution.py:750
  185.1 6.5 %shard_map.306 = bf16[16,32,1536]{2,1,0:T(8,128)(2,1)} custom-call(bf16[16,96,1536]{2,1,0:T(8,128)(2,1)} %all_to_all.30.x_ref, bf16[4,1536,768]{2,1,0:T(8,128)(2,1)} %bitcast.71, bf16[4,1536,768]{2,1,0:T(8,128)(2,1)} %collective-permute-done.5.peer_ref), custom_call_target="tpu_custom_call" | custom-call | flops 2415919104 | bytes 7864320 | tf_op jit(solution)/shard_map/pallas_call | solution.py:358
  196.0 19.5 %shard_map.305 = (bf16[16,96,1536]{2,1,0:T(8,128)(2,1)}, bf16[3,512,768]{2,1,0:T(8,128)(2,1)}, bf16[3,512,768]{2,1,0:T(8,128)(2,1)}) custom-call(bf16[16,96,1536]{2,1,0:T(8,128)(2,1)} %all_to_all.30.x_ref, bf16[16,32,1536]{2,1,0:T(8,128)(2,1)} %all-to-all-done.g1_ref, bf16[16,64,1536]{2,1,0:T(8,128)(2,1)} %all-to-all-done.1.g2_ref, ...), custom_call_target="tpu_custom_call" | custom-call | flops 12683575296 | bytes 28311552 | tf_op jit(solution)/shard_map/pallas_call | solution.py:424
  216.4 5.8 %all-to-all-start.4 = ((bf16[16,96,1536]{2,1,0:T(8,128)(2,1)}), bf16[16,96,1536]{2,1,0:T(8,128)(2,1)}, u32[]{:S(2)}, u32[]{:S(2)}) async-start(bf16[16,96,1536]{2,1,0:T(8,128)(2,1)} %get-tuple-element.78), calls=%async_computation.4 | async-start | bytes 9437184 | tf_op jit(solution)/shard_map/all_to_all | solution.py:750
  222.4 17.8 %shard_map.307 = (bf16[3,1536,768]{2,1,0:T(8,128)(2,1)}, bf16[3,1536,256]{2,1,0:T(8,128)(2,1)}, bf16[3,1536,256]{2,1,0:T(8,128)(2,1)}, bf16[3,1536,256]{2,1,0:T(8,128)(2,1)}, bf16[16,64,1536]{2,1,0:T(8,128)(2,1)}) custom-call(bf16[16,96,1536]{2,1,0:T(8,128)(2,1)} %all_to_all.30.x_ref, bf16[16,32,1536]{2,1,0:T(8,128)(2,1)} %all-to-all-done.g1_ref, ...), custom_call_target="tpu_custom_call" | custom-call | flops 10871635968 | bytes 31850496 | tf_op jit(solution)/shard_map/pallas_call | solution.py:489
  254.5 11.8 %shard_map.308 = bf16[4,1536,768]{2,1,0:T(8,128)(2,1)} custom-call(bf16[3,1536,768]{2,1,0:T(8,128)(2,1)} %get-tuple-element.81.own_ref, bf16[3,1536,256]{2,1,0:T(8,128)(2,1)} %collective-permute-done.6.refs_0_, bf16[3,1536,256]{2,1,0:T(8,128)(2,1)} %collective-permute-done.7.refs_1_, bf16[3,1536,256]{2,1,0:T(8,128)(2,1)} %collective-permute-done.8.refs_2_), custom_call_target="tpu_custom_call" | custom-call | flops 4718592 | bytes 28311552 | tf_op jit(solution)/shard_map/pallas_call | solution.py:530
  266.4 12.2 %all-to-all-done.4.rows_ref = bf16[16,96,1536]{2,1,0:T(8,128)(2,1)} async-done(((bf16[16,96,1536]{2,1,0:T(8,128)(2,1)}), bf16[16,96,1536]{2,1,0:T(8,128)(2,1)}, u32[]{:S(2)}, u32[]{:S(2)}) %all-to-all-start.4) | async-done | bytes 4718624 | tf_op jit(solution)/shard_map/all_to_all | solution.py:750
  278.6 5.1 shard_map.309
  283.6 6.4 %collective-permute-start.9 = (bf16[256,1536]{1,0:T(8,128)(2,1)}, bf16[256,1536]{1,0:T(8,128)(2,1)}, u32[]{:S(2)}, u32[]{:S(2)}) collective-permute-start(bf16[256,1536]{1,0:T(8,128)(2,1)} %shard_map.309), channel_id=1, source_target_pairs={{0,1},{1,0},{2,3},{3,2},{4,5},{5,4},{6,7},{7,6},{8,9},{9,8},{10,11... | collective-permute-start | bytes 2359304 | tf_op jit(solution)/shard_map/ppermute | solution.py:41
  302.1 19.5 %shard_map.310 = (bf16[768,256]{1,0:T(8,128)(2,1)S(1)}, bf16[512,256]{1,0:T(8,128)(2,1)S(1)}, bf16[512,256]{1,0:T(8,128)(2,1)S(1)}, bf16[512,256]{1,0:T(8,128)(2...) custom-call(bf16[768,256]{1,0:T(8,128)(2,1)S(1)} %copy-done.15, bf16[768,256]{1,0:T(8,128)(2,1)S(1)} %fusion.12.g_ref, ...), custom_call_target="tpu_custom_call" | custom-call | flops 125829120000 | bytes 3883008 | tf_op jit(solution)/shard_map/pallas_call | solution.py:189
  328.8 6.8 %shard_map.311._ = bf16[1536,2304]{1,0:T(8,128)(2,1)} custom-call(bf16[256,1536]{1,0:T(8,128)(2,1)} %copy-done.8, bf16[768,256]{1,0:T(8,128)(2,1)} %copy-done.12, bf16[768,256]{1,0:T(8,128)(2,1)} %copy-done.11, bf16[256,1536]{1,0:T(8,128)(2,1)} %copy-done.25), custom_call_target="tpu_custom_call" | custom-call | flops 1207959552 | bytes 4718592 | tf_op jit(solution)/shard_map/pallas_call | solution.py:559
  338.2 8.7 %collective-permute-done.11 = bf16[512,256]{1,0:T(8,128)(2,1)S(1)} collective-permute-done((bf16[512,256]{1,0:T(8,128)(2,1)S(1)}, bf16[512,256]{1,0:T(8,128)(2,1)S(1)}, u32[]{:S(2)}, u32[]{:S(2)}) %collective-permute-start.11) | collective-permute-done | bytes 262176 | tf_op jit(solution)/shard_map/ppermute | solution.py:51
  363.5 5.0 pad_maximum_fusion.rows_ref
  368.5 5.2 shard_map.313
  381.0 153.1 %all-reduce.3.cloned.1.call-done.in_ref = bf16[1536,2304]{1,0:T(8,128)(2,1)} async-done(((bf16[1536,2304]{1,0:T(8,128)(2,1)}), bf16[1536,2304]{1,0:T(8,128)(2,1)}) %all-reduce.3.cloned.1.call-update) | async-done | bytes 7077904 | tf_op jit(solution)/shard_map/psum | solution.py:840
  534.1 10.3 %shard_map.314 = (f32[768,1536]{1,0:T(8,128)}, f32[1536,768]{1,0:T(8,128)}, f32[1536,256]{1,0:T(8,128)}, f32[1536,256]{1,0:T(8,128)}, f32[1536]{0:T(1024)}, /*in...) custom-call(bf16[1536,2304]{1,0:T(8,128)(2,1)} %all-reduce.3.cloned.1.call-done.in_ref, ...), custom_call_target="tpu_custom_call" | custom-call | flops 3538944 | bytes 28311552 | tf_op jit(solution)/shard_map/pallas_call | solution.py:648
  (206 shorter events, 110.9 us)
Async XLA Ops:
  7.2 103.6 %all-gather.3.cloned.1.call-start = ((), (), s32[]{:S(2)}) async-start(), calls=%async_computation.9 | async-start | bytes 11796480 | tf_op jit(solution)/shard_map/all_gather | solution.py:772
  17.6 41.2 %all-to-all-start = ((bf16[16,32,1536]{2,1,0:T(8,128)(2,1)}), bf16[16,32,1536]{2,1,0:T(8,128)(2,1)}, u32[]{:S(2)}, u32[]{:S(2)}) async-start(bf16[16,32,1536]{2,1,0:T(8,128)(2,1)} %bitcast.74), calls=%async_computation | async-start | bytes 3145728 | tf_op jit(solution)/shard_map/all_to_all | solution.py:750
  36.8 21.7 %collective-permute-start = (bf16[528,256]{1,0:T(8,128)(2,1)}, bf16[528,256]{1,0:T(8,128)(2,1)}, u32[]{:S(2)}, u32[]{:S(2)}) collective-permute-start(bf16[528,256]{1,0:T(8,128)(2,1)} %get-tuple-element.70.k0), channel_id=1, source_target_pairs={{0,8},{2,10},{4,12},{6,14},{8,16},{10,18},{12,20},{14,22},{16,24},... | collective-permute-start | bytes 811016 | tf_op jit(solution)/shard_map/ppermute | solution.py:51
  40.9 17.7 %collective-permute-start.1 = (bf16[528,256]{1,0:T(8,128)(2,1)}, bf16[528,256]{1,0:T(8,128)(2,1)}, u32[]{:S(2)}, u32[]{:S(2)}) collective-permute-start(bf16[528,256]{1,0:T(8,128)(2,1)} %get-tuple-element.70.k0), channel_id=1, source_target_pairs={{0,6},{2,8},{4,10},{6,12},{8,14},{10,16},{12,18},{14,20},{16,22},{... | collective-permute-start | bytes 811016 | tf_op jit(solution)/shard_map/ppermute | solution.py:51
  45.9 12.7 %collective-permute-start.2 = (bf16[528,256]{1,0:T(8,128)(2,1)}, bf16[528,256]{1,0:T(8,128)(2,1)}, u32[]{:S(2)}, u32[]{:S(2)}) collective-permute-start(bf16[528,256]{1,0:T(8,128)(2,1)} %get-tuple-element.70.k0), channel_id=1, source_target_pairs={{0,4},{2,6},{4,8},{6,10},{8,12},{10,14},{12,16},{14,18},{16,20},{1... | collective-permute-start | bytes 811016 | tf_op jit(solution)/shard_map/ppermute | solution.py:51
  49.3 9.4 %collective-permute-start.3 = (bf16[528,256]{1,0:T(8,128)(2,1)}, bf16[528,256]{1,0:T(8,128)(2,1)}, u32[]{:S(2)}, u32[]{:S(2)}) collective-permute-start(bf16[528,256]{1,0:T(8,128)(2,1)} %get-tuple-element.70.k0), channel_id=1, source_target_pairs={{0,2},{2,4},{4,6},{6,8},{8,10},{10,12},{12,14},{14,16},{16,18},{18... | collective-permute-start | bytes 811016 | tf_op jit(solution)/shard_map/ppermute | solution.py:51
  58.7 52.1 %all-to-all-start.1 = ((bf16[16,64,1536]{2,1,0:T(8,128)(2,1)}), bf16[16,64,1536]{2,1,0:T(8,128)(2,1)}, u32[]{:S(2)}, u32[]{:S(2)}) async-start(bf16[16,64,1536]{2,1,0:T(8,128)(2,1)} %bitcast.69), calls=%async_computation.1 | async-start | bytes 6291456 | tf_op jit(solution)/shard_map/all_to_all | solution.py:750
  89.0 5.4 collective-permute-start.4
  110.8 74.3 %collective-permute-start.5 = (bf16[4,1536,768]{2,1,0:T(8,128)(2,1)}, bf16[4,1536,768]{2,1,0:T(8,128)(2,1)}, u32[]{:S(2)}, u32[]{:S(2)}) collective-permute-start(bf16[4,1536,768]{2,1,0:T(8,128)(2,1)} %bitcast.70), channel_id=1, source_target_pairs={{0,1},{1,0},{2,3},{3,2},{4,5},{5,4},{6,7},{7,6},{8,9},{9,8},{10,11... | collective-permute-start | bytes 28311560 | tf_op jit(solution)/shard_map/ppermute | solution.py:41
  191.6 24.8 %all-to-all-start.3 = ((bf16[16,32,1536]{2,1,0:T(8,128)(2,1)}), bf16[16,32,1536]{2,1,0:T(8,128)(2,1)}, u32[]{:S(2)}, u32[]{:S(2)}) async-start(bf16[16,32,1536]{2,1,0:T(8,128)(2,1)} %shard_map.306), calls=%async_computation.3 | async-start | bytes 3145728 | tf_op jit(solution)/shard_map/all_to_all | solution.py:750
  216.4 62.2 %all-to-all-start.4 = ((bf16[16,96,1536]{2,1,0:T(8,128)(2,1)}), bf16[16,96,1536]{2,1,0:T(8,128)(2,1)}, u32[]{:S(2)}, u32[]{:S(2)}) async-start(bf16[16,96,1536]{2,1,0:T(8,128)(2,1)} %get-tuple-element.78), calls=%async_computation.4 | async-start | bytes 9437184 | tf_op jit(solution)/shard_map/all_to_all | solution.py:750
  222.2 136.6 %reduce-scatter.2.cloned.1.call-start = ((), (), s32[]{:S(2)}) async-start(), calls=%async_computation.7 | async-start | bytes 11796480 | tf_op jit(solution)/shard_map/reduce_scatter | solution.py:797
  240.2 7.5 %collective-permute-start.6 = (bf16[3,1536,256]{2,1,0:T(8,128)(2,1)}, bf16[3,1536,256]{2,1,0:T(8,128)(2,1)}, u32[]{:S(2)}, u32[]{:S(2)}) collective-permute-start(bf16[3,1536,256]{2,1,0:T(8,128)(2,1)} %get-tuple-element.82), channel_id=1, source_target_pairs={{0,1},{1,0},{2,3},{3,2},{4,5},{5,4},{6,7},{7,6},{8,9},{9,8},{10,11... | collective-permute-start | bytes 7077896 | tf_op jit(solution)/shard_map/ppermute | solution.py:41
  243.3 7.9 %collective-permute-start.7 = (bf16[3,1536,256]{2,1,0:T(8,128)(2,1)}, bf16[3,1536,256]{2,1,0:T(8,128)(2,1)}, u32[]{:S(2)}, u32[]{:S(2)}) collective-permute-start(bf16[3,1536,256]{2,1,0:T(8,128)(2,1)} %get-tuple-element.83), channel_id=1, source_target_pairs={{0,1},{1,0},{2,3},{3,2},{4,5},{5,4},{6,7},{7,6},{8,9},{9,8},{10,11... | collective-permute-start | bytes 7077896 | tf_op jit(solution)/shard_map/ppermute | solution.py:41
  243.4 11.2 %collective-permute-start.8 = (bf16[3,1536,256]{2,1,0:T(8,128)(2,1)}, bf16[3,1536,256]{2,1,0:T(8,128)(2,1)}, u32[]{:S(2)}, u32[]{:S(2)}) collective-permute-start(bf16[3,1536,256]{2,1,0:T(8,128)(2,1)} %get-tuple-element.84), channel_id=1, source_target_pairs={{0,1},{1,0},{2,3},{3,2},{4,5},{5,4},{6,7},{7,6},{8,9},{9,8},{10,11... | collective-permute-start | bytes 7077896 | tf_op jit(solution)/shard_map/ppermute | solution.py:41
  283.6 11.9 %collective-permute-start.9 = (bf16[256,1536]{1,0:T(8,128)(2,1)}, bf16[256,1536]{1,0:T(8,128)(2,1)}, u32[]{:S(2)}, u32[]{:S(2)}) collective-permute-start(bf16[256,1536]{1,0:T(8,128)(2,1)} %shard_map.309), channel_id=1, source_target_pairs={{0,1},{1,0},{2,3},{3,2},{4,5},{5,4},{6,7},{7,6},{8,9},{9,8},{10,11... | collective-permute-start | bytes 2359304 | tf_op jit(solution)/shard_map/ppermute | solution.py:41
  290.9 67.9 %all-to-all-start.5 = ((bf16[16,64,1536]{2,1,0:T(8,128)(2,1)}), bf16[16,64,1536]{2,1,0:T(8,128)(2,1)}, u32[]{:S(2)}, u32[]{:S(2)}) async-start(bf16[16,64,1536]{2,1,0:T(8,128)(2,1)} %get-tuple-element.100), calls=%async_computation.6 | async-start | bytes 6291456 | tf_op jit(solution)/shard_map/all_to_all | solution.py:750
  295.5 238.6 %all-reduce.3.cloned.1.call-start = ((), (), s32[]{:S(2)}) async-start(), calls=%async_computation.8 | async-start | bytes 14155776 | tf_op jit(solution)/shard_map/psum | solution.py:840
  321.6 16.6 %collective-permute-start.10 = (bf16[512,256]{1,0:T(8,128)(2,1)S(1)}, bf16[512,256]{1,0:T(8,128)(2,1)S(1)}, u32[]{:S(2)}, u32[]{:S(2)}) collective-permute-start(bf16[512,256]{1,0:T(8,128)(2,1)S(1)} %get-tuple-element.88), channel_id=1, source_target_pairs={{8,0},{10,2},{12,4},{14,6},{16,8},{18,10},{20,12},{22,14},{24,16},... | collective-permute-start | bytes 786440 | tf_op jit(solution)/shard_map/ppermute | solution.py:51
  322.9 24.1 %collective-permute-start.11 = (bf16[512,256]{1,0:T(8,128)(2,1)S(1)}, bf16[512,256]{1,0:T(8,128)(2,1)S(1)}, u32[]{:S(2)}, u32[]{:S(2)}) collective-permute-start(bf16[512,256]{1,0:T(8,128)(2,1)S(1)} %get-tuple-element.89), channel_id=1, source_target_pairs={{6,0},{8,2},{10,4},{12,6},{14,8},{16,10},{18,12},{20,14},{22,16},{... | collective-permute-start | bytes 786440 | tf_op jit(solution)/shard_map/ppermute | solution.py:51
  324.2 22.8 %collective-permute-start.12 = (bf16[512,256]{1,0:T(8,128)(2,1)S(1)}, bf16[512,256]{1,0:T(8,128)(2,1)S(1)}, u32[]{:S(2)}, u32[]{:S(2)}) collective-permute-start(bf16[512,256]{1,0:T(8,128)(2,1)S(1)} %get-tuple-element.90), channel_id=1, source_target_pairs={{4,0},{6,2},{8,4},{10,6},{12,8},{14,10},{16,12},{18,14},{20,16},{2... | collective-permute-start | bytes 786440 | tf_op jit(solution)/shard_map/ppermute | solution.py:51
  325.5 21.5 %collective-permute-start.13 = (bf16[512,256]{1,0:T(8,128)(2,1)S(1)}, bf16[512,256]{1,0:T(8,128)(2,1)S(1)}, u32[]{:S(2)}, u32[]{:S(2)}) collective-permute-start(bf16[512,256]{1,0:T(8,128)(2,1)S(1)} %get-tuple-element.91), channel_id=1, source_target_pairs={{2,0},{4,2},{6,4},{8,6},{10,8},{12,10},{14,12},{16,14},{18,16},{20... | collective-permute-start | bytes 786440 | tf_op jit(solution)/shard_map/ppermute | solution.py:51
  350.2 2.6 collective-permute-start.14
  373.7 6.2 %collective-permute-start.15 = (bf16[256,1536]{1,0:T(8,128)(2,1)}, bf16[256,1536]{1,0:T(8,128)(2,1)S(1)}, u32[]{:S(2)}, u32[]{:S(2)}) collective-permute-start(bf16[256,1536]{1,0:T(8,128)(2,1)} %shard_map.313), channel_id=1, source_target_pairs={{0,1},{1,0},{2,3},{3,2},{4,5},{5,4},{6,7},{7,6},{8,9},{9,8},{10,11... | collective-permute-start | bytes 2359304 | tf_op jit(solution)/shard_map/ppermute | solution.py:41
  (48 other events, 403.6 us)
Sparse Core Ops, SparseCore 0:
  10.4 97.0 all-gather.2
  266.5 91.4 reduce-scatter.1
  362.9 171.1 all-reduce.2

commit v14 on v13

--- a/solution.py
+++ b/solution.py
@@ -100,22 +100,24 @@
     fill_bias(blocks, bias)
     kv_rows = (k0.shape[0] - AUX) // 2
 
-    def one_head(head, _):
-        at = pl.multiple_of(head // group * HD, HD)
+    def one_group(g, _):
+        at = pl.multiple_of(g * HD, HD)
         keys = all_keys(blocks, at)
         values = all_keys(blocks, kv_rows + at)
-        here = pl.ds(pl.multiple_of(head * HD, HD), HD)
-        scores = contract(keys, q_ref[here, :], TN) + bias[...]
-        peak = jnp.max(scores, axis=0, keepdims=True)
-        weight = jnp.exp(scores - peak)
-        total = jnp.sum(weight, axis=0, keepdims=True)
-        mixed = contract(values, weight.astype(BF16), NN) * (1.0 / total)
-        out_ref[here, :] = mixed.astype(BF16)
-        log_ref[pl.ds(head, 1), :] = peak + jnp.log(total)
-        peak_ref[pl.ds(head, 1), :] = peak
+        for j in range(group):
+            head = g * group + j
+            here = pl.ds(pl.multiple_of(head * HD, HD), HD)
+            scores = contract(keys, q_ref[here, :], TN) + bias[...]
+            peak = jnp.max(scores, axis=0, keepdims=True)
+            weight = jnp.exp(scores - peak)
+            total = jnp.sum(weight, axis=0, keepdims=True)
+            mixed = contract(values, weight.astype(BF16), NN) * (1.0 / total)
+            out_ref[here, :] = mixed.astype(BF16)
+            log_ref[pl.ds(head, 1), :] = peak + jnp.log(total)
+            peak_ref[pl.ds(head, 1), :] = peak
         return 0
 
-    lax.fori_loop(0, group * kv_rows // HD, one_head, 0)
+    lax.fori_loop(0, kv_rows // HD, one_group, 0)
 
 
 def attend(q, blocks, group):
@@ -153,8 +155,9 @@
         at = pl.multiple_of(g * HD, HD)
         keys = all_keys(blocks, at)
         values = all_keys(blocks, kv_rows + at)
-
-        def one_head(head, sums):
+        key_sum = value_sum = None
+        for j in range(group):
+            head = g * group + j
             start = pl.multiple_of(head * HD, HD)
             query, grad = (q_ref[pl.ds(start, HD), :], g_ref[pl.ds(start, HD), :])
             scores = contract(keys, query, TN) + bias[...]
@@ -162,18 +165,15 @@
             grad_probs = contract(values, grad, TN)
             delta = jnp.sum(probs * grad_probs, axis=0, keepdims=True)
             grad_scores = (probs * (grad_probs - delta)).astype(BF16)
+            key_part = contract(query, grad_scores, NT)
+            value_part = contract(grad, probs.astype(BF16), NT)
+            key_sum = key_part if key_sum is None else key_sum + key_part
+            value_sum = value_part if value_sum is None else value_sum + value_part
             turned = contract(keys, grad_scores, NN) * (HD**-0.5)
             first, second = (turned[:half], turned[half:])
             cosine, sine = (cos_ref[...], sin_ref[...])
             dq_ref[pl.ds(start, half), :] = (first * cosine + second * sine).astype(BF16)
             dq_ref[pl.ds(start + half, half), :] = (second * cosine - first * sine).astype(BF16)
-            return (
-                sums[0] + contract(query, grad_scores, NT),
-                sums[1] + contract(grad, probs.astype(BF16), NT),
-            )
-
-        zero = jnp.zeros(keys.shape, F32)
-        key_sum, value_sum = lax.fori_loop(g * group, (g + 1) * group, one_head, (zero, zero))
         for number, grad_ref in enumerate(grads):
             piece = slice(number * tok, (number + 1) * tok)
             grad_ref[pl.ds(at, HD), :] = key_sum[:, piece].astype(grad_ref.dtype)

time: 553 us -> 553 us (level)
  transfers between devices with their start and end apart: 24 -> 24, of which waited for: 12 -> 12; matrix products, arithmetic and copies ran while one was open for 8% -> 8% of each run, Pallas kernels for 22% -> 21%
where the time goes in v14:
time: 553 us; the launch traced here: 551 us
  waiting for transfers between devices  202 us (37%)
  Pallas kernels  136 us (25%)
  starting transfers between devices  78.1 us (14%)
  blocking collectives  67.8 us (12%)
  other arithmetic  25.4 us (5%)
  local copies, waits for them, and re-layouts  21.2 us (4%)
  between operations  14.4 us (3%)
  matrix products  5.7 us (1%)
    psum x1, waiting for transfers between devices, shards(): summed = lax.psum(parts, 'dp')  153 us
    all_to_all x1, blocking collectives, in_plane(): lax.all_to_all(rows, 'dp', 0, 0, tiled=True, axis_index_groups=plane_groups)  67.8 us
    all_to_all x5, starting transfers between devices, in_plane(): lax.all_to_all(rows, 'dp', 0, 0, tiled=True, axis_index_groups=plane_groups)  38.5 us
    ppermute x8, starting transfers between devices, passed_along(): lax.ppermute(value, 'dp', [(s, s + steps) for s in range(first, last)])  20.4 us
    all_to_all x5, waiting for transfers between devices, in_plane(): lax.all_to_all(rows, 'dp', 0, 0, tiled=True, axis_index_groups=plane_groups)  19.7 us
    pallas_call x1, Pallas kernels, expert_back(): pl.pallas_call(expert_kernel, grid=(segments,), in_specs=[*specs, weight,...  19.5 us
    ppermute x8, starting transfers between devices, swapped(): return lax.ppermute(array, 'tensor', [(0, 1), (1, 0)])  19.2 us
    pallas_call x1, Pallas kernels, expert_sums(): pl.pallas_call(expert_sums_kernel, grid=(segments,), in_specs=[*segment_s...  17.8 us
  transfers between devices with their start and end apart: 24, of which 12 were waited for; matrix products, arithmetic and copies ran while one was open for 8% of the time, Pallas kernels for 21%

profile of v14, /device:TPU:1, one launch (start us, length us, event | category | flops | bytes accessed | tf_op | source)
XLA Modules:
  0.0 550.7 jit_solution(65549314294479054)
XLA Ops:
  17.6 8.6 %all-to-all-start = ((bf16[16,32,1536]{2,1,0:T(8,128)(2,1)}), bf16[16,32,1536]{2,1,0:T(8,128)(2,1)}, u32[]{:S(2)}, u32[]{:S(2)}) async-start(bf16[16,32,1536]{2,1,0:T(8,128)(2,1)} %bitcast.74), calls=%async_computation | async-start | bytes 3145728 | tf_op jit(solution)/shard_map/all_to_all | solution.py:750
  40.9 5.0 collective-permute-start.1
  58.7 14.8 %all-to-all-start.1 = ((bf16[16,64,1536]{2,1,0:T(8,128)(2,1)}), bf16[16,64,1536]{2,1,0:T(8,128)(2,1)}, u32[]{:S(2)}, u32[]{:S(2)}) async-start(bf16[16,64,1536]{2,1,0:T(8,128)(2,1)} %bitcast.69), calls=%async_computation.1 | async-start | bytes 6291456 | tf_op jit(solution)/shard_map/all_to_all | solution.py:750
  74.6 11.6 %shard_map.302 = (bf16[768,256]{1,0:T(8,128)(2,1)S(1)}, f32[12,256]{1,0:T(8,128)S(1)}, f32[12,256]{1,0:T(8,128)S(1)}) custom-call(bf16[768,256]{1,0:T(8,128)(2,1)S(1)} %copy-done.14, bf16[528,256]{1,0:T(8,128)(2,1)} %collective-permute-done.k4, bf16[528,256]{1,0:T(8,128)(2,1)} %collective-permute-done.1.k3, bf16[528,256]{1,0:T(8,128)(2,1)} %collective-permute-done.2.k2, ...), custom_call_target="tpu_custom_call" | custom-call | flops 1006632960 | bytes 2138112 | tf_op jit(solution)/shard_map/pallas_call | solution.py:126
  97.9 6.2 %shard_map.303 = bf16[1536,1536]{1,0:T(8,128)(2,1)} custom-call(bf16[1536,256]{1,0:T(8,128)(2,1)} %fusion.8.pick_ref.weight_ref, bf16[256,1536]{1,0:T(8,128)(2,1)} %multiply_convert_fusion.rows_ref), custom_call_target="tpu_custom_call" | custom-call | flops 1207959552 | bytes 5505024 | tf_op jit(solution)/shard_map/pallas_call | solution.py:216
  104.2 6.6 %all-to-all-done.1.g2_ref = bf16[16,64,1536]{2,1,0:T(8,128)(2,1)} async-done(((bf16[16,64,1536]{2,1,0:T(8,128)(2,1)}), bf16[16,64,1536]{2,1,0:T(8,128)(2,1)}, u32[]{:S(2)}, u32[]{:S(2)}) %all-to-all-start.1) | async-done | bytes 3145760 | tf_op jit(solution)/shard_map/all_to_all | solution.py:750
  110.8 6.5 %collective-permute-start.5 = (bf16[4,1536,768]{2,1,0:T(8,128)(2,1)}, bf16[4,1536,768]{2,1,0:T(8,128)(2,1)}, u32[]{:S(2)}, u32[]{:S(2)}) collective-permute-start(bf16[4,1536,768]{2,1,0:T(8,128)(2,1)} %bitcast.70), channel_id=1, source_target_pairs={{0,1},{1,0},{2,3},{3,2},{4,5},{5,4},{6,7},{7,6},{8,9},{9,8},{10,11... | collective-permute-start | bytes 28311560 | tf_op jit(solution)/shard_map/ppermute | solution.py:41
  117.3 67.8 %all_to_all.30.x_ref = bf16[16,96,1536]{2,1,0:T(8,128)(2,1)} all-to-all(bf16[16,96,1536]{2,1,0:T(8,128)(2,1)} %bitcast.66), channel_id=1, replica_groups={{0,2,4,6,8,10,12,14,16,18,20,22,24,26,28,30},{32,34,36,38,40,42,44,46,4..., dimensions={0} | all-to-all | bytes 9437184 | tf_op jit(solution)/shard_map/all_to_all | solution.py:750
  185.1 6.5 %shard_map.306 = bf16[16,32,1536]{2,1,0:T(8,128)(2,1)} custom-call(bf16[16,96,1536]{2,1,0:T(8,128)(2,1)} %all_to_all.30.x_ref, bf16[4,1536,768]{2,1,0:T(8,128)(2,1)} %bitcast.71, bf16[4,1536,768]{2,1,0:T(8,128)(2,1)} %collective-permute-done.5.peer_ref), custom_call_target="tpu_custom_call" | custom-call | flops 2415919104 | bytes 7864320 | tf_op jit(solution)/shard_map/pallas_call | solution.py:358
  196.2 19.5 %shard_map.305 = (bf16[16,96,1536]{2,1,0:T(8,128)(2,1)}, bf16[3,512,768]{2,1,0:T(8,128)(2,1)}, bf16[3,512,768]{2,1,0:T(8,128)(2,1)}) custom-call(bf16[16,96,1536]{2,1,0:T(8,128)(2,1)} %all_to_all.30.x_ref, bf16[16,32,1536]{2,1,0:T(8,128)(2,1)} %all-to-all-done.g1_ref, bf16[16,64,1536]{2,1,0:T(8,128)(2,1)} %all-to-all-done.1.g2_ref, ...), custom_call_target="tpu_custom_call" | custom-call | flops 12683575296 | bytes 28311552 | tf_op jit(solution)/shard_map/pallas_call | solution.py:424
  216.4 5.8 %all-to-all-start.4 = ((bf16[16,96,1536]{2,1,0:T(8,128)(2,1)}), bf16[16,96,1536]{2,1,0:T(8,128)(2,1)}, u32[]{:S(2)}, u32[]{:S(2)}) async-start(bf16[16,96,1536]{2,1,0:T(8,128)(2,1)} %get-tuple-element.78), calls=%async_computation.4 | async-start | bytes 9437184 | tf_op jit(solution)/shard_map/all_to_all | solution.py:750
  222.2 17.8 %shard_map.307 = (bf16[3,1536,768]{2,1,0:T(8,128)(2,1)}, bf16[3,1536,256]{2,1,0:T(8,128)(2,1)}, bf16[3,1536,256]{2,1,0:T(8,128)(2,1)}, bf16[3,1536,256]{2,1,0:T(8,128)(2,1)}, bf16[16,64,1536]{2,1,0:T(8,128)(2,1)}) custom-call(bf16[16,96,1536]{2,1,0:T(8,128)(2,1)} %all_to_all.30.x_ref, bf16[16,32,1536]{2,1,0:T(8,128)(2,1)} %all-to-all-done.g1_ref, ...), custom_call_target="tpu_custom_call" | custom-call | flops 10871635968 | bytes 31850496 | tf_op jit(solution)/shard_map/pallas_call | solution.py:489
  254.3 11.8 %shard_map.308 = bf16[4,1536,768]{2,1,0:T(8,128)(2,1)} custom-call(bf16[3,1536,768]{2,1,0:T(8,128)(2,1)} %get-tuple-element.81.own_ref, bf16[3,1536,256]{2,1,0:T(8,128)(2,1)} %collective-permute-done.6.refs_0_, bf16[3,1536,256]{2,1,0:T(8,128)(2,1)} %collective-permute-done.7.refs_1_, bf16[3,1536,256]{2,1,0:T(8,128)(2,1)} %collective-permute-done.8.refs_2_), custom_call_target="tpu_custom_call" | custom-call | flops 4718592 | bytes 28311552 | tf_op jit(solution)/shard_map/pallas_call | solution.py:530
  266.2 12.4 %all-to-all-done.4.rows_ref = bf16[16,96,1536]{2,1,0:T(8,128)(2,1)} async-done(((bf16[16,96,1536]{2,1,0:T(8,128)(2,1)}), bf16[16,96,1536]{2,1,0:T(8,128)(2,1)}, u32[]{:S(2)}, u32[]{:S(2)}) %all-to-all-start.4) | async-done | bytes 4718624 | tf_op jit(solution)/shard_map/all_to_all | solution.py:750
  278.6 5.1 shard_map.309
  283.6 6.5 %collective-permute-start.9 = (bf16[256,1536]{1,0:T(8,128)(2,1)}, bf16[256,1536]{1,0:T(8,128)(2,1)}, u32[]{:S(2)}, u32[]{:S(2)}) collective-permute-start(bf16[256,1536]{1,0:T(8,128)(2,1)} %shard_map.309), channel_id=1, source_target_pairs={{0,1},{1,0},{2,3},{3,2},{4,5},{5,4},{6,7},{7,6},{8,9},{9,8},{10,11... | collective-permute-start | bytes 2359304 | tf_op jit(solution)/shard_map/ppermute | solution.py:41
  302.1 15.9 %shard_map.310 = (bf16[768,256]{1,0:T(8,128)(2,1)S(1)}, bf16[512,256]{1,0:T(8,128)(2,1)S(1)}, bf16[512,256]{1,0:T(8,128)(2,1)S(1)}, bf16[512,256]{1,0:T(8,128)(2...) custom-call(bf16[768,256]{1,0:T(8,128)(2,1)S(1)} %copy-done.15, bf16[768,256]{1,0:T(8,128)(2,1)S(1)} %fusion.12.g_ref, ...), custom_call_target="tpu_custom_call" | custom-call | flops 125829120000 | bytes 3883008 | tf_op jit(solution)/shard_map/pallas_call | solution.py:189
  325.4 6.8 %shard_map.311._ = bf16[1536,2304]{1,0:T(8,128)(2,1)} custom-call(bf16[256,1536]{1,0:T(8,128)(2,1)} %copy-done.8, bf16[768,256]{1,0:T(8,128)(2,1)} %copy-done.12, bf16[768,256]{1,0:T(8,128)(2,1)} %copy-done.11, bf16[256,1536]{1,0:T(8,128)(2,1)} %copy-done.25), custom_call_target="tpu_custom_call" | custom-call | flops 1207959552 | bytes 4718592 | tf_op jit(solution)/shard_map/pallas_call | solution.py:559
  332.2 6.1 %collective-permute-done.10 = bf16[512,256]{1,0:T(8,128)(2,1)S(1)} collective-permute-done((bf16[512,256]{1,0:T(8,128)(2,1)S(1)}, bf16[512,256]{1,0:T(8,128)(2,1)S(1)}, u32[]{:S(2)}, u32[]{:S(2)}) %collective-permute-start.10) | collective-permute-done | bytes 262176 | tf_op jit(solution)/shard_map/ppermute | solution.py:51
  338.3 8.7 %collective-permute-done.11 = bf16[512,256]{1,0:T(8,128)(2,1)S(1)} collective-permute-done((bf16[512,256]{1,0:T(8,128)(2,1)S(1)}, bf16[512,256]{1,0:T(8,128)(2,1)S(1)}, u32[]{:S(2)}, u32[]{:S(2)}) %collective-permute-start.11) | collective-permute-done | bytes 262176 | tf_op jit(solution)/shard_map/ppermute | solution.py:51
  363.4 5.0 pad_maximum_fusion.rows_ref
  368.3 5.2 shard_map.313
  380.8 153.1 %all-reduce.3.cloned.1.call-done.in_ref = bf16[1536,2304]{1,0:T(8,128)(2,1)} async-done(((bf16[1536,2304]{1,0:T(8,128)(2,1)}), bf16[1536,2304]{1,0:T(8,128)(2,1)}) %all-reduce.3.cloned.1.call-update) | async-done | bytes 7077904 | tf_op jit(solution)/shard_map/psum | solution.py:840
  533.9 10.3 %shard_map.314 = (f32[768,1536]{1,0:T(8,128)}, f32[1536,768]{1,0:T(8,128)}, f32[1536,256]{1,0:T(8,128)}, f32[1536,256]{1,0:T(8,128)}, f32[1536]{0:T(1024)}, /*in...) custom-call(bf16[1536,2304]{1,0:T(8,128)(2,1)} %all-reduce.3.cloned.1.call-done.in_ref, ...), custom_call_target="tpu_custom_call" | custom-call | flops 3538944 | bytes 28311552 | tf_op jit(solution)/shard_map/pallas_call | solution.py:648
  (206 shorter events, 112.9 us)
Async XLA Ops:
  7.2 103.6 %all-gather.3.cloned.1.call-start = ((), (), s32[]{:S(2)}) async-start(), calls=%async_computation.9 | async-start | bytes 11796480 | tf_op jit(solution)/shard_map/all_gather | solution.py:772
  17.6 41.2 %all-to-all-start = ((bf16[16,32,1536]{2,1,0:T(8,128)(2,1)}), bf16[16,32,1536]{2,1,0:T(8,128)(2,1)}, u32[]{:S(2)}, u32[]{:S(2)}) async-start(bf16[16,32,1536]{2,1,0:T(8,128)(2,1)} %bitcast.74), calls=%async_computation | async-start | bytes 3145728 | tf_op jit(solution)/shard_map/all_to_all | solution.py:750
  36.8 21.7 %collective-permute-start = (bf16[528,256]{1,0:T(8,128)(2,1)}, bf16[528,256]{1,0:T(8,128)(2,1)}, u32[]{:S(2)}, u32[]{:S(2)}) collective-permute-start(bf16[528,256]{1,0:T(8,128)(2,1)} %get-tuple-element.70.k0), channel_id=1, source_target_pairs={{0,8},{2,10},{4,12},{6,14},{8,16},{10,18},{12,20},{14,22},{16,24},... | collective-permute-start | bytes 811016 | tf_op jit(solution)/shard_map/ppermute | solution.py:51
  40.9 17.7 %collective-permute-start.1 = (bf16[528,256]{1,0:T(8,128)(2,1)}, bf16[528,256]{1,0:T(8,128)(2,1)}, u32[]{:S(2)}, u32[]{:S(2)}) collective-permute-start(bf16[528,256]{1,0:T(8,128)(2,1)} %get-tuple-element.70.k0), channel_id=1, source_target_pairs={{0,6},{2,8},{4,10},{6,12},{8,14},{10,16},{12,18},{14,20},{16,22},{... | collective-permute-start | bytes 811016 | tf_op jit(solution)/shard_map/ppermute | solution.py:51
  45.9 12.7 %collective-permute-start.2 = (bf16[528,256]{1,0:T(8,128)(2,1)}, bf16[528,256]{1,0:T(8,128)(2,1)}, u32[]{:S(2)}, u32[]{:S(2)}) collective-permute-start(bf16[528,256]{1,0:T(8,128)(2,1)} %get-tuple-element.70.k0), channel_id=1, source_target_pairs={{0,4},{2,6},{4,8},{6,10},{8,12},{10,14},{12,16},{14,18},{16,20},{1... | collective-permute-start | bytes 811016 | tf_op jit(solution)/shard_map/ppermute | solution.py:51
  49.3 9.4 %collective-permute-start.3 = (bf16[528,256]{1,0:T(8,128)(2,1)}, bf16[528,256]{1,0:T(8,128)(2,1)}, u32[]{:S(2)}, u32[]{:S(2)}) collective-permute-start(bf16[528,256]{1,0:T(8,128)(2,1)} %get-tuple-element.70.k0), channel_id=1, source_target_pairs={{0,2},{2,4},{4,6},{6,8},{8,10},{10,12},{12,14},{14,16},{16,18},{18... | collective-permute-start | bytes 811016 | tf_op jit(solution)/shard_map/ppermute | solution.py:51
  58.7 52.1 %all-to-all-start.1 = ((bf16[16,64,1536]{2,1,0:T(8,128)(2,1)}), bf16[16,64,1536]{2,1,0:T(8,128)(2,1)}, u32[]{:S(2)}, u32[]{:S(2)}) async-start(bf16[16,64,1536]{2,1,0:T(8,128)(2,1)} %bitcast.69), calls=%async_computation.1 | async-start | bytes 6291456 | tf_op jit(solution)/shard_map/all_to_all | solution.py:750
  88.1 5.4 collective-permute-start.4
  110.8 74.3 %collective-permute-start.5 = (bf16[4,1536,768]{2,1,0:T(8,128)(2,1)}, bf16[4,1536,768]{2,1,0:T(8,128)(2,1)}, u32[]{:S(2)}, u32[]{:S(2)}) collective-permute-start(bf16[4,1536,768]{2,1,0:T(8,128)(2,1)} %bitcast.70), channel_id=1, source_target_pairs={{0,1},{1,0},{2,3},{3,2},{4,5},{5,4},{6,7},{7,6},{8,9},{9,8},{10,11... | collective-permute-start | bytes 28311560 | tf_op jit(solution)/shard_map/ppermute | solution.py:41
  191.6 24.8 %all-to-all-start.3 = ((bf16[16,32,1536]{2,1,0:T(8,128)(2,1)}), bf16[16,32,1536]{2,1,0:T(8,128)(2,1)}, u32[]{:S(2)}, u32[]{:S(2)}) async-start(bf16[16,32,1536]{2,1,0:T(8,128)(2,1)} %shard_map.306), calls=%async_computation.3 | async-start | bytes 3145728 | tf_op jit(solution)/shard_map/all_to_all | solution.py:750
  216.4 62.2 %all-to-all-start.4 = ((bf16[16,96,1536]{2,1,0:T(8,128)(2,1)}), bf16[16,96,1536]{2,1,0:T(8,128)(2,1)}, u32[]{:S(2)}, u32[]{:S(2)}) async-start(bf16[16,96,1536]{2,1,0:T(8,128)(2,1)} %get-tuple-element.78), calls=%async_computation.4 | async-start | bytes 9437184 | tf_op jit(solution)/shard_map/all_to_all | solution.py:750
  222.2 136.4 %reduce-scatter.2.cloned.1.call-start = ((), (), s32[]{:S(2)}) async-start(), calls=%async_computation.7 | async-start | bytes 11796480 | tf_op jit(solution)/shard_map/reduce_scatter | solution.py:797
  240.1 7.5 %collective-permute-start.6 = (bf16[3,1536,256]{2,1,0:T(8,128)(2,1)}, bf16[3,1536,256]{2,1,0:T(8,128)(2,1)}, u32[]{:S(2)}, u32[]{:S(2)}) collective-permute-start(bf16[3,1536,256]{2,1,0:T(8,128)(2,1)} %get-tuple-element.82), channel_id=1, source_target_pairs={{0,1},{1,0},{2,3},{3,2},{4,5},{5,4},{6,7},{7,6},{8,9},{9,8},{10,11... | collective-permute-start | bytes 7077896 | tf_op jit(solution)/shard_map/ppermute | solution.py:41
  243.1 7.9 %collective-permute-start.7 = (bf16[3,1536,256]{2,1,0:T(8,128)(2,1)}, bf16[3,1536,256]{2,1,0:T(8,128)(2,1)}, u32[]{:S(2)}, u32[]{:S(2)}) collective-permute-start(bf16[3,1536,256]{2,1,0:T(8,128)(2,1)} %get-tuple-element.83), channel_id=1, source_target_pairs={{0,1},{1,0},{2,3},{3,2},{4,5},{5,4},{6,7},{7,6},{8,9},{9,8},{10,11... | collective-permute-start | bytes 7077896 | tf_op jit(solution)/shard_map/ppermute | solution.py:41
  243.2 11.2 %collective-permute-start.8 = (bf16[3,1536,256]{2,1,0:T(8,128)(2,1)}, bf16[3,1536,256]{2,1,0:T(8,128)(2,1)}, u32[]{:S(2)}, u32[]{:S(2)}) collective-permute-start(bf16[3,1536,256]{2,1,0:T(8,128)(2,1)} %get-tuple-element.84), channel_id=1, source_target_pairs={{0,1},{1,0},{2,3},{3,2},{4,5},{5,4},{6,7},{7,6},{8,9},{9,8},{10,11... | collective-permute-start | bytes 7077896 | tf_op jit(solution)/shard_map/ppermute | solution.py:41
  283.6 12.0 %collective-permute-start.9 = (bf16[256,1536]{1,0:T(8,128)(2,1)}, bf16[256,1536]{1,0:T(8,128)(2,1)}, u32[]{:S(2)}, u32[]{:S(2)}) collective-permute-start(bf16[256,1536]{1,0:T(8,128)(2,1)} %shard_map.309), channel_id=1, source_target_pairs={{0,1},{1,0},{2,3},{3,2},{4,5},{5,4},{6,7},{7,6},{8,9},{9,8},{10,11... | collective-permute-start | bytes 2359304 | tf_op jit(solution)/shard_map/ppermute | solution.py:41
  290.9 67.7 %all-to-all-start.5 = ((bf16[16,64,1536]{2,1,0:T(8,128)(2,1)}), bf16[16,64,1536]{2,1,0:T(8,128)(2,1)}, u32[]{:S(2)}, u32[]{:S(2)}) async-start(bf16[16,64,1536]{2,1,0:T(8,128)(2,1)} %get-tuple-element.100), calls=%async_computation.6 | async-start | bytes 6291456 | tf_op jit(solution)/shard_map/all_to_all | solution.py:750
  295.5 238.3 %all-reduce.3.cloned.1.call-start = ((), (), s32[]{:S(2)}) async-start(), calls=%async_computation.8 | async-start | bytes 14155776 | tf_op jit(solution)/shard_map/psum | solution.py:840
  318.0 20.2 %collective-permute-start.10 = (bf16[512,256]{1,0:T(8,128)(2,1)S(1)}, bf16[512,256]{1,0:T(8,128)(2,1)S(1)}, u32[]{:S(2)}, u32[]{:S(2)}) collective-permute-start(bf16[512,256]{1,0:T(8,128)(2,1)S(1)} %get-tuple-element.88), channel_id=1, source_target_pairs={{8,0},{10,2},{12,4},{14,6},{16,8},{18,10},{20,12},{22,14},{24,16},... | collective-permute-start | bytes 786440 | tf_op jit(solution)/shard_map/ppermute | solution.py:51
  319.3 27.6 %collective-permute-start.11 = (bf16[512,256]{1,0:T(8,128)(2,1)S(1)}, bf16[512,256]{1,0:T(8,128)(2,1)S(1)}, u32[]{:S(2)}, u32[]{:S(2)}) collective-permute-start(bf16[512,256]{1,0:T(8,128)(2,1)S(1)} %get-tuple-element.89), channel_id=1, source_target_pairs={{6,0},{8,2},{10,4},{12,6},{14,8},{16,10},{18,12},{20,14},{22,16},{... | collective-permute-start | bytes 786440 | tf_op jit(solution)/shard_map/ppermute | solution.py:51
  320.6 26.4 %collective-permute-start.12 = (bf16[512,256]{1,0:T(8,128)(2,1)S(1)}, bf16[512,256]{1,0:T(8,128)(2,1)S(1)}, u32[]{:S(2)}, u32[]{:S(2)}) collective-permute-start(bf16[512,256]{1,0:T(8,128)(2,1)S(1)} %get-tuple-element.90), channel_id=1, source_target_pairs={{4,0},{6,2},{8,4},{10,6},{12,8},{14,10},{16,12},{18,14},{20,16},{2... | collective-permute-start | bytes 786440 | tf_op jit(solution)/shard_map/ppermute | solution.py:51
  321.9 25.1 %collective-permute-start.13 = (bf16[512,256]{1,0:T(8,128)(2,1)S(1)}, bf16[512,256]{1,0:T(8,128)(2,1)S(1)}, u32[]{:S(2)}, u32[]{:S(2)}) collective-permute-start(bf16[512,256]{1,0:T(8,128)(2,1)S(1)} %get-tuple-element.91), channel_id=1, source_target_pairs={{2,0},{4,2},{6,4},{8,6},{10,8},{12,10},{14,12},{16,14},{18,16},{20... | collective-permute-start | bytes 786440 | tf_op jit(solution)/shard_map/ppermute | solution.py:51
  350.3 2.4 collective-permute-start.14
  373.5 6.1 %collective-permute-start.15 = (bf16[256,1536]{1,0:T(8,128)(2,1)}, bf16[256,1536]{1,0:T(8,128)(2,1)S(1)}, u32[]{:S(2)}, u32[]{:S(2)}) collective-permute-start(bf16[256,1536]{1,0:T(8,128)(2,1)} %shard_map.313), channel_id=1, source_target_pairs={{0,1},{1,0},{2,3},{3,2},{4,5},{5,4},{6,7},{7,6},{8,9},{9,8},{10,11... | collective-permute-start | bytes 2359304 | tf_op jit(solution)/shard_map/ppermute | solution.py:41
  (48 other events, 401.6 us)
Sparse Core Ops, SparseCore 0:
  10.4 97.0 all-gather.2
  266.3 91.4 reduce-scatter.1
  362.7 171.1 all-reduce.2
